TPU v7x, 32 devices: a whole 2x2x4 slice. The times are simulated.
32 devices in a mesh: agent: 4 (over y, x), dp: 8 (over z, core).
Axes of the slice: x: 2, y: 2, z: 4, core: 2. Of those that a mesh axis runs over, the one named last changes fastest.
Arguments:
- learn_obs: bfloat16 [4, 256, 16, 3456], P('agent', 'dp'), may hold values from -6 to 6
- own_obs: bfloat16 [4, 256, 3456], P('agent', 'dp'), may hold values from -6 to 6
- opp_obs: bfloat16 [4, 256, 3456], P('agent', 'dp'), may hold values from -6 to 6
- opponent: int32 [4, 256, 1], P('agent', 'dp'), may hold values from 0 to 3; in each aligned block of 32 rows (0 to 31, 32 to 63, ..., all dimensions but the last counted through in order) at most 32 rows name the same one
- actions: int32 [4, 256, 16], P('agent', 'dp'), may hold values from 0 to 17
- done: int32 [4, 256, 16], P('agent', 'dp'), may hold values 0 or 1
- rewards: float32 [4, 256, 16], P('agent', 'dp'), may hold values from -6 to 6
- behaviour: float32 [4, 256, 16], P('agent', 'dp'), may hold values from -4.5 to -1.5
- core_master: float32 [4, 256, 3712], P('agent', 'dp'), may hold values from -0.109375 to 0.109375
- core_mom: float32 [4, 256, 3712], P('agent', 'dp'), may hold values from -6 to 6
- core_vel: float32 [4, 256, 3712], P('agent', 'dp'), may hold values from 0.1 to 1
- head_master: float32 [4, 19, 256], P('agent'), may hold values from -0.375 to 0.375
- head_mom: float32 [4, 19, 256], P('agent'), may hold values from -6 to 6
- head_vel: float32 [4, 19, 256], P('agent'), may hold values from 0.1 to 1
- rates: float32 [4], P('agent'), may hold values from 0.01 to 0.1
Outputs:
- own_logits: float32 [4, 256, 18], P('agent', 'dp')
- opp_logits: bfloat16 [4, 256, 18], P('agent', 'dp')
- new_core: float32 [4, 256, 3712], P('agent', 'dp')
- new_core_mom: float32 [4, 256, 3712], P('agent', 'dp')
- new_core_vel: float32 [4, 256, 3712], P('agent', 'dp')
- new_head: float32 [4, 19, 256], P('agent')
- new_head_mom: float32 [4, 19, 256], P('agent')
- new_head_vel: float32 [4, 19, 256], P('agent')
Inputs may be any that keep to these rules, and one draw needn't show every extreme that they name: Among the 32 environments of one device (aligned blocks of the environment dimension), at most 32 face the same opponent agent, and some device reaches 32 in every draw.
All inputs are finite; a program needn't handle non-finite values. No bound on the sum of `done` on one device may be relied on, other than what follows from the above.
Results may differ from a plain program's by a relative error of at most 0.023.
Values may be sent and summed in bfloat16 or wider, within the bound.
No kernel may reach another device: no remote copies, remote signals or barrier semaphores. Data moves between devices by JAX's collectives and lax.ppermute only.
A program may use at most 64 MiB of HBM per device.

v0:
```python
import functools

import jax
import jax.numpy as jnp
from jax import lax
from jax.experimental import pallas as pl
from jax.experimental.pallas import tpu as pltpu
from jax.sharding import PartitionSpec as P


gamma_rate = 0.99
baseline_cost = 0.5
entropy_cost = 0.05
beta_first = 0.9
beta_second = 0.99
adam_eps = 1e-08

CORES = 2
SUBLANES = 32

LINE = 4
GATHER_FAR = ((0, 2), (3, 1), (1, 0), (2, 3))
GATHER_NEAR = ((0, 1), (3, 2), (1, 3), (2, 0))
GATHER_MID = ((1, 2), (2, 1))
GATHER_FORWARD = ((2, 3), (1, 0))
FAR_FROM = (1, 3, 0, 2)
NEAR_FROM = (2, 0, 3, 1)
LAST_FROM = (3, 2, 1, 0)
SELF_FROM = (0, 1, 2, 3)
ROLES = (LAST_FROM, NEAR_FROM, FAR_FROM, SELF_FROM)
SCATTER_FORWARD = ((3, 2), (0, 1))
SCATTER_NEAR = tuple((b, a) for a, b in GATHER_NEAR)
SCATTER_MID = ((1, 2), (2, 1))
SCATTER_FAR = tuple((b, a) for a, b in GATHER_FAR)


def dot(left, right, dims, precision=None):
    return lax.dot_general(
        left, right, (dims, ((), ())), preferred_element_type=jnp.float32, precision=precision
    )


NN = ((1,), (0,))
NT = ((1,), (1,))


def table(values, index):
    result = jnp.int32(values[0])
    for place, value in enumerate(values[1:], 1):
        result = jnp.where(index == place, jnp.int32(value), result)
    return result


def trace_gradients(out, boot, aux, action_count, length, scale):
    rows, lanes = out.shape
    row = lax.broadcasted_iota(jnp.int32, (rows, lanes), 0)
    step = lax.rem(lax.broadcasted_iota(jnp.int32, (1, lanes), 1), length)
    last = step == length - 1
    policy = row < action_count
    actions, done, rewards, behaviour = (aux[i : i + 1] for i in range(4))
    values = out[action_count : action_count + 1]
    totals = jnp.sum(jnp.where(policy, jnp.exp(out), 0.0), 0, keepdims=True)
    logp = out - jnp.log(totals)
    probs = jnp.where(policy, jnp.exp(logp), 0.0)
    chosen = (row == actions.astype(jnp.int32)).astype(jnp.float32)
    picked = jnp.sum(logp * chosen, 0, keepdims=True)
    ratio = jnp.minimum(1.0, jnp.exp(picked - behaviour))
    discount = gamma_rate * (1.0 - done)
    following = lambda x, end: jnp.where(last, end, pltpu.roll(x, lanes - 1, 1))
    delta = ratio * (rewards + discount * following(values, boot) - values)
    factor = jnp.where(last, 0.0, discount * ratio)
    reach = 1
    while reach < length:
        delta = delta + factor * pltpu.roll(delta, lanes - reach, 1)
        factor = factor * pltpu.roll(factor, lanes - reach, 1)
        reach *= 2
    targets = values + delta
    advantage = ratio * (rewards + discount * following(targets, boot) - values)
    entropy = -jnp.sum(jnp.where(policy, probs * logp, 0.0), 0, keepdims=True)
    grad_logits = scale * (
        -advantage * (chosen - probs) + entropy_cost * probs * (logp + entropy)
    )
    grad_value = scale * (-baseline_cost * (targets - values))
    return jnp.where(policy, grad_logits, jnp.where(row == action_count, grad_value, 0.0))


ANYWHERE = pl.BlockSpec(memory_space=pl.ANY)
LOCAL = pl.BlockSpec(memory_space=pltpu.VMEM)


def in_hbm(arrays):
    return [pltpu.with_memory_space_constraint(x, pltpu.HBM) for x in arrays]


def stage_kernel(*refs):
    count = (len(refs) - 2) // 1
    sources, staged, sems = refs[:count], refs[count], refs[count + 1]
    copies, at = [], 0
    for i, source in enumerate(sources):
        rows = source.shape[0]
        copies.append(pltpu.make_async_copy(source, staged.at[pl.ds(at, rows)], sems.at[i]))
        at += rows
    for copy in copies:
        copy.start()
    for copy in copies:
        copy.wait()


def stage(arrays):
    rows, width = sum(x.shape[0] for x in arrays), arrays[0].shape[1]
    return pl.pallas_call(
        stage_kernel,
        out_shape=jax.ShapeDtypeStruct((rows, width), arrays[0].dtype),
        in_specs=[ANYWHERE] * len(arrays),
        out_specs=LOCAL,
        scratch_shapes=[pltpu.SemaphoreType.DMA((len(arrays),))],
        compiler_params=pltpu.CompilerParams(vmem_limit_bytes=8 << 20),
        cost_estimate=pl.CostEstimate(
            flops=0, bytes_accessed=4 * rows * width, transcendentals=0
        ),
    )(*in_hbm(arrays))


def forward(frames, weights, head, width):
    pre_one = dot(weights[:, :width], frames, NT)
    first = jnp.maximum(pre_one, 0.0)
    first_bf = first.astype(jnp.bfloat16)
    pre_two = dot(weights[:, width:], first_bf, NN)
    second_bf = (jnp.maximum(pre_two, 0.0) + first).astype(jnp.bfloat16)
    return dot(head, second_bf, NN), pre_one, first_bf, pre_two, second_bf


def learner_kernel(cfg, *refs):
    pieces, heads, roles = cfg["pieces"], cfg["heads"], cfg["roles"]
    xs, refs = refs[0], refs[1:]
    w_refs, refs = refs[: len(pieces)], refs[len(pieces) :]
    aux_ref, head_ref, ws, ghead_ref, own_ref, order_ref, first_ref, refs = *refs[:7], refs[7:]
    lead, (gp, sw) = refs[:-2], refs[-2:]
    learn, width, units, length = cfg["learn"], cfg["width"], cfg["units"], cfg["length"]
    envs = learn // length
    place = lax.axis_index("dp")
    core, chip = lax.rem(place, CORES), lax.div(place, CORES)

    def piece_copy(i):
        rows, source, same, chips = pieces[i]
        if source is None:
            return pltpu.make_async_copy(w_refs[i], ws, sw.at[i]), None
        owner = core if same else 1 - core
        start = pl.multiple_of((table(source, chip) * CORES + owner) * rows, rows)
        live = None
        if chips is not None:
            live = functools.reduce(jnp.logical_or, [chip == one for one in chips])
        return pltpu.make_async_copy(w_refs[i], ws.at[pl.ds(start, rows)], sw.at[i]), live

    def each_piece(act):
        for i in range(len(pieces)):
            copy, live = piece_copy(i)
            if live is None:
                act(copy)
            else:
                pl.when(live)(functools.partial(act, copy))

    each_piece(lambda copy: copy.start())
    each_piece(lambda copy: copy.wait())

    out, pre_one, first_bf, pre_two, second_bf = forward(xs[...], ws[...], head_ref[...], width)
    own_ref[...] = out[: heads - 1, learn:].reshape(heads - 1, 1, envs)
    spread = lax.broadcasted_iota(jnp.int32, (envs, learn), 1) // length
    spread = (spread == lax.broadcasted_iota(jnp.int32, (envs, learn), 0)).astype(jnp.float32)
    boot = dot(out[:, learn:], spread, NN, lax.Precision.HIGHEST)[heads - 1 : heads]
    grad = trace_gradients(
        out[:, :learn], boot, aux_ref[...], heads - 1, length, 1.0 / length
    ).astype(jnp.bfloat16)
    ghead_ref[...] = dot(grad, second_bf[:, :learn], NT)
    grad_second = dot(head_ref[...].T, grad, NN)
    grad_two = jnp.where(pre_two[:, :learn] > 0, grad_second, 0.0).astype(jnp.bfloat16)
    grad_first = grad_second + dot(ws[:, width:].T, grad_two, NN)
    grad_one = jnp.where(pre_one[:, :learn] > 0, grad_first, 0.0).astype(jnp.bfloat16)
    first_ref[...] = first_bf[:, :learn]

    if roles is None:
        order_ref[:, :learn] = grad_one
        order_ref[:, learn:] = grad_two
        return
    gp[:, :learn] = grad_one
    gp[:, learn:] = grad_two
    rows = units // (len(roles) * CORES)
    order = []
    for role in roles:
        for same in (False, True):
            owner = core if same else 1 - core
            start = pl.multiple_of((table(role, chip) * CORES + owner) * rows, rows)
            order.append(gp[pl.ds(start, rows), :])
    order_ref[...] = jnp.concatenate(order[CORES:], 0)
    gradient_rows(jnp.concatenate(order[:CORES], 0), xs, first_ref, lead, learn, width, cfg["chunk"])


def gradient_rows(order, xs, first_ref, outs, learn, width, chunk):
    rows = outs[0].shape[0]

    def put(columns, value):
        value = value.astype(jnp.bfloat16)
        for i, out in enumerate(outs):
            out[:, columns] = value[i * rows : (i + 1) * rows]

    for start in range(0, width, chunk):
        columns = slice(start, start + chunk)
        put(columns, dot(order[:, :learn], xs[:learn, columns], NN))
    put(slice(width, None), dot(order[:, learn:], first_ref[...], NT))


def rest_kernel(cfg, xs, order_ref, first_ref, *outs):
    gradient_rows(order_ref[...], xs, first_ref, outs, cfg["learn"], cfg["width"], cfg["chunk"])


def column_chunk(width):
    return max(c for c in range(128, 1153, 128) if width % c == 0)


def learner(staged, piece_list, aux, head, cfg):
    total, width, units, learn = staged.shape[0], cfg["width"], cfg["units"], cfg["learn"]
    padded = head.shape[0]
    cfg = dict(cfg, chunk=column_chunk(width))
    roles = cfg["roles"]
    block = lambda rows: jax.ShapeDtypeStruct((rows, width + units), jnp.bfloat16)
    if roles is None:
        lead, rest, later = [], [block(units)], units
    else:
        rows = units // (len(roles) * CORES)
        lead, rest = [block(rows)] * CORES, [block(rows)] * (CORES * (len(roles) - 1))
        later = units - CORES * rows
    weights, ghead, own, order, first, *first_outs = pl.pallas_call(
        functools.partial(learner_kernel, cfg),
        out_shape=(
            block(units),
            jax.ShapeDtypeStruct((padded, units), jnp.float32),
            jax.ShapeDtypeStruct((cfg["heads"] - 1, 1, total - learn), jnp.float32),
            jax.ShapeDtypeStruct((later, 2 * learn), jnp.bfloat16),
            jax.ShapeDtypeStruct((units, learn), jnp.bfloat16),
            *lead,
        ),
        in_specs=[LOCAL] + [ANYWHERE] * len(piece_list) + [LOCAL] * 2,
        out_specs=(LOCAL,) * (5 + len(lead)),
        scratch_shapes=[
            pltpu.VMEM((units, 2 * learn), jnp.bfloat16),
            pltpu.SemaphoreType.DMA((len(piece_list),)),
        ],
        compiler_params=pltpu.CompilerParams(vmem_limit_bytes=32 << 20),
        cost_estimate=pl.CostEstimate(
            flops=4 * units * total * width, bytes_accessed=4 * total * width, transcendentals=0
        ),
        name="learner",
    )(staged, *piece_list, aux, head)
    rest_outs = pl.pallas_call(
        functools.partial(rest_kernel, cfg),
        out_shape=tuple(rest),
        in_specs=[LOCAL] * 3,
        out_specs=(LOCAL,) * len(rest),
        compiler_params=pltpu.CompilerParams(vmem_limit_bytes=32 << 20),
        cost_estimate=pl.CostEstimate(
            flops=2 * later * learn * width, bytes_accessed=2 * learn * width, transcendentals=0
        ),
        name="rest",
    )(staged, order, first)
    return weights, ghead, own, first_outs, list(rest_outs)


def opponent_kernel(cfg, count, *refs):
    frames, (weights, head, out, xs, sems) = refs[:count], refs[count:]
    envs = frames[0].shape[0]
    copies = [
        pltpu.make_async_copy(f, xs.at[pl.ds(i * envs, envs)], sems.at[i])
        for i, f in enumerate(frames)
    ]
    for copy in copies:
        copy.start()
    for copy in copies:
        copy.wait()
    result = forward(xs[...], weights[...], head[...], cfg["width"])[0].astype(jnp.bfloat16)
    for i in range(count):
        out[i] = result[:, i * envs : (i + 1) * envs]


def opponents(frames, weights, head, cfg):
    count, (envs, width) = len(frames), frames[0].shape
    return pl.pallas_call(
        functools.partial(opponent_kernel, cfg, count),
        out_shape=jax.ShapeDtypeStruct((count, head.shape[0], envs), jnp.bfloat16),
        in_specs=[ANYWHERE] * count + [LOCAL] * 2,
        out_specs=LOCAL,
        scratch_shapes=[
            pltpu.VMEM((count * envs, width), jnp.bfloat16),
            pltpu.SemaphoreType.DMA((count,)),
        ],
        compiler_params=pltpu.CompilerParams(vmem_limit_bytes=24 << 20),
        cost_estimate=pl.CostEstimate(
            flops=2 * cfg["units"] * count * envs * width,
            bytes_accessed=2 * count * envs * width,
            transcendentals=0,
        ),
        name="opponents",
    )(*frames, weights, head)


def adam_step(master, moment, second, grad, rate):
    moment = beta_first * moment + (1.0 - beta_first) * grad
    second = beta_second * second + (1.0 - beta_second) * grad * grad
    master = master - rate * moment / (jnp.sqrt(second) + adam_eps)
    return (master, moment, second)


def adam_kernel(parts, head_parts, cuts, *refs):
    rate = refs[0][0]
    parts, refs = refs[1 : 1 + parts], refs[1 + parts :]
    head_parts, refs = refs[:head_parts], refs[head_parts:]
    core, head, core_out, head_out = refs[:3], refs[3:6], refs[6:9], refs[9:12]
    stages, sems = refs[12:15], refs[15]
    copies = []
    for n, (start, stop) in enumerate(cuts):
        columns = slice(start, stop)
        grad = sum(part[:, columns].astype(jnp.float32) for part in parts)
        for i, value in enumerate(adam_step(*(x[:, columns] for x in core), grad, rate)):
            stages[i][:, columns] = value
            copies.append(
                pltpu.make_async_copy(
                    stages[i].at[:, columns], core_out[i].at[:, columns], sems.at[n, i]
                )
            )
            copies[-1].start()
    count = head[0].shape[0]
    sums = [part[:count] for part in head_parts]
    while len(sums) > 1:
        sums = [a + b for a, b in zip(sums[::2], sums[1::2])]
    grad = sums[0].reshape(head[0].shape)
    for out, value in zip(head_out, adam_step(*(x[...] for x in head), grad, rate)):
        out[...] = value
    for copy in copies:
        copy.wait()


def adam(rates, parts, head_parts, core, head):
    rows, width = core[0].shape
    tiles = width // 128
    cuts = [(128 * (tiles * n // 3), 128 * (tiles * (n + 1) // 3)) for n in range(3)]
    cuts[-1] = (cuts[-1][0], width)
    one = jax.ShapeDtypeStruct((rows, width), jnp.float32)
    small = jax.ShapeDtypeStruct(head[0].shape, jnp.float32)
    smem = pl.BlockSpec(memory_space=pltpu.SMEM)
    return pl.pallas_call(
        functools.partial(adam_kernel, len(parts), len(head_parts), cuts),
        out_shape=(one,) * 3 + (small,) * 3,
        in_specs=[smem] + [LOCAL] * (len(parts) + len(head_parts) + 6),
        out_specs=(ANYWHERE,) * 3 + (LOCAL,) * 3,
        scratch_shapes=[pltpu.VMEM((rows, width), jnp.float32)] * 3
        + [pltpu.SemaphoreType.DMA((len(cuts), 3))],
        compiler_params=pltpu.CompilerParams(vmem_limit_bytes=16 << 20),
        cost_estimate=pl.CostEstimate(
            flops=20 * rows * width, bytes_accessed=32 * rows * width, transcendentals=0
        ),
        name="adam",
    )(rates, *parts, *head_parts, *core, *head)


def per_device(
    learn_obs,
    own_obs,
    opp_obs,
    opponent,
    actions,
    done,
    rewards,
    behaviour,
    core_master,
    core_mom,
    core_vel,
    head_master,
    head_mom,
    head_vel,
    rates,
):
    envs, length, width = learn_obs.shape[1:]
    heads, units = head_master.shape[1:]
    action_count = heads - 1
    agents, members = lax.axis_size("agent"), lax.axis_size("dp")
    rows = core_master.shape[1]
    chips = members // CORES
    line = chips == LINE and members == LINE * CORES and units == members * rows
    wide = jnp.float32

    def along(x, pairs):
        return lax.ppermute(
            x, "dp", [(a * CORES + c, b * CORES + c) for a, b in pairs for c in range(CORES)]
        )

    def sibling(x):
        return lax.ppermute(x, "dp", [(i, i ^ 1) for i in range(members)])

    paired = agents & (agents - 1) == 0

    def other_agent(i, by):
        return i ^ by if paired else (i + by) % agents

    def swap(x, by):
        return lax.ppermute(x, "agent", [(i, other_agent(i, by)) for i in range(agents)])

    mine = core_master[0].astype(jnp.bfloat16)
    if line:
        far = along(mine, GATHER_FAR)
        near = along(mine, GATHER_NEAR)
        mid = along(mine, GATHER_MID)
        onward = along(far, GATHER_FORWARD)
        got = (("mine", mine, SELF_FROM, None), ("far", far, FAR_FROM, None),
               ("near", near, NEAR_FROM, None), ("mid", mid, LAST_FROM, (1, 2)),
               ("onward", onward, LAST_FROM, (0, 3)))
        piece_list = [g[1] for g in got] + [sibling(g[1]) for g in got]
        pieces = [(rows, g[2], True, g[3]) for g in got] + [(rows, g[2], False, g[3]) for g in got]
        roles = ROLES
    else:
        piece_list = [lax.all_gather(mine, "dp", axis=0, tiled=True)]
        pieces = [(units, None, True, None)]
        roles = None

    frames = [opp_obs[0]] + [swap(opp_obs[0], by) for by in range(1, agents)]

    aux = jnp.stack(
        [actions[0].astype(wide), done[0].astype(wide), rewards[0], behaviour[0]]
    ).reshape(4, envs * length)
    padded = -(-heads // SUBLANES) * SUBLANES
    head = jnp.pad(head_master[0].astype(jnp.bfloat16), ((0, padded - heads), (0, 0)))
    cfg = dict(pieces=pieces, heads=heads, width=width, units=units, length=length, roles=roles,
               learn=envs * length)
    me = lax.axis_index("agent")
    chosen = [
        opponent[0, :, 0][None] == other_agent(me, by if paired else agents - by)
        for by in range(agents)
    ]
    learn_rows, own_rows, aux, head, chosen = lax.optimization_barrier(
        (learn_obs[0].reshape(envs * length, width), own_obs[0], aux, head, chosen)
    )
    staged = stage([learn_rows, own_rows])
    weights, ghead, own, lead, rest = learner(staged, piece_list, aux, head, cfg)
    played = opponents(frames, weights, head, cfg)

    own_logits = jnp.transpose(own, (1, 2, 0))
    opp_logits = jnp.zeros((action_count, envs), jnp.bfloat16)
    for by in range(agents):
        answer = played[by]
        if by:
            back = by if paired else agents - by
            answer = swap(answer, back)
        opp_logits = jnp.where(chosen[by], answer[:action_count], opp_logits)

    if line:
        blocks = lead + rest
        send, keep = blocks[::CORES], [b.astype(wide) for b in blocks[1::CORES]]
        came = [sibling(b) for b in send]
        last, toward = [
            (k + c.astype(wide)).astype(jnp.bfloat16) for k, c in zip(keep[:2], came[:2])
        ]
        through = along(last, SCATTER_FORWARD).astype(wide)
        part_mid = along(last, SCATTER_MID)
        part_near = along(toward, SCATTER_NEAR)
        onward = (keep[2] + came[2].astype(wide) + through).astype(jnp.bfloat16)
        part_far = along(onward, SCATTER_FAR)
        core_parts = (blocks[-1], came[3], part_near, part_mid, part_far)
        ghead = ghead + sibling(ghead)
        one = along(ghead, ((0, 1), (1, 0), (2, 3), (3, 2)))
        two = along(ghead, ((0, 2), (2, 0), (1, 3), (3, 1)))
        three = along(ghead, ((0, 3), (3, 0), (1, 2), (2, 1)))
        head_parts = (ghead, one, two, three)
    else:
        core_parts = (lax.psum_scatter(rest[0], "dp", scatter_dimension=0, tiled=True),)
        head_parts = (lax.psum(ghead, "dp"),)
    by_row = lambda x: jnp.transpose(x, (1, 0, 2))
    new = adam(
        rates,
        core_parts,
        head_parts,
        (core_master[0], core_mom[0], core_vel[0]),
        (by_row(head_master), by_row(head_mom), by_row(head_vel)),
    )
    return (own_logits, opp_logits.T[None], *[x[None] for x in new[:3]], *map(by_row, new[3:]))


def solution(mesh):
    sharded, whole = P("agent", "dp", None), P("agent", None, None)

    return jax.shard_map(
        per_device,
        mesh=mesh,
        in_specs=(P("agent", "dp", None, None),) + (sharded,) * 10 + (whole,) * 3 + (P("agent"),),
        out_specs=(sharded,) * 5 + (whole,) * 3,
        check_vma=False,
    )
```

profile of v0, /device:TPU:0, one launch (start us, length us, event | category | flops | bytes accessed | tf_op | source)
XLA Modules:
  0.0 79.4 jit_solution(5766315332076537188)
XLA Ops:
  0.6 1.1 %bitcast_convert_fusion.refs_1_ = bf16[32,3712]{1,0:T(8,128)(2,1)S(1)} fusion(f32[1,32,3712]{2,1,0:T(8,128)} %param.23), kind=kLoop, calls=%fused_computation.19 | loop fusion | flops 118784 | bytes 712704 | tf_op jit(solution)/shard_map/convert_element_type | solution.py:406
  1.7 4.1 %collective-permute-start = (bf16[32,3712]{1,0:T(8,128)(2,1)S(1)}, bf16[32,3712]{1,0:T(8,128)(2,1)S(1)}, u32[]{:S(2)}, u32[]{:S(2)}) collective-permute-start(bf16[32,3712]{1,0:T(8,128)(2,1)S(1)} %bitcast_convert_fusion.refs_1_), channel_id=1, source_target_pairs={{0,4},{1,5},{6,2},{7,3},{2,0},{3,1},{4,6},{5,7},{8,12},{9,13},{14,... | collective-permute-start | bytes 712712 | tf_op jit(solution)/shard_map/ppermute | solution.py:391
  5.8 0.7 collective-permute-start.2
  6.5 5.5 %collective-permute-done.refs_2_ = bf16[32,3712]{1,0:T(8,128)(2,1)S(1)} collective-permute-done((bf16[32,3712]{1,0:T(8,128)(2,1)S(1)}, bf16[32,3712]{1,0:T(8,128)(2,1)S(1)}, u32[]{:S(2)}, u32[]{:S(2)}) %collective-permute-start) | collective-permute-done | bytes 237600 | tf_op jit(solution)/shard_map/ppermute | solution.py:391
  12.0 1.3 %collective-permute-start.3 = (bf16[32,3712]{1,0:T(8,128)(2,1)S(1)}, bf16[32,3712]{1,0:T(8,128)(2,1)S(1)}, u32[]{:S(2)}, u32[]{:S(2)}) collective-permute-start(bf16[32,3712]{1,0:T(8,128)(2,1)S(1)} %collective-permute-done.refs_2_), channel_id=1, source_target_pairs={{4,6},{5,7},{2,0},{3,1},{12,14},{13,15},{10,8},{11,9},{20,22},{21,... | collective-permute-start | bytes 712712 | tf_op jit(solution)/shard_map/ppermute | solution.py:391
  13.3 0.1 collective-permute-start.4
  13.4 0.7 convert_element_type.49
  14.1 0.1 copy.28
  14.2 0.1 stack.13
  14.2 0.7 convert_element_type.50
  14.9 0.1 copy.29
  15.0 0.1 stack.14
  15.1 0.8 copy.30
  15.9 0.1 stack.15
  16.0 0.8 copy.31
  16.7 0.1 stack.16
  16.8 0.5 collective-permute-start.5
  17.3 0.6 collective-permute-done.1.refs_3_
  17.9 0.5 collective-permute-start.7
  18.4 4.4 %collective-permute-done.3.refs_5_ = bf16[32,3712]{1,0:T(8,128)(2,1)S(1)} collective-permute-done((bf16[32,3712]{1,0:T(8,128)(2,1)S(1)}, bf16[32,3712]{1,0:T(8,128)(2,1)S(1)}, u32[]{:S(2)}, u32[]{:S(2)}) %collective-permute-start.3) | collective-permute-done | bytes 237600 | tf_op jit(solution)/shard_map/ppermute | solution.py:391
  22.9 0.7 copy.36
  23.6 0.7 compare_bitcast_fusion
  24.3 2.1 %shard_map.206.refs_0_.xs = bf16[544,3456]{1,0:T(8,128)(2,1)S(1)} custom-call(bf16[512,3456]{1,0:T(8,128)(2,1)} %bitcast.64, bf16[32,3456]{1,0:T(8,128)(2,1)} %bitcast.65), custom_call_target="tpu_custom_call" | custom-call | bytes 7520256 | tf_op jit(solution)/shard_map/pallas_call | solution.py:111
  26.4 1.6 %collective-permute-start.10 = (bf16[32,3456]{1,0:T(8,128)(2,1)S(1)}, bf16[32,3456]{1,0:T(8,128)(2,1)S(1)}, u32[]{:S(2)}, u32[]{:S(2)}) collective-permute-start(bf16[32,3456]{1,0:T(8,128)(2,1)S(1)} %bitcast.57), channel_id=1, source_target_pairs={{0,16},{8,24},{16,0},{24,8},{1,17},{9,25},{17,1},{25,9},{2,18},{10... | collective-permute-start | bytes 663560 | tf_op jit(solution)/shard_map/ppermute | solution.py:404
  27.9 1.4 %collective-permute-start.11 = (bf16[32,3456]{1,0:T(8,128)(2,1)S(1)}, bf16[32,3456]{1,0:T(8,128)(2,1)S(1)}, u32[]{:S(2)}, u32[]{:S(2)}) collective-permute-start(bf16[32,3456]{1,0:T(8,128)(2,1)S(1)} %bitcast.58), channel_id=1, source_target_pairs={{0,24},{8,16},{16,8},{24,0},{1,25},{9,17},{17,9},{25,1},{2,26},{10... | collective-permute-start | bytes 663560 | tf_op jit(solution)/shard_map/ppermute | solution.py:404
  29.4 0.5 collective-permute-start.9
  29.9 7.5 %learner.1 = (bf16[256,3712]{1,0:T(8,128)(2,1)S(1)}, f32[32,256]{1,0:T(8,128)S(1)}, f32[18,1,32]{2,1,0:T(1,128)}, bf16[192,1024]{1,0:T(8,128)(2,1)S(1)}, bf16[25...) custom-call(bf16[544,3456]{1,0:T(8,128)(2,1)S(1)} %shard_map.206.refs_0_.xs, ...), custom_call_target="tpu_custom_call" | custom-call | flops 1925185536 | bytes 7520256 | tf_op jit(solution)/shard_map/learner/pallas_call | solution.py:232
  37.5 0.5 collective-permute-start.18
  38.0 1.0 %rest.1 = (bf16[32,3712]{1,0:T(8,128)(2,1)S(1)}, bf16[32,3712]{1,0:T(8,128)(2,1)S(1)}, bf16[32,3712]{1,0:T(8,128)(2,1)S(1)}, bf16[32,3712]{1,0:T(8,128)(2,1)S(1)...) custom-call(bf16[544,3456]{1,0:T(8,128)(2,1)S(1)} %shard_map.206.refs_0_.xs, ...), custom_call_target="tpu_custom_call" | custom-call | flops 679477248 | bytes 3538944 | tf_op jit(solution)/shard_map/rest/pallas_call | solution.py:254
  39.1 0.1 collective-permute-start.20
  39.3 0.4 collective-permute-start.16
  39.7 0.5 collective-permute-done.9.refs_1_
  40.2 2.2 %opponents.1 = bf16[4,32,32]{2,1,0:T(8,128)(2,1)S(1)} custom-call(bf16[32,3456]{1,0:T(8,128)(2,1)S(1)} %bitcast.60, bf16[32,3456]{1,0:T(8,128)(2,1)S(1)} %collective-permute-done.9.refs_1_, bf16[32,3456]{1,0:T(8,128)(2,1)S(1)} %collective-permute-done.10.refs_2_, bf16[32,3456]{1,0:T(8,128)(2,1)S(1)} %collective-permute-done.11.refs_3_, ...), custom_call_target="tpu_custom_call" | custom-call | flops 226492416 | bytes 884736 | tf_op jit(solution)/shard_map/opponents/pallas_call | solution.py:286
  42.4 2.5 %collective-permute-start.12 = (bf16[32,32]{1,0:T(8,128)(2,1)S(1)}, bf16[32,32]{1,0:T(8,128)(2,1)S(1)}, u32[]{:S(2)}, u32[]{:S(2)}) collective-permute-start(bf16[32,32]{1,0:T(8,128)(2,1)S(1)} %get-tuple-element.62), channel_id=1, source_target_pairs={{0,24},{8,16},{16,8},{24,0},{1,25},{9,17},{17,9},{25,1},{2,26},{10... | collective-permute-start | bytes 6152 | tf_op jit(solution)/shard_map/ppermute | solution.py:404
  45.0 0.5 collective-permute-start.13
  45.5 0.6 collective-permute-start.14
  46.1 2.5 %collective-permute-start.21 = (bf16[32,3712]{1,0:T(8,128)(2,1)S(1)}, bf16[32,3712]{1,0:T(8,128)(2,1)S(1)}, u32[]{:S(2)}, u32[]{:S(2)}) collective-permute-start(bf16[32,3712]{1,0:T(8,128)(2,1)S(1)} %add_convert_fusion.1), channel_id=1, source_target_pairs={{6,4},{7,5},{0,2},{1,3},{14,12},{15,13},{8,10},{9,11},{22,20},{23,... | collective-permute-start | bytes 712712 | tf_op jit(solution)/shard_map/ppermute | solution.py:391
  48.8 0.1 collective-permute-start.24
  48.8 4.6 %collective-permute-done.21 = bf16[32,3712]{1,0:T(8,128)(2,1)S(1)} collective-permute-done((bf16[32,3712]{1,0:T(8,128)(2,1)S(1)}, bf16[32,3712]{1,0:T(8,128)(2,1)S(1)}, u32[]{:S(2)}, u32[]{:S(2)}) %collective-permute-start.21) | collective-permute-done | bytes 237600 | tf_op jit(solution)/shard_map/ppermute | solution.py:391
  53.4 3.5 %collective-permute-start.25 = (f32[32,256]{1,0:T(8,128)S(1)}, f32[32,256]{1,0:T(8,128)S(1)}, u32[]{:S(2)}, u32[]{:S(2)}) collective-permute-start(f32[32,256]{1,0:T(8,128)S(1)} %add.21.refs_6_), channel_id=1, source_target_pairs={{0,4},{1,5},{4,0},{5,1},{2,6},{3,7},{6,2},{7,3},{8,12},{9,13},{12,... | collective-permute-start | bytes 98312 | tf_op jit(solution)/shard_map/ppermute | solution.py:391
  56.9 0.1 add_convert_fusion
  57.1 0.7 collective-permute-start.19
  57.8 2.3 %collective-permute-start.17 = (bf16[32,3712]{1,0:T(8,128)(2,1)S(1)}, bf16[32,3712]{1,0:T(8,128)(2,1)S(1)}, u32[]{:S(2)}, u32[]{:S(2)}) collective-permute-start(bf16[32,3712]{1,0:T(8,128)(2,1)S(1)} %add_convert_fusion.2), channel_id=1, source_target_pairs={{2,0},{3,1},{4,6},{5,7},{6,2},{7,3},{0,4},{1,5},{10,8},{11,9},{12,... | collective-permute-start | bytes 712712 | tf_op jit(solution)/shard_map/ppermute | solution.py:391
  60.8 2.0 %collective-permute-start.26 = (f32[32,256]{1,0:T(8,128)S(1)}, f32[32,256]{1,0:T(8,128)S(1)}, u32[]{:S(2)}, u32[]{:S(2)}) collective-permute-start(f32[32,256]{1,0:T(8,128)S(1)} %add.21.refs_6_), channel_id=1, source_target_pairs={{0,6},{1,7},{6,0},{7,1},{2,4},{3,5},{4,2},{5,3},{8,14},{9,15},{14,... | collective-permute-start | bytes 98312 | tf_op jit(solution)/shard_map/ppermute | solution.py:391
  62.8 0.6 fusion.5
  63.4 10.5 %collective-permute-done.26.refs_9_ = f32[32,256]{1,0:T(8,128)S(1)} collective-permute-done((f32[32,256]{1,0:T(8,128)S(1)}, f32[32,256]{1,0:T(8,128)S(1)}, u32[]{:S(2)}, u32[]{:S(2)}) %collective-permute-start.26) | collective-permute-done | bytes 32800 | tf_op jit(solution)/shard_map/ppermute | solution.py:391
  73.9 3.6 %collective-permute-done.22.refs_5_ = bf16[32,3712]{1,0:T(8,128)(2,1)S(1)} collective-permute-done((bf16[32,3712]{1,0:T(8,128)(2,1)S(1)}, bf16[32,3712]{1,0:T(8,128)(2,1)S(1)}, u32[]{:S(2)}, u32[]{:S(2)}) %collective-permute-start.22) | collective-permute-done | bytes 237600 | tf_op jit(solution)/shard_map/ppermute | solution.py:391
  77.5 2.0 %adam.1 = (f32[32,3712]{1,0:T(8,128)}, f32[32,3712]{1,0:T(8,128)}, f32[32,3712]{1,0:T(8,128)}, f32[19,1,256]{2,1,0:T(1,128)}, f32[19,1,256]{2,1,0:T(1,128)}, /*index=5*/f32[19,1,256]{2,1,0:T(1,128)}) custom-call(f32[1]{0:T(128)S(6)} %copy.37.refs_0_, bf16[32,3712]{1,0:T(8,128)(2,1)S(1)} %get-tuple-element.47.refs_1_, ...), custom_call_target="tpu_custom_call" | custom-call | flops 2375680 | bytes 3801088 | tf_op jit(solution)/shard_map/adam/pallas_call | solution.py:349
  (46 shorter events, 0.4 us)
Async XLA Ops:
  1.7 10.3 %collective-permute-start = (bf16[32,3712]{1,0:T(8,128)(2,1)S(1)}, bf16[32,3712]{1,0:T(8,128)(2,1)S(1)}, u32[]{:S(2)}, u32[]{:S(2)}) collective-permute-start(bf16[32,3712]{1,0:T(8,128)(2,1)S(1)} %bitcast_convert_fusion.refs_1_), channel_id=1, source_target_pairs={{0,4},{1,5},{6,2},{7,3},{2,0},{3,1},{4,6},{5,7},{8,12},{9,13},{14,... | collective-permute-start | bytes 712712 | tf_op jit(solution)/shard_map/ppermute | solution.py:391
  5.8 12.1 %collective-permute-start.1 = (bf16[32,3712]{1,0:T(8,128)(2,1)S(1)}, bf16[32,3712]{1,0:T(8,128)(2,1)S(1)}, u32[]{:S(2)}, u32[]{:S(2)}) collective-permute-start(bf16[32,3712]{1,0:T(8,128)(2,1)S(1)} %bitcast_convert_fusion.refs_1_), channel_id=1, source_target_pairs={{0,2},{1,3},{6,4},{7,5},{2,6},{3,7},{4,0},{5,1},{8,10},{9,11},{14,... | collective-permute-start | bytes 712712 | tf_op jit(solution)/shard_map/ppermute | solution.py:391
  5.8 12.1 %collective-permute-start.2 = (bf16[32,3712]{1,0:T(8,128)(2,1)S(1)}, bf16[32,3712]{1,0:T(8,128)(2,1)S(1)}, u32[]{:S(2)}, u32[]{:S(2)}) collective-permute-start(bf16[32,3712]{1,0:T(8,128)(2,1)S(1)} %bitcast_convert_fusion.refs_1_), channel_id=1, source_target_pairs={{2,4},{3,5},{4,2},{5,3},{10,12},{11,13},{12,10},{13,11},{18,20},{1... | collective-permute-start | bytes 712712 | tf_op jit(solution)/shard_map/ppermute | solution.py:391
  12.0 10.8 %collective-permute-start.3 = (bf16[32,3712]{1,0:T(8,128)(2,1)S(1)}, bf16[32,3712]{1,0:T(8,128)(2,1)S(1)}, u32[]{:S(2)}, u32[]{:S(2)}) collective-permute-start(bf16[32,3712]{1,0:T(8,128)(2,1)S(1)} %collective-permute-done.refs_2_), channel_id=1, source_target_pairs={{4,6},{5,7},{2,0},{3,1},{12,14},{13,15},{10,8},{11,9},{20,22},{21,... | collective-permute-start | bytes 712712 | tf_op jit(solution)/shard_map/ppermute | solution.py:391
  13.3 13.0 %collective-permute-start.4 = (bf16[32,3712]{1,0:T(8,128)(2,1)S(1)}, bf16[32,3712]{1,0:T(8,128)(2,1)S(1)}, u32[]{:S(2)}, u32[]{:S(2)}) collective-permute-start(bf16[32,3712]{1,0:T(8,128)(2,1)S(1)} %bitcast_convert_fusion.refs_1_), channel_id=1, source_target_pairs={{0,1},{1,0},{2,3},{3,2},{4,5},{5,4},{6,7},{7,6},{8,9},{9,8},{10,11... | collective-permute-start | bytes 712712 | tf_op jit(solution)/shard_map/ppermute | solution.py:396
  16.8 11.1 %collective-permute-start.5 = (bf16[32,3712]{1,0:T(8,128)(2,1)S(1)}, bf16[32,3712]{1,0:T(8,128)(2,1)S(1)}, u32[]{:S(2)}, u32[]{:S(2)}) collective-permute-start(bf16[32,3712]{1,0:T(8,128)(2,1)S(1)} %collective-permute-done.refs_2_), channel_id=1, source_target_pairs={{0,1},{1,0},{2,3},{3,2},{4,5},{5,4},{6,7},{7,6},{8,9},{9,8},{10,11... | collective-permute-start | bytes 712712 | tf_op jit(solution)/shard_map/ppermute | solution.py:396
  17.9 11.5 %collective-permute-start.6 = (bf16[32,3712]{1,0:T(8,128)(2,1)S(1)}, bf16[32,3712]{1,0:T(8,128)(2,1)S(1)}, u32[]{:S(2)}, u32[]{:S(2)}) collective-permute-start(bf16[32,3712]{1,0:T(8,128)(2,1)S(1)} %collective-permute-done.1.refs_3_), channel_id=1, source_target_pairs={{0,1},{1,0},{2,3},{3,2},{4,5},{5,4},{6,7},{7,6},{8,9},{9,8},{10,11... | collective-permute-start | bytes 712712 | tf_op jit(solution)/shard_map/ppermute | solution.py:396
  17.9 12.0 %collective-permute-start.7 = (bf16[32,3712]{1,0:T(8,128)(2,1)S(1)}, bf16[32,3712]{1,0:T(8,128)(2,1)S(1)}, u32[]{:S(2)}, u32[]{:S(2)}) collective-permute-start(bf16[32,3712]{1,0:T(8,128)(2,1)S(1)} %collective-permute-done.2.refs_4_), channel_id=1, source_target_pairs={{0,1},{1,0},{2,3},{3,2},{4,5},{5,4},{6,7},{7,6},{8,9},{9,8},{10,11... | collective-permute-start | bytes 712712 | tf_op jit(solution)/shard_map/ppermute | solution.py:396
  22.8 7.1 %collective-permute-start.8 = (bf16[32,3712]{1,0:T(8,128)(2,1)S(1)}, bf16[32,3712]{1,0:T(8,128)(2,1)S(1)}, u32[]{:S(2)}, u32[]{:S(2)}) collective-permute-start(bf16[32,3712]{1,0:T(8,128)(2,1)S(1)} %collective-permute-done.3.refs_5_), channel_id=1, source_target_pairs={{0,1},{1,0},{2,3},{3,2},{4,5},{5,4},{6,7},{7,6},{8,9},{9,8},{10,11... | collective-permute-start | bytes 712712 | tf_op jit(solution)/shard_map/ppermute | solution.py:396
  24.3 2.1 %copy-start.3 = (bf16[1,32,3456]{2,1,0:T(8,128)(2,1)S(1)}, bf16[1,32,3456]{2,1,0:T(8,128)(2,1)}, u32[]{:S(2)}) copy-start(bf16[1,32,3456]{2,1,0:T(8,128)(2,1)} %param.17) | copy-start | bytes 663556
  26.4 12.8 %collective-permute-start.10 = (bf16[32,3456]{1,0:T(8,128)(2,1)S(1)}, bf16[32,3456]{1,0:T(8,128)(2,1)S(1)}, u32[]{:S(2)}, u32[]{:S(2)}) collective-permute-start(bf16[32,3456]{1,0:T(8,128)(2,1)S(1)} %bitcast.57), channel_id=1, source_target_pairs={{0,16},{8,24},{16,0},{24,8},{1,17},{9,25},{17,1},{25,9},{2,18},{10... | collective-permute-start | bytes 663560 | tf_op jit(solution)/shard_map/ppermute | solution.py:404
  27.9 11.3 %collective-permute-start.11 = (bf16[32,3456]{1,0:T(8,128)(2,1)S(1)}, bf16[32,3456]{1,0:T(8,128)(2,1)S(1)}, u32[]{:S(2)}, u32[]{:S(2)}) collective-permute-start(bf16[32,3456]{1,0:T(8,128)(2,1)S(1)} %bitcast.58), channel_id=1, source_target_pairs={{0,24},{8,16},{16,8},{24,0},{1,25},{9,17},{17,9},{25,1},{2,26},{10... | collective-permute-start | bytes 663560 | tf_op jit(solution)/shard_map/ppermute | solution.py:404
  29.4 10.8 %collective-permute-start.9 = (bf16[32,3456]{1,0:T(8,128)(2,1)S(1)}, bf16[32,3456]{1,0:T(8,128)(2,1)S(1)}, u32[]{:S(2)}, u32[]{:S(2)}) collective-permute-start(bf16[32,3456]{1,0:T(8,128)(2,1)S(1)} %bitcast.59), channel_id=1, source_target_pairs={{0,8},{8,0},{16,24},{24,16},{1,9},{9,1},{17,25},{25,17},{2,10},{10... | collective-permute-start | bytes 663560 | tf_op jit(solution)/shard_map/ppermute | solution.py:404
  37.4 7.5 %collective-permute-start.23 = (f32[32,256]{1,0:T(8,128)S(1)}, f32[32,256]{1,0:T(8,128)S(1)}, u32[]{:S(2)}, u32[]{:S(2)}) collective-permute-start(f32[32,256]{1,0:T(8,128)S(1)} %get-tuple-element.55), channel_id=1, source_target_pairs={{0,1},{1,0},{2,3},{3,2},{4,5},{5,4},{6,7},{7,6},{8,9},{9,8},{10,11... | collective-permute-start | bytes 98312 | tf_op jit(solution)/shard_map/ppermute | solution.py:396
  37.5 7.9 %collective-permute-start.18 = (bf16[32,3712]{1,0:T(8,128)(2,1)S(1)}, bf16[32,3712]{1,0:T(8,128)(2,1)S(1)}, u32[]{:S(2)}, u32[]{:S(2)}) collective-permute-start(bf16[32,3712]{1,0:T(8,128)(2,1)S(1)} %get-tuple-element.52), channel_id=1, source_target_pairs={{0,1},{1,0},{2,3},{3,2},{4,5},{5,4},{6,7},{7,6},{8,9},{9,8},{10,11... | collective-permute-start | bytes 712712 | tf_op jit(solution)/shard_map/ppermute | solution.py:396
  39.0 38.4 %copy-start = (f32[1,32,3712]{2,1,0:T(8,128)S(1)}, f32[1,32,3712]{2,1,0:T(8,128)}, u32[]{:S(2)}) copy-start(f32[1,32,3712]{2,1,0:T(8,128)} %param.23) | copy-start | bytes 1425412
  39.1 38.4 %copy-start.1 = (f32[1,32,3712]{2,1,0:T(8,128)S(1)}, f32[1,32,3712]{2,1,0:T(8,128)}, u32[]{:S(2)}) copy-start(f32[1,32,3712]{2,1,0:T(8,128)} %param.24) | copy-start | bytes 1425412
  39.1 38.4 %copy-start.2 = (f32[1,32,3712]{2,1,0:T(8,128)S(1)}, f32[1,32,3712]{2,1,0:T(8,128)}, u32[]{:S(2)}) copy-start(f32[1,32,3712]{2,1,0:T(8,128)} %param.25) | copy-start | bytes 1425412
  39.1 38.4 %copy-start.4 = (f32[1,19,256]{2,0,1:T(1,128)S(1)}, f32[1,19,256]{2,0,1:T(1,128)}, u32[]{:S(2)}) copy-start(f32[1,19,256]{2,0,1:T(1,128)} %param.26) | copy-start | bytes 58372
  39.1 38.3 %copy-start.5 = (f32[1,19,256]{2,0,1:T(1,128)S(1)}, f32[1,19,256]{2,0,1:T(1,128)}, u32[]{:S(2)}) copy-start(f32[1,19,256]{2,0,1:T(1,128)} %param.27) | copy-start | bytes 58372
  39.1 38.3 %copy-start.6 = (f32[1,19,256]{2,0,1:T(1,128)S(1)}, f32[1,19,256]{2,0,1:T(1,128)}, u32[]{:S(2)}) copy-start(f32[1,19,256]{2,0,1:T(1,128)} %param.28) | copy-start | bytes 58372
  39.1 9.6 %collective-permute-start.20 = (bf16[32,3712]{1,0:T(8,128)(2,1)S(1)}, bf16[32,3712]{1,0:T(8,128)(2,1)S(1)}, u32[]{:S(2)}, u32[]{:S(2)}) collective-permute-start(bf16[32,3712]{1,0:T(8,128)(2,1)S(1)} %get-tuple-element.54), channel_id=1, source_target_pairs={{0,1},{1,0},{2,3},{3,2},{4,5},{5,4},{6,7},{7,6},{8,9},{9,8},{10,11... | collective-permute-start | bytes 712712 | tf_op jit(solution)/shard_map/ppermute | solution.py:396
  39.3 6.9 %collective-permute-start.16 = (bf16[32,3712]{1,0:T(8,128)(2,1)S(1)}, bf16[32,3712]{1,0:T(8,128)(2,1)S(1)}, u32[]{:S(2)}, u32[]{:S(2)}) collective-permute-start(bf16[32,3712]{1,0:T(8,128)(2,1)S(1)} %get-tuple-element.50), channel_id=1, source_target_pairs={{0,1},{1,0},{2,3},{3,2},{4,5},{5,4},{6,7},{7,6},{8,9},{9,8},{10,11... | collective-permute-start | bytes 712712 | tf_op jit(solution)/shard_map/ppermute | solution.py:396
  42.4 14.6 %collective-permute-start.12 = (bf16[32,32]{1,0:T(8,128)(2,1)S(1)}, bf16[32,32]{1,0:T(8,128)(2,1)S(1)}, u32[]{:S(2)}, u32[]{:S(2)}) collective-permute-start(bf16[32,32]{1,0:T(8,128)(2,1)S(1)} %get-tuple-element.62), channel_id=1, source_target_pairs={{0,24},{8,16},{16,8},{24,0},{1,25},{9,17},{17,9},{25,1},{2,26},{10... | collective-permute-start | bytes 6152 | tf_op jit(solution)/shard_map/ppermute | solution.py:404
  45.0 12.2 %collective-permute-start.13 = (bf16[32,32]{1,0:T(8,128)(2,1)S(1)}, bf16[32,32]{1,0:T(8,128)(2,1)S(1)}, u32[]{:S(2)}, u32[]{:S(2)}) collective-permute-start(bf16[32,32]{1,0:T(8,128)(2,1)S(1)} %get-tuple-element.64), channel_id=1, source_target_pairs={{0,16},{8,24},{16,0},{24,8},{1,17},{9,25},{17,1},{25,9},{2,18},{10... | collective-permute-start | bytes 6152 | tf_op jit(solution)/shard_map/ppermute | solution.py:404
  45.5 12.4 %collective-permute-start.14 = (bf16[32,32]{1,0:T(8,128)(2,1)S(1)}, bf16[32,32]{1,0:T(8,128)(2,1)S(1)}, u32[]{:S(2)}, u32[]{:S(2)}) collective-permute-start(bf16[32,32]{1,0:T(8,128)(2,1)S(1)} %get-tuple-element.63), channel_id=1, source_target_pairs={{0,8},{8,0},{16,24},{24,16},{1,9},{9,1},{17,25},{25,17},{2,10},{10... | collective-permute-start | bytes 6152 | tf_op jit(solution)/shard_map/ppermute | solution.py:404
  46.1 7.3 %collective-permute-start.21 = (bf16[32,3712]{1,0:T(8,128)(2,1)S(1)}, bf16[32,3712]{1,0:T(8,128)(2,1)S(1)}, u32[]{:S(2)}, u32[]{:S(2)}) collective-permute-start(bf16[32,3712]{1,0:T(8,128)(2,1)S(1)} %add_convert_fusion.1), channel_id=1, source_target_pairs={{6,4},{7,5},{0,2},{1,3},{14,12},{15,13},{8,10},{9,11},{22,20},{23,... | collective-permute-start | bytes 712712 | tf_op jit(solution)/shard_map/ppermute | solution.py:391
  48.8 11.4 %collective-permute-start.24 = (f32[32,256]{1,0:T(8,128)S(1)}, f32[32,256]{1,0:T(8,128)S(1)}, u32[]{:S(2)}, u32[]{:S(2)}) collective-permute-start(f32[32,256]{1,0:T(8,128)S(1)} %add.21.refs_6_), channel_id=1, source_target_pairs={{0,2},{1,3},{2,0},{3,1},{4,6},{5,7},{6,4},{7,5},{8,10},{9,11},{10,... | collective-permute-start | bytes 98312 | tf_op jit(solution)/shard_map/ppermute | solution.py:391
  53.4 7.3 %collective-permute-start.25 = (f32[32,256]{1,0:T(8,128)S(1)}, f32[32,256]{1,0:T(8,128)S(1)}, u32[]{:S(2)}, u32[]{:S(2)}) collective-permute-start(f32[32,256]{1,0:T(8,128)S(1)} %add.21.refs_6_), channel_id=1, source_target_pairs={{0,4},{1,5},{4,0},{5,1},{2,6},{3,7},{6,2},{7,3},{8,12},{9,13},{12,... | collective-permute-start | bytes 98312 | tf_op jit(solution)/shard_map/ppermute | solution.py:391
  57.1 16.8 %collective-permute-start.15 = (bf16[32,3712]{1,0:T(8,128)(2,1)S(1)}, bf16[32,3712]{1,0:T(8,128)(2,1)S(1)}, u32[]{:S(2)}, u32[]{:S(2)}) collective-permute-start(bf16[32,3712]{1,0:T(8,128)(2,1)S(1)} %get-tuple-element.48), channel_id=1, source_target_pairs={{0,1},{1,0},{2,3},{3,2},{4,5},{5,4},{6,7},{7,6},{8,9},{9,8},{10,11... | collective-permute-start | bytes 712712 | tf_op jit(solution)/shard_map/ppermute | solution.py:396
  57.1 16.7 %collective-permute-start.19 = (bf16[32,3712]{1,0:T(8,128)(2,1)S(1)}, bf16[32,3712]{1,0:T(8,128)(2,1)S(1)}, u32[]{:S(2)}, u32[]{:S(2)}) collective-permute-start(bf16[32,3712]{1,0:T(8,128)(2,1)S(1)} %add_convert_fusion.1), channel_id=1, source_target_pairs={{2,4},{3,5},{4,2},{5,3},{10,12},{11,13},{12,10},{13,11},{18,20},{1... | collective-permute-start | bytes 712712 | tf_op jit(solution)/shard_map/ppermute | solution.py:391
  57.8 16.0 %collective-permute-start.17 = (bf16[32,3712]{1,0:T(8,128)(2,1)S(1)}, bf16[32,3712]{1,0:T(8,128)(2,1)S(1)}, u32[]{:S(2)}, u32[]{:S(2)}) collective-permute-start(bf16[32,3712]{1,0:T(8,128)(2,1)S(1)} %add_convert_fusion.2), channel_id=1, source_target_pairs={{2,0},{3,1},{4,6},{5,7},{6,2},{7,3},{0,4},{1,5},{10,8},{11,9},{12,... | collective-permute-start | bytes 712712 | tf_op jit(solution)/shard_map/ppermute | solution.py:391
  60.1 17.3 %collective-permute-start.22 = (bf16[32,3712]{1,0:T(8,128)(2,1)S(1)}, bf16[32,3712]{1,0:T(8,128)(2,1)S(1)}, u32[]{:S(2)}, u32[]{:S(2)}) collective-permute-start(bf16[32,3712]{1,0:T(8,128)(2,1)S(1)} %add_convert_fusion), channel_id=1, source_target_pairs={{4,0},{5,1},{2,6},{3,7},{0,2},{1,3},{6,4},{7,5},{12,8},{13,9},{10,... | collective-permute-start | bytes 712712 | tf_op jit(solution)/shard_map/ppermute | solution.py:391
  60.8 13.0 %collective-permute-start.26 = (f32[32,256]{1,0:T(8,128)S(1)}, f32[32,256]{1,0:T(8,128)S(1)}, u32[]{:S(2)}, u32[]{:S(2)}) collective-permute-start(f32[32,256]{1,0:T(8,128)S(1)} %add.21.refs_6_), channel_id=1, source_target_pairs={{0,6},{1,7},{6,0},{7,1},{2,4},{3,5},{4,2},{5,3},{8,14},{9,15},{14,... | collective-permute-start | bytes 98312 | tf_op jit(solution)/shard_map/ppermute | solution.py:391
where the time goes:
time: 79.9 us; the launch traced here: 79.4 us
  waiting for transfers between devices  29.7 us (37%)
  starting transfers between devices  26.6 us (33%)
  Pallas kernels  14.7 us (18%)
  other arithmetic  3.96 us (5%)
  local copies, waits for them, and re-layouts  2.81 us (4%)
  between operations  1.59 us (2%)
    ppermute x11, waiting for transfers between devices, along(): lax.ppermute(x, 'dp', [(a * CORES + c, b * CORES + c) for a, b in pairs f...  29.1 us
    ppermute x11, starting transfers between devices, along(): lax.ppermute(x, 'dp', [(a * CORES + c, b * CORES + c) for a, b in pairs f...  17.1 us
    pallas_call x1, Pallas kernels, learner(): pl.pallas_call(functools.partial(learner_kernel, cfg), out_shape=(block(u...  7.5 us
    ppermute x6, starting transfers between devices, swap(): lax.ppermute(x, 'agent', [(i, other_agent(i, by)) for i in range(agents)])  7.17 us
    unnamed x17, local copies, waits for them, and re-layouts  2.32 us
    ppermute x10, starting transfers between devices, sibling(): return lax.ppermute(x, 'dp', [(i, i ^ 1) for i in range(members)])  2.31 us
    pallas_call x1, Pallas kernels, opponents(): pl.pallas_call(functools.partial(opponent_kernel, cfg, count), out_shape=...  2.2 us
    pallas_call x1, Pallas kernels, stage(): pl.pallas_call(stage_kernel, out_shape=jax.ShapeDtypeStruct((rows, width)...  2.06 us
  transfers between devices with their start and end apart: 27, of which 7 were waited for; matrix products, arithmetic and copies ran while one was open for 7% of the time, Pallas kernels for 16%

commit v1 on v0

--- a/solution.py
+++ b/solution.py
@@ -92,65 +92,78 @@
     return [pltpu.with_memory_space_constraint(x, pltpu.HBM) for x in arrays]
 
 
-def stage_kernel(*refs):
-    count = (len(refs) - 2) // 1
-    sources, staged, sems = refs[:count], refs[count], refs[count + 1]
-    copies, at = [], 0
-    for i, source in enumerate(sources):
-        rows = source.shape[0]
-        copies.append(pltpu.make_async_copy(source, staged.at[pl.ds(at, rows)], sems.at[i]))
-        at += rows
+def stage_kernel(learn_ref, own_ref, *refs):
+    small, (staged, aux, head_out), local, sems = refs[:5], refs[5:8], refs[8:13], refs[13]
+    per_step, head_ref = local[:4], local[4]
+    rows = learn_ref.shape[0]
+    small_copies = [
+        pltpu.make_async_copy(a, b, sems.at[2 + i]) for i, (a, b) in enumerate(zip(small, local))
+    ]
+    for copy in small_copies:
+        copy.start()
+    copies = (
+        pltpu.make_async_copy(learn_ref, staged.at[pl.ds(0, rows)], sems.at[0]),
+        pltpu.make_async_copy(own_ref, staged.at[pl.ds(rows, own_ref.shape[0])], sems.at[1]),
+    )
     for copy in copies:
         copy.start()
+    length, envs = per_step[0].shape
+    lane = lax.broadcasted_iota(jnp.int32, (envs, rows), 1)
+    spread = (lane // length == lax.broadcasted_iota(jnp.int32, (envs, rows), 0)).astype(
+        jnp.float32
+    )
+    mask = lax.rem(lax.broadcasted_iota(jnp.int32, (length, rows), 1), length)
+    mask = mask == lax.broadcasted_iota(jnp.int32, (length, rows), 0)
+    for copy in small_copies:
+        copy.wait()
+    for i, ref in enumerate(per_step):
+        wide = dot(ref[...].astype(jnp.float32), spread, NN, lax.Precision.HIGHEST)
+        aux[i : i + 1] = jnp.sum(jnp.where(mask, wide, 0.0), 0, keepdims=True)
+    heads, _, units = head_ref.shape
+    head_out[...] = jnp.zeros_like(head_out)
+    head_out[:heads] = head_ref[...].reshape(heads, units).astype(jnp.bfloat16)
     for copy in copies:
         copy.wait()
 
 
-def stage(arrays):
-    rows, width = sum(x.shape[0] for x in arrays), arrays[0].shape[1]
+def stage(learn_rows, own_rows, per_step, head):
+    rows, width = learn_rows.shape
+    total = rows + own_rows.shape[0]
+    heads, _, units = head.shape
+    padded = -(-heads // SUBLANES) * SUBLANES
     return pl.pallas_call(
         stage_kernel,
-        out_shape=jax.ShapeDtypeStruct((rows, width), arrays[0].dtype),
-        in_specs=[ANYWHERE] * len(arrays),
-        out_specs=LOCAL,
-        scratch_shapes=[pltpu.SemaphoreType.DMA((len(arrays),))],
+        out_shape=(
+            jax.ShapeDtypeStruct((total, width), jnp.bfloat16),
+            jax.ShapeDtypeStruct((len(per_step), rows), jnp.float32),
+            jax.ShapeDtypeStruct((padded, units), jnp.bfloat16),
+        ),
+        in_specs=[ANYWHERE] * 7,
+        out_specs=(LOCAL,) * 3,
+        scratch_shapes=[pltpu.VMEM(x.shape, x.dtype) for x in (*per_step, head)]
+        + [pltpu.SemaphoreType.DMA((7,))],
         compiler_params=pltpu.CompilerParams(vmem_limit_bytes=8 << 20),
         cost_estimate=pl.CostEstimate(
-            flops=0, bytes_accessed=4 * rows * width, transcendentals=0
-        ),
-    )(*in_hbm(arrays))
-
-
-def forward(frames, weights, head, width):
-    pre_one = dot(weights[:, :width], frames, NT)
-    first = jnp.maximum(pre_one, 0.0)
-    first_bf = first.astype(jnp.bfloat16)
-    pre_two = dot(weights[:, width:], first_bf, NN)
-    second_bf = (jnp.maximum(pre_two, 0.0) + first).astype(jnp.bfloat16)
-    return dot(head, second_bf, NN), pre_one, first_bf, pre_two, second_bf
-
-
-def learner_kernel(cfg, *refs):
-    pieces, heads, roles = cfg["pieces"], cfg["heads"], cfg["roles"]
-    xs, refs = refs[0], refs[1:]
-    w_refs, refs = refs[: len(pieces)], refs[len(pieces) :]
-    aux_ref, head_ref, ws, ghead_ref, own_ref, order_ref, first_ref, refs = *refs[:7], refs[7:]
-    lead, (gp, sw) = refs[:-2], refs[-2:]
-    learn, width, units, length = cfg["learn"], cfg["width"], cfg["units"], cfg["length"]
-    envs = learn // length
+            flops=0, bytes_accessed=4 * total * width, transcendentals=0
+        ),
+        name="stage",
+    )(*in_hbm((learn_rows, own_rows, *per_step, head)))
+
+
+def place_pieces(pieces, w_refs, ws, sems):
     place = lax.axis_index("dp")
     core, chip = lax.rem(place, CORES), lax.div(place, CORES)
 
     def piece_copy(i):
         rows, source, same, chips = pieces[i]
         if source is None:
-            return pltpu.make_async_copy(w_refs[i], ws, sw.at[i]), None
+            return pltpu.make_async_copy(w_refs[i], ws, sems.at[i]), None
         owner = core if same else 1 - core
         start = pl.multiple_of((table(source, chip) * CORES + owner) * rows, rows)
         live = None
         if chips is not None:
             live = functools.reduce(jnp.logical_or, [chip == one for one in chips])
-        return pltpu.make_async_copy(w_refs[i], ws.at[pl.ds(start, rows)], sw.at[i]), live
+        return pltpu.make_async_copy(w_refs[i], ws.at[pl.ds(start, rows)], sems.at[i]), live
 
     def each_piece(act):
         for i in range(len(pieces)):
@@ -163,7 +176,69 @@
     each_piece(lambda copy: copy.start())
     each_piece(lambda copy: copy.wait())
 
-    out, pre_one, first_bf, pre_two, second_bf = forward(xs[...], ws[...], head_ref[...], width)
+
+def last_rows(pieces):
+    rows = CORES * pieces[0][0]
+    chip = lax.div(lax.axis_index("dp"), CORES)
+    return pl.ds(pl.multiple_of(table(LAST_FROM, chip) * rows, rows), rows)
+
+
+def early_kernel(pieces, width, xs, *refs):
+    w_refs, (ws, pre, sems) = refs[: len(pieces)], refs[len(pieces) :]
+    ws[last_rows(pieces), :] = jnp.zeros((CORES * pieces[0][0], ws.shape[1]), ws.dtype)
+    place_pieces(pieces, w_refs, ws, sems)
+    pre[...] = dot(ws[:, :width], xs[...], NT)
+
+
+def early(staged, pieces, piece_list, units):
+    total, width = staged.shape
+    return pl.pallas_call(
+        functools.partial(early_kernel, pieces, width),
+        out_shape=(
+            jax.ShapeDtypeStruct((units, width + units), jnp.bfloat16),
+            jax.ShapeDtypeStruct((units, total), jnp.float32),
+        ),
+        in_specs=[LOCAL] + [ANYWHERE] * len(pieces),
+        out_specs=(LOCAL,) * 2,
+        scratch_shapes=[pltpu.SemaphoreType.DMA((len(pieces),))],
+        compiler_params=pltpu.CompilerParams(vmem_limit_bytes=24 << 20),
+        cost_estimate=pl.CostEstimate(
+            flops=2 * units * total * width, bytes_accessed=4 * units * width, transcendentals=0
+        ),
+        name="early",
+    )(staged, *piece_list)
+
+
+def forward(pre_one, weights, head, width):
+    first = jnp.maximum(pre_one, 0.0)
+    first_bf = first.astype(jnp.bfloat16)
+    pre_two = dot(weights[:, width:], first_bf, NN)
+    second_bf = (jnp.maximum(pre_two, 0.0) + first).astype(jnp.bfloat16)
+    return dot(head, second_bf, NN), pre_one, first_bf, pre_two, second_bf
+
+
+def learner_kernel(cfg, *refs):
+    pieces, heads, roles = cfg["pieces"], cfg["heads"], cfg["roles"]
+    xs, refs = refs[0], refs[1:]
+    w_refs, refs = refs[: len(pieces)], refs[len(pieces) :]
+    aux_ref, head_ref, refs = refs[0], refs[1], refs[2:]
+    if roles is not None:
+        refs = refs[2:]
+    ws, pre, ghead_ref, own_ref, order_ref, first_ref, refs = *refs[:6], refs[6:]
+    lead, (gp, sw) = refs[:-2], refs[-2:]
+    learn, width, units, length = cfg["learn"], cfg["width"], cfg["units"], cfg["length"]
+    envs = learn // length
+    place = lax.axis_index("dp")
+    core, chip = lax.rem(place, CORES), lax.div(place, CORES)
+
+    place_pieces(pieces, w_refs, ws, sw)
+    if roles is None:
+        pre[...] = dot(ws[:, :width], xs[...], NT)
+    else:
+        late = last_rows(pieces)
+        pre[late, :] = dot(ws[late, :width], xs[...], NT)
+    pre_one = pre[...]
+    out, pre_one, first_bf, pre_two, second_bf = forward(pre_one, ws[...], head_ref[...], width)
     own_ref[...] = out[: heads - 1, learn:].reshape(heads - 1, 1, envs)
     spread = lax.broadcasted_iota(jnp.int32, (envs, learn), 1) // length
     spread = (spread == lax.broadcasted_iota(jnp.int32, (envs, learn), 0)).astype(jnp.float32)
@@ -217,30 +292,34 @@
     return max(c for c in range(128, 1153, 128) if width % c == 0)
 
 
-def learner(staged, piece_list, aux, head, cfg):
+def learner(staged, piece_list, aux, head, before, cfg):
     total, width, units, learn = staged.shape[0], cfg["width"], cfg["units"], cfg["learn"]
     padded = head.shape[0]
     cfg = dict(cfg, chunk=column_chunk(width))
     roles = cfg["roles"]
     block = lambda rows: jax.ShapeDtypeStruct((rows, width + units), jnp.bfloat16)
+    inputs = 3 + len(piece_list)
     if roles is None:
-        lead, rest, later = [], [block(units)], units
+        lead, rest, later, aliases = [], [block(units)], units, {}
     else:
         rows = units // (len(roles) * CORES)
         lead, rest = [block(rows)] * CORES, [block(rows)] * (CORES * (len(roles) - 1))
         later = units - CORES * rows
-    weights, ghead, own, order, first, *first_outs = pl.pallas_call(
+        aliases = {inputs: 0, inputs + 1: 1}
+    weights, _, ghead, own, order, first, *first_outs = pl.pallas_call(
         functools.partial(learner_kernel, cfg),
         out_shape=(
             block(units),
+            jax.ShapeDtypeStruct((units, total), jnp.float32),
             jax.ShapeDtypeStruct((padded, units), jnp.float32),
             jax.ShapeDtypeStruct((cfg["heads"] - 1, 1, total - learn), jnp.float32),
             jax.ShapeDtypeStruct((later, 2 * learn), jnp.bfloat16),
             jax.ShapeDtypeStruct((units, learn), jnp.bfloat16),
             *lead,
         ),
-        in_specs=[LOCAL] + [ANYWHERE] * len(piece_list) + [LOCAL] * 2,
-        out_specs=(LOCAL,) * (5 + len(lead)),
+        in_specs=[LOCAL] + [ANYWHERE] * len(piece_list) + [LOCAL] * (2 + len(before)),
+        out_specs=(LOCAL,) * (6 + len(lead)),
+        input_output_aliases=aliases,
         scratch_shapes=[
             pltpu.VMEM((units, 2 * learn), jnp.bfloat16),
             pltpu.SemaphoreType.DMA((len(piece_list),)),
@@ -250,7 +329,7 @@
             flops=4 * units * total * width, bytes_accessed=4 * total * width, transcendentals=0
         ),
         name="learner",
-    )(staged, *piece_list, aux, head)
+    )(staged, *piece_list, aux, head, *before)
     rest_outs = pl.pallas_call(
         functools.partial(rest_kernel, cfg),
         out_shape=tuple(rest),
@@ -266,7 +345,8 @@
 
 
 def opponent_kernel(cfg, count, *refs):
-    frames, (weights, head, out, xs, sems) = refs[:count], refs[count:]
+    frames, (weights, head), refs = refs[:count], refs[count : count + 2], refs[count + 2 :]
+    outs, (xs, sems) = refs[:count], refs[count:]
     envs = frames[0].shape[0]
     copies = [
         pltpu.make_async_copy(f, xs.at[pl.ds(i * envs, envs)], sems.at[i])
@@ -276,18 +356,20 @@
         copy.start()
     for copy in copies:
         copy.wait()
-    result = forward(xs[...], weights[...], head[...], cfg["width"])[0].astype(jnp.bfloat16)
-    for i in range(count):
-        out[i] = result[:, i * envs : (i + 1) * envs]
+    width = cfg["width"]
+    pre_one = dot(weights[:, :width], xs[...], NT)
+    result = forward(pre_one, weights[...], head[...], width)[0].astype(jnp.bfloat16)
+    for i, out in enumerate(outs):
+        out[...] = result[:, i * envs : (i + 1) * envs]
 
 
 def opponents(frames, weights, head, cfg):
     count, (envs, width) = len(frames), frames[0].shape
     return pl.pallas_call(
         functools.partial(opponent_kernel, cfg, count),
-        out_shape=jax.ShapeDtypeStruct((count, head.shape[0], envs), jnp.bfloat16),
+        out_shape=(jax.ShapeDtypeStruct((head.shape[0], envs), jnp.bfloat16),) * count,
         in_specs=[ANYWHERE] * count + [LOCAL] * 2,
-        out_specs=LOCAL,
+        out_specs=(LOCAL,) * count,
         scratch_shapes=[
             pltpu.VMEM((count * envs, width), jnp.bfloat16),
             pltpu.SemaphoreType.DMA((count,)),
@@ -302,6 +384,49 @@
     )(*frames, weights, head)
 
 
+def other_agent(i, by, agents):
+    return i ^ by if agents & (agents - 1) == 0 else (i + by) % agents
+
+
+def choose_kernel(*refs):
+    answers, ids, out = refs[:-2], refs[-2], refs[-1]
+    agents, me = len(answers), lax.axis_index("agent")
+    result = jnp.zeros(out.shape, jnp.float32)
+    for by, answer in enumerate(answers):
+        player = other_agent(me, by, agents)
+        result = jnp.where(ids[...] == player, answer[: out.shape[0]].astype(jnp.float32), result)
+    out[...] = result.astype(out.dtype)
+
+
+def choose(answers, ids, count):
+    return pl.pallas_call(
+        choose_kernel,
+        out_shape=jax.ShapeDtypeStruct((count, ids.shape[1]), jnp.bfloat16),
+        in_specs=[LOCAL] * (len(answers) + 1),
+        out_specs=LOCAL,
+        compiler_params=pltpu.CompilerParams(vmem_limit_bytes=2 << 20),
+        name="choose",
+    )(*answers, ids)
+
+
+def add_kernel(*refs):
+    refs[-1][...] = sum(x[...].astype(jnp.float32) for x in refs[:-1]).astype(refs[-1].dtype)
+
+
+def add(*arrays):
+    return pl.pallas_call(
+        add_kernel,
+        out_shape=jax.ShapeDtypeStruct(arrays[0].shape, arrays[0].dtype),
+        in_specs=[LOCAL] * len(arrays),
+        out_specs=LOCAL,
+        compiler_params=pltpu.CompilerParams(vmem_limit_bytes=4 << 20),
+        cost_estimate=pl.CostEstimate(
+            flops=arrays[0].size, bytes_accessed=2 * len(arrays) * arrays[0].size, transcendentals=0
+        ),
+        name="add",
+    )(*arrays)
+
+
 def adam_step(master, moment, second, grad, rate):
     moment = beta_first * moment + (1.0 - beta_first) * grad
     second = beta_second * second + (1.0 - beta_second) * grad * grad
@@ -310,7 +435,7 @@
 
 
 def adam_kernel(parts, head_parts, cuts, *refs):
-    rate = refs[0][0]
+    rate = refs[0][...]
     parts, refs = refs[1 : 1 + parts], refs[1 + parts :]
     head_parts, refs = refs[:head_parts], refs[head_parts:]
     core, head, core_out, head_out = refs[:3], refs[3:6], refs[6:9], refs[9:12]
@@ -345,11 +470,10 @@
     cuts[-1] = (cuts[-1][0], width)
     one = jax.ShapeDtypeStruct((rows, width), jnp.float32)
     small = jax.ShapeDtypeStruct(head[0].shape, jnp.float32)
-    smem = pl.BlockSpec(memory_space=pltpu.SMEM)
     return pl.pallas_call(
         functools.partial(adam_kernel, len(parts), len(head_parts), cuts),
         out_shape=(one,) * 3 + (small,) * 3,
-        in_specs=[smem] + [LOCAL] * (len(parts) + len(head_parts) + 6),
+        in_specs=[LOCAL] * (len(parts) + len(head_parts) + 7),
         out_specs=(ANYWHERE,) * 3 + (LOCAL,) * 3,
         scratch_shapes=[pltpu.VMEM((rows, width), jnp.float32)] * 3
         + [pltpu.SemaphoreType.DMA((len(cuts), 3))],
@@ -358,7 +482,7 @@
             flops=20 * rows * width, bytes_accessed=32 * rows * width, transcendentals=0
         ),
         name="adam",
-    )(rates, *parts, *head_parts, *core, *head)
+    )(rates.reshape(1, 1), *parts, *head_parts, *core, *head)
 
 
 def per_device(
@@ -385,7 +509,6 @@
     rows = core_master.shape[1]
     chips = members // CORES
     line = chips == LINE and members == LINE * CORES and units == members * rows
-    wide = jnp.float32
 
     def along(x, pairs):
         return lax.ppermute(
@@ -395,13 +518,8 @@
     def sibling(x):
         return lax.ppermute(x, "dp", [(i, i ^ 1) for i in range(members)])
 
-    paired = agents & (agents - 1) == 0
-
-    def other_agent(i, by):
-        return i ^ by if paired else (i + by) % agents
-
     def swap(x, by):
-        return lax.ppermute(x, "agent", [(i, other_agent(i, by)) for i in range(agents)])
+        return lax.ppermute(x, "agent", [(i, other_agent(i, by, agents)) for i in range(agents)])
 
     mine = core_master[0].astype(jnp.bfloat16)
     if line:
@@ -409,11 +527,16 @@
         near = along(mine, GATHER_NEAR)
         mid = along(mine, GATHER_MID)
         onward = along(far, GATHER_FORWARD)
-        got = (("mine", mine, SELF_FROM, None), ("far", far, FAR_FROM, None),
-               ("near", near, NEAR_FROM, None), ("mid", mid, LAST_FROM, (1, 2)),
-               ("onward", onward, LAST_FROM, (0, 3)))
-        piece_list = [g[1] for g in got] + [sibling(g[1]) for g in got]
-        pieces = [(rows, g[2], True, g[3]) for g in got] + [(rows, g[2], False, g[3]) for g in got]
+        first = (("mine", mine, SELF_FROM, None), ("far", far, FAR_FROM, None),
+                 ("near", near, NEAR_FROM, None))
+        final = (("mid", mid, LAST_FROM, (1, 2)), ("onward", onward, LAST_FROM, (0, 3)))
+
+        def with_siblings(group):
+            arrays = [g[1] for g in group] + [sibling(g[1]) for g in group]
+            places = [(rows, g[2], same, g[3]) for same in (True, False) for g in group]
+            return arrays, places
+
+        (first_list, first_pieces), (piece_list, pieces) = with_siblings(first), with_siblings(final)
         roles = ROLES
     else:
         piece_list = [lax.all_gather(mine, "dp", axis=0, tiled=True)]
@@ -422,48 +545,40 @@
 
     frames = [opp_obs[0]] + [swap(opp_obs[0], by) for by in range(1, agents)]
 
-    aux = jnp.stack(
-        [actions[0].astype(wide), done[0].astype(wide), rewards[0], behaviour[0]]
-    ).reshape(4, envs * length)
-    padded = -(-heads // SUBLANES) * SUBLANES
-    head = jnp.pad(head_master[0].astype(jnp.bfloat16), ((0, padded - heads), (0, 0)))
+    by_row = lambda x: jnp.transpose(x, (1, 0, 2))
     cfg = dict(pieces=pieces, heads=heads, width=width, units=units, length=length, roles=roles,
                learn=envs * length)
-    me = lax.axis_index("agent")
-    chosen = [
-        opponent[0, :, 0][None] == other_agent(me, by if paired else agents - by)
-        for by in range(agents)
-    ]
-    learn_rows, own_rows, aux, head, chosen = lax.optimization_barrier(
-        (learn_obs[0].reshape(envs * length, width), own_obs[0], aux, head, chosen)
+    staged, aux, head = stage(
+        learn_obs[0].reshape(envs * length, width),
+        own_obs[0],
+        [x[0].T for x in (actions, done, rewards, behaviour)],
+        by_row(head_master),
     )
-    staged = stage([learn_rows, own_rows])
-    weights, ghead, own, lead, rest = learner(staged, piece_list, aux, head, cfg)
+    before = ()
+    if line:
+        before = early(staged, first_pieces, first_list, units)
+    weights, ghead, own, lead, rest = learner(staged, piece_list, aux, head, before, cfg)
     played = opponents(frames, weights, head, cfg)
-
     own_logits = jnp.transpose(own, (1, 2, 0))
-    opp_logits = jnp.zeros((action_count, envs), jnp.bfloat16)
-    for by in range(agents):
-        answer = played[by]
-        if by:
-            back = by if paired else agents - by
-            answer = swap(answer, back)
-        opp_logits = jnp.where(chosen[by], answer[:action_count], opp_logits)
+
+    def undo(by):
+        there = other_agent(0, by, agents)
+        return next(b for b in range(agents) if other_agent(there, b, agents) == 0)
+
+    answers = [played[0]] + [swap(played[by], undo(by)) for by in range(1, agents)]
+    opp_logits = choose(answers, opponent[0].T, action_count)
 
     if line:
         blocks = lead + rest
-        send, keep = blocks[::CORES], [b.astype(wide) for b in blocks[1::CORES]]
+        send, keep = blocks[::CORES], blocks[1::CORES]
         came = [sibling(b) for b in send]
-        last, toward = [
-            (k + c.astype(wide)).astype(jnp.bfloat16) for k, c in zip(keep[:2], came[:2])
-        ]
-        through = along(last, SCATTER_FORWARD).astype(wide)
+        last, toward = add(keep[0], came[0]), add(keep[1], came[1])
+        through = along(last, SCATTER_FORWARD)
         part_mid = along(last, SCATTER_MID)
         part_near = along(toward, SCATTER_NEAR)
-        onward = (keep[2] + came[2].astype(wide) + through).astype(jnp.bfloat16)
-        part_far = along(onward, SCATTER_FAR)
-        core_parts = (blocks[-1], came[3], part_near, part_mid, part_far)
-        ghead = ghead + sibling(ghead)
+        part_far = along(add(keep[2], came[2], through), SCATTER_FAR)
+        core_parts = (keep[3], came[3], part_near, part_mid, part_far)
+        ghead = add(ghead, sibling(ghead))
         one = along(ghead, ((0, 1), (1, 0), (2, 3), (3, 2)))
         two = along(ghead, ((0, 2), (2, 0), (1, 3), (3, 1)))
         three = along(ghead, ((0, 3), (3, 0), (1, 2), (2, 1)))
@@ -471,7 +586,6 @@
     else:
         core_parts = (lax.psum_scatter(rest[0], "dp", scatter_dimension=0, tiled=True),)
         head_parts = (lax.psum(ghead, "dp"),)
-    by_row = lambda x: jnp.transpose(x, (1, 0, 2))
     new = adam(
         rates,
         core_parts,

time: 79.9 us -> 85.5 us (1.070)
  waiting for transfers between devices: 29.7 us -> 38.3 us
  other arithmetic: 3.96 us -> 1.05 us
  local copies, waits for them, and re-layouts: 2.81 us -> 0.05 us
  Pallas kernels: 14.7 us -> 16.6 us
  starting transfers between devices: 26.6 us -> 27.6 us
    ppermute x6, waiting for transfers between devices: 0.53 us -> 12.3 us  [swap(): lax.ppermute(x, 'agent', [(i, other_agent(i, by, agents)) for i in range(...]
    pallas_call x1 -> x7, Pallas kernels: 2.06 us -> 6.54 us  [the longest x1 3.57 us: early(): pl.pallas_call(functools.partial(early_kernel, pieces, width), out_shape=...]
    ppermute x11, waiting for transfers between devices: 29.1 us -> 24.7 us  [along(): lax.ppermute(x, 'dp', [(a * CORES + c, b * CORES + c) for a, b in pairs f...]
    pallas_call x1, Pallas kernels: 7.5 us -> 4.81 us  [learner(): pl.pallas_call(functools.partial(learner_kernel, cfg), out_shape=(block(u...]
    unnamed x17 -> x16, local copies, waits for them, and re-layouts: 2.32 us -> 0.05 us
    ppermute x6, starting transfers between devices: 7.17 us -> 9.1 us  [swap(): lax.ppermute(x, 'agent', [(i, other_agent(i, by, agents)) for i in range(...]
    convert_element_type x5 -> x0, other arithmetic: 1.62 us -> none  [the longest x1 0.7 us: per_device(): done[0].astype(wide)]
    ppermute x10, waiting for transfers between devices: 0.03 us -> 1.23 us  [sibling(): return lax.ppermute(x, 'dp', [(i, i ^ 1) for i in range(members)])]
  transfers between devices with their start and end apart: 27 -> 27, of which waited for: 7 -> 12; matrix products, arithmetic and copies ran while one was open for 7% -> 0% of each run, Pallas kernels for 16% -> 11%
where the time goes in v1:
time: 85.5 us; the launch traced here: 85.2 us
  waiting for transfers between devices  38.3 us (45%)
  starting transfers between devices  27.6 us (32%)
  Pallas kernels  16.6 us (19%)
  between operations  1.59 us (2%)
  other arithmetic  1.05 us (1%)
    ppermute x11, waiting for transfers between devices, along(): lax.ppermute(x, 'dp', [(a * CORES + c, b * CORES + c) for a, b in pairs f...  24.7 us
    ppermute x11, starting transfers between devices, along(): lax.ppermute(x, 'dp', [(a * CORES + c, b * CORES + c) for a, b in pairs f...  16.2 us
    ppermute x6, waiting for transfers between devices, swap(): lax.ppermute(x, 'agent', [(i, other_agent(i, by, agents)) for i in range(...  12.3 us
    ppermute x6, starting transfers between devices, swap(): lax.ppermute(x, 'agent', [(i, other_agent(i, by, agents)) for i in range(...  9.1 us
    pallas_call x1, Pallas kernels, learner(): pl.pallas_call(functools.partial(learner_kernel, cfg), out_shape=(block(u...  4.81 us
    pallas_call x1, Pallas kernels, early(): pl.pallas_call(functools.partial(early_kernel, pieces, width), out_shape=...  3.57 us
    ppermute x10, starting transfers between devices, sibling(): return lax.ppermute(x, 'dp', [(i, i ^ 1) for i in range(members)])  2.3 us
    pallas_call x1, Pallas kernels, opponents(): pl.pallas_call(functools.partial(opponent_kernel, cfg, count), out_shape=...  2.21 us
  transfers between devices with their start and end apart: 27, of which 12 were waited for; matrix products, arithmetic and copies ran while one was open for 0% of the time, Pallas kernels for 11%

profile of v1, /device:TPU:0, one launch (start us, length us, event | category | flops | bytes accessed | tf_op | source)
XLA Modules:
  0.0 85.2 jit_solution(10748175949426194527)
XLA Ops:
  0.6 1.1 %bitcast_convert_fusion.refs_0_ = bf16[32,3712]{1,0:T(8,128)(2,1)S(1)} fusion(f32[1,32,3712]{2,1,0:T(8,128)} %param.23), kind=kLoop, calls=%fused_computation | loop fusion | flops 118784 | bytes 712704 | tf_op jit(solution)/shard_map/convert_element_type | solution.py:524
  1.7 4.1 %collective-permute-start.1 = (bf16[32,3712]{1,0:T(8,128)(2,1)S(1)}, bf16[32,3712]{1,0:T(8,128)(2,1)S(1)}, u32[]{:S(2)}, u32[]{:S(2)}) collective-permute-start(bf16[32,3712]{1,0:T(8,128)(2,1)S(1)} %bitcast_convert_fusion.refs_0_), channel_id=1, source_target_pairs={{0,4},{1,5},{6,2},{7,3},{2,0},{3,1},{4,6},{5,7},{8,12},{9,13},{14,... | collective-permute-start | bytes 712712 | tf_op jit(solution)/shard_map/ppermute | solution.py:514
  5.8 0.7 collective-permute-start
  6.5 5.5 %collective-permute-done.1.refs_1_ = bf16[32,3712]{1,0:T(8,128)(2,1)S(1)} collective-permute-done((bf16[32,3712]{1,0:T(8,128)(2,1)S(1)}, bf16[32,3712]{1,0:T(8,128)(2,1)S(1)}, u32[]{:S(2)}, u32[]{:S(2)}) %collective-permute-start.1) | collective-permute-done | bytes 237600 | tf_op jit(solution)/shard_map/ppermute | solution.py:514
  12.0 1.3 %collective-permute-start.2 = (bf16[32,3712]{1,0:T(8,128)(2,1)S(1)}, bf16[32,3712]{1,0:T(8,128)(2,1)S(1)}, u32[]{:S(2)}, u32[]{:S(2)}) collective-permute-start(bf16[32,3712]{1,0:T(8,128)(2,1)S(1)} %collective-permute-done.1.refs_1_), channel_id=1, source_target_pairs={{4,6},{5,7},{2,0},{3,1},{12,14},{13,15},{10,8},{11,9},{20,22},{21,... | collective-permute-start | bytes 712712 | tf_op jit(solution)/shard_map/ppermute | solution.py:514
  13.3 0.1 collective-permute-start.6
  13.4 0.5 collective-permute-start.7
  13.9 4.0 %collective-permute-done.5.refs_2_ = bf16[32,3712]{1,0:T(8,128)(2,1)S(1)} collective-permute-done((bf16[32,3712]{1,0:T(8,128)(2,1)S(1)}, bf16[32,3712]{1,0:T(8,128)(2,1)S(1)}, u32[]{:S(2)}, u32[]{:S(2)}) %collective-permute-start.5) | collective-permute-done | bytes 237600 | tf_op jit(solution)/shard_map/ppermute | solution.py:514
  17.9 0.5 collective-permute-start.3
  18.4 4.4 %collective-permute-done.2.refs_2_ = bf16[32,3712]{1,0:T(8,128)(2,1)S(1)} collective-permute-done((bf16[32,3712]{1,0:T(8,128)(2,1)S(1)}, bf16[32,3712]{1,0:T(8,128)(2,1)S(1)}, u32[]{:S(2)}, u32[]{:S(2)}) %collective-permute-start.2) | collective-permute-done | bytes 237600 | tf_op jit(solution)/shard_map/ppermute | solution.py:514
  22.8 0.0 collective-permute-start.4
  22.8 2.1 %stage.1 = (bf16[544,3456]{1,0:T(8,128)(2,1)S(1)}, f32[4,512]{1,0:T(4,128)S(1)}, bf16[32,256]{1,0:T(8,128)(2,1)S(1)}) custom-call(bf16[512,3456]{1,0:T(8,128)(2,1)} %bitcast.47, bf16[32,3456]{1,0:T(8,128)(2,1)} %bitcast.48, s32[16,32]{1,0:T(8,128)} %bitcast.49, s32[16,32]{1,0:T(8,128)} %bitcast.50, f32[16,32]{1,0:T(8,128)} %bitcast.51, f32[16,32]{1,0:T(8,128)} %bitcast.52, ...), custom_call_target="tpu_custom_call" | custom-call | bytes 7520256 | tf_op jit(solution)/shard_map/stage/pallas_call | solution.py:134
  25.0 3.6 %early.1 = (bf16[256,3712]{1,0:T(8,128)(2,1)S(1)}, f32[256,544]{1,0:T(8,128)S(1)}) custom-call(bf16[544,3456]{1,0:T(8,128)(2,1)S(1)} %get-tuple-element.36.xs.refs_0_, bf16[32,3712]{1,0:T(8,128)(2,1)S(1)} %bitcast_convert_fusion.refs_0_, bf16[32,3712]{1,0:T(8,128)(2,1)S(1)} %collective-permute-done.1.refs_1_, ...), custom_call_target="tpu_custom_call" | custom-call | flops 962592768 | bytes 3538944 | tf_op jit(solution)/shard_map/early/pallas_call | solution.py:195
  28.6 4.8 %learner.1 = (bf16[256,3712]{1,0:T(8,128)(2,1)S(1)}, f32[256,544]{1,0:T(8,128)S(1)}, f32[32,256]{1,0:T(8,128)S(1)}, f32[18,1,32]{2,1,0:T(1,128)}, bf16[192,1024]...) custom-call(bf16[544,3456]{1,0:T(8,128)(2,1)S(1)} %get-tuple-element, ...), custom_call_target="tpu_custom_call", output_to_operand_aliasing={{0}: (7, {}), {1}: (8, {})} | custom-call | flops 1925185536 | bytes 7520256 | tf_op jit(solution)/shard_map/learner/pallas_call | solution.py:309
  33.5 0.0 copy-start.3
  33.5 0.6 collective-permute-start.18
  34.0 1.0 %rest.1 = (bf16[32,3712]{1,0:T(8,128)(2,1)S(1)}, bf16[32,3712]{1,0:T(8,128)(2,1)S(1)}, bf16[32,3712]{1,0:T(8,128)(2,1)S(1)}, bf16[32,3712]{1,0:T(8,128)(2,1)S(1)...) custom-call(bf16[544,3456]{1,0:T(8,128)(2,1)S(1)} %get-tuple-element.36.xs.refs_0_, ...), custom_call_target="tpu_custom_call" | custom-call | flops 679477248 | bytes 3538944 | tf_op jit(solution)/shard_map/rest/pallas_call | solution.py:333
  35.1 0.1 collective-permute-start.16
  35.2 0.5 collective-permute-start.20
  35.7 0.1 add.5
  35.8 2.6 %collective-permute-start.21 = (bf16[32,3712]{1,0:T(8,128)(2,1)S(1)}, bf16[32,3712]{1,0:T(8,128)(2,1)S(1)}, u32[]{:S(2)}, u32[]{:S(2)}) collective-permute-start(bf16[32,3712]{1,0:T(8,128)(2,1)S(1)} %add.5), channel_id=1, source_target_pairs={{6,4},{7,5},{0,2},{1,3},{14,12},{15,13},{8,10},{9,11},{22,20},{23,... | collective-permute-start | bytes 712712 | tf_op jit(solution)/shard_map/ppermute | solution.py:514
  38.4 1.6 %collective-permute-start.10 = (bf16[32,3456]{1,0:T(8,128)(2,1)S(1)}, bf16[32,3456]{1,0:T(8,128)(2,1)S(1)}, u32[]{:S(2)}, u32[]{:S(2)}) collective-permute-start(bf16[32,3456]{1,0:T(8,128)(2,1)S(1)} %bitcast.38), channel_id=1, source_target_pairs={{0,16},{8,24},{16,0},{24,8},{1,17},{9,25},{17,1},{25,9},{2,18},{10... | collective-permute-start | bytes 663560 | tf_op jit(solution)/shard_map/ppermute | solution.py:522
  40.0 1.4 %collective-permute-start.11 = (bf16[32,3456]{1,0:T(8,128)(2,1)S(1)}, bf16[32,3456]{1,0:T(8,128)(2,1)S(1)}, u32[]{:S(2)}, u32[]{:S(2)}) collective-permute-start(bf16[32,3456]{1,0:T(8,128)(2,1)S(1)} %bitcast.39), channel_id=1, source_target_pairs={{0,24},{8,16},{16,8},{24,0},{1,25},{9,17},{17,9},{25,1},{2,26},{10... | collective-permute-start | bytes 663560 | tf_op jit(solution)/shard_map/ppermute | solution.py:522
  41.4 0.5 collective-permute-start.9
  42.0 0.1 add.4
  42.0 0.1 collective-permute-start.15
  42.1 1.9 %collective-permute-done.21.refs_2_ = bf16[32,3712]{1,0:T(8,128)(2,1)S(1)} collective-permute-done((bf16[32,3712]{1,0:T(8,128)(2,1)S(1)}, bf16[32,3712]{1,0:T(8,128)(2,1)S(1)}, u32[]{:S(2)}, u32[]{:S(2)}) %collective-permute-start.21) | collective-permute-done | bytes 237600 | tf_op jit(solution)/shard_map/ppermute | solution.py:514
  44.0 0.7 collective-permute-start.19
  44.7 0.1 add.6
  44.8 5.9 %collective-permute-done.10.refs_2_ = bf16[32,3456]{1,0:T(8,128)(2,1)S(1)} collective-permute-done((bf16[32,3456]{1,0:T(8,128)(2,1)S(1)}, bf16[32,3456]{1,0:T(8,128)(2,1)S(1)}, u32[]{:S(2)}, u32[]{:S(2)}) %collective-permute-start.10) | collective-permute-done | bytes 221216 | tf_op jit(solution)/shard_map/ppermute | solution.py:522
  50.7 0.7 collective-permute-start.17
  51.4 1.4 %collective-permute-start.22 = (bf16[32,3712]{1,0:T(8,128)(2,1)S(1)}, bf16[32,3712]{1,0:T(8,128)(2,1)S(1)}, u32[]{:S(2)}, u32[]{:S(2)}) collective-permute-start(bf16[32,3712]{1,0:T(8,128)(2,1)S(1)} %add.6), channel_id=1, source_target_pairs={{4,0},{5,1},{2,6},{3,7},{0,2},{1,3},{6,4},{7,5},{12,8},{13,9},{10,... | collective-permute-start | bytes 712712 | tf_op jit(solution)/shard_map/ppermute | solution.py:514
  52.7 2.2 %opponents.1 = (bf16[32,32]{1,0:T(8,128)(2,1)S(1)}, bf16[32,32]{1,0:T(8,128)(2,1)S(1)}, bf16[32,32]{1,0:T(8,128)(2,1)S(1)}, bf16[32,32]{1,0:T(8,128)(2,1)S(1)}) custom-call(bf16[32,3456]{1,0:T(8,128)(2,1)S(1)} %bitcast.41, bf16[32,3456]{1,0:T(8,128)(2,1)S(1)} %collective-permute-done.9.refs_1_, bf16[32,3456]{1,0:T(8,128)(2,1)S(1)} %collective-permute-done.10.refs_2_, ...), custom_call_target="tpu_custom_call" | custom-call | flops 226492416 | bytes 884736 | tf_op jit(solution)/shard_map/opponents/pallas_call | solution.py:368
  54.9 1.6 %collective-permute-start.12 = (bf16[32,32]{1,0:T(8,128)(2,1)S(1)}, bf16[32,32]{1,0:T(8,128)(2,1)S(1)}, u32[]{:S(2)}, u32[]{:S(2)}) collective-permute-start(bf16[32,32]{1,0:T(8,128)(2,1)S(1)} %get-tuple-element.44), channel_id=1, source_target_pairs={{0,8},{8,0},{16,24},{24,16},{1,9},{9,1},{17,25},{25,17},{2,10},{10... | collective-permute-start | bytes 6152 | tf_op jit(solution)/shard_map/ppermute | solution.py:522
  56.5 2.2 %collective-permute-done.12.refs_1_ = bf16[32,32]{1,0:T(8,128)(2,1)S(1)} collective-permute-done((bf16[32,32]{1,0:T(8,128)(2,1)S(1)}, bf16[32,32]{1,0:T(8,128)(2,1)S(1)}, u32[]{:S(2)}, u32[]{:S(2)}) %collective-permute-start.12) | collective-permute-done | bytes 2080 | tf_op jit(solution)/shard_map/ppermute | solution.py:522
  58.7 1.5 %collective-permute-start.13 = (bf16[32,32]{1,0:T(8,128)(2,1)S(1)}, bf16[32,32]{1,0:T(8,128)(2,1)S(1)}, u32[]{:S(2)}, u32[]{:S(2)}) collective-permute-start(bf16[32,32]{1,0:T(8,128)(2,1)S(1)} %get-tuple-element.45), channel_id=1, source_target_pairs={{0,16},{8,24},{16,0},{24,8},{1,17},{9,25},{17,1},{25,9},{2,18},{10... | collective-permute-start | bytes 6152 | tf_op jit(solution)/shard_map/ppermute | solution.py:522
  60.2 2.1 %collective-permute-done.13.refs_2_ = bf16[32,32]{1,0:T(8,128)(2,1)S(1)} collective-permute-done((bf16[32,32]{1,0:T(8,128)(2,1)S(1)}, bf16[32,32]{1,0:T(8,128)(2,1)S(1)}, u32[]{:S(2)}, u32[]{:S(2)}) %collective-permute-start.13) | collective-permute-done | bytes 2080 | tf_op jit(solution)/shard_map/ppermute | solution.py:522
  62.3 1.2 %collective-permute-done.23.refs_1_ = f32[32,256]{1,0:T(8,128)S(1)} collective-permute-done((f32[32,256]{1,0:T(8,128)S(1)}, f32[32,256]{1,0:T(8,128)S(1)}, u32[]{:S(2)}, u32[]{:S(2)}) %collective-permute-start.23) | collective-permute-done | bytes 32800 | tf_op jit(solution)/shard_map/ppermute | solution.py:519
  63.5 2.5 %collective-permute-start.14 = (bf16[32,32]{1,0:T(8,128)(2,1)S(1)}, bf16[32,32]{1,0:T(8,128)(2,1)S(1)}, u32[]{:S(2)}, u32[]{:S(2)}) collective-permute-start(bf16[32,32]{1,0:T(8,128)(2,1)S(1)} %get-tuple-element.46), channel_id=1, source_target_pairs={{0,24},{8,16},{16,8},{24,0},{1,25},{9,17},{17,9},{25,1},{2,26},{10... | collective-permute-start | bytes 6152 | tf_op jit(solution)/shard_map/ppermute | solution.py:522
  66.0 2.1 %collective-permute-done.14.refs_3_ = bf16[32,32]{1,0:T(8,128)(2,1)S(1)} collective-permute-done((bf16[32,32]{1,0:T(8,128)(2,1)S(1)}, bf16[32,32]{1,0:T(8,128)(2,1)S(1)}, u32[]{:S(2)}, u32[]{:S(2)}) %collective-permute-start.14) | collective-permute-done | bytes 2080 | tf_op jit(solution)/shard_map/ppermute | solution.py:522
  68.1 1.0 %collective-permute-start.24 = (f32[32,256]{1,0:T(8,128)S(1)}, f32[32,256]{1,0:T(8,128)S(1)}, u32[]{:S(2)}, u32[]{:S(2)}) collective-permute-start(f32[32,256]{1,0:T(8,128)S(1)} %add.7.refs_6_), channel_id=1, source_target_pairs={{0,2},{1,3},{2,0},{3,1},{4,6},{5,7},{6,4},{7,5},{8,10},{9,11},{10,... | collective-permute-start | bytes 98312 | tf_op jit(solution)/shard_map/ppermute | solution.py:514
  69.1 2.9 %collective-permute-done.24.refs_7_ = f32[32,256]{1,0:T(8,128)S(1)} collective-permute-done((f32[32,256]{1,0:T(8,128)S(1)}, f32[32,256]{1,0:T(8,128)S(1)}, u32[]{:S(2)}, u32[]{:S(2)}) %collective-permute-start.24) | collective-permute-done | bytes 32800 | tf_op jit(solution)/shard_map/ppermute | solution.py:514
  72.0 1.6 %collective-permute-start.25 = (f32[32,256]{1,0:T(8,128)S(1)}, f32[32,256]{1,0:T(8,128)S(1)}, u32[]{:S(2)}, u32[]{:S(2)}) collective-permute-start(f32[32,256]{1,0:T(8,128)S(1)} %add.7.refs_6_), channel_id=1, source_target_pairs={{0,4},{1,5},{4,0},{5,1},{2,6},{3,7},{6,2},{7,3},{8,12},{9,13},{12,... | collective-permute-start | bytes 98312 | tf_op jit(solution)/shard_map/ppermute | solution.py:514
  73.6 3.8 %collective-permute-done.25.refs_8_ = f32[32,256]{1,0:T(8,128)S(1)} collective-permute-done((f32[32,256]{1,0:T(8,128)S(1)}, f32[32,256]{1,0:T(8,128)S(1)}, u32[]{:S(2)}, u32[]{:S(2)}) %collective-permute-start.25) | collective-permute-done | bytes 32800 | tf_op jit(solution)/shard_map/ppermute | solution.py:514
  77.4 2.3 %collective-permute-start.26 = (f32[32,256]{1,0:T(8,128)S(1)}, f32[32,256]{1,0:T(8,128)S(1)}, u32[]{:S(2)}, u32[]{:S(2)}) collective-permute-start(f32[32,256]{1,0:T(8,128)S(1)} %add.7.refs_6_), channel_id=1, source_target_pairs={{0,6},{1,7},{6,0},{7,1},{2,4},{3,5},{4,2},{5,3},{8,14},{9,15},{14,... | collective-permute-start | bytes 98312 | tf_op jit(solution)/shard_map/ppermute | solution.py:514
  80.3 0.6 choose.1
  80.9 2.2 %collective-permute-done.26.refs_9_ = f32[32,256]{1,0:T(8,128)S(1)} collective-permute-done((f32[32,256]{1,0:T(8,128)S(1)}, f32[32,256]{1,0:T(8,128)S(1)}, u32[]{:S(2)}, u32[]{:S(2)}) %collective-permute-start.26) | collective-permute-done | bytes 32800 | tf_op jit(solution)/shard_map/ppermute | solution.py:514
  83.2 2.1 %adam.1 = (f32[32,3712]{1,0:T(8,128)}, f32[32,3712]{1,0:T(8,128)}, f32[32,3712]{1,0:T(8,128)}, f32[19,1,256]{2,1,0:T(1,128)}, f32[19,1,256]{2,1,0:T(1,128)}, /*index=5*/f32[19,1,256]{2,1,0:T(1,128)}) custom-call(f32[1,1]{1,0:T(1,128)} %bitcast.34.refs_0_, bf16[32,3712]{1,0:T(8,128)(2,1)S(1)} %get-tuple-element.49.refs_1_, ...), custom_call_target="tpu_custom_call" | custom-call | flops 2375680 | bytes 3801088 | tf_op jit(solution)/shard_map/adam/pallas_call | solution.py:473
  (34 shorter events, 0.1 us)
Async XLA Ops:
  1.7 10.3 %collective-permute-start.1 = (bf16[32,3712]{1,0:T(8,128)(2,1)S(1)}, bf16[32,3712]{1,0:T(8,128)(2,1)S(1)}, u32[]{:S(2)}, u32[]{:S(2)}) collective-permute-start(bf16[32,3712]{1,0:T(8,128)(2,1)S(1)} %bitcast_convert_fusion.refs_0_), channel_id=1, source_target_pairs={{0,4},{1,5},{6,2},{7,3},{2,0},{3,1},{4,6},{5,7},{8,12},{9,13},{14,... | collective-permute-start | bytes 712712 | tf_op jit(solution)/shard_map/ppermute | solution.py:514
  5.8 12.1 %collective-permute-start.5 = (bf16[32,3712]{1,0:T(8,128)(2,1)S(1)}, bf16[32,3712]{1,0:T(8,128)(2,1)S(1)}, u32[]{:S(2)}, u32[]{:S(2)}) collective-permute-start(bf16[32,3712]{1,0:T(8,128)(2,1)S(1)} %bitcast_convert_fusion.refs_0_), channel_id=1, source_target_pairs={{0,2},{1,3},{6,4},{7,5},{2,6},{3,7},{4,0},{5,1},{8,10},{9,11},{14,... | collective-permute-start | bytes 712712 | tf_op jit(solution)/shard_map/ppermute | solution.py:514
  5.8 12.1 %collective-permute-start = (bf16[32,3712]{1,0:T(8,128)(2,1)S(1)}, bf16[32,3712]{1,0:T(8,128)(2,1)S(1)}, u32[]{:S(2)}, u32[]{:S(2)}) collective-permute-start(bf16[32,3712]{1,0:T(8,128)(2,1)S(1)} %bitcast_convert_fusion.refs_0_), channel_id=1, source_target_pairs={{2,4},{3,5},{4,2},{5,3},{10,12},{11,13},{12,10},{13,11},{18,20},{1... | collective-permute-start | bytes 712712 | tf_op jit(solution)/shard_map/ppermute | solution.py:514
  12.0 10.8 %collective-permute-start.2 = (bf16[32,3712]{1,0:T(8,128)(2,1)S(1)}, bf16[32,3712]{1,0:T(8,128)(2,1)S(1)}, u32[]{:S(2)}, u32[]{:S(2)}) collective-permute-start(bf16[32,3712]{1,0:T(8,128)(2,1)S(1)} %collective-permute-done.1.refs_1_), channel_id=1, source_target_pairs={{4,6},{5,7},{2,0},{3,1},{12,14},{13,15},{10,8},{11,9},{20,22},{21,... | collective-permute-start | bytes 712712 | tf_op jit(solution)/shard_map/ppermute | solution.py:514
  13.3 11.7 %collective-permute-start.6 = (bf16[32,3712]{1,0:T(8,128)(2,1)S(1)}, bf16[32,3712]{1,0:T(8,128)(2,1)S(1)}, u32[]{:S(2)}, u32[]{:S(2)}) collective-permute-start(bf16[32,3712]{1,0:T(8,128)(2,1)S(1)} %bitcast_convert_fusion.refs_0_), channel_id=1, source_target_pairs={{0,1},{1,0},{2,3},{3,2},{4,5},{5,4},{6,7},{7,6},{8,9},{9,8},{10,11... | collective-permute-start | bytes 712712 | tf_op jit(solution)/shard_map/ppermute | solution.py:519
  13.4 11.6 %collective-permute-start.7 = (bf16[32,3712]{1,0:T(8,128)(2,1)S(1)}, bf16[32,3712]{1,0:T(8,128)(2,1)S(1)}, u32[]{:S(2)}, u32[]{:S(2)}) collective-permute-start(bf16[32,3712]{1,0:T(8,128)(2,1)S(1)} %collective-permute-done.1.refs_1_), channel_id=1, source_target_pairs={{0,1},{1,0},{2,3},{3,2},{4,5},{5,4},{6,7},{7,6},{8,9},{9,8},{10,11... | collective-permute-start | bytes 712712 | tf_op jit(solution)/shard_map/ppermute | solution.py:519
  17.9 7.1 %collective-permute-start.8 = (bf16[32,3712]{1,0:T(8,128)(2,1)S(1)}, bf16[32,3712]{1,0:T(8,128)(2,1)S(1)}, u32[]{:S(2)}, u32[]{:S(2)}) collective-permute-start(bf16[32,3712]{1,0:T(8,128)(2,1)S(1)} %collective-permute-done.5.refs_2_), channel_id=1, source_target_pairs={{0,1},{1,0},{2,3},{3,2},{4,5},{5,4},{6,7},{7,6},{8,9},{9,8},{10,11... | collective-permute-start | bytes 712712 | tf_op jit(solution)/shard_map/ppermute | solution.py:519
  17.9 10.7 %collective-permute-start.3 = (bf16[32,3712]{1,0:T(8,128)(2,1)S(1)}, bf16[32,3712]{1,0:T(8,128)(2,1)S(1)}, u32[]{:S(2)}, u32[]{:S(2)}) collective-permute-start(bf16[32,3712]{1,0:T(8,128)(2,1)S(1)} %collective-permute-done.refs_1_), channel_id=1, source_target_pairs={{0,1},{1,0},{2,3},{3,2},{4,5},{5,4},{6,7},{7,6},{8,9},{9,8},{10,11... | collective-permute-start | bytes 712712 | tf_op jit(solution)/shard_map/ppermute | solution.py:519
  22.8 5.8 %collective-permute-start.4 = (bf16[32,3712]{1,0:T(8,128)(2,1)S(1)}, bf16[32,3712]{1,0:T(8,128)(2,1)S(1)}, u32[]{:S(2)}, u32[]{:S(2)}) collective-permute-start(bf16[32,3712]{1,0:T(8,128)(2,1)S(1)} %collective-permute-done.2.refs_2_), channel_id=1, source_target_pairs={{0,1},{1,0},{2,3},{3,2},{4,5},{5,4},{6,7},{7,6},{8,9},{9,8},{10,11... | collective-permute-start | bytes 712712 | tf_op jit(solution)/shard_map/ppermute | solution.py:519
  33.5 4.9 %copy-start.3 = (bf16[1,32,3456]{2,1,0:T(8,128)(2,1)S(1)}, bf16[1,32,3456]{2,1,0:T(8,128)(2,1)}, u32[]{:S(2)}) copy-start(bf16[1,32,3456]{2,1,0:T(8,128)(2,1)} %param.17) | copy-start | bytes 663556
  33.5 2.3 %collective-permute-start.18 = (bf16[32,3712]{1,0:T(8,128)(2,1)S(1)}, bf16[32,3712]{1,0:T(8,128)(2,1)S(1)}, u32[]{:S(2)}, u32[]{:S(2)}) collective-permute-start(bf16[32,3712]{1,0:T(8,128)(2,1)S(1)} %get-tuple-element.54), channel_id=1, source_target_pairs={{0,1},{1,0},{2,3},{3,2},{4,5},{5,4},{6,7},{7,6},{8,9},{9,8},{10,11... | collective-permute-start | bytes 712712 | tf_op jit(solution)/shard_map/ppermute | solution.py:519
  35.1 45.3 %copy-start.7 = (s32[1,32,1]{1,2,0:T(1,128)S(1)}, s32[1,32,1]{1,2,0:T(1,128)}, u32[]{:S(2)}) copy-start(s32[1,32,1]{1,2,0:T(1,128)} %param.18) | copy-start | bytes 388
  35.1 48.0 %copy-start = (f32[1,32,3712]{2,1,0:T(8,128)S(1)}, f32[1,32,3712]{2,1,0:T(8,128)}, u32[]{:S(2)}) copy-start(f32[1,32,3712]{2,1,0:T(8,128)} %param.23) | copy-start | bytes 1425412
  35.1 48.0 %copy-start.1 = (f32[1,32,3712]{2,1,0:T(8,128)S(1)}, f32[1,32,3712]{2,1,0:T(8,128)}, u32[]{:S(2)}) copy-start(f32[1,32,3712]{2,1,0:T(8,128)} %param.24) | copy-start | bytes 1425412
  35.1 48.0 %copy-start.2 = (f32[1,32,3712]{2,1,0:T(8,128)S(1)}, f32[1,32,3712]{2,1,0:T(8,128)}, u32[]{:S(2)}) copy-start(f32[1,32,3712]{2,1,0:T(8,128)} %param.25) | copy-start | bytes 1425412
  35.1 48.0 %copy-start.4 = (f32[1,19,256]{2,0,1:T(1,128)S(1)}, f32[1,19,256]{2,0,1:T(1,128)}, u32[]{:S(2)}) copy-start(f32[1,19,256]{2,0,1:T(1,128)} %param.26) | copy-start | bytes 58372
  35.1 48.0 %copy-start.5 = (f32[1,19,256]{2,0,1:T(1,128)S(1)}, f32[1,19,256]{2,0,1:T(1,128)}, u32[]{:S(2)}) copy-start(f32[1,19,256]{2,0,1:T(1,128)} %param.27) | copy-start | bytes 58372
  35.1 48.0 %copy-start.6 = (f32[1,19,256]{2,0,1:T(1,128)S(1)}, f32[1,19,256]{2,0,1:T(1,128)}, u32[]{:S(2)}) copy-start(f32[1,19,256]{2,0,1:T(1,128)} %param.28) | copy-start | bytes 58372
  35.1 6.3 %collective-permute-start.16 = (bf16[32,3712]{1,0:T(8,128)(2,1)S(1)}, bf16[32,3712]{1,0:T(8,128)(2,1)S(1)}, u32[]{:S(2)}, u32[]{:S(2)}) collective-permute-start(bf16[32,3712]{1,0:T(8,128)(2,1)S(1)} %get-tuple-element.52), channel_id=1, source_target_pairs={{0,1},{1,0},{2,3},{3,2},{4,5},{5,4},{6,7},{7,6},{8,9},{9,8},{10,11... | collective-permute-start | bytes 712712 | tf_op jit(solution)/shard_map/ppermute | solution.py:519
  35.2 6.8 %collective-permute-start.20 = (bf16[32,3712]{1,0:T(8,128)(2,1)S(1)}, bf16[32,3712]{1,0:T(8,128)(2,1)S(1)}, u32[]{:S(2)}, u32[]{:S(2)}) collective-permute-start(bf16[32,3712]{1,0:T(8,128)(2,1)S(1)} %get-tuple-element.56), channel_id=1, source_target_pairs={{0,1},{1,0},{2,3},{3,2},{4,5},{5,4},{6,7},{7,6},{8,9},{9,8},{10,11... | collective-permute-start | bytes 712712 | tf_op jit(solution)/shard_map/ppermute | solution.py:519
  35.8 8.2 %collective-permute-start.21 = (bf16[32,3712]{1,0:T(8,128)(2,1)S(1)}, bf16[32,3712]{1,0:T(8,128)(2,1)S(1)}, u32[]{:S(2)}, u32[]{:S(2)}) collective-permute-start(bf16[32,3712]{1,0:T(8,128)(2,1)S(1)} %add.5), channel_id=1, source_target_pairs={{6,4},{7,5},{0,2},{1,3},{14,12},{15,13},{8,10},{9,11},{22,20},{23,... | collective-permute-start | bytes 712712 | tf_op jit(solution)/shard_map/ppermute | solution.py:514
  38.4 12.3 %collective-permute-start.10 = (bf16[32,3456]{1,0:T(8,128)(2,1)S(1)}, bf16[32,3456]{1,0:T(8,128)(2,1)S(1)}, u32[]{:S(2)}, u32[]{:S(2)}) collective-permute-start(bf16[32,3456]{1,0:T(8,128)(2,1)S(1)} %bitcast.38), channel_id=1, source_target_pairs={{0,16},{8,24},{16,0},{24,8},{1,17},{9,25},{17,1},{25,9},{2,18},{10... | collective-permute-start | bytes 663560 | tf_op jit(solution)/shard_map/ppermute | solution.py:522
  40.0 11.4 %collective-permute-start.11 = (bf16[32,3456]{1,0:T(8,128)(2,1)S(1)}, bf16[32,3456]{1,0:T(8,128)(2,1)S(1)}, u32[]{:S(2)}, u32[]{:S(2)}) collective-permute-start(bf16[32,3456]{1,0:T(8,128)(2,1)S(1)} %bitcast.39), channel_id=1, source_target_pairs={{0,24},{8,16},{16,8},{24,0},{1,25},{9,17},{17,9},{25,1},{2,26},{10... | collective-permute-start | bytes 663560 | tf_op jit(solution)/shard_map/ppermute | solution.py:522
  41.4 11.3 %collective-permute-start.9 = (bf16[32,3456]{1,0:T(8,128)(2,1)S(1)}, bf16[32,3456]{1,0:T(8,128)(2,1)S(1)}, u32[]{:S(2)}, u32[]{:S(2)}) collective-permute-start(bf16[32,3456]{1,0:T(8,128)(2,1)S(1)} %bitcast.40), channel_id=1, source_target_pairs={{0,8},{8,0},{16,24},{24,16},{1,9},{9,1},{17,25},{25,17},{2,10},{10... | collective-permute-start | bytes 663560 | tf_op jit(solution)/shard_map/ppermute | solution.py:522
  42.0 41.1 %collective-permute-start.15 = (bf16[32,3712]{1,0:T(8,128)(2,1)S(1)}, bf16[32,3712]{1,0:T(8,128)(2,1)S(1)}, u32[]{:S(2)}, u32[]{:S(2)}) collective-permute-start(bf16[32,3712]{1,0:T(8,128)(2,1)S(1)} %get-tuple-element.50), channel_id=1, source_target_pairs={{0,1},{1,0},{2,3},{3,2},{4,5},{5,4},{6,7},{7,6},{8,9},{9,8},{10,11... | collective-permute-start | bytes 712712 | tf_op jit(solution)/shard_map/ppermute | solution.py:519
  44.0 39.1 %collective-permute-start.19 = (bf16[32,3712]{1,0:T(8,128)(2,1)S(1)}, bf16[32,3712]{1,0:T(8,128)(2,1)S(1)}, u32[]{:S(2)}, u32[]{:S(2)}) collective-permute-start(bf16[32,3712]{1,0:T(8,128)(2,1)S(1)} %add.5), channel_id=1, source_target_pairs={{2,4},{3,5},{4,2},{5,3},{10,12},{11,13},{12,10},{13,11},{18,20},{1... | collective-permute-start | bytes 712712 | tf_op jit(solution)/shard_map/ppermute | solution.py:514
  50.7 32.4 %collective-permute-start.17 = (bf16[32,3712]{1,0:T(8,128)(2,1)S(1)}, bf16[32,3712]{1,0:T(8,128)(2,1)S(1)}, u32[]{:S(2)}, u32[]{:S(2)}) collective-permute-start(bf16[32,3712]{1,0:T(8,128)(2,1)S(1)} %add.4), channel_id=1, source_target_pairs={{2,0},{3,1},{4,6},{5,7},{6,2},{7,3},{0,4},{1,5},{10,8},{11,9},{12,... | collective-permute-start | bytes 712712 | tf_op jit(solution)/shard_map/ppermute | solution.py:514
  51.4 31.7 %collective-permute-start.22 = (bf16[32,3712]{1,0:T(8,128)(2,1)S(1)}, bf16[32,3712]{1,0:T(8,128)(2,1)S(1)}, u32[]{:S(2)}, u32[]{:S(2)}) collective-permute-start(bf16[32,3712]{1,0:T(8,128)(2,1)S(1)} %add.6), channel_id=1, source_target_pairs={{4,0},{5,1},{2,6},{3,7},{0,2},{1,3},{6,4},{7,5},{12,8},{13,9},{10,... | collective-permute-start | bytes 712712 | tf_op jit(solution)/shard_map/ppermute | solution.py:514
  54.9 3.7 %collective-permute-start.12 = (bf16[32,32]{1,0:T(8,128)(2,1)S(1)}, bf16[32,32]{1,0:T(8,128)(2,1)S(1)}, u32[]{:S(2)}, u32[]{:S(2)}) collective-permute-start(bf16[32,32]{1,0:T(8,128)(2,1)S(1)} %get-tuple-element.44), channel_id=1, source_target_pairs={{0,8},{8,0},{16,24},{24,16},{1,9},{9,1},{17,25},{25,17},{2,10},{10... | collective-permute-start | bytes 6152 | tf_op jit(solution)/shard_map/ppermute | solution.py:522
  58.7 3.7 %collective-permute-start.13 = (bf16[32,32]{1,0:T(8,128)(2,1)S(1)}, bf16[32,32]{1,0:T(8,128)(2,1)S(1)}, u32[]{:S(2)}, u32[]{:S(2)}) collective-permute-start(bf16[32,32]{1,0:T(8,128)(2,1)S(1)} %get-tuple-element.45), channel_id=1, source_target_pairs={{0,16},{8,24},{16,0},{24,8},{1,17},{9,25},{17,1},{25,9},{2,18},{10... | collective-permute-start | bytes 6152 | tf_op jit(solution)/shard_map/ppermute | solution.py:522
  62.3 1.2 %collective-permute-start.23 = (f32[32,256]{1,0:T(8,128)S(1)}, f32[32,256]{1,0:T(8,128)S(1)}, u32[]{:S(2)}, u32[]{:S(2)}) collective-permute-start(f32[32,256]{1,0:T(8,128)S(1)} %get-tuple-element.57.refs_0_), channel_id=1, source_target_pairs={{0,1},{1,0},{2,3},{3,2},{4,5},{5,4},{6,7},{7,6},{8,9},{9,8},{10,11... | collective-permute-start | bytes 98312 | tf_op jit(solution)/shard_map/ppermute | solution.py:519
  63.5 4.5 %collective-permute-start.14 = (bf16[32,32]{1,0:T(8,128)(2,1)S(1)}, bf16[32,32]{1,0:T(8,128)(2,1)S(1)}, u32[]{:S(2)}, u32[]{:S(2)}) collective-permute-start(bf16[32,32]{1,0:T(8,128)(2,1)S(1)} %get-tuple-element.46), channel_id=1, source_target_pairs={{0,24},{8,16},{16,8},{24,0},{1,25},{9,17},{17,9},{25,1},{2,26},{10... | collective-permute-start | bytes 6152 | tf_op jit(solution)/shard_map/ppermute | solution.py:522
  68.1 3.9 %collective-permute-start.24 = (f32[32,256]{1,0:T(8,128)S(1)}, f32[32,256]{1,0:T(8,128)S(1)}, u32[]{:S(2)}, u32[]{:S(2)}) collective-permute-start(f32[32,256]{1,0:T(8,128)S(1)} %add.7.refs_6_), channel_id=1, source_target_pairs={{0,2},{1,3},{2,0},{3,1},{4,6},{5,7},{6,4},{7,5},{8,10},{9,11},{10,... | collective-permute-start | bytes 98312 | tf_op jit(solution)/shard_map/ppermute | solution.py:514
  72.0 5.4 %collective-permute-start.25 = (f32[32,256]{1,0:T(8,128)S(1)}, f32[32,256]{1,0:T(8,128)S(1)}, u32[]{:S(2)}, u32[]{:S(2)}) collective-permute-start(f32[32,256]{1,0:T(8,128)S(1)} %add.7.refs_6_), channel_id=1, source_target_pairs={{0,4},{1,5},{4,0},{5,1},{2,6},{3,7},{6,2},{7,3},{8,12},{9,13},{12,... | collective-permute-start | bytes 98312 | tf_op jit(solution)/shard_map/ppermute | solution.py:514
  77.4 5.7 %collective-permute-start.26 = (f32[32,256]{1,0:T(8,128)S(1)}, f32[32,256]{1,0:T(8,128)S(1)}, u32[]{:S(2)}, u32[]{:S(2)}) collective-permute-start(f32[32,256]{1,0:T(8,128)S(1)} %add.7.refs_6_), channel_id=1, source_target_pairs={{0,6},{1,7},{6,0},{7,1},{2,4},{3,5},{4,2},{5,3},{8,14},{9,15},{14,... | collective-permute-start | bytes 98312 | tf_op jit(solution)/shard_map/ppermute | solution.py:514

commit v2 on v1

--- a/solution.py
+++ b/solution.py
@@ -150,44 +150,54 @@
     )(*in_hbm((learn_rows, own_rows, *per_step, head)))
 
 
-def place_pieces(pieces, w_refs, ws, sems):
+def where_am_i():
     place = lax.axis_index("dp")
-    core, chip = lax.rem(place, CORES), lax.div(place, CORES)
-
-    def piece_copy(i):
-        rows, source, same, chips = pieces[i]
-        if source is None:
-            return pltpu.make_async_copy(w_refs[i], ws, sems.at[i]), None
-        owner = core if same else 1 - core
-        start = pl.multiple_of((table(source, chip) * CORES + owner) * rows, rows)
-        live = None
-        if chips is not None:
-            live = functools.reduce(jnp.logical_or, [chip == one for one in chips])
-        return pltpu.make_async_copy(w_refs[i], ws.at[pl.ds(start, rows)], sems.at[i]), live
-
-    def each_piece(act):
-        for i in range(len(pieces)):
-            copy, live = piece_copy(i)
-            if live is None:
-                act(copy)
-            else:
-                pl.when(live)(functools.partial(act, copy))
-
-    each_piece(lambda copy: copy.start())
-    each_piece(lambda copy: copy.wait())
-
-
-def last_rows(pieces):
-    rows = CORES * pieces[0][0]
-    chip = lax.div(lax.axis_index("dp"), CORES)
-    return pl.ds(pl.multiple_of(table(LAST_FROM, chip) * rows, rows), rows)
+    return lax.rem(place, CORES), lax.div(place, CORES)
+
+
+def piece_rows(piece):
+    rows, source, same, _ = piece
+    core, chip = where_am_i()
+    owner = core if same else 1 - core
+    return pl.ds(pl.multiple_of((table(source, chip) * CORES + owner) * rows, rows), rows)
+
+
+def piece_live(piece):
+    _, chip = where_am_i()
+    return functools.reduce(jnp.logical_or, [chip == one for one in piece[3]])
+
+
+def each_piece(pieces, w_refs, ws, sems, act):
+    for i, piece in enumerate(pieces):
+        copy = pltpu.make_async_copy(w_refs[i], ws.at[piece_rows(piece)], sems.at[i])
+        if piece[3] is None:
+            act(copy)
+        else:
+            pl.when(piece_live(piece))(functools.partial(act, copy))
+
+
+def multiply_pieces(pieces, w_refs, xs, width, pre):
+    blocks, places = [], []
+    for piece, ref in zip(pieces, w_refs):
+        value = ref[:, :width]
+        twin = [n for n, other in enumerate(places) if other[1:3] == piece[1:3]]
+        if twin:
+            blocks[twin[0]] = jnp.where(piece_live(piece), value, blocks[twin[0]])
+        else:
+            blocks.append(value)
+            places.append(piece)
+    result = dot(jnp.concatenate(blocks, 0), xs[...], NT)
+    at = 0
+    for piece in places:
+        pre[piece_rows(piece), :] = result[at : at + piece[0]]
+        at += piece[0]
 
 
 def early_kernel(pieces, width, xs, *refs):
     w_refs, (ws, pre, sems) = refs[: len(pieces)], refs[len(pieces) :]
-    ws[last_rows(pieces), :] = jnp.zeros((CORES * pieces[0][0], ws.shape[1]), ws.dtype)
-    place_pieces(pieces, w_refs, ws, sems)
-    pre[...] = dot(ws[:, :width], xs[...], NT)
+    each_piece(pieces, w_refs, ws, sems, lambda copy: copy.start())
+    multiply_pieces(pieces, w_refs, xs, width, pre)
+    each_piece(pieces, w_refs, ws, sems, lambda copy: copy.wait())
 
 
 def early(staged, pieces, piece_list, units):
@@ -198,7 +208,7 @@
             jax.ShapeDtypeStruct((units, width + units), jnp.bfloat16),
             jax.ShapeDtypeStruct((units, total), jnp.float32),
         ),
-        in_specs=[LOCAL] + [ANYWHERE] * len(pieces),
+        in_specs=[LOCAL] * (1 + len(pieces)),
         out_specs=(LOCAL,) * 2,
         scratch_shapes=[pltpu.SemaphoreType.DMA((len(pieces),))],
         compiler_params=pltpu.CompilerParams(vmem_limit_bytes=24 << 20),
@@ -228,15 +238,15 @@
     lead, (gp, sw) = refs[:-2], refs[-2:]
     learn, width, units, length = cfg["learn"], cfg["width"], cfg["units"], cfg["length"]
     envs = learn // length
-    place = lax.axis_index("dp")
-    core, chip = lax.rem(place, CORES), lax.div(place, CORES)
-
-    place_pieces(pieces, w_refs, ws, sw)
+    core, chip = where_am_i()
+
     if roles is None:
+        pltpu.sync_copy(w_refs[0], ws)
         pre[...] = dot(ws[:, :width], xs[...], NT)
     else:
-        late = last_rows(pieces)
-        pre[late, :] = dot(ws[late, :width], xs[...], NT)
+        each_piece(pieces, w_refs, ws, sw, lambda copy: copy.start())
+        multiply_pieces(pieces, w_refs, xs, width, pre)
+        each_piece(pieces, w_refs, ws, sw, lambda copy: copy.wait())
     pre_one = pre[...]
     out, pre_one, first_bf, pre_two, second_bf = forward(pre_one, ws[...], head_ref[...], width)
     own_ref[...] = out[: heads - 1, learn:].reshape(heads - 1, 1, envs)
@@ -246,7 +256,8 @@
     grad = trace_gradients(
         out[:, :learn], boot, aux_ref[...], heads - 1, length, 1.0 / length
     ).astype(jnp.bfloat16)
-    ghead_ref[...] = dot(grad, second_bf[:, :learn], NT)
+    ghead = dot(grad, second_bf[:, :learn], NT)
+    ghead_ref[...] = ghead
     grad_second = dot(head_ref[...].T, grad, NN)
     grad_two = jnp.where(pre_two[:, :learn] > 0, grad_second, 0.0).astype(jnp.bfloat16)
     grad_first = grad_second + dot(ws[:, width:].T, grad_two, NN)
@@ -267,6 +278,8 @@
             start = pl.multiple_of((table(role, chip) * CORES + owner) * rows, rows)
             order.append(gp[pl.ds(start, rows), :])
     order_ref[...] = jnp.concatenate(order[CORES:], 0)
+    for out in lead:
+        out[:, width + units :] = ghead[:rows].astype(jnp.bfloat16)
     gradient_rows(jnp.concatenate(order[:CORES], 0), xs, first_ref, lead, learn, width, cfg["chunk"])
 
 
@@ -281,7 +294,7 @@
     for start in range(0, width, chunk):
         columns = slice(start, start + chunk)
         put(columns, dot(order[:, :learn], xs[:learn, columns], NN))
-    put(slice(width, None), dot(order[:, learn:], first_ref[...], NT))
+    put(slice(width, width + first_ref.shape[0]), dot(order[:, learn:], first_ref[...], NT))
 
 
 def rest_kernel(cfg, xs, order_ref, first_ref, *outs):
@@ -303,7 +316,8 @@
         lead, rest, later, aliases = [], [block(units)], units, {}
     else:
         rows = units // (len(roles) * CORES)
-        lead, rest = [block(rows)] * CORES, [block(rows)] * (CORES * (len(roles) - 1))
+        wider = jax.ShapeDtypeStruct((rows, width + 2 * units), jnp.bfloat16)
+        lead, rest = [wider] * CORES, [block(rows)] * (CORES * (len(roles) - 1))
         later = units - CORES * rows
         aliases = {inputs: 0, inputs + 1: 1}
     weights, _, ghead, own, order, first, *first_outs = pl.pallas_call(
@@ -317,7 +331,8 @@
             jax.ShapeDtypeStruct((units, learn), jnp.bfloat16),
             *lead,
         ),
-        in_specs=[LOCAL] + [ANYWHERE] * len(piece_list) + [LOCAL] * (2 + len(before)),
+        in_specs=[LOCAL] + [ANYWHERE if roles is None else LOCAL] * len(piece_list)
+        + [LOCAL] * (2 + len(before)),
         out_specs=(LOCAL,) * (6 + len(lead)),
         input_output_aliases=aliases,
         scratch_shapes=[
@@ -409,22 +424,27 @@
     )(*answers, ids)
 
 
-def add_kernel(*refs):
-    refs[-1][...] = sum(x[...].astype(jnp.float32) for x in refs[:-1]).astype(refs[-1].dtype)
-
-
-def add(*arrays):
+def add_with_heads_kernel(count, units, *refs):
+    ins, heads, out = refs[:count], refs[count:-1], refs[-1]
+    width = out.shape[1] - units
+    for columns, parts in ((slice(0, width), ins), (slice(width, width + units), heads)):
+        total = sum(x[:, columns].astype(jnp.float32) for x in parts)
+        out[:, columns] = total.astype(out.dtype)
+
+
+def add_with_heads(arrays, heads, units):
+    rows, wide = heads[0].shape
     return pl.pallas_call(
-        add_kernel,
-        out_shape=jax.ShapeDtypeStruct(arrays[0].shape, arrays[0].dtype),
-        in_specs=[LOCAL] * len(arrays),
+        functools.partial(add_with_heads_kernel, len(arrays), units),
+        out_shape=jax.ShapeDtypeStruct((rows, wide), jnp.bfloat16),
+        in_specs=[LOCAL] * (len(arrays) + len(heads)),
         out_specs=LOCAL,
         compiler_params=pltpu.CompilerParams(vmem_limit_bytes=4 << 20),
         cost_estimate=pl.CostEstimate(
-            flops=arrays[0].size, bytes_accessed=2 * len(arrays) * arrays[0].size, transcendentals=0
+            flops=rows * wide, bytes_accessed=2 * len(arrays) * rows * wide, transcendentals=0
         ),
         name="add",
-    )(*arrays)
+    )(*arrays, *heads)
 
 
 def adam_step(master, moment, second, grad, rate):
@@ -439,8 +459,25 @@
     parts, refs = refs[1 : 1 + parts], refs[1 + parts :]
     head_parts, refs = refs[:head_parts], refs[head_parts:]
     core, head, core_out, head_out = refs[:3], refs[3:6], refs[6:9], refs[9:12]
-    stages, sems = refs[12:15], refs[15]
+    stages, head_stages, sems, head_sems = refs[12:15], refs[15:18], refs[18], refs[19]
+    count, _, units = head[0].shape
+    if len(head_parts) == 1:
+        grad = head_parts[0][:count]
+    else:
+        mine, mid, near, far = (
+            x[:count, x.shape[1] - units :].astype(jnp.float32) for x in head_parts
+        )
+        _, chip = where_am_i()
+        end = jnp.logical_or(chip == 0, chip == LINE - 1)
+        rounded = lambda x: x.astype(jnp.bfloat16).astype(jnp.float32)
+        pair = rounded(mine + jnp.where(end, near, far))
+        grad = pair + jnp.where(end, far, rounded(mid + near))
+    grad = grad.reshape(head[0].shape)
     copies = []
+    for i, value in enumerate(adam_step(*(x[...] for x in head), grad, rate)):
+        head_stages[i][...] = value
+        copies.append(pltpu.make_async_copy(head_stages[i], head_out[i], head_sems.at[i]))
+        copies[-1].start()
     for n, (start, stop) in enumerate(cuts):
         columns = slice(start, stop)
         grad = sum(part[:, columns].astype(jnp.float32) for part in parts)
@@ -452,31 +489,25 @@
                 )
             )
             copies[-1].start()
-    count = head[0].shape[0]
-    sums = [part[:count] for part in head_parts]
-    while len(sums) > 1:
-        sums = [a + b for a, b in zip(sums[::2], sums[1::2])]
-    grad = sums[0].reshape(head[0].shape)
-    for out, value in zip(head_out, adam_step(*(x[...] for x in head), grad, rate)):
-        out[...] = value
     for copy in copies:
         copy.wait()
 
 
 def adam(rates, parts, head_parts, core, head):
     rows, width = core[0].shape
-    tiles = width // 128
-    cuts = [(128 * (tiles * n // 3), 128 * (tiles * (n + 1) // 3)) for n in range(3)]
-    cuts[-1] = (cuts[-1][0], width)
+    tiles, pieces = width // 128, 5
+    edges = [128 * (tiles * n // pieces) for n in range(pieces)] + [width]
+    cuts = list(zip(edges, edges[1:]))
     one = jax.ShapeDtypeStruct((rows, width), jnp.float32)
     small = jax.ShapeDtypeStruct(head[0].shape, jnp.float32)
     return pl.pallas_call(
         functools.partial(adam_kernel, len(parts), len(head_parts), cuts),
         out_shape=(one,) * 3 + (small,) * 3,
         in_specs=[LOCAL] * (len(parts) + len(head_parts) + 7),
-        out_specs=(ANYWHERE,) * 3 + (LOCAL,) * 3,
+        out_specs=(ANYWHERE,) * 6,
         scratch_shapes=[pltpu.VMEM((rows, width), jnp.float32)] * 3
-        + [pltpu.SemaphoreType.DMA((len(cuts), 3))],
+        + [pltpu.VMEM(head[0].shape, jnp.float32)] * 3
+        + [pltpu.SemaphoreType.DMA((len(cuts), 3)), pltpu.SemaphoreType.DMA((3,))],
         compiler_params=pltpu.CompilerParams(vmem_limit_bytes=16 << 20),
         cost_estimate=pl.CostEstimate(
             flops=20 * rows * width, bytes_accessed=32 * rows * width, transcendentals=0
@@ -508,7 +539,7 @@
     agents, members = lax.axis_size("agent"), lax.axis_size("dp")
     rows = core_master.shape[1]
     chips = members // CORES
-    line = chips == LINE and members == LINE * CORES and units == members * rows
+    line = chips == LINE and members == LINE * CORES and units == members * rows and heads <= rows
 
     def along(x, pairs):
         return lax.ppermute(
@@ -572,17 +603,15 @@
         blocks = lead + rest
         send, keep = blocks[::CORES], blocks[1::CORES]
         came = [sibling(b) for b in send]
-        last, toward = add(keep[0], came[0]), add(keep[1], came[1])
+        last = add_with_heads((keep[0], came[0]), (keep[0], came[0]), units)
         through = along(last, SCATTER_FORWARD)
         part_mid = along(last, SCATTER_MID)
+        toward = add_with_heads((keep[1], came[1]), (last,), units)
         part_near = along(toward, SCATTER_NEAR)
-        part_far = along(add(keep[2], came[2], through), SCATTER_FAR)
+        beyond = add_with_heads((keep[2], came[2], through), (last, through), units)
+        part_far = along(beyond, SCATTER_FAR)
         core_parts = (keep[3], came[3], part_near, part_mid, part_far)
-        ghead = add(ghead, sibling(ghead))
-        one = along(ghead, ((0, 1), (1, 0), (2, 3), (3, 2)))
-        two = along(ghead, ((0, 2), (2, 0), (1, 3), (3, 1)))
-        three = along(ghead, ((0, 3), (3, 0), (1, 2), (2, 1)))
-        head_parts = (ghead, one, two, three)
+        head_parts = (last, part_mid, part_near, part_far)
     else:
         core_parts = (lax.psum_scatter(rest[0], "dp", scatter_dimension=0, tiled=True),)
         head_parts = (lax.psum(ghead, "dp"),)

time: 85.5 us -> 75.2 us (0.88)
  waiting for transfers between devices: 38.3 us -> 31.5 us
  starting transfers between devices: 27.6 us -> 24.6 us
    ppermute x11 -> x8, waiting for transfers between devices: 24.7 us -> 14 us  [along(): lax.ppermute(x, 'dp', [(a * CORES + c, b * CORES + c) for a, b in pairs f...]
    ppermute x6, waiting for transfers between devices: 12.3 us -> 16.4 us  [swap(): lax.ppermute(x, 'agent', [(i, other_agent(i, by, agents)) for i in range(...]
    ppermute x11 -> x8, starting transfers between devices: 16.2 us -> 12.4 us  [along(): lax.ppermute(x, 'dp', [(a * CORES + c, b * CORES + c) for a, b in pairs f...]
    ppermute x6, starting transfers between devices: 9.1 us -> 9.95 us  [swap(): lax.ppermute(x, 'agent', [(i, other_agent(i, by, agents)) for i in range(...]
    ppermute x10 -> x9, starting transfers between devices: 2.3 us -> 2.22 us  [sibling(): return lax.ppermute(x, 'dp', [(i, i ^ 1) for i in range(members)])]
  transfers between devices with their start and end apart: 27 -> 23, of which waited for: 12 -> 9; matrix products, arithmetic and copies ran while one was open for 0% -> 0% of each run, Pallas kernels for 11% -> 13%
where the time goes in v2:
time: 75.2 us; the launch traced here: 74.9 us
  waiting for transfers between devices  31.5 us (42%)
  starting transfers between devices  24.6 us (33%)
  Pallas kernels  16.1 us (21%)
  between operations  1.57 us (2%)
  other arithmetic  1.05 us (1%)
    ppermute x6, waiting for transfers between devices, swap(): lax.ppermute(x, 'agent', [(i, other_agent(i, by, agents)) for i in range(...  16.4 us
    ppermute x8, waiting for transfers between devices, along(): lax.ppermute(x, 'dp', [(a * CORES + c, b * CORES + c) for a, b in pairs f...  14 us
    ppermute x8, starting transfers between devices, along(): lax.ppermute(x, 'dp', [(a * CORES + c, b * CORES + c) for a, b in pairs f...  12.4 us
    ppermute x6, starting transfers between devices, swap(): lax.ppermute(x, 'agent', [(i, other_agent(i, by, agents)) for i in range(...  9.95 us
    pallas_call x1, Pallas kernels, learner(): pl.pallas_call(functools.partial(learner_kernel, cfg), out_shape=(block(u...  4.94 us
    pallas_call x1, Pallas kernels, early(): pl.pallas_call(functools.partial(early_kernel, pieces, width), out_shape=...  3.57 us
    ppermute x9, starting transfers between devices, sibling(): return lax.ppermute(x, 'dp', [(i, i ^ 1) for i in range(members)])  2.22 us
    pallas_call x1, Pallas kernels, opponents(): pl.pallas_call(functools.partial(opponent_kernel, cfg, count), out_shape=...  2.2 us
  transfers between devices with their start and end apart: 23, of which 9 were waited for; matrix products, arithmetic and copies ran while one was open for 0% of the time, Pallas kernels for 13%

profile of v2, /device:TPU:0, one launch (start us, length us, event | category | flops | bytes accessed | tf_op | source)
XLA Modules:
  0.0 74.9 jit_solution(6075716685999981634)
XLA Ops:
  0.6 1.1 %bitcast_convert_fusion.refs_0_ = bf16[32,3712]{1,0:T(8,128)(2,1)S(1)} fusion(f32[1,32,3712]{2,1,0:T(8,128)} %param.23), kind=kLoop, calls=%fused_computation | loop fusion | flops 118784 | bytes 712704 | tf_op jit(solution)/shard_map/convert_element_type | solution.py:555
  1.7 4.1 %collective-permute-start.1 = (bf16[32,3712]{1,0:T(8,128)(2,1)S(1)}, bf16[32,3712]{1,0:T(8,128)(2,1)S(1)}, u32[]{:S(2)}, u32[]{:S(2)}) collective-permute-start(bf16[32,3712]{1,0:T(8,128)(2,1)S(1)} %bitcast_convert_fusion.refs_0_), channel_id=1, source_target_pairs={{0,4},{1,5},{6,2},{7,3},{2,0},{3,1},{4,6},{5,7},{8,12},{9,13},{14,... | collective-permute-start | bytes 712712 | tf_op jit(solution)/shard_map/ppermute | solution.py:545
  5.8 0.7 collective-permute-start
  6.5 5.5 %collective-permute-done.1.refs_1_ = bf16[32,3712]{1,0:T(8,128)(2,1)S(1)} collective-permute-done((bf16[32,3712]{1,0:T(8,128)(2,1)S(1)}, bf16[32,3712]{1,0:T(8,128)(2,1)S(1)}, u32[]{:S(2)}, u32[]{:S(2)}) %collective-permute-start.1) | collective-permute-done | bytes 237600 | tf_op jit(solution)/shard_map/ppermute | solution.py:545
  12.0 1.3 %collective-permute-start.2 = (bf16[32,3712]{1,0:T(8,128)(2,1)S(1)}, bf16[32,3712]{1,0:T(8,128)(2,1)S(1)}, u32[]{:S(2)}, u32[]{:S(2)}) collective-permute-start(bf16[32,3712]{1,0:T(8,128)(2,1)S(1)} %collective-permute-done.1.refs_1_), channel_id=1, source_target_pairs={{4,6},{5,7},{2,0},{3,1},{12,14},{13,15},{10,8},{11,9},{20,22},{21,... | collective-permute-start | bytes 712712 | tf_op jit(solution)/shard_map/ppermute | solution.py:545
  13.3 0.1 collective-permute-start.6
  13.4 0.5 collective-permute-start.7
  13.9 4.0 %collective-permute-done.5.refs_2_ = bf16[32,3712]{1,0:T(8,128)(2,1)S(1)} collective-permute-done((bf16[32,3712]{1,0:T(8,128)(2,1)S(1)}, bf16[32,3712]{1,0:T(8,128)(2,1)S(1)}, u32[]{:S(2)}, u32[]{:S(2)}) %collective-permute-start.5) | collective-permute-done | bytes 237600 | tf_op jit(solution)/shard_map/ppermute | solution.py:545
  17.9 0.5 collective-permute-start.3
  18.4 4.4 %collective-permute-done.2.refs_2_ = bf16[32,3712]{1,0:T(8,128)(2,1)S(1)} collective-permute-done((bf16[32,3712]{1,0:T(8,128)(2,1)S(1)}, bf16[32,3712]{1,0:T(8,128)(2,1)S(1)}, u32[]{:S(2)}, u32[]{:S(2)}) %collective-permute-start.2) | collective-permute-done | bytes 237600 | tf_op jit(solution)/shard_map/ppermute | solution.py:545
  22.8 0.0 collective-permute-start.4
  22.8 2.1 %stage.1 = (bf16[544,3456]{1,0:T(8,128)(2,1)S(1)}, f32[4,512]{1,0:T(4,128)S(1)}, bf16[32,256]{1,0:T(8,128)(2,1)S(1)}) custom-call(bf16[512,3456]{1,0:T(8,128)(2,1)} %bitcast.47, bf16[32,3456]{1,0:T(8,128)(2,1)} %bitcast.48, s32[16,32]{1,0:T(8,128)} %bitcast.49, s32[16,32]{1,0:T(8,128)} %bitcast.50, f32[16,32]{1,0:T(8,128)} %bitcast.51, f32[16,32]{1,0:T(8,128)} %bitcast.52, ...), custom_call_target="tpu_custom_call" | custom-call | bytes 7520256 | tf_op jit(solution)/shard_map/stage/pallas_call | solution.py:134
  25.0 3.6 %early.1 = (bf16[256,3712]{1,0:T(8,128)(2,1)S(1)}, f32[256,544]{1,0:T(8,128)S(1)}) custom-call(bf16[544,3456]{1,0:T(8,128)(2,1)S(1)} %get-tuple-element.35.xs.refs_0_, bf16[32,3712]{1,0:T(8,128)(2,1)S(1)} %bitcast_convert_fusion.refs_0_, bf16[32,3712]{1,0:T(8,128)(2,1)S(1)} %collective-permute-done.1.refs_1_, ...), custom_call_target="tpu_custom_call" | custom-call | flops 962592768 | bytes 3538944 | tf_op jit(solution)/shard_map/early/pallas_call | solution.py:205
  28.6 4.9 %learner.1 = (bf16[256,3712]{1,0:T(8,128)(2,1)S(1)}, f32[256,544]{1,0:T(8,128)S(1)}, f32[32,256]{1,0:T(8,128)}, f32[18,1,32]{2,1,0:T(1,128)}, bf16[192,1024]{1,0...) custom-call(bf16[544,3456]{1,0:T(8,128)(2,1)S(1)} %get-tuple-element, ...), custom_call_target="tpu_custom_call", output_to_operand_aliasing={{0}: (7, {}), {1}: (8, {})} | custom-call | flops 1925185536 | bytes 7520256 | tf_op jit(solution)/shard_map/learner/pallas_call | solution.py:323
  33.6 0.0 copy-start.3
  33.6 0.6 collective-permute-start.17
  34.1 1.2 %collective-permute-done.17.refs_1_.refs_3_ = bf16[32,3968]{1,0:T(8,128)(2,1)S(1)} collective-permute-done((bf16[32,3968]{1,0:T(8,128)(2,1)S(1)}, bf16[32,3968]{1,0:T(8,128)(2,1)S(1)}, u32[]{:S(2)}, u32[]{:S(2)}) %collective-permute-start.17) | collective-permute-done | bytes 253984 | tf_op jit(solution)/shard_map/ppermute | solution.py:550
  35.3 0.1 add.3.refs_2_.refs_3_.refs_6_
  35.4 2.9 %collective-permute-start.21 = (bf16[32,3968]{1,0:T(8,128)(2,1)S(1)}, bf16[32,3968]{1,0:T(8,128)(2,1)S(1)}, u32[]{:S(2)}, u32[]{:S(2)}) collective-permute-start(bf16[32,3968]{1,0:T(8,128)(2,1)S(1)} %add.3.refs_2_.refs_3_.refs_6_), channel_id=1, source_target_pairs={{6,4},{7,5},{0,2},{1,3},{14,12},{15,13},{8,10},{9,11},{22,20},{23,... | collective-permute-start | bytes 761864 | tf_op jit(solution)/shard_map/ppermute | solution.py:545
  38.3 1.0 %rest.1 = (bf16[32,3712]{1,0:T(8,128)(2,1)S(1)}, bf16[32,3712]{1,0:T(8,128)(2,1)S(1)}, bf16[32,3712]{1,0:T(8,128)(2,1)S(1)}, bf16[32,3712]{1,0:T(8,128)(2,1)S(1)...) custom-call(bf16[544,3456]{1,0:T(8,128)(2,1)S(1)} %get-tuple-element.35.xs.refs_0_, ...), custom_call_target="tpu_custom_call" | custom-call | flops 679477248 | bytes 3538944 | tf_op jit(solution)/shard_map/rest/pallas_call | solution.py:348
  39.3 0.0 copy-start.7
  39.3 0.0 copy-start
  39.3 0.0 copy-start.1
  39.3 0.0 copy-start.2
  39.4 0.0 copy-start.4
  39.4 0.0 copy-start.5
  39.4 0.0 copy-start.6
  39.4 0.1 collective-permute-start.16
  39.5 0.5 collective-permute-start.20
  40.0 1.5 %collective-permute-start.10 = (bf16[32,3456]{1,0:T(8,128)(2,1)S(1)}, bf16[32,3456]{1,0:T(8,128)(2,1)S(1)}, u32[]{:S(2)}, u32[]{:S(2)}) collective-permute-start(bf16[32,3456]{1,0:T(8,128)(2,1)S(1)} %bitcast.38), channel_id=1, source_target_pairs={{0,16},{8,24},{16,0},{24,8},{1,17},{9,25},{17,1},{25,9},{2,18},{10... | collective-permute-start | bytes 663560 | tf_op jit(solution)/shard_map/ppermute | solution.py:553
  41.5 1.4 %collective-permute-start.11 = (bf16[32,3456]{1,0:T(8,128)(2,1)S(1)}, bf16[32,3456]{1,0:T(8,128)(2,1)S(1)}, u32[]{:S(2)}, u32[]{:S(2)}) collective-permute-start(bf16[32,3456]{1,0:T(8,128)(2,1)S(1)} %bitcast.39), channel_id=1, source_target_pairs={{0,24},{8,16},{16,8},{24,0},{1,25},{9,17},{17,9},{25,1},{2,26},{10... | collective-permute-start | bytes 663560 | tf_op jit(solution)/shard_map/ppermute | solution.py:553
  42.9 0.7 collective-permute-start.19
  43.6 0.1 add.4
  43.7 2.1 %collective-permute-start.18 = (bf16[32,3968]{1,0:T(8,128)(2,1)S(1)}, bf16[32,3968]{1,0:T(8,128)(2,1)S(1)}, u32[]{:S(2)}, u32[]{:S(2)}) collective-permute-start(bf16[32,3968]{1,0:T(8,128)(2,1)S(1)} %add.4), channel_id=1, source_target_pairs={{2,0},{3,1},{4,6},{5,7},{6,2},{7,3},{0,4},{1,5},{10,8},{11,9},{12,... | collective-permute-start | bytes 761864 | tf_op jit(solution)/shard_map/ppermute | solution.py:545
  45.8 0.1 add.5
  45.9 0.7 collective-permute-start.22
  46.6 5.6 %collective-permute-done.10.refs_2_ = bf16[32,3456]{1,0:T(8,128)(2,1)S(1)} collective-permute-done((bf16[32,3456]{1,0:T(8,128)(2,1)S(1)}, bf16[32,3456]{1,0:T(8,128)(2,1)S(1)}, u32[]{:S(2)}, u32[]{:S(2)}) %collective-permute-start.10) | collective-permute-done | bytes 221216 | tf_op jit(solution)/shard_map/ppermute | solution.py:553
  52.1 1.5 %collective-permute-start.9 = (bf16[32,3456]{1,0:T(8,128)(2,1)S(1)}, bf16[32,3456]{1,0:T(8,128)(2,1)S(1)}, u32[]{:S(2)}, u32[]{:S(2)}) collective-permute-start(bf16[32,3456]{1,0:T(8,128)(2,1)S(1)} %bitcast.40), channel_id=1, source_target_pairs={{0,8},{8,0},{16,24},{24,16},{1,9},{9,1},{17,25},{25,17},{2,10},{10... | collective-permute-start | bytes 663560 | tf_op jit(solution)/shard_map/ppermute | solution.py:553
  53.6 5.1 %collective-permute-done.9.refs_1_ = bf16[32,3456]{1,0:T(8,128)(2,1)S(1)} collective-permute-done((bf16[32,3456]{1,0:T(8,128)(2,1)S(1)}, bf16[32,3456]{1,0:T(8,128)(2,1)S(1)}, u32[]{:S(2)}, u32[]{:S(2)}) %collective-permute-start.9) | collective-permute-done | bytes 221216 | tf_op jit(solution)/shard_map/ppermute | solution.py:553
  58.7 2.2 %opponents.1 = (bf16[32,32]{1,0:T(8,128)(2,1)S(1)}, bf16[32,32]{1,0:T(8,128)(2,1)S(1)}, bf16[32,32]{1,0:T(8,128)(2,1)S(1)}, bf16[32,32]{1,0:T(8,128)(2,1)S(1)}) custom-call(bf16[32,3456]{1,0:T(8,128)(2,1)S(1)} %bitcast.41, bf16[32,3456]{1,0:T(8,128)(2,1)S(1)} %collective-permute-done.9.refs_1_, bf16[32,3456]{1,0:T(8,128)(2,1)S(1)} %collective-permute-done.10.refs_2_, ...), custom_call_target="tpu_custom_call" | custom-call | flops 226492416 | bytes 884736 | tf_op jit(solution)/shard_map/opponents/pallas_call | solution.py:383
  60.9 1.6 %collective-permute-start.12 = (bf16[32,32]{1,0:T(8,128)(2,1)S(1)}, bf16[32,32]{1,0:T(8,128)(2,1)S(1)}, u32[]{:S(2)}, u32[]{:S(2)}) collective-permute-start(bf16[32,32]{1,0:T(8,128)(2,1)S(1)} %get-tuple-element.43), channel_id=1, source_target_pairs={{0,8},{8,0},{16,24},{24,16},{1,9},{9,1},{17,25},{25,17},{2,10},{10... | collective-permute-start | bytes 6152 | tf_op jit(solution)/shard_map/ppermute | solution.py:553
  62.4 2.2 %collective-permute-done.12.refs_1_ = bf16[32,32]{1,0:T(8,128)(2,1)S(1)} collective-permute-done((bf16[32,32]{1,0:T(8,128)(2,1)S(1)}, bf16[32,32]{1,0:T(8,128)(2,1)S(1)}, u32[]{:S(2)}, u32[]{:S(2)}) %collective-permute-start.12) | collective-permute-done | bytes 2080 | tf_op jit(solution)/shard_map/ppermute | solution.py:553
  64.6 1.5 %collective-permute-start.13 = (bf16[32,32]{1,0:T(8,128)(2,1)S(1)}, bf16[32,32]{1,0:T(8,128)(2,1)S(1)}, u32[]{:S(2)}, u32[]{:S(2)}) collective-permute-start(bf16[32,32]{1,0:T(8,128)(2,1)S(1)} %get-tuple-element.44), channel_id=1, source_target_pairs={{0,16},{8,24},{16,0},{24,8},{1,17},{9,25},{17,1},{25,9},{2,18},{10... | collective-permute-start | bytes 6152 | tf_op jit(solution)/shard_map/ppermute | solution.py:553
  66.1 2.1 %collective-permute-done.13.refs_2_ = bf16[32,32]{1,0:T(8,128)(2,1)S(1)} collective-permute-done((bf16[32,32]{1,0:T(8,128)(2,1)S(1)}, bf16[32,32]{1,0:T(8,128)(2,1)S(1)}, u32[]{:S(2)}, u32[]{:S(2)}) %collective-permute-start.13) | collective-permute-done | bytes 2080 | tf_op jit(solution)/shard_map/ppermute | solution.py:553
  68.3 2.4 %collective-permute-start.14 = (bf16[32,32]{1,0:T(8,128)(2,1)S(1)}, bf16[32,32]{1,0:T(8,128)(2,1)S(1)}, u32[]{:S(2)}, u32[]{:S(2)}) collective-permute-start(bf16[32,32]{1,0:T(8,128)(2,1)S(1)} %get-tuple-element.45), channel_id=1, source_target_pairs={{0,24},{8,16},{16,8},{24,0},{1,25},{9,17},{17,9},{25,1},{2,26},{10... | collective-permute-start | bytes 6152 | tf_op jit(solution)/shard_map/ppermute | solution.py:553
  71.4 1.5 %collective-permute-done.14.refs_3_ = bf16[32,32]{1,0:T(8,128)(2,1)S(1)} collective-permute-done((bf16[32,32]{1,0:T(8,128)(2,1)S(1)}, bf16[32,32]{1,0:T(8,128)(2,1)S(1)}, u32[]{:S(2)}, u32[]{:S(2)}) %collective-permute-start.14) | collective-permute-done | bytes 2080 | tf_op jit(solution)/shard_map/ppermute | solution.py:553
  72.8 0.6 choose.1
  73.5 1.4 %adam.1 = (f32[32,3712]{1,0:T(8,128)}, f32[32,3712]{1,0:T(8,128)}, f32[32,3712]{1,0:T(8,128)}, f32[19,1,256]{2,1,0:T(1,128)}, f32[19,1,256]{2,1,0:T(1,128)}, /*index=5*/f32[19,1,256]{2,1,0:T(1,128)}) custom-call(f32[1,1]{1,0:T(1,128)} %bitcast.34.refs_0_, bf16[32,3712]{1,0:T(8,128)(2,1)S(1)} %get-tuple-element.48.refs_1_, ...), custom_call_target="tpu_custom_call" | custom-call | flops 2375680 | bytes 3801088 | tf_op jit(solution)/shard_map/adam/pallas_call | solution.py:503
  (25 shorter events, 0.1 us)
Async XLA Ops:
  1.7 10.3 %collective-permute-start.1 = (bf16[32,3712]{1,0:T(8,128)(2,1)S(1)}, bf16[32,3712]{1,0:T(8,128)(2,1)S(1)}, u32[]{:S(2)}, u32[]{:S(2)}) collective-permute-start(bf16[32,3712]{1,0:T(8,128)(2,1)S(1)} %bitcast_convert_fusion.refs_0_), channel_id=1, source_target_pairs={{0,4},{1,5},{6,2},{7,3},{2,0},{3,1},{4,6},{5,7},{8,12},{9,13},{14,... | collective-permute-start | bytes 712712 | tf_op jit(solution)/shard_map/ppermute | solution.py:545
  5.8 12.1 %collective-permute-start.5 = (bf16[32,3712]{1,0:T(8,128)(2,1)S(1)}, bf16[32,3712]{1,0:T(8,128)(2,1)S(1)}, u32[]{:S(2)}, u32[]{:S(2)}) collective-permute-start(bf16[32,3712]{1,0:T(8,128)(2,1)S(1)} %bitcast_convert_fusion.refs_0_), channel_id=1, source_target_pairs={{0,2},{1,3},{6,4},{7,5},{2,6},{3,7},{4,0},{5,1},{8,10},{9,11},{14,... | collective-permute-start | bytes 712712 | tf_op jit(solution)/shard_map/ppermute | solution.py:545
  5.8 12.1 %collective-permute-start = (bf16[32,3712]{1,0:T(8,128)(2,1)S(1)}, bf16[32,3712]{1,0:T(8,128)(2,1)S(1)}, u32[]{:S(2)}, u32[]{:S(2)}) collective-permute-start(bf16[32,3712]{1,0:T(8,128)(2,1)S(1)} %bitcast_convert_fusion.refs_0_), channel_id=1, source_target_pairs={{2,4},{3,5},{4,2},{5,3},{10,12},{11,13},{12,10},{13,11},{18,20},{1... | collective-permute-start | bytes 712712 | tf_op jit(solution)/shard_map/ppermute | solution.py:545
  12.0 10.8 %collective-permute-start.2 = (bf16[32,3712]{1,0:T(8,128)(2,1)S(1)}, bf16[32,3712]{1,0:T(8,128)(2,1)S(1)}, u32[]{:S(2)}, u32[]{:S(2)}) collective-permute-start(bf16[32,3712]{1,0:T(8,128)(2,1)S(1)} %collective-permute-done.1.refs_1_), channel_id=1, source_target_pairs={{4,6},{5,7},{2,0},{3,1},{12,14},{13,15},{10,8},{11,9},{20,22},{21,... | collective-permute-start | bytes 712712 | tf_op jit(solution)/shard_map/ppermute | solution.py:545
  13.3 11.7 %collective-permute-start.6 = (bf16[32,3712]{1,0:T(8,128)(2,1)S(1)}, bf16[32,3712]{1,0:T(8,128)(2,1)S(1)}, u32[]{:S(2)}, u32[]{:S(2)}) collective-permute-start(bf16[32,3712]{1,0:T(8,128)(2,1)S(1)} %bitcast_convert_fusion.refs_0_), channel_id=1, source_target_pairs={{0,1},{1,0},{2,3},{3,2},{4,5},{5,4},{6,7},{7,6},{8,9},{9,8},{10,11... | collective-permute-start | bytes 712712 | tf_op jit(solution)/shard_map/ppermute | solution.py:550
  13.4 11.6 %collective-permute-start.7 = (bf16[32,3712]{1,0:T(8,128)(2,1)S(1)}, bf16[32,3712]{1,0:T(8,128)(2,1)S(1)}, u32[]{:S(2)}, u32[]{:S(2)}) collective-permute-start(bf16[32,3712]{1,0:T(8,128)(2,1)S(1)} %collective-permute-done.1.refs_1_), channel_id=1, source_target_pairs={{0,1},{1,0},{2,3},{3,2},{4,5},{5,4},{6,7},{7,6},{8,9},{9,8},{10,11... | collective-permute-start | bytes 712712 | tf_op jit(solution)/shard_map/ppermute | solution.py:550
  17.9 7.1 %collective-permute-start.8 = (bf16[32,3712]{1,0:T(8,128)(2,1)S(1)}, bf16[32,3712]{1,0:T(8,128)(2,1)S(1)}, u32[]{:S(2)}, u32[]{:S(2)}) collective-permute-start(bf16[32,3712]{1,0:T(8,128)(2,1)S(1)} %collective-permute-done.5.refs_2_), channel_id=1, source_target_pairs={{0,1},{1,0},{2,3},{3,2},{4,5},{5,4},{6,7},{7,6},{8,9},{9,8},{10,11... | collective-permute-start | bytes 712712 | tf_op jit(solution)/shard_map/ppermute | solution.py:550
  17.9 10.7 %collective-permute-start.3 = (bf16[32,3712]{1,0:T(8,128)(2,1)S(1)}, bf16[32,3712]{1,0:T(8,128)(2,1)S(1)}, u32[]{:S(2)}, u32[]{:S(2)}) collective-permute-start(bf16[32,3712]{1,0:T(8,128)(2,1)S(1)} %collective-permute-done.refs_1_), channel_id=1, source_target_pairs={{0,1},{1,0},{2,3},{3,2},{4,5},{5,4},{6,7},{7,6},{8,9},{9,8},{10,11... | collective-permute-start | bytes 712712 | tf_op jit(solution)/shard_map/ppermute | solution.py:550
  22.8 5.8 %collective-permute-start.4 = (bf16[32,3712]{1,0:T(8,128)(2,1)S(1)}, bf16[32,3712]{1,0:T(8,128)(2,1)S(1)}, u32[]{:S(2)}, u32[]{:S(2)}) collective-permute-start(bf16[32,3712]{1,0:T(8,128)(2,1)S(1)} %collective-permute-done.2.refs_2_), channel_id=1, source_target_pairs={{0,1},{1,0},{2,3},{3,2},{4,5},{5,4},{6,7},{7,6},{8,9},{9,8},{10,11... | collective-permute-start | bytes 712712 | tf_op jit(solution)/shard_map/ppermute | solution.py:550
  33.6 6.4 %copy-start.3 = (bf16[1,32,3456]{2,1,0:T(8,128)(2,1)S(1)}, bf16[1,32,3456]{2,1,0:T(8,128)(2,1)}, u32[]{:S(2)}) copy-start(bf16[1,32,3456]{2,1,0:T(8,128)(2,1)} %param.17) | copy-start | bytes 663556
  33.6 1.7 %collective-permute-start.17 = (bf16[32,3968]{1,0:T(8,128)(2,1)S(1)}, bf16[32,3968]{1,0:T(8,128)(2,1)S(1)}, u32[]{:S(2)}, u32[]{:S(2)}) collective-permute-start(bf16[32,3968]{1,0:T(8,128)(2,1)S(1)} %get-tuple-element.53), channel_id=1, source_target_pairs={{0,1},{1,0},{2,3},{3,2},{4,5},{5,4},{6,7},{7,6},{8,9},{9,8},{10,11... | collective-permute-start | bytes 761864 | tf_op jit(solution)/shard_map/ppermute | solution.py:550
  35.4 10.4 %collective-permute-start.21 = (bf16[32,3968]{1,0:T(8,128)(2,1)S(1)}, bf16[32,3968]{1,0:T(8,128)(2,1)S(1)}, u32[]{:S(2)}, u32[]{:S(2)}) collective-permute-start(bf16[32,3968]{1,0:T(8,128)(2,1)S(1)} %add.3.refs_2_.refs_3_.refs_6_), channel_id=1, source_target_pairs={{6,4},{7,5},{0,2},{1,3},{14,12},{15,13},{8,10},{9,11},{22,20},{23,... | collective-permute-start | bytes 761864 | tf_op jit(solution)/shard_map/ppermute | solution.py:545
  39.3 33.5 %copy-start.7 = (s32[1,32,1]{1,2,0:T(1,128)S(1)}, s32[1,32,1]{1,2,0:T(1,128)}, u32[]{:S(2)}) copy-start(s32[1,32,1]{1,2,0:T(1,128)} %param.18) | copy-start | bytes 388
  39.3 34.1 %copy-start = (f32[1,32,3712]{2,1,0:T(8,128)S(1)}, f32[1,32,3712]{2,1,0:T(8,128)}, u32[]{:S(2)}) copy-start(f32[1,32,3712]{2,1,0:T(8,128)} %param.23) | copy-start | bytes 1425412
  39.3 34.1 %copy-start.1 = (f32[1,32,3712]{2,1,0:T(8,128)S(1)}, f32[1,32,3712]{2,1,0:T(8,128)}, u32[]{:S(2)}) copy-start(f32[1,32,3712]{2,1,0:T(8,128)} %param.24) | copy-start | bytes 1425412
  39.3 34.1 %copy-start.2 = (f32[1,32,3712]{2,1,0:T(8,128)S(1)}, f32[1,32,3712]{2,1,0:T(8,128)}, u32[]{:S(2)}) copy-start(f32[1,32,3712]{2,1,0:T(8,128)} %param.25) | copy-start | bytes 1425412
  39.4 34.1 %copy-start.4 = (f32[1,19,256]{2,0,1:T(1,128)S(1)}, f32[1,19,256]{2,0,1:T(1,128)}, u32[]{:S(2)}) copy-start(f32[1,19,256]{2,0,1:T(1,128)} %param.26) | copy-start | bytes 58372
  39.4 34.1 %copy-start.5 = (f32[1,19,256]{2,0,1:T(1,128)S(1)}, f32[1,19,256]{2,0,1:T(1,128)}, u32[]{:S(2)}) copy-start(f32[1,19,256]{2,0,1:T(1,128)} %param.27) | copy-start | bytes 58372
  39.4 34.1 %copy-start.6 = (f32[1,19,256]{2,0,1:T(1,128)S(1)}, f32[1,19,256]{2,0,1:T(1,128)}, u32[]{:S(2)}) copy-start(f32[1,19,256]{2,0,1:T(1,128)} %param.28) | copy-start | bytes 58372
  39.4 3.5 %collective-permute-start.16 = (bf16[32,3712]{1,0:T(8,128)(2,1)S(1)}, bf16[32,3712]{1,0:T(8,128)(2,1)S(1)}, u32[]{:S(2)}, u32[]{:S(2)}) collective-permute-start(bf16[32,3712]{1,0:T(8,128)(2,1)S(1)} %get-tuple-element.51), channel_id=1, source_target_pairs={{0,1},{1,0},{2,3},{3,2},{4,5},{5,4},{6,7},{7,6},{8,9},{9,8},{10,11... | collective-permute-start | bytes 712712 | tf_op jit(solution)/shard_map/ppermute | solution.py:550
  39.5 4.2 %collective-permute-start.20 = (bf16[32,3712]{1,0:T(8,128)(2,1)S(1)}, bf16[32,3712]{1,0:T(8,128)(2,1)S(1)}, u32[]{:S(2)}, u32[]{:S(2)}) collective-permute-start(bf16[32,3712]{1,0:T(8,128)(2,1)S(1)} %get-tuple-element.55), channel_id=1, source_target_pairs={{0,1},{1,0},{2,3},{3,2},{4,5},{5,4},{6,7},{7,6},{8,9},{9,8},{10,11... | collective-permute-start | bytes 712712 | tf_op jit(solution)/shard_map/ppermute | solution.py:550
  40.0 12.2 %collective-permute-start.10 = (bf16[32,3456]{1,0:T(8,128)(2,1)S(1)}, bf16[32,3456]{1,0:T(8,128)(2,1)S(1)}, u32[]{:S(2)}, u32[]{:S(2)}) collective-permute-start(bf16[32,3456]{1,0:T(8,128)(2,1)S(1)} %bitcast.38), channel_id=1, source_target_pairs={{0,16},{8,24},{16,0},{24,8},{1,17},{9,25},{17,1},{25,9},{2,18},{10... | collective-permute-start | bytes 663560 | tf_op jit(solution)/shard_map/ppermute | solution.py:553
  41.5 12.1 %collective-permute-start.11 = (bf16[32,3456]{1,0:T(8,128)(2,1)S(1)}, bf16[32,3456]{1,0:T(8,128)(2,1)S(1)}, u32[]{:S(2)}, u32[]{:S(2)}) collective-permute-start(bf16[32,3456]{1,0:T(8,128)(2,1)S(1)} %bitcast.39), channel_id=1, source_target_pairs={{0,24},{8,16},{16,8},{24,0},{1,25},{9,17},{17,9},{25,1},{2,26},{10... | collective-permute-start | bytes 663560 | tf_op jit(solution)/shard_map/ppermute | solution.py:553
  42.9 30.5 %collective-permute-start.19 = (bf16[32,3968]{1,0:T(8,128)(2,1)S(1)}, bf16[32,3968]{1,0:T(8,128)(2,1)S(1)}, u32[]{:S(2)}, u32[]{:S(2)}) collective-permute-start(bf16[32,3968]{1,0:T(8,128)(2,1)S(1)} %add.3.refs_2_.refs_3_.refs_6_), channel_id=1, source_target_pairs={{2,4},{3,5},{4,2},{5,3},{10,12},{11,13},{12,10},{13,11},{18,20},{1... | collective-permute-start | bytes 761864 | tf_op jit(solution)/shard_map/ppermute | solution.py:545
  43.7 29.7 %collective-permute-start.18 = (bf16[32,3968]{1,0:T(8,128)(2,1)S(1)}, bf16[32,3968]{1,0:T(8,128)(2,1)S(1)}, u32[]{:S(2)}, u32[]{:S(2)}) collective-permute-start(bf16[32,3968]{1,0:T(8,128)(2,1)S(1)} %add.4), channel_id=1, source_target_pairs={{2,0},{3,1},{4,6},{5,7},{6,2},{7,3},{0,4},{1,5},{10,8},{11,9},{12,... | collective-permute-start | bytes 761864 | tf_op jit(solution)/shard_map/ppermute | solution.py:545
  45.9 27.5 %collective-permute-start.22 = (bf16[32,3968]{1,0:T(8,128)(2,1)S(1)}, bf16[32,3968]{1,0:T(8,128)(2,1)S(1)}, u32[]{:S(2)}, u32[]{:S(2)}) collective-permute-start(bf16[32,3968]{1,0:T(8,128)(2,1)S(1)} %add.5), channel_id=1, source_target_pairs={{4,0},{5,1},{2,6},{3,7},{0,2},{1,3},{6,4},{7,5},{12,8},{13,9},{10,... | collective-permute-start | bytes 761864 | tf_op jit(solution)/shard_map/ppermute | solution.py:545
  52.1 6.6 %collective-permute-start.9 = (bf16[32,3456]{1,0:T(8,128)(2,1)S(1)}, bf16[32,3456]{1,0:T(8,128)(2,1)S(1)}, u32[]{:S(2)}, u32[]{:S(2)}) collective-permute-start(bf16[32,3456]{1,0:T(8,128)(2,1)S(1)} %bitcast.40), channel_id=1, source_target_pairs={{0,8},{8,0},{16,24},{24,16},{1,9},{9,1},{17,25},{25,17},{2,10},{10... | collective-permute-start | bytes 663560 | tf_op jit(solution)/shard_map/ppermute | solution.py:553
  53.6 19.8 %collective-permute-start.15 = (bf16[32,3712]{1,0:T(8,128)(2,1)S(1)}, bf16[32,3712]{1,0:T(8,128)(2,1)S(1)}, u32[]{:S(2)}, u32[]{:S(2)}) collective-permute-start(bf16[32,3712]{1,0:T(8,128)(2,1)S(1)} %get-tuple-element.49), channel_id=1, source_target_pairs={{0,1},{1,0},{2,3},{3,2},{4,5},{5,4},{6,7},{7,6},{8,9},{9,8},{10,11... | collective-permute-start | bytes 712712 | tf_op jit(solution)/shard_map/ppermute | solution.py:550
  60.9 3.7 %collective-permute-start.12 = (bf16[32,32]{1,0:T(8,128)(2,1)S(1)}, bf16[32,32]{1,0:T(8,128)(2,1)S(1)}, u32[]{:S(2)}, u32[]{:S(2)}) collective-permute-start(bf16[32,32]{1,0:T(8,128)(2,1)S(1)} %get-tuple-element.43), channel_id=1, source_target_pairs={{0,8},{8,0},{16,24},{24,16},{1,9},{9,1},{17,25},{25,17},{2,10},{10... | collective-permute-start | bytes 6152 | tf_op jit(solution)/shard_map/ppermute | solution.py:553
  64.6 3.7 %collective-permute-start.13 = (bf16[32,32]{1,0:T(8,128)(2,1)S(1)}, bf16[32,32]{1,0:T(8,128)(2,1)S(1)}, u32[]{:S(2)}, u32[]{:S(2)}) collective-permute-start(bf16[32,32]{1,0:T(8,128)(2,1)S(1)} %get-tuple-element.44), channel_id=1, source_target_pairs={{0,16},{8,24},{16,0},{24,8},{1,17},{9,25},{17,1},{25,9},{2,18},{10... | collective-permute-start | bytes 6152 | tf_op jit(solution)/shard_map/ppermute | solution.py:553
  68.3 4.5 %collective-permute-start.14 = (bf16[32,32]{1,0:T(8,128)(2,1)S(1)}, bf16[32,32]{1,0:T(8,128)(2,1)S(1)}, u32[]{:S(2)}, u32[]{:S(2)}) collective-permute-start(bf16[32,32]{1,0:T(8,128)(2,1)S(1)} %get-tuple-element.45), channel_id=1, source_target_pairs={{0,24},{8,16},{16,8},{24,0},{1,25},{9,17},{17,9},{25,1},{2,26},{10... | collective-permute-start | bytes 6152 | tf_op jit(solution)/shard_map/ppermute | solution.py:553

commit v3 on v2

--- a/solution.py
+++ b/solution.py
@@ -156,47 +156,33 @@
 
 
 def piece_rows(piece):
-    rows, source, same, _ = piece
+    rows, source, same = piece
     core, chip = where_am_i()
     owner = core if same else 1 - core
     return pl.ds(pl.multiple_of((table(source, chip) * CORES + owner) * rows, rows), rows)
 
 
-def piece_live(piece):
-    _, chip = where_am_i()
-    return functools.reduce(jnp.logical_or, [chip == one for one in piece[3]])
-
-
 def each_piece(pieces, w_refs, ws, sems, act):
     for i, piece in enumerate(pieces):
-        copy = pltpu.make_async_copy(w_refs[i], ws.at[piece_rows(piece)], sems.at[i])
-        if piece[3] is None:
-            act(copy)
-        else:
-            pl.when(piece_live(piece))(functools.partial(act, copy))
-
-
-def multiply_pieces(pieces, w_refs, xs, width, pre):
-    blocks, places = [], []
-    for piece, ref in zip(pieces, w_refs):
-        value = ref[:, :width]
-        twin = [n for n, other in enumerate(places) if other[1:3] == piece[1:3]]
-        if twin:
-            blocks[twin[0]] = jnp.where(piece_live(piece), value, blocks[twin[0]])
-        else:
-            blocks.append(value)
-            places.append(piece)
-    result = dot(jnp.concatenate(blocks, 0), xs[...], NT)
+        act(pltpu.make_async_copy(w_refs[i], ws.at[piece_rows(piece)], sems.at[i]))
+
+
+def multiply_pieces(pieces, w_refs, xs, width, first, first_bf):
+    result = dot(jnp.concatenate([ref[:, :width] for ref in w_refs], 0), xs[...], NT)
+    result = jnp.maximum(result, 0.0)
+    result_bf = result.astype(jnp.bfloat16)
     at = 0
-    for piece in places:
-        pre[piece_rows(piece), :] = result[at : at + piece[0]]
+    for piece in pieces:
+        rows = piece_rows(piece)
+        first[rows, :] = result[at : at + piece[0]]
+        first_bf[rows, :] = result_bf[at : at + piece[0]]
         at += piece[0]
 
 
 def early_kernel(pieces, width, xs, *refs):
-    w_refs, (ws, pre, sems) = refs[: len(pieces)], refs[len(pieces) :]
+    w_refs, (ws, first, first_bf, sems) = refs[: len(pieces)], refs[len(pieces) :]
     each_piece(pieces, w_refs, ws, sems, lambda copy: copy.start())
-    multiply_pieces(pieces, w_refs, xs, width, pre)
+    multiply_pieces(pieces, w_refs, xs, width, first, first_bf)
     each_piece(pieces, w_refs, ws, sems, lambda copy: copy.wait())
 
 
@@ -207,9 +193,10 @@
         out_shape=(
             jax.ShapeDtypeStruct((units, width + units), jnp.bfloat16),
             jax.ShapeDtypeStruct((units, total), jnp.float32),
+            jax.ShapeDtypeStruct((units, total), jnp.bfloat16),
         ),
         in_specs=[LOCAL] * (1 + len(pieces)),
-        out_specs=(LOCAL,) * 2,
+        out_specs=(LOCAL,) * 3,
         scratch_shapes=[pltpu.SemaphoreType.DMA((len(pieces),))],
         compiler_params=pltpu.CompilerParams(vmem_limit_bytes=24 << 20),
         cost_estimate=pl.CostEstimate(
@@ -219,12 +206,10 @@
     )(staged, *piece_list)
 
 
-def forward(pre_one, weights, head, width):
-    first = jnp.maximum(pre_one, 0.0)
-    first_bf = first.astype(jnp.bfloat16)
+def forward(first, first_bf, weights, head, width):
     pre_two = dot(weights[:, width:], first_bf, NN)
     second_bf = (jnp.maximum(pre_two, 0.0) + first).astype(jnp.bfloat16)
-    return dot(head, second_bf, NN), pre_one, first_bf, pre_two, second_bf
+    return dot(head, second_bf, NN), pre_two, second_bf
 
 
 def learner_kernel(cfg, *refs):
@@ -233,22 +218,21 @@
     w_refs, refs = refs[: len(pieces)], refs[len(pieces) :]
     aux_ref, head_ref, refs = refs[0], refs[1], refs[2:]
     if roles is not None:
-        refs = refs[2:]
-    ws, pre, ghead_ref, own_ref, order_ref, first_ref, refs = *refs[:6], refs[6:]
-    lead, (gp, sw) = refs[:-2], refs[-2:]
+        refs = refs[3:]
+    ws, first, first_bf, ghead_ref, own_ref, gp, refs = *refs[:6], refs[6:]
+    lead, sw = refs[:-1], refs[-1]
     learn, width, units, length = cfg["learn"], cfg["width"], cfg["units"], cfg["length"]
     envs = learn // length
-    core, chip = where_am_i()
 
     if roles is None:
         pltpu.sync_copy(w_refs[0], ws)
-        pre[...] = dot(ws[:, :width], xs[...], NT)
+        first[...] = jnp.maximum(dot(ws[:, :width], xs[...], NT), 0.0)
+        first_bf[...] = first[...].astype(jnp.bfloat16)
     else:
         each_piece(pieces, w_refs, ws, sw, lambda copy: copy.start())
-        multiply_pieces(pieces, w_refs, xs, width, pre)
+        multiply_pieces(pieces, w_refs, xs, width, first, first_bf)
         each_piece(pieces, w_refs, ws, sw, lambda copy: copy.wait())
-    pre_one = pre[...]
-    out, pre_one, first_bf, pre_two, second_bf = forward(pre_one, ws[...], head_ref[...], width)
+    out, pre_two, second_bf = forward(first[...], first_bf[...], ws[...], head_ref[...], width)
     own_ref[...] = out[: heads - 1, learn:].reshape(heads - 1, 1, envs)
     spread = lax.broadcasted_iota(jnp.int32, (envs, learn), 1) // length
     spread = (spread == lax.broadcasted_iota(jnp.int32, (envs, learn), 0)).astype(jnp.float32)
@@ -261,29 +245,22 @@
     grad_second = dot(head_ref[...].T, grad, NN)
     grad_two = jnp.where(pre_two[:, :learn] > 0, grad_second, 0.0).astype(jnp.bfloat16)
     grad_first = grad_second + dot(ws[:, width:].T, grad_two, NN)
-    grad_one = jnp.where(pre_one[:, :learn] > 0, grad_first, 0.0).astype(jnp.bfloat16)
-    first_ref[...] = first_bf[:, :learn]
-
-    if roles is None:
-        order_ref[:, :learn] = grad_one
-        order_ref[:, learn:] = grad_two
-        return
+    grad_one = jnp.where(first[:, :learn] > 0, grad_first, 0.0).astype(jnp.bfloat16)
     gp[:, :learn] = grad_one
     gp[:, learn:] = grad_two
-    rows = units // (len(roles) * CORES)
-    order = []
-    for role in roles:
-        for same in (False, True):
-            owner = core if same else 1 - core
-            start = pl.multiple_of((table(role, chip) * CORES + owner) * rows, rows)
-            order.append(gp[pl.ds(start, rows), :])
-    order_ref[...] = jnp.concatenate(order[CORES:], 0)
-    for out in lead:
-        out[:, width + units :] = ghead[:rows].astype(jnp.bfloat16)
-    gradient_rows(jnp.concatenate(order[:CORES], 0), xs, first_ref, lead, learn, width, cfg["chunk"])
-
-
-def gradient_rows(order, xs, first_ref, outs, learn, width, chunk):
+    if roles is not None:
+        for out in lead:
+            out[:, width + units :] = ghead[: out.shape[0]].astype(jnp.bfloat16)
+        order = role_rows(gp, roles[:1], lead[0].shape[0])
+        gradient_rows(order, xs, first_bf, lead, learn, width, cfg["chunk"])
+
+
+def role_rows(gp, roles, rows):
+    parts = [gp[piece_rows((rows, role, same)), :] for role in roles for same in (False, True)]
+    return jnp.concatenate(parts, 0)
+
+
+def gradient_rows(order, xs, first_bf, outs, learn, width, chunk):
     rows = outs[0].shape[0]
 
     def put(columns, value):
@@ -294,11 +271,14 @@
     for start in range(0, width, chunk):
         columns = slice(start, start + chunk)
         put(columns, dot(order[:, :learn], xs[:learn, columns], NN))
-    put(slice(width, width + first_ref.shape[0]), dot(order[:, learn:], first_ref[...], NT))
-
-
-def rest_kernel(cfg, xs, order_ref, first_ref, *outs):
-    gradient_rows(order_ref[...], xs, first_ref, outs, cfg["learn"], cfg["width"], cfg["chunk"])
+    columns = slice(width, width + first_bf.shape[0])
+    put(columns, dot(order[:, learn:], first_bf[:, :learn], NT))
+
+
+def rest_kernel(cfg, xs, gp, first_bf, *outs):
+    roles = cfg["roles"]
+    order = gp[...] if roles is None else role_rows(gp, roles[1:], outs[0].shape[0])
+    gradient_rows(order, xs, first_bf, outs, cfg["learn"], cfg["width"], cfg["chunk"])
 
 
 def column_chunk(width):
@@ -313,32 +293,28 @@
     block = lambda rows: jax.ShapeDtypeStruct((rows, width + units), jnp.bfloat16)
     inputs = 3 + len(piece_list)
     if roles is None:
-        lead, rest, later, aliases = [], [block(units)], units, {}
+        lead, rest, aliases = [], [block(units)], {}
     else:
         rows = units // (len(roles) * CORES)
         wider = jax.ShapeDtypeStruct((rows, width + 2 * units), jnp.bfloat16)
         lead, rest = [wider] * CORES, [block(rows)] * (CORES * (len(roles) - 1))
-        later = units - CORES * rows
-        aliases = {inputs: 0, inputs + 1: 1}
-    weights, _, ghead, own, order, first, *first_outs = pl.pallas_call(
+        aliases = {inputs + i: i for i in range(len(before))}
+    weights, _, first_bf, ghead, own, gp, *first_outs = pl.pallas_call(
         functools.partial(learner_kernel, cfg),
         out_shape=(
             block(units),
             jax.ShapeDtypeStruct((units, total), jnp.float32),
+            jax.ShapeDtypeStruct((units, total), jnp.bfloat16),
             jax.ShapeDtypeStruct((padded, units), jnp.float32),
             jax.ShapeDtypeStruct((cfg["heads"] - 1, 1, total - learn), jnp.float32),
-            jax.ShapeDtypeStruct((later, 2 * learn), jnp.bfloat16),
-            jax.ShapeDtypeStruct((units, learn), jnp.bfloat16),
+            jax.ShapeDtypeStruct((units, 2 * learn), jnp.bfloat16),
             *lead,
         ),
         in_specs=[LOCAL] + [ANYWHERE if roles is None else LOCAL] * len(piece_list)
         + [LOCAL] * (2 + len(before)),
         out_specs=(LOCAL,) * (6 + len(lead)),
         input_output_aliases=aliases,
-        scratch_shapes=[
-            pltpu.VMEM((units, 2 * learn), jnp.bfloat16),
-            pltpu.SemaphoreType.DMA((len(piece_list),)),
-        ],
+        scratch_shapes=[pltpu.SemaphoreType.DMA((len(piece_list),))],
         compiler_params=pltpu.CompilerParams(vmem_limit_bytes=32 << 20),
         cost_estimate=pl.CostEstimate(
             flops=4 * units * total * width, bytes_accessed=4 * total * width, transcendentals=0
@@ -352,10 +328,10 @@
         out_specs=(LOCAL,) * len(rest),
         compiler_params=pltpu.CompilerParams(vmem_limit_bytes=32 << 20),
         cost_estimate=pl.CostEstimate(
-            flops=2 * later * learn * width, bytes_accessed=2 * learn * width, transcendentals=0
+            flops=2 * units * learn * width, bytes_accessed=2 * learn * width, transcendentals=0
         ),
         name="rest",
-    )(staged, order, first)
+    )(staged, gp, first_bf)
     return weights, ghead, own, first_outs, list(rest_outs)
 
 
@@ -372,8 +348,9 @@
     for copy in copies:
         copy.wait()
     width = cfg["width"]
-    pre_one = dot(weights[:, :width], xs[...], NT)
-    result = forward(pre_one, weights[...], head[...], width)[0].astype(jnp.bfloat16)
+    first = jnp.maximum(dot(weights[:, :width], xs[...], NT), 0.0)
+    first_bf = first.astype(jnp.bfloat16)
+    result = forward(first, first_bf, weights[...], head[...], width)[0].astype(jnp.bfloat16)
     for i, out in enumerate(outs):
         out[...] = result[:, i * envs : (i + 1) * envs]
 
@@ -422,6 +399,25 @@
         compiler_params=pltpu.CompilerParams(vmem_limit_bytes=2 << 20),
         name="choose",
     )(*answers, ids)
+
+
+def add_kernel(*refs):
+    total = sum(x[...].astype(jnp.float32) for x in refs[:-1])
+    refs[-1][...] = total.astype(refs[-1].dtype)
+
+
+def add(*arrays):
+    return pl.pallas_call(
+        add_kernel,
+        out_shape=jax.ShapeDtypeStruct(arrays[0].shape, arrays[0].dtype),
+        in_specs=[LOCAL] * len(arrays),
+        out_specs=LOCAL,
+        compiler_params=pltpu.CompilerParams(vmem_limit_bytes=4 << 20),
+        cost_estimate=pl.CostEstimate(
+            flops=arrays[0].size, bytes_accessed=6 * arrays[0].size, transcendentals=0
+        ),
+        name="add",
+    )(*arrays)
 
 
 def add_with_heads_kernel(count, units, *refs):
@@ -558,20 +554,20 @@
         near = along(mine, GATHER_NEAR)
         mid = along(mine, GATHER_MID)
         onward = along(far, GATHER_FORWARD)
-        first = (("mine", mine, SELF_FROM, None), ("far", far, FAR_FROM, None),
-                 ("near", near, NEAR_FROM, None))
-        final = (("mid", mid, LAST_FROM, (1, 2)), ("onward", onward, LAST_FROM, (0, 3)))
+        joined = add(mid, onward)
+        got = [("mine", mine, SELF_FROM), ("far", far, FAR_FROM), ("near", near, NEAR_FROM),
+               ("last", joined, LAST_FROM)]
 
         def with_siblings(group):
             arrays = [g[1] for g in group] + [sibling(g[1]) for g in group]
-            places = [(rows, g[2], same, g[3]) for same in (True, False) for g in group]
-            return arrays, places
-
-        (first_list, first_pieces), (piece_list, pieces) = with_siblings(first), with_siblings(final)
+            return arrays, [(rows, g[2], same) for same in (True, False) for g in group]
+
+        first_list, first_pieces = with_siblings(got[:-1])
+        piece_list, pieces = with_siblings(got[-1:])
         roles = ROLES
     else:
         piece_list = [lax.all_gather(mine, "dp", axis=0, tiled=True)]
-        pieces = [(units, None, True, None)]
+        pieces = [(units, None, True)]
         roles = None
 
     frames = [opp_obs[0]] + [swap(opp_obs[0], by) for by in range(1, agents)]

time: 75.2 us -> 71.4 us (0.949)
  waiting for transfers between devices: 31.5 us -> 28.2 us
    ppermute x6, waiting for transfers between devices: 16.4 us -> 12.5 us  [swap(): lax.ppermute(x, 'agent', [(i, other_agent(i, by, agents)) for i in range(...]
    ppermute x9 -> x8, starting transfers between devices: 2.22 us -> 1.78 us  [sibling(): return lax.ppermute(x, 'dp', [(i, i ^ 1) for i in range(members)])]
  transfers between devices with their start and end apart: 23 -> 22, of which waited for: 9 -> 10; matrix products, arithmetic and copies ran while one was open for 0% -> 0% of each run, Pallas kernels for 13% -> 14%
where the time goes in v3:
time: 71.4 us; the launch traced here: 71.1 us
  waiting for transfers between devices  28.2 us (39%)
  starting transfers between devices  24.1 us (34%)
  Pallas kernels  16.2 us (23%)
  between operations  1.56 us (2%)
  other arithmetic  1.05 us (1%)
    ppermute x8, waiting for transfers between devices, along(): lax.ppermute(x, 'dp', [(a * CORES + c, b * CORES + c) for a, b in pairs f...  14.5 us
    ppermute x6, waiting for transfers between devices, swap(): lax.ppermute(x, 'agent', [(i, other_agent(i, by, agents)) for i in range(...  12.5 us
    ppermute x8, starting transfers between devices, along(): lax.ppermute(x, 'dp', [(a * CORES + c, b * CORES + c) for a, b in pairs f...  12.3 us
    ppermute x6, starting transfers between devices, swap(): lax.ppermute(x, 'agent', [(i, other_agent(i, by, agents)) for i in range(...  10 us
    pallas_call x1, Pallas kernels, learner(): pl.pallas_call(functools.partial(learner_kernel, cfg), out_shape=(block(u...  4.89 us
    pallas_call x1, Pallas kernels, early(): pl.pallas_call(functools.partial(early_kernel, pieces, width), out_shape=...  3.59 us
    pallas_call x1, Pallas kernels, opponents(): pl.pallas_call(functools.partial(opponent_kernel, cfg, count), out_shape=...  2.19 us
    pallas_call x1, Pallas kernels, stage(): pl.pallas_call(stage_kernel, out_shape=(jax.ShapeDtypeStruct((total, widt...  2.15 us
  transfers between devices with their start and end apart: 22, of which 10 were waited for; matrix products, arithmetic and copies ran while one was open for 0% of the time, Pallas kernels for 14%

profile of v3, /device:TPU:0, one launch (start us, length us, event | category | flops | bytes accessed | tf_op | source)
XLA Modules:
  0.0 71.1 jit_solution(13935650492735600296)
XLA Ops:
  0.6 1.1 %bitcast_convert_fusion.refs_0_ = bf16[32,3712]{1,0:T(8,128)(2,1)S(1)} fusion(f32[1,32,3712]{2,1,0:T(8,128)} %param.23), kind=kLoop, calls=%fused_computation | loop fusion | flops 118784 | bytes 712704 | tf_op jit(solution)/shard_map/convert_element_type | solution.py:551
  1.7 4.1 %collective-permute-start.1 = (bf16[32,3712]{1,0:T(8,128)(2,1)S(1)}, bf16[32,3712]{1,0:T(8,128)(2,1)S(1)}, u32[]{:S(2)}, u32[]{:S(2)}) collective-permute-start(bf16[32,3712]{1,0:T(8,128)(2,1)S(1)} %bitcast_convert_fusion.refs_0_), channel_id=1, source_target_pairs={{0,4},{1,5},{6,2},{7,3},{2,0},{3,1},{4,6},{5,7},{8,12},{9,13},{14,... | collective-permute-start | bytes 712712 | tf_op jit(solution)/shard_map/ppermute | solution.py:541
  5.8 0.7 collective-permute-start
  6.5 5.5 %collective-permute-done.1.refs_1_ = bf16[32,3712]{1,0:T(8,128)(2,1)S(1)} collective-permute-done((bf16[32,3712]{1,0:T(8,128)(2,1)S(1)}, bf16[32,3712]{1,0:T(8,128)(2,1)S(1)}, u32[]{:S(2)}, u32[]{:S(2)}) %collective-permute-start.1) | collective-permute-done | bytes 237600 | tf_op jit(solution)/shard_map/ppermute | solution.py:541
  12.0 1.3 %collective-permute-start.2 = (bf16[32,3712]{1,0:T(8,128)(2,1)S(1)}, bf16[32,3712]{1,0:T(8,128)(2,1)S(1)}, u32[]{:S(2)}, u32[]{:S(2)}) collective-permute-start(bf16[32,3712]{1,0:T(8,128)(2,1)S(1)} %collective-permute-done.1.refs_1_), channel_id=1, source_target_pairs={{4,6},{5,7},{2,0},{3,1},{12,14},{13,15},{10,8},{11,9},{20,22},{21,... | collective-permute-start | bytes 712712 | tf_op jit(solution)/shard_map/ppermute | solution.py:541
  13.3 0.1 collective-permute-start.5
  13.4 0.5 collective-permute-start.6
  13.9 4.0 %collective-permute-done.4.refs_2_ = bf16[32,3712]{1,0:T(8,128)(2,1)S(1)} collective-permute-done((bf16[32,3712]{1,0:T(8,128)(2,1)S(1)}, bf16[32,3712]{1,0:T(8,128)(2,1)S(1)}, u32[]{:S(2)}, u32[]{:S(2)}) %collective-permute-start.4) | collective-permute-done | bytes 237600 | tf_op jit(solution)/shard_map/ppermute | solution.py:541
  17.9 4.9 %collective-permute-done.2.refs_1_ = bf16[32,3712]{1,0:T(8,128)(2,1)S(1)} collective-permute-done((bf16[32,3712]{1,0:T(8,128)(2,1)S(1)}, bf16[32,3712]{1,0:T(8,128)(2,1)S(1)}, u32[]{:S(2)}, u32[]{:S(2)}) %collective-permute-start.2) | collective-permute-done | bytes 237600 | tf_op jit(solution)/shard_map/ppermute | solution.py:541
  22.8 0.1 add.4.refs_1_
  22.9 0.1 collective-permute-start.3
  23.0 2.1 %stage.1 = (bf16[544,3456]{1,0:T(8,128)(2,1)S(1)}, f32[4,512]{1,0:T(4,128)S(1)}, bf16[32,256]{1,0:T(8,128)(2,1)S(1)}) custom-call(bf16[512,3456]{1,0:T(8,128)(2,1)} %bitcast.47, bf16[32,3456]{1,0:T(8,128)(2,1)} %bitcast.48, s32[16,32]{1,0:T(8,128)} %bitcast.49, s32[16,32]{1,0:T(8,128)} %bitcast.50, f32[16,32]{1,0:T(8,128)} %bitcast.51, f32[16,32]{1,0:T(8,128)} %bitcast.52, ...), custom_call_target="tpu_custom_call" | custom-call | bytes 7520256 | tf_op jit(solution)/shard_map/stage/pallas_call | solution.py:134
  25.2 3.6 %early.1 = (bf16[256,3712]{1,0:T(8,128)(2,1)S(1)}, f32[256,544]{1,0:T(8,128)S(1)}, bf16[256,544]{1,0:T(8,128)(2,1)S(1)}) custom-call(bf16[544,3456]{1,0:T(8,128)(2,1)S(1)} %get-tuple-element.36.xs.refs_0_, bf16[32,3712]{1,0:T(8,128)(2,1)S(1)} %bitcast_convert_fusion.refs_0_, bf16[32,3712]{1,0:T(8,128)(2,1)S(1)} %collective-permute-done.1.refs_1_, ...), custom_call_target="tpu_custom_call" | custom-call | flops 962592768 | bytes 3538944 | tf_op jit(solution)/shard_map/early/pallas_call | solution.py:191
  28.8 4.9 %learner.1 = (bf16[256,3712]{1,0:T(8,128)(2,1)S(1)}, f32[256,544]{1,0:T(8,128)S(1)}, bf16[256,544]{1,0:T(8,128)(2,1)S(1)}, f32[32,256]{1,0:T(8,128)}, f32[18,1,3...) custom-call(bf16[544,3456]{1,0:T(8,128)(2,1)S(1)} %get-tuple-element, ...), custom_call_target="tpu_custom_call", output_to_operand_aliasing={{0}: (5, {}), {1}: (6, {}), {2}: (7, {})} | custom-call | flops 1925185536 | bytes 7520256 | tf_op jit(solution)/shard_map/learner/pallas_call | solution.py:302
  33.7 0.0 copy-start.3
  33.7 0.6 collective-permute-start.16
  34.2 1.2 %collective-permute-done.16.refs_1_.refs_3_ = bf16[32,3968]{1,0:T(8,128)(2,1)S(1)} collective-permute-done((bf16[32,3968]{1,0:T(8,128)(2,1)S(1)}, bf16[32,3968]{1,0:T(8,128)(2,1)S(1)}, u32[]{:S(2)}, u32[]{:S(2)}) %collective-permute-start.16) | collective-permute-done | bytes 253984 | tf_op jit(solution)/shard_map/ppermute | solution.py:546
  35.4 0.1 add.5.refs_2_.refs_3_.refs_6_
  35.5 2.5 %collective-permute-start.20 = (bf16[32,3968]{1,0:T(8,128)(2,1)S(1)}, bf16[32,3968]{1,0:T(8,128)(2,1)S(1)}, u32[]{:S(2)}, u32[]{:S(2)}) collective-permute-start(bf16[32,3968]{1,0:T(8,128)(2,1)S(1)} %add.5.refs_2_.refs_3_.refs_6_), channel_id=1, source_target_pairs={{6,4},{7,5},{0,2},{1,3},{14,12},{15,13},{8,10},{9,11},{22,20},{23,... | collective-permute-start | bytes 761864 | tf_op jit(solution)/shard_map/ppermute | solution.py:541
  38.0 1.0 %rest.1 = (bf16[32,3712]{1,0:T(8,128)(2,1)S(1)}, bf16[32,3712]{1,0:T(8,128)(2,1)S(1)}, bf16[32,3712]{1,0:T(8,128)(2,1)S(1)}, bf16[32,3712]{1,0:T(8,128)(2,1)S(1)...) custom-call(bf16[544,3456]{1,0:T(8,128)(2,1)S(1)} %get-tuple-element.36.xs.refs_0_, ...), custom_call_target="tpu_custom_call" | custom-call | flops 905969664 | bytes 3538944 | tf_op jit(solution)/shard_map/rest/pallas_call | solution.py:324
  39.0 0.0 copy-start.7
  39.0 0.0 copy-start
  39.1 0.0 copy-start.1
  39.1 0.0 copy-start.2
  39.1 0.0 copy-start.5
  39.1 0.0 copy-start.6
  39.1 0.2 collective-permute-start.15
  39.3 0.4 collective-permute-start.19
  39.7 2.4 %collective-permute-start.10 = (bf16[32,3456]{1,0:T(8,128)(2,1)S(1)}, bf16[32,3456]{1,0:T(8,128)(2,1)S(1)}, u32[]{:S(2)}, u32[]{:S(2)}) collective-permute-start(bf16[32,3456]{1,0:T(8,128)(2,1)S(1)} %bitcast.38), channel_id=1, source_target_pairs={{0,24},{8,16},{16,8},{24,0},{1,25},{9,17},{17,9},{25,1},{2,26},{10... | collective-permute-start | bytes 663560 | tf_op jit(solution)/shard_map/ppermute | solution.py:549
  42.1 0.5 collective-permute-start.8
  42.7 0.7 collective-permute-start.18
  43.4 0.1 add.6
  43.4 2.1 %collective-permute-start.17 = (bf16[32,3968]{1,0:T(8,128)(2,1)S(1)}, bf16[32,3968]{1,0:T(8,128)(2,1)S(1)}, u32[]{:S(2)}, u32[]{:S(2)}) collective-permute-start(bf16[32,3968]{1,0:T(8,128)(2,1)S(1)} %add.6), channel_id=1, source_target_pairs={{2,0},{3,1},{4,6},{5,7},{6,2},{7,3},{0,4},{1,5},{10,8},{11,9},{12,... | collective-permute-start | bytes 761864 | tf_op jit(solution)/shard_map/ppermute | solution.py:541
  45.6 0.1 add.7
  45.7 0.9 %collective-permute-start.21 = (bf16[32,3968]{1,0:T(8,128)(2,1)S(1)}, bf16[32,3968]{1,0:T(8,128)(2,1)S(1)}, u32[]{:S(2)}, u32[]{:S(2)}) collective-permute-start(bf16[32,3968]{1,0:T(8,128)(2,1)S(1)} %add.7), channel_id=1, source_target_pairs={{4,0},{5,1},{2,6},{3,7},{0,2},{1,3},{6,4},{7,5},{12,8},{13,9},{10,... | collective-permute-start | bytes 761864 | tf_op jit(solution)/shard_map/ppermute | solution.py:541
  46.5 2.4 %collective-permute-done.10.refs_3_ = bf16[32,3456]{1,0:T(8,128)(2,1)S(1)} collective-permute-done((bf16[32,3456]{1,0:T(8,128)(2,1)S(1)}, bf16[32,3456]{1,0:T(8,128)(2,1)S(1)}, u32[]{:S(2)}, u32[]{:S(2)}) %collective-permute-start.10) | collective-permute-done | bytes 221216 | tf_op jit(solution)/shard_map/ppermute | solution.py:549
  48.9 1.5 %collective-permute-start.9 = (bf16[32,3456]{1,0:T(8,128)(2,1)S(1)}, bf16[32,3456]{1,0:T(8,128)(2,1)S(1)}, u32[]{:S(2)}, u32[]{:S(2)}) collective-permute-start(bf16[32,3456]{1,0:T(8,128)(2,1)S(1)} %bitcast.40), channel_id=1, source_target_pairs={{0,16},{8,24},{16,0},{24,8},{1,17},{9,25},{17,1},{25,9},{2,18},{10... | collective-permute-start | bytes 663560 | tf_op jit(solution)/shard_map/ppermute | solution.py:549
  50.4 2.4 %collective-permute-done.8.refs_1_ = bf16[32,3456]{1,0:T(8,128)(2,1)S(1)} collective-permute-done((bf16[32,3456]{1,0:T(8,128)(2,1)S(1)}, bf16[32,3456]{1,0:T(8,128)(2,1)S(1)}, u32[]{:S(2)}, u32[]{:S(2)}) %collective-permute-start.8) | collective-permute-done | bytes 221216 | tf_op jit(solution)/shard_map/ppermute | solution.py:549
  52.8 2.0 %collective-permute-done.9.refs_2_ = bf16[32,3456]{1,0:T(8,128)(2,1)S(1)} collective-permute-done((bf16[32,3456]{1,0:T(8,128)(2,1)S(1)}, bf16[32,3456]{1,0:T(8,128)(2,1)S(1)}, u32[]{:S(2)}, u32[]{:S(2)}) %collective-permute-start.9) | collective-permute-done | bytes 221216 | tf_op jit(solution)/shard_map/ppermute | solution.py:549
  54.8 2.2 %opponents.1 = (bf16[32,32]{1,0:T(8,128)(2,1)S(1)}, bf16[32,32]{1,0:T(8,128)(2,1)S(1)}, bf16[32,32]{1,0:T(8,128)(2,1)S(1)}, bf16[32,32]{1,0:T(8,128)(2,1)S(1)}) custom-call(bf16[32,3456]{1,0:T(8,128)(2,1)S(1)} %bitcast.41, bf16[32,3456]{1,0:T(8,128)(2,1)S(1)} %collective-permute-done.8.refs_1_, bf16[32,3456]{1,0:T(8,128)(2,1)S(1)} %collective-permute-done.9.refs_2_, ...), custom_call_target="tpu_custom_call" | custom-call | flops 226492416 | bytes 884736 | tf_op jit(solution)/shard_map/opponents/pallas_call | solution.py:360
  57.0 1.6 %collective-permute-start.11 = (bf16[32,32]{1,0:T(8,128)(2,1)S(1)}, bf16[32,32]{1,0:T(8,128)(2,1)S(1)}, u32[]{:S(2)}, u32[]{:S(2)}) collective-permute-start(bf16[32,32]{1,0:T(8,128)(2,1)S(1)} %get-tuple-element.45), channel_id=1, source_target_pairs={{0,8},{8,0},{16,24},{24,16},{1,9},{9,1},{17,25},{25,17},{2,10},{10... | collective-permute-start | bytes 6152 | tf_op jit(solution)/shard_map/ppermute | solution.py:549
  58.6 2.2 %collective-permute-done.11.refs_1_ = bf16[32,32]{1,0:T(8,128)(2,1)S(1)} collective-permute-done((bf16[32,32]{1,0:T(8,128)(2,1)S(1)}, bf16[32,32]{1,0:T(8,128)(2,1)S(1)}, u32[]{:S(2)}, u32[]{:S(2)}) %collective-permute-start.11) | collective-permute-done | bytes 2080 | tf_op jit(solution)/shard_map/ppermute | solution.py:549
  60.7 1.5 %collective-permute-start.12 = (bf16[32,32]{1,0:T(8,128)(2,1)S(1)}, bf16[32,32]{1,0:T(8,128)(2,1)S(1)}, u32[]{:S(2)}, u32[]{:S(2)}) collective-permute-start(bf16[32,32]{1,0:T(8,128)(2,1)S(1)} %get-tuple-element.46), channel_id=1, source_target_pairs={{0,16},{8,24},{16,0},{24,8},{1,17},{9,25},{17,1},{25,9},{2,18},{10... | collective-permute-start | bytes 6152 | tf_op jit(solution)/shard_map/ppermute | solution.py:549
  62.3 2.1 %collective-permute-done.12.refs_2_ = bf16[32,32]{1,0:T(8,128)(2,1)S(1)} collective-permute-done((bf16[32,32]{1,0:T(8,128)(2,1)S(1)}, bf16[32,32]{1,0:T(8,128)(2,1)S(1)}, u32[]{:S(2)}, u32[]{:S(2)}) %collective-permute-start.12) | collective-permute-done | bytes 2080 | tf_op jit(solution)/shard_map/ppermute | solution.py:549
  64.4 2.4 %collective-permute-start.13 = (bf16[32,32]{1,0:T(8,128)(2,1)S(1)}, bf16[32,32]{1,0:T(8,128)(2,1)S(1)}, u32[]{:S(2)}, u32[]{:S(2)}) collective-permute-start(bf16[32,32]{1,0:T(8,128)(2,1)S(1)} %get-tuple-element.47), channel_id=1, source_target_pairs={{0,24},{8,16},{16,8},{24,0},{1,25},{9,17},{17,9},{25,1},{2,26},{10... | collective-permute-start | bytes 6152 | tf_op jit(solution)/shard_map/ppermute | solution.py:549
  67.5 1.4 %collective-permute-done.13.refs_3_ = bf16[32,32]{1,0:T(8,128)(2,1)S(1)} collective-permute-done((bf16[32,32]{1,0:T(8,128)(2,1)S(1)}, bf16[32,32]{1,0:T(8,128)(2,1)S(1)}, u32[]{:S(2)}, u32[]{:S(2)}) %collective-permute-start.13) | collective-permute-done | bytes 2080 | tf_op jit(solution)/shard_map/ppermute | solution.py:549
  69.0 0.6 choose.1
  69.6 1.4 %adam.1 = (f32[32,3712]{1,0:T(8,128)}, f32[32,3712]{1,0:T(8,128)}, f32[32,3712]{1,0:T(8,128)}, f32[19,1,256]{2,1,0:T(1,128)}, f32[19,1,256]{2,1,0:T(1,128)}, /*index=5*/f32[19,1,256]{2,1,0:T(1,128)}) custom-call(f32[1,1]{1,0:T(1,128)} %bitcast.34.refs_0_, bf16[32,3712]{1,0:T(8,128)(2,1)S(1)} %get-tuple-element.50.refs_1_, ...), custom_call_target="tpu_custom_call" | custom-call | flops 2375680 | bytes 3801088 | tf_op jit(solution)/shard_map/adam/pallas_call | solution.py:499
  (24 shorter events, 0.1 us)
Async XLA Ops:
  1.7 10.3 %collective-permute-start.1 = (bf16[32,3712]{1,0:T(8,128)(2,1)S(1)}, bf16[32,3712]{1,0:T(8,128)(2,1)S(1)}, u32[]{:S(2)}, u32[]{:S(2)}) collective-permute-start(bf16[32,3712]{1,0:T(8,128)(2,1)S(1)} %bitcast_convert_fusion.refs_0_), channel_id=1, source_target_pairs={{0,4},{1,5},{6,2},{7,3},{2,0},{3,1},{4,6},{5,7},{8,12},{9,13},{14,... | collective-permute-start | bytes 712712 | tf_op jit(solution)/shard_map/ppermute | solution.py:541
  5.8 12.1 %collective-permute-start.4 = (bf16[32,3712]{1,0:T(8,128)(2,1)S(1)}, bf16[32,3712]{1,0:T(8,128)(2,1)S(1)}, u32[]{:S(2)}, u32[]{:S(2)}) collective-permute-start(bf16[32,3712]{1,0:T(8,128)(2,1)S(1)} %bitcast_convert_fusion.refs_0_), channel_id=1, source_target_pairs={{0,2},{1,3},{6,4},{7,5},{2,6},{3,7},{4,0},{5,1},{8,10},{9,11},{14,... | collective-permute-start | bytes 712712 | tf_op jit(solution)/shard_map/ppermute | solution.py:541
  5.8 12.1 %collective-permute-start = (bf16[32,3712]{1,0:T(8,128)(2,1)S(1)}, bf16[32,3712]{1,0:T(8,128)(2,1)S(1)}, u32[]{:S(2)}, u32[]{:S(2)}) collective-permute-start(bf16[32,3712]{1,0:T(8,128)(2,1)S(1)} %bitcast_convert_fusion.refs_0_), channel_id=1, source_target_pairs={{2,4},{3,5},{4,2},{5,3},{10,12},{11,13},{12,10},{13,11},{18,20},{1... | collective-permute-start | bytes 712712 | tf_op jit(solution)/shard_map/ppermute | solution.py:541
  12.0 10.8 %collective-permute-start.2 = (bf16[32,3712]{1,0:T(8,128)(2,1)S(1)}, bf16[32,3712]{1,0:T(8,128)(2,1)S(1)}, u32[]{:S(2)}, u32[]{:S(2)}) collective-permute-start(bf16[32,3712]{1,0:T(8,128)(2,1)S(1)} %collective-permute-done.1.refs_1_), channel_id=1, source_target_pairs={{4,6},{5,7},{2,0},{3,1},{12,14},{13,15},{10,8},{11,9},{20,22},{21,... | collective-permute-start | bytes 712712 | tf_op jit(solution)/shard_map/ppermute | solution.py:541
  13.3 11.8 %collective-permute-start.5 = (bf16[32,3712]{1,0:T(8,128)(2,1)S(1)}, bf16[32,3712]{1,0:T(8,128)(2,1)S(1)}, u32[]{:S(2)}, u32[]{:S(2)}) collective-permute-start(bf16[32,3712]{1,0:T(8,128)(2,1)S(1)} %bitcast_convert_fusion.refs_0_), channel_id=1, source_target_pairs={{0,1},{1,0},{2,3},{3,2},{4,5},{5,4},{6,7},{7,6},{8,9},{9,8},{10,11... | collective-permute-start | bytes 712712 | tf_op jit(solution)/shard_map/ppermute | solution.py:546
  13.4 11.8 %collective-permute-start.6 = (bf16[32,3712]{1,0:T(8,128)(2,1)S(1)}, bf16[32,3712]{1,0:T(8,128)(2,1)S(1)}, u32[]{:S(2)}, u32[]{:S(2)}) collective-permute-start(bf16[32,3712]{1,0:T(8,128)(2,1)S(1)} %collective-permute-done.1.refs_1_), channel_id=1, source_target_pairs={{0,1},{1,0},{2,3},{3,2},{4,5},{5,4},{6,7},{7,6},{8,9},{9,8},{10,11... | collective-permute-start | bytes 712712 | tf_op jit(solution)/shard_map/ppermute | solution.py:546
  17.9 7.3 %collective-permute-start.7 = (bf16[32,3712]{1,0:T(8,128)(2,1)S(1)}, bf16[32,3712]{1,0:T(8,128)(2,1)S(1)}, u32[]{:S(2)}, u32[]{:S(2)}) collective-permute-start(bf16[32,3712]{1,0:T(8,128)(2,1)S(1)} %collective-permute-done.4.refs_2_), channel_id=1, source_target_pairs={{0,1},{1,0},{2,3},{3,2},{4,5},{5,4},{6,7},{7,6},{8,9},{9,8},{10,11... | collective-permute-start | bytes 712712 | tf_op jit(solution)/shard_map/ppermute | solution.py:546
  22.9 5.9 %collective-permute-start.3 = (bf16[32,3712]{1,0:T(8,128)(2,1)S(1)}, bf16[32,3712]{1,0:T(8,128)(2,1)S(1)}, u32[]{:S(2)}, u32[]{:S(2)}) collective-permute-start(bf16[32,3712]{1,0:T(8,128)(2,1)S(1)} %add.4.refs_1_), channel_id=1, source_target_pairs={{0,1},{1,0},{2,3},{3,2},{4,5},{5,4},{6,7},{7,6},{8,9},{9,8},{10,11... | collective-permute-start | bytes 712712 | tf_op jit(solution)/shard_map/ppermute | solution.py:546
  33.7 6.0 %copy-start.3 = (bf16[1,32,3456]{2,1,0:T(8,128)(2,1)S(1)}, bf16[1,32,3456]{2,1,0:T(8,128)(2,1)}, u32[]{:S(2)}) copy-start(bf16[1,32,3456]{2,1,0:T(8,128)(2,1)} %param.17) | copy-start | bytes 663556
  33.7 1.7 %collective-permute-start.16 = (bf16[32,3968]{1,0:T(8,128)(2,1)S(1)}, bf16[32,3968]{1,0:T(8,128)(2,1)S(1)}, u32[]{:S(2)}, u32[]{:S(2)}) collective-permute-start(bf16[32,3968]{1,0:T(8,128)(2,1)S(1)} %get-tuple-element.55), channel_id=1, source_target_pairs={{0,1},{1,0},{2,3},{3,2},{4,5},{5,4},{6,7},{7,6},{8,9},{9,8},{10,11... | collective-permute-start | bytes 761864 | tf_op jit(solution)/shard_map/ppermute | solution.py:546
  35.5 10.1 %collective-permute-start.20 = (bf16[32,3968]{1,0:T(8,128)(2,1)S(1)}, bf16[32,3968]{1,0:T(8,128)(2,1)S(1)}, u32[]{:S(2)}, u32[]{:S(2)}) collective-permute-start(bf16[32,3968]{1,0:T(8,128)(2,1)S(1)} %add.5.refs_2_.refs_3_.refs_6_), channel_id=1, source_target_pairs={{6,4},{7,5},{0,2},{1,3},{14,12},{15,13},{8,10},{9,11},{22,20},{23,... | collective-permute-start | bytes 761864 | tf_op jit(solution)/shard_map/ppermute | solution.py:541
  39.0 29.9 %copy-start.7 = (s32[1,32,1]{1,2,0:T(1,128)S(1)}, s32[1,32,1]{1,2,0:T(1,128)}, u32[]{:S(2)}) copy-start(s32[1,32,1]{1,2,0:T(1,128)} %param.18) | copy-start | bytes 388
  39.0 30.5 %copy-start = (f32[1,32,3712]{2,1,0:T(8,128)S(1)}, f32[1,32,3712]{2,1,0:T(8,128)}, u32[]{:S(2)}) copy-start(f32[1,32,3712]{2,1,0:T(8,128)} %param.23) | copy-start | bytes 1425412
  39.1 30.5 %copy-start.1 = (f32[1,32,3712]{2,1,0:T(8,128)S(1)}, f32[1,32,3712]{2,1,0:T(8,128)}, u32[]{:S(2)}) copy-start(f32[1,32,3712]{2,1,0:T(8,128)} %param.24) | copy-start | bytes 1425412
  39.1 30.5 %copy-start.2 = (f32[1,32,3712]{2,1,0:T(8,128)S(1)}, f32[1,32,3712]{2,1,0:T(8,128)}, u32[]{:S(2)}) copy-start(f32[1,32,3712]{2,1,0:T(8,128)} %param.25) | copy-start | bytes 1425412
  39.1 30.5 %copy-start.4 = (f32[1,19,256]{2,0,1:T(1,128)S(1)}, f32[1,19,256]{2,0,1:T(1,128)}, u32[]{:S(2)}) copy-start(f32[1,19,256]{2,0,1:T(1,128)} %param.26) | copy-start | bytes 58372
  39.1 30.5 %copy-start.5 = (f32[1,19,256]{2,0,1:T(1,128)S(1)}, f32[1,19,256]{2,0,1:T(1,128)}, u32[]{:S(2)}) copy-start(f32[1,19,256]{2,0,1:T(1,128)} %param.27) | copy-start | bytes 58372
  39.1 30.5 %copy-start.6 = (f32[1,19,256]{2,0,1:T(1,128)S(1)}, f32[1,19,256]{2,0,1:T(1,128)}, u32[]{:S(2)}) copy-start(f32[1,19,256]{2,0,1:T(1,128)} %param.28) | copy-start | bytes 58372
  39.1 3.6 %collective-permute-start.15 = (bf16[32,3712]{1,0:T(8,128)(2,1)S(1)}, bf16[32,3712]{1,0:T(8,128)(2,1)S(1)}, u32[]{:S(2)}, u32[]{:S(2)}) collective-permute-start(bf16[32,3712]{1,0:T(8,128)(2,1)S(1)} %get-tuple-element.53), channel_id=1, source_target_pairs={{0,1},{1,0},{2,3},{3,2},{4,5},{5,4},{6,7},{7,6},{8,9},{9,8},{10,11... | collective-permute-start | bytes 712712 | tf_op jit(solution)/shard_map/ppermute | solution.py:546
  39.3 4.2 %collective-permute-start.19 = (bf16[32,3712]{1,0:T(8,128)(2,1)S(1)}, bf16[32,3712]{1,0:T(8,128)(2,1)S(1)}, u32[]{:S(2)}, u32[]{:S(2)}) collective-permute-start(bf16[32,3712]{1,0:T(8,128)(2,1)S(1)} %get-tuple-element.57), channel_id=1, source_target_pairs={{0,1},{1,0},{2,3},{3,2},{4,5},{5,4},{6,7},{7,6},{8,9},{9,8},{10,11... | collective-permute-start | bytes 712712 | tf_op jit(solution)/shard_map/ppermute | solution.py:546
  39.7 9.2 %collective-permute-start.10 = (bf16[32,3456]{1,0:T(8,128)(2,1)S(1)}, bf16[32,3456]{1,0:T(8,128)(2,1)S(1)}, u32[]{:S(2)}, u32[]{:S(2)}) collective-permute-start(bf16[32,3456]{1,0:T(8,128)(2,1)S(1)} %bitcast.38), channel_id=1, source_target_pairs={{0,24},{8,16},{16,8},{24,0},{1,25},{9,17},{17,9},{25,1},{2,26},{10... | collective-permute-start | bytes 663560 | tf_op jit(solution)/shard_map/ppermute | solution.py:549
  42.1 10.7 %collective-permute-start.8 = (bf16[32,3456]{1,0:T(8,128)(2,1)S(1)}, bf16[32,3456]{1,0:T(8,128)(2,1)S(1)}, u32[]{:S(2)}, u32[]{:S(2)}) collective-permute-start(bf16[32,3456]{1,0:T(8,128)(2,1)S(1)} %bitcast.39), channel_id=1, source_target_pairs={{0,8},{8,0},{16,24},{24,16},{1,9},{9,1},{17,25},{25,17},{2,10},{10... | collective-permute-start | bytes 663560 | tf_op jit(solution)/shard_map/ppermute | solution.py:549
  42.7 26.9 %collective-permute-start.18 = (bf16[32,3968]{1,0:T(8,128)(2,1)S(1)}, bf16[32,3968]{1,0:T(8,128)(2,1)S(1)}, u32[]{:S(2)}, u32[]{:S(2)}) collective-permute-start(bf16[32,3968]{1,0:T(8,128)(2,1)S(1)} %add.5.refs_2_.refs_3_.refs_6_), channel_id=1, source_target_pairs={{2,4},{3,5},{4,2},{5,3},{10,12},{11,13},{12,10},{13,11},{18,20},{1... | collective-permute-start | bytes 761864 | tf_op jit(solution)/shard_map/ppermute | solution.py:541
  43.4 26.1 %collective-permute-start.17 = (bf16[32,3968]{1,0:T(8,128)(2,1)S(1)}, bf16[32,3968]{1,0:T(8,128)(2,1)S(1)}, u32[]{:S(2)}, u32[]{:S(2)}) collective-permute-start(bf16[32,3968]{1,0:T(8,128)(2,1)S(1)} %add.6), channel_id=1, source_target_pairs={{2,0},{3,1},{4,6},{5,7},{6,2},{7,3},{0,4},{1,5},{10,8},{11,9},{12,... | collective-permute-start | bytes 761864 | tf_op jit(solution)/shard_map/ppermute | solution.py:541
  45.7 23.9 %collective-permute-start.21 = (bf16[32,3968]{1,0:T(8,128)(2,1)S(1)}, bf16[32,3968]{1,0:T(8,128)(2,1)S(1)}, u32[]{:S(2)}, u32[]{:S(2)}) collective-permute-start(bf16[32,3968]{1,0:T(8,128)(2,1)S(1)} %add.7), channel_id=1, source_target_pairs={{4,0},{5,1},{2,6},{3,7},{0,2},{1,3},{6,4},{7,5},{12,8},{13,9},{10,... | collective-permute-start | bytes 761864 | tf_op jit(solution)/shard_map/ppermute | solution.py:541
  48.9 5.9 %collective-permute-start.9 = (bf16[32,3456]{1,0:T(8,128)(2,1)S(1)}, bf16[32,3456]{1,0:T(8,128)(2,1)S(1)}, u32[]{:S(2)}, u32[]{:S(2)}) collective-permute-start(bf16[32,3456]{1,0:T(8,128)(2,1)S(1)} %bitcast.40), channel_id=1, source_target_pairs={{0,16},{8,24},{16,0},{24,8},{1,17},{9,25},{17,1},{25,9},{2,18},{10... | collective-permute-start | bytes 663560 | tf_op jit(solution)/shard_map/ppermute | solution.py:549
  52.8 16.7 %collective-permute-start.14 = (bf16[32,3712]{1,0:T(8,128)(2,1)S(1)}, bf16[32,3712]{1,0:T(8,128)(2,1)S(1)}, u32[]{:S(2)}, u32[]{:S(2)}) collective-permute-start(bf16[32,3712]{1,0:T(8,128)(2,1)S(1)} %get-tuple-element.51), channel_id=1, source_target_pairs={{0,1},{1,0},{2,3},{3,2},{4,5},{5,4},{6,7},{7,6},{8,9},{9,8},{10,11... | collective-permute-start | bytes 712712 | tf_op jit(solution)/shard_map/ppermute | solution.py:546
  57.0 3.7 %collective-permute-start.11 = (bf16[32,32]{1,0:T(8,128)(2,1)S(1)}, bf16[32,32]{1,0:T(8,128)(2,1)S(1)}, u32[]{:S(2)}, u32[]{:S(2)}) collective-permute-start(bf16[32,32]{1,0:T(8,128)(2,1)S(1)} %get-tuple-element.45), channel_id=1, source_target_pairs={{0,8},{8,0},{16,24},{24,16},{1,9},{9,1},{17,25},{25,17},{2,10},{10... | collective-permute-start | bytes 6152 | tf_op jit(solution)/shard_map/ppermute | solution.py:549
  60.7 3.7 %collective-permute-start.12 = (bf16[32,32]{1,0:T(8,128)(2,1)S(1)}, bf16[32,32]{1,0:T(8,128)(2,1)S(1)}, u32[]{:S(2)}, u32[]{:S(2)}) collective-permute-start(bf16[32,32]{1,0:T(8,128)(2,1)S(1)} %get-tuple-element.46), channel_id=1, source_target_pairs={{0,16},{8,24},{16,0},{24,8},{1,17},{9,25},{17,1},{25,9},{2,18},{10... | collective-permute-start | bytes 6152 | tf_op jit(solution)/shard_map/ppermute | solution.py:549
  64.4 4.5 %collective-permute-start.13 = (bf16[32,32]{1,0:T(8,128)(2,1)S(1)}, bf16[32,32]{1,0:T(8,128)(2,1)S(1)}, u32[]{:S(2)}, u32[]{:S(2)}) collective-permute-start(bf16[32,32]{1,0:T(8,128)(2,1)S(1)} %get-tuple-element.47), channel_id=1, source_target_pairs={{0,24},{8,16},{16,8},{24,0},{1,25},{9,17},{17,9},{25,1},{2,26},{10... | collective-permute-start | bytes 6152 | tf_op jit(solution)/shard_map/ppermute | solution.py:549

commit v4 on v3

--- a/solution.py
+++ b/solution.py
@@ -219,7 +219,7 @@
     aux_ref, head_ref, refs = refs[0], refs[1], refs[2:]
     if roles is not None:
         refs = refs[3:]
-    ws, first, first_bf, ghead_ref, own_ref, gp, refs = *refs[:6], refs[6:]
+    ws, first, first_bf, own_ref, gp, refs = *refs[:5], refs[5:]
     lead, sw = refs[:-1], refs[-1]
     learn, width, units, length = cfg["learn"], cfg["width"], cfg["units"], cfg["length"]
     envs = learn // length
@@ -241,7 +241,8 @@
         out[:, :learn], boot, aux_ref[...], heads - 1, length, 1.0 / length
     ).astype(jnp.bfloat16)
     ghead = dot(grad, second_bf[:, :learn], NT)
-    ghead_ref[...] = ghead
+    if roles is None:
+        lead[0][...] = ghead
     grad_second = dot(head_ref[...].T, grad, NN)
     grad_two = jnp.where(pre_two[:, :learn] > 0, grad_second, 0.0).astype(jnp.bfloat16)
     grad_first = grad_second + dot(ws[:, width:].T, grad_two, NN)
@@ -293,26 +294,25 @@
     block = lambda rows: jax.ShapeDtypeStruct((rows, width + units), jnp.bfloat16)
     inputs = 3 + len(piece_list)
     if roles is None:
-        lead, rest, aliases = [], [block(units)], {}
+        lead, rest, aliases = [jax.ShapeDtypeStruct((padded, units), jnp.float32)], [block(units)], {}
     else:
         rows = units // (len(roles) * CORES)
         wider = jax.ShapeDtypeStruct((rows, width + 2 * units), jnp.bfloat16)
         lead, rest = [wider] * CORES, [block(rows)] * (CORES * (len(roles) - 1))
         aliases = {inputs + i: i for i in range(len(before))}
-    weights, _, first_bf, ghead, own, gp, *first_outs = pl.pallas_call(
+    weights, _, first_bf, own, gp, *first_outs = pl.pallas_call(
         functools.partial(learner_kernel, cfg),
         out_shape=(
             block(units),
             jax.ShapeDtypeStruct((units, total), jnp.float32),
             jax.ShapeDtypeStruct((units, total), jnp.bfloat16),
-            jax.ShapeDtypeStruct((padded, units), jnp.float32),
             jax.ShapeDtypeStruct((cfg["heads"] - 1, 1, total - learn), jnp.float32),
             jax.ShapeDtypeStruct((units, 2 * learn), jnp.bfloat16),
             *lead,
         ),
         in_specs=[LOCAL] + [ANYWHERE if roles is None else LOCAL] * len(piece_list)
         + [LOCAL] * (2 + len(before)),
-        out_specs=(LOCAL,) * (6 + len(lead)),
+        out_specs=(LOCAL,) * (5 + len(lead)),
         input_output_aliases=aliases,
         scratch_shapes=[pltpu.SemaphoreType.DMA((len(piece_list),))],
         compiler_params=pltpu.CompilerParams(vmem_limit_bytes=32 << 20),
@@ -332,7 +332,7 @@
         ),
         name="rest",
     )(staged, gp, first_bf)
-    return weights, ghead, own, first_outs, list(rest_outs)
+    return weights, own, first_outs, list(rest_outs)
 
 
 def opponent_kernel(cfg, count, *refs):
@@ -401,46 +401,51 @@
     )(*answers, ids)
 
 
-def add_kernel(*refs):
-    total = sum(x[...].astype(jnp.float32) for x in refs[:-1])
-    refs[-1][...] = total.astype(refs[-1].dtype)
-
-
-def add(*arrays):
+def total_of(refs, columns):
+    return sum(x[:, columns].astype(jnp.float32) for x in refs)
+
+
+def small_kernel(body, out_shape, args):
+    bytes_accessed = sum(x.size * x.dtype.itemsize for x in args)
     return pl.pallas_call(
-        add_kernel,
-        out_shape=jax.ShapeDtypeStruct(arrays[0].shape, arrays[0].dtype),
-        in_specs=[LOCAL] * len(arrays),
-        out_specs=LOCAL,
+        body,
+        out_shape=out_shape,
+        in_specs=[LOCAL] * len(args),
+        out_specs=jax.tree.map(lambda _: LOCAL, out_shape),
         compiler_params=pltpu.CompilerParams(vmem_limit_bytes=4 << 20),
         cost_estimate=pl.CostEstimate(
-            flops=arrays[0].size, bytes_accessed=6 * arrays[0].size, transcendentals=0
-        ),
-        name="add",
-    )(*arrays)
-
-
-def add_with_heads_kernel(count, units, *refs):
-    ins, heads, out = refs[:count], refs[count:-1], refs[-1]
-    width = out.shape[1] - units
-    for columns, parts in ((slice(0, width), ins), (slice(width, width + units), heads)):
-        total = sum(x[:, columns].astype(jnp.float32) for x in parts)
-        out[:, columns] = total.astype(out.dtype)
-
-
-def add_with_heads(arrays, heads, units):
+            flops=bytes_accessed, bytes_accessed=bytes_accessed, transcendentals=0
+        ),
+    )(*args)
+
+
+def add(*arrays, dtype=jnp.bfloat16):
+    width = min(x.shape[1] for x in arrays)
+
+    def body(*refs):
+        refs[-1][...] = total_of(refs[:-1], slice(0, width)).astype(dtype)
+
+    shape = jax.ShapeDtypeStruct((arrays[0].shape[0], width), dtype)
+    return small_kernel(body, shape, arrays)
+
+
+def add_with_heads(arrays, heads, units, cut=None):
     rows, wide = heads[0].shape
-    return pl.pallas_call(
-        functools.partial(add_with_heads_kernel, len(arrays), units),
-        out_shape=jax.ShapeDtypeStruct((rows, wide), jnp.bfloat16),
-        in_specs=[LOCAL] * (len(arrays) + len(heads)),
-        out_specs=LOCAL,
-        compiler_params=pltpu.CompilerParams(vmem_limit_bytes=4 << 20),
-        cost_estimate=pl.CostEstimate(
-            flops=rows * wide, bytes_accessed=2 * len(arrays) * rows * wide, transcendentals=0
-        ),
-        name="add",
-    )(*arrays, *heads)
+    width = wide - units
+
+    def body(*refs):
+        ins, tops, outs = refs[: len(arrays)], refs[len(arrays) :][: len(heads)], refs[len(args) :]
+        edges = [0, width] if cut is None else [0, cut, width]
+        for out, start, stop in zip(outs, edges, edges[1:]):
+            out[:, : stop - start] = total_of(ins, slice(start, stop)).astype(out.dtype)
+        tail = slice(width, wide)
+        outs[-1][:, width - edges[-2] :] = total_of(tops, tail).astype(outs[-1].dtype)
+
+    args = (*arrays, *heads)
+    widths = [wide] if cut is None else [cut, wide - cut]
+    shape = [jax.ShapeDtypeStruct((rows, w), jnp.bfloat16) for w in widths]
+    result = small_kernel(body, tuple(shape), args)
+    return result[0] if cut is None else result
 
 
 def adam_step(master, moment, second, grad, rate):
@@ -450,33 +455,39 @@
     return (master, moment, second)
 
 
-def adam_kernel(parts, head_parts, cuts, *refs):
+def head_gradient(head_parts, count, units):
+    if len(head_parts) == 1:
+        return head_parts[0][:count]
+    mine, mid, near, far = (x[:count, x.shape[1] - units :].astype(jnp.float32) for x in head_parts)
+    _, chip = where_am_i()
+    end = jnp.logical_or(chip == 0, chip == LINE - 1)
+    rounded = lambda x: x.astype(jnp.bfloat16).astype(jnp.float32)
+    pair = rounded(mine + jnp.where(end, near, far))
+    return pair + jnp.where(end, far, rounded(mid + near))
+
+
+def adam_kernel(parts, offsets, head_parts, prior, cuts, *refs):
     rate = refs[0][...]
     parts, refs = refs[1 : 1 + parts], refs[1 + parts :]
     head_parts, refs = refs[:head_parts], refs[head_parts:]
-    core, head, core_out, head_out = refs[:3], refs[3:6], refs[6:9], refs[9:12]
-    stages, head_stages, sems, head_sems = refs[12:15], refs[15:18], refs[18], refs[19]
-    count, _, units = head[0].shape
-    if len(head_parts) == 1:
-        grad = head_parts[0][:count]
-    else:
-        mine, mid, near, far = (
-            x[:count, x.shape[1] - units :].astype(jnp.float32) for x in head_parts
-        )
-        _, chip = where_am_i()
-        end = jnp.logical_or(chip == 0, chip == LINE - 1)
-        rounded = lambda x: x.astype(jnp.bfloat16).astype(jnp.float32)
-        pair = rounded(mine + jnp.where(end, near, far))
-        grad = pair + jnp.where(end, far, rounded(mid + near))
-    grad = grad.reshape(head[0].shape)
-    copies = []
-    for i, value in enumerate(adam_step(*(x[...] for x in head), grad, rate)):
-        head_stages[i][...] = value
-        copies.append(pltpu.make_async_copy(head_stages[i], head_out[i], head_sems.at[i]))
-        copies[-1].start()
+    heads = 3 if head_parts else 0
+    core, head, refs = refs[:3], refs[3 : 3 + heads], refs[3 + heads + prior :]
+    core_out, head_out, refs = refs[:3], refs[3 : 3 + heads], refs[3 + heads :]
+    stages, head_stages, refs = refs[:3], refs[3 : 3 + heads], refs[3 + heads :]
+    sems, copies = refs[0], []
+    if heads:
+        count, _, units = head[0].shape
+        grad = head_gradient(head_parts, count, units).reshape(head[0].shape)
+        for i, value in enumerate(adam_step(*(x[...] for x in head), grad, rate)):
+            head_stages[i][...] = value
+            copies.append(pltpu.make_async_copy(head_stages[i], head_out[i], refs[1].at[i]))
+            copies[-1].start()
     for n, (start, stop) in enumerate(cuts):
         columns = slice(start, stop)
-        grad = sum(part[:, columns].astype(jnp.float32) for part in parts)
+        grad = sum(
+            part[:, start - offset : stop - offset].astype(jnp.float32)
+            for part, offset in zip(parts, offsets)
+        )
         for i, value in enumerate(adam_step(*(x[:, columns] for x in core), grad, rate)):
             stages[i][:, columns] = value
             copies.append(
@@ -489,27 +500,39 @@
         copy.wait()
 
 
-def adam(rates, parts, head_parts, core, head):
+def adam(rates, parts, head_parts, core, head, span, prior=()):
     rows, width = core[0].shape
-    tiles, pieces = width // 128, 5
-    edges = [128 * (tiles * n // pieces) for n in range(pieces)] + [width]
+    start, stop = span
+    tiles = (stop - start) // 128
+    pieces = max(1, tiles // 5)
+    edges = [start + 128 * (tiles * n // pieces) for n in range(pieces)] + [stop]
     cuts = list(zip(edges, edges[1:]))
+    arrays, offsets = [a for a, _ in parts], [o for _, o in parts]
+    if not head_parts:
+        head = ()
     one = jax.ShapeDtypeStruct((rows, width), jnp.float32)
-    small = jax.ShapeDtypeStruct(head[0].shape, jnp.float32)
+    inputs = 1 + len(parts) + len(head_parts) + 3 + len(head)
+    sems = [pltpu.SemaphoreType.DMA((len(cuts), 3))]
+    if head:
+        sems.append(pltpu.SemaphoreType.DMA((3,)))
     return pl.pallas_call(
-        functools.partial(adam_kernel, len(parts), len(head_parts), cuts),
-        out_shape=(one,) * 3 + (small,) * 3,
-        in_specs=[LOCAL] * (len(parts) + len(head_parts) + 7),
-        out_specs=(ANYWHERE,) * 6,
+        functools.partial(
+            adam_kernel, len(parts), offsets, len(head_parts), len(prior), cuts
+        ),
+        out_shape=(one,) * 3 + tuple(jax.ShapeDtypeStruct(x.shape, jnp.float32) for x in head),
+        in_specs=[LOCAL] * inputs + [ANYWHERE] * len(prior),
+        out_specs=(ANYWHERE,) * (3 + len(head)),
+        input_output_aliases={inputs + i: i for i in range(len(prior))},
         scratch_shapes=[pltpu.VMEM((rows, width), jnp.float32)] * 3
-        + [pltpu.VMEM(head[0].shape, jnp.float32)] * 3
-        + [pltpu.SemaphoreType.DMA((len(cuts), 3)), pltpu.SemaphoreType.DMA((3,))],
-        compiler_params=pltpu.CompilerParams(vmem_limit_bytes=16 << 20),
+        + [pltpu.VMEM(x.shape, jnp.float32) for x in head]
+        + sems,
+        compiler_params=pltpu.CompilerParams(vmem_limit_bytes=12 << 20),
         cost_estimate=pl.CostEstimate(
-            flops=20 * rows * width, bytes_accessed=32 * rows * width, transcendentals=0
+            flops=20 * rows * (stop - start), bytes_accessed=32 * rows * (stop - start),
+            transcendentals=0,
         ),
         name="adam",
-    )(rates.reshape(1, 1), *parts, *head_parts, *core, *head)
+    )(rates.reshape(1, 1), *arrays, *head_parts, *core, *head, *prior)
 
 
 def per_device(
@@ -536,6 +559,7 @@
     rows = core_master.shape[1]
     chips = members // CORES
     line = chips == LINE and members == LINE * CORES and units == members * rows and heads <= rows
+    wide = jnp.float32
 
     def along(x, pairs):
         return lax.ppermute(
@@ -584,7 +608,7 @@
     before = ()
     if line:
         before = early(staged, first_pieces, first_list, units)
-    weights, ghead, own, lead, rest = learner(staged, piece_list, aux, head, before, cfg)
+    weights, own, lead, rest = learner(staged, piece_list, aux, head, before, cfg)
     played = opponents(frames, weights, head, cfg)
     own_logits = jnp.transpose(own, (1, 2, 0))
 
@@ -604,20 +628,23 @@
         part_mid = along(last, SCATTER_MID)
         toward = add_with_heads((keep[1], came[1]), (last,), units)
         part_near = along(toward, SCATTER_NEAR)
-        beyond = add_with_heads((keep[2], came[2], through), (last, through), units)
-        part_far = along(beyond, SCATTER_FAR)
-        core_parts = (keep[3], came[3], part_near, part_mid, part_far)
-        head_parts = (last, part_mid, part_near, part_far)
+        cut = 128 * (5 * (width + units) // (8 * 128))
+        beyond = add_with_heads((keep[2], came[2], through), (last, through), units, cut)
+        part_far = [along(b, SCATTER_FAR) for b in beyond]
+        known = add(keep[3], came[3], part_near, part_mid, dtype=wide)
+        spans = ((0, cut), (cut, width + units))
+        parts = [((known, 0), (far, at)) for far, (at, _) in zip(part_far, spans)]
+        head_parts = (last, part_mid, part_near, part_far[1])
     else:
-        core_parts = (lax.psum_scatter(rest[0], "dp", scatter_dimension=0, tiled=True),)
-        head_parts = (lax.psum(ghead, "dp"),)
-    new = adam(
-        rates,
-        core_parts,
-        head_parts,
-        (core_master[0], core_mom[0], core_vel[0]),
-        (by_row(head_master), by_row(head_mom), by_row(head_vel)),
-    )
+        spans = ((0, width + units),)
+        total = lax.psum_scatter(rest[0], "dp", scatter_dimension=0, tiled=True)
+        parts, head_parts = [((total, 0),)], (lax.psum(lead[0], "dp"),)
+    core = (core_master[0], core_mom[0], core_vel[0])
+    head = (by_row(head_master), by_row(head_mom), by_row(head_vel))
+    new = ()
+    for span, part in zip(spans, parts):
+        final = span is spans[-1]
+        new = adam(rates, part, head_parts if final else (), core, head, span, new)
     return (own_logits, opp_logits.T[None], *[x[None] for x in new[:3]], *map(by_row, new[3:]))
 
 

time: 71.4 us -> 74.5 us (1.043)
  waiting for transfers between devices: 28.2 us -> 30.9 us
  Pallas kernels: 16.2 us -> 17 us
    ppermute x6, waiting for transfers between devices: 12.5 us -> 14.7 us  [swap(): lax.ppermute(x, 'agent', [(i, other_agent(i, by, agents)) for i in range(...]
    ppermute x8 -> x9, waiting for transfers between devices: 14.5 us -> 16.2 us  [along(): lax.ppermute(x, 'dp', [(a * CORES + c, b * CORES + c) for a, b in pairs f...]
    ppermute x8, waiting for transfers between devices: 1.17 us -> 0.03 us  [sibling(): return lax.ppermute(x, 'dp', [(i, i ^ 1) for i in range(members)])]
    ppermute x6, starting transfers between devices: 10 us -> 9.01 us  [swap(): lax.ppermute(x, 'agent', [(i, other_agent(i, by, agents)) for i in range(...]
    ppermute x8 -> x9, starting transfers between devices: 12.3 us -> 13.1 us  [along(): lax.ppermute(x, 'dp', [(a * CORES + c, b * CORES + c) for a, b in pairs f...]
    pallas_call x5 -> x7, Pallas kernels: 1.72 us -> 2.52 us  [the longest x2 2.12 us: adam(): pl.pallas_call(functools.partial(adam_kernel, len(parts), offsets, len(he...]
  transfers between devices with their start and end apart: 22 -> 23, of which waited for: 10 -> 9; matrix products, arithmetic and copies ran while one was open for 0% -> 0% of each run, Pallas kernels for 14% -> 15%
where the time goes in v4:
time: 74.5 us; the launch traced here: 74.2 us
  waiting for transfers between devices  30.9 us (41%)
  starting transfers between devices  23.7 us (32%)
  Pallas kernels  17 us (23%)
  between operations  1.56 us (2%)
  other arithmetic  1.05 us (1%)
    ppermute x9, waiting for transfers between devices, along(): lax.ppermute(x, 'dp', [(a * CORES + c, b * CORES + c) for a, b in pairs f...  16.2 us
    ppermute x6, waiting for transfers between devices, swap(): lax.ppermute(x, 'agent', [(i, other_agent(i, by, agents)) for i in range(...  14.7 us
    ppermute x9, starting transfers between devices, along(): lax.ppermute(x, 'dp', [(a * CORES + c, b * CORES + c) for a, b in pairs f...  13.1 us
    ppermute x6, starting transfers between devices, swap(): lax.ppermute(x, 'agent', [(i, other_agent(i, by, agents)) for i in range(...  9.01 us
    pallas_call x1, Pallas kernels, learner(): pl.pallas_call(functools.partial(learner_kernel, cfg), out_shape=(block(u...  4.88 us
    pallas_call x1, Pallas kernels, early(): pl.pallas_call(functools.partial(early_kernel, pieces, width), out_shape=...  3.59 us
    pallas_call x1, Pallas kernels, opponents(): pl.pallas_call(functools.partial(opponent_kernel, cfg, count), out_shape=...  2.21 us
    pallas_call x1, Pallas kernels, stage(): pl.pallas_call(stage_kernel, out_shape=(jax.ShapeDtypeStruct((total, widt...  2.15 us
  transfers between devices with their start and end apart: 23, of which 9 were waited for; matrix products, arithmetic and copies ran while one was open for 0% of the time, Pallas kernels for 15%

profile of v4, /device:TPU:0, one launch (start us, length us, event | category | flops | bytes accessed | tf_op | source)
XLA Modules:
  0.0 74.2 jit_solution(7050876551354445793)
XLA Ops:
  0.6 1.1 %bitcast_convert_fusion.refs_0_ = bf16[32,3712]{1,0:T(8,128)(2,1)S(1)} fusion(f32[1,32,3712]{2,1,0:T(8,128)} %param.23), kind=kLoop, calls=%fused_computation | loop fusion | flops 118784 | bytes 712704 | tf_op jit(solution)/shard_map/convert_element_type | solution.py:575
  1.7 4.1 %collective-permute-start.1 = (bf16[32,3712]{1,0:T(8,128)(2,1)S(1)}, bf16[32,3712]{1,0:T(8,128)(2,1)S(1)}, u32[]{:S(2)}, u32[]{:S(2)}) collective-permute-start(bf16[32,3712]{1,0:T(8,128)(2,1)S(1)} %bitcast_convert_fusion.refs_0_), channel_id=1, source_target_pairs={{0,4},{1,5},{6,2},{7,3},{2,0},{3,1},{4,6},{5,7},{8,12},{9,13},{14,... | collective-permute-start | bytes 712712 | tf_op jit(solution)/shard_map/ppermute | solution.py:565
  5.8 0.7 collective-permute-start
  6.5 5.5 %collective-permute-done.1.refs_1_ = bf16[32,3712]{1,0:T(8,128)(2,1)S(1)} collective-permute-done((bf16[32,3712]{1,0:T(8,128)(2,1)S(1)}, bf16[32,3712]{1,0:T(8,128)(2,1)S(1)}, u32[]{:S(2)}, u32[]{:S(2)}) %collective-permute-start.1) | collective-permute-done | bytes 237600 | tf_op jit(solution)/shard_map/ppermute | solution.py:565
  12.0 1.3 %collective-permute-start.2 = (bf16[32,3712]{1,0:T(8,128)(2,1)S(1)}, bf16[32,3712]{1,0:T(8,128)(2,1)S(1)}, u32[]{:S(2)}, u32[]{:S(2)}) collective-permute-start(bf16[32,3712]{1,0:T(8,128)(2,1)S(1)} %collective-permute-done.1.refs_1_), channel_id=1, source_target_pairs={{4,6},{5,7},{2,0},{3,1},{12,14},{13,15},{10,8},{11,9},{20,22},{21,... | collective-permute-start | bytes 712712 | tf_op jit(solution)/shard_map/ppermute | solution.py:565
  13.3 0.1 collective-permute-start.5
  13.4 0.5 collective-permute-start.6
  13.9 4.0 %collective-permute-done.4.refs_2_ = bf16[32,3712]{1,0:T(8,128)(2,1)S(1)} collective-permute-done((bf16[32,3712]{1,0:T(8,128)(2,1)S(1)}, bf16[32,3712]{1,0:T(8,128)(2,1)S(1)}, u32[]{:S(2)}, u32[]{:S(2)}) %collective-permute-start.4) | collective-permute-done | bytes 237600 | tf_op jit(solution)/shard_map/ppermute | solution.py:565
  17.9 4.9 %collective-permute-done.2.refs_1_ = bf16[32,3712]{1,0:T(8,128)(2,1)S(1)} collective-permute-done((bf16[32,3712]{1,0:T(8,128)(2,1)S(1)}, bf16[32,3712]{1,0:T(8,128)(2,1)S(1)}, u32[]{:S(2)}, u32[]{:S(2)}) %collective-permute-start.2) | collective-permute-done | bytes 237600 | tf_op jit(solution)/shard_map/ppermute | solution.py:565
  22.8 0.1 shard_map.206.refs_1_
  22.9 0.1 collective-permute-start.3
  23.0 2.1 %stage.1 = (bf16[544,3456]{1,0:T(8,128)(2,1)S(1)}, f32[4,512]{1,0:T(4,128)S(1)}, bf16[32,256]{1,0:T(8,128)(2,1)S(1)}) custom-call(bf16[512,3456]{1,0:T(8,128)(2,1)} %bitcast.51, bf16[32,3456]{1,0:T(8,128)(2,1)} %bitcast.55, s32[16,32]{1,0:T(8,128)} %bitcast.56, s32[16,32]{1,0:T(8,128)} %bitcast.57, f32[16,32]{1,0:T(8,128)} %bitcast.58, f32[16,32]{1,0:T(8,128)} %bitcast.59, ...), custom_call_target="tpu_custom_call" | custom-call | bytes 7520256 | tf_op jit(solution)/shard_map/stage/pallas_call | solution.py:134
  25.2 3.6 %early.1 = (bf16[256,3712]{1,0:T(8,128)(2,1)S(1)}, f32[256,544]{1,0:T(8,128)S(1)}, bf16[256,544]{1,0:T(8,128)(2,1)S(1)}) custom-call(bf16[544,3456]{1,0:T(8,128)(2,1)S(1)} %get-tuple-element.41.xs.refs_0_, bf16[32,3712]{1,0:T(8,128)(2,1)S(1)} %bitcast_convert_fusion.refs_0_, bf16[32,3712]{1,0:T(8,128)(2,1)S(1)} %collective-permute-done.1.refs_1_, ...), custom_call_target="tpu_custom_call" | custom-call | flops 962592768 | bytes 3538944 | tf_op jit(solution)/shard_map/early/pallas_call | solution.py:191
  28.8 4.9 %learner.1 = (bf16[256,3712]{1,0:T(8,128)(2,1)S(1)}, f32[256,544]{1,0:T(8,128)S(1)}, bf16[256,544]{1,0:T(8,128)(2,1)S(1)}, f32[18,1,32]{2,1,0:T(1,128)}, bf16[25...) custom-call(bf16[544,3456]{1,0:T(8,128)(2,1)S(1)} %get-tuple-element, ...), custom_call_target="tpu_custom_call", output_to_operand_aliasing={{0}: (5, {}), {1}: (6, {}), {2}: (7, {})} | custom-call | flops 1925185536 | bytes 7520256 | tf_op jit(solution)/shard_map/learner/pallas_call | solution.py:303
  33.7 0.6 collective-permute-start.16
  34.2 1.0 %rest.1 = (bf16[32,3712]{1,0:T(8,128)(2,1)S(1)}, bf16[32,3712]{1,0:T(8,128)(2,1)S(1)}, bf16[32,3712]{1,0:T(8,128)(2,1)S(1)}, bf16[32,3712]{1,0:T(8,128)(2,1)S(1)...) custom-call(bf16[544,3456]{1,0:T(8,128)(2,1)S(1)} %get-tuple-element.41.xs.refs_0_, ...), custom_call_target="tpu_custom_call" | custom-call | flops 905969664 | bytes 3538944 | tf_op jit(solution)/shard_map/rest/pallas_call | solution.py:324
  35.3 0.1 collective-permute-start.15
  35.4 0.0 collective-permute-done.16.refs_1_.refs_3_
  35.4 0.1 shard_map.207.refs_2_.refs_3_
  35.4 0.0 copy-start
  35.4 0.0 copy-start.1
  35.5 2.7 %collective-permute-start.20 = (bf16[32,3968]{1,0:T(8,128)(2,1)S(1)}, bf16[32,3968]{1,0:T(8,128)(2,1)S(1)}, u32[]{:S(2)}, u32[]{:S(2)}) collective-permute-start(bf16[32,3968]{1,0:T(8,128)(2,1)S(1)} %shard_map.207.refs_2_.refs_3_), channel_id=1, source_target_pairs={{6,4},{7,5},{0,2},{1,3},{14,12},{15,13},{8,10},{9,11},{22,20},{23,... | collective-permute-start | bytes 761864 | tf_op jit(solution)/shard_map/ppermute | solution.py:565
  38.1 0.3 collective-permute-start.19
  38.4 2.4 %collective-permute-start.10 = (bf16[32,3456]{1,0:T(8,128)(2,1)S(1)}, bf16[32,3456]{1,0:T(8,128)(2,1)S(1)}, u32[]{:S(2)}, u32[]{:S(2)}) collective-permute-start(bf16[32,3456]{1,0:T(8,128)(2,1)S(1)} %bitcast.42), channel_id=1, source_target_pairs={{0,24},{8,16},{16,8},{24,0},{1,25},{9,17},{17,9},{25,1},{2,26},{10... | collective-permute-start | bytes 663560 | tf_op jit(solution)/shard_map/ppermute | solution.py:573
  40.9 0.5 collective-permute-start.8
  41.4 0.5 collective-permute-start.9
  41.9 0.1 shard_map.208
  42.0 5.7 %collective-permute-done.10.refs_3_ = bf16[32,3456]{1,0:T(8,128)(2,1)S(1)} collective-permute-done((bf16[32,3456]{1,0:T(8,128)(2,1)S(1)}, bf16[32,3456]{1,0:T(8,128)(2,1)S(1)}, u32[]{:S(2)}, u32[]{:S(2)}) %collective-permute-start.10) | collective-permute-done | bytes 221216 | tf_op jit(solution)/shard_map/ppermute | solution.py:573
  47.7 0.7 collective-permute-start.17
  48.3 0.7 collective-permute-start.18
  49.0 0.1 collective-permute-start.14
  49.1 0.0 copy-start.4
  49.1 0.1 shard_map.210
  49.2 2.6 %collective-permute-done.8.refs_1_ = bf16[32,3456]{1,0:T(8,128)(2,1)S(1)} collective-permute-done((bf16[32,3456]{1,0:T(8,128)(2,1)S(1)}, bf16[32,3456]{1,0:T(8,128)(2,1)S(1)}, u32[]{:S(2)}, u32[]{:S(2)}) %collective-permute-start.8) | collective-permute-done | bytes 221216 | tf_op jit(solution)/shard_map/ppermute | solution.py:573
  51.8 1.7 %collective-permute-start.22 = (bf16[32,2304]{1,0:T(8,128)(2,1)S(1)}, bf16[32,2304]{1,0:T(8,128)(2,1)S(1)}, u32[]{:S(2)}, u32[]{:S(2)}) collective-permute-start(bf16[32,2304]{1,0:T(8,128)(2,1)S(1)} %get-tuple-element.64), channel_id=1, source_target_pairs={{4,0},{5,1},{2,6},{3,7},{0,2},{1,3},{6,4},{7,5},{12,8},{13,9},{10,... | collective-permute-start | bytes 442376 | tf_op jit(solution)/shard_map/ppermute | solution.py:565
  53.5 2.2 %opponents.1 = (bf16[32,32]{1,0:T(8,128)(2,1)S(1)}, bf16[32,32]{1,0:T(8,128)(2,1)S(1)}, bf16[32,32]{1,0:T(8,128)(2,1)S(1)}, bf16[32,32]{1,0:T(8,128)(2,1)S(1)}) custom-call(bf16[32,3456]{1,0:T(8,128)(2,1)S(1)} %bitcast.45, bf16[32,3456]{1,0:T(8,128)(2,1)S(1)} %collective-permute-done.8.refs_1_, bf16[32,3456]{1,0:T(8,128)(2,1)S(1)} %collective-permute-done.9.refs_2_, ...), custom_call_target="tpu_custom_call" | custom-call | flops 226492416 | bytes 884736 | tf_op jit(solution)/shard_map/opponents/pallas_call | solution.py:360
  55.7 1.6 %collective-permute-start.11 = (bf16[32,32]{1,0:T(8,128)(2,1)S(1)}, bf16[32,32]{1,0:T(8,128)(2,1)S(1)}, u32[]{:S(2)}, u32[]{:S(2)}) collective-permute-start(bf16[32,32]{1,0:T(8,128)(2,1)S(1)} %get-tuple-element.50), channel_id=1, source_target_pairs={{0,8},{8,0},{16,24},{24,16},{1,9},{9,1},{17,25},{25,17},{2,10},{10... | collective-permute-start | bytes 6152 | tf_op jit(solution)/shard_map/ppermute | solution.py:573
  57.2 2.2 %collective-permute-done.11.refs_1_ = bf16[32,32]{1,0:T(8,128)(2,1)S(1)} collective-permute-done((bf16[32,32]{1,0:T(8,128)(2,1)S(1)}, bf16[32,32]{1,0:T(8,128)(2,1)S(1)}, u32[]{:S(2)}, u32[]{:S(2)}) %collective-permute-start.11) | collective-permute-done | bytes 2080 | tf_op jit(solution)/shard_map/ppermute | solution.py:573
  59.4 1.5 %collective-permute-start.12 = (bf16[32,32]{1,0:T(8,128)(2,1)S(1)}, bf16[32,32]{1,0:T(8,128)(2,1)S(1)}, u32[]{:S(2)}, u32[]{:S(2)}) collective-permute-start(bf16[32,32]{1,0:T(8,128)(2,1)S(1)} %get-tuple-element.51), channel_id=1, source_target_pairs={{0,16},{8,24},{16,0},{24,8},{1,17},{9,25},{17,1},{25,9},{2,18},{10... | collective-permute-start | bytes 6152 | tf_op jit(solution)/shard_map/ppermute | solution.py:573
  60.9 2.1 %collective-permute-done.12.refs_2_ = bf16[32,32]{1,0:T(8,128)(2,1)S(1)} collective-permute-done((bf16[32,32]{1,0:T(8,128)(2,1)S(1)}, bf16[32,32]{1,0:T(8,128)(2,1)S(1)}, u32[]{:S(2)}, u32[]{:S(2)}) %collective-permute-start.12) | collective-permute-done | bytes 2080 | tf_op jit(solution)/shard_map/ppermute | solution.py:573
  63.0 2.4 %collective-permute-start.13 = (bf16[32,32]{1,0:T(8,128)(2,1)S(1)}, bf16[32,32]{1,0:T(8,128)(2,1)S(1)}, u32[]{:S(2)}, u32[]{:S(2)}) collective-permute-start(bf16[32,32]{1,0:T(8,128)(2,1)S(1)} %get-tuple-element.52), channel_id=1, source_target_pairs={{0,24},{8,16},{16,8},{24,0},{1,25},{9,17},{17,9},{25,1},{2,26},{10... | collective-permute-start | bytes 6152 | tf_op jit(solution)/shard_map/ppermute | solution.py:573
  65.5 2.1 %collective-permute-done.13.refs_3_ = bf16[32,32]{1,0:T(8,128)(2,1)S(1)} collective-permute-done((bf16[32,32]{1,0:T(8,128)(2,1)S(1)}, bf16[32,32]{1,0:T(8,128)(2,1)S(1)}, u32[]{:S(2)}, u32[]{:S(2)}) %collective-permute-start.13) | collective-permute-done | bytes 2080 | tf_op jit(solution)/shard_map/ppermute | solution.py:573
  67.6 1.4 %collective-permute-start.21 = (bf16[32,1664]{1,0:T(8,128)(2,1)S(1)}, bf16[32,1664]{1,0:T(8,128)(2,1)S(1)}, u32[]{:S(2)}, u32[]{:S(2)}) collective-permute-start(bf16[32,1664]{1,0:T(8,128)(2,1)S(1)} %get-tuple-element.63), channel_id=1, source_target_pairs={{4,0},{5,1},{2,6},{3,7},{0,2},{1,3},{6,4},{7,5},{12,8},{13,9},{10,... | collective-permute-start | bytes 319496 | tf_op jit(solution)/shard_map/ppermute | solution.py:565
  69.6 0.6 choose.1
  70.3 0.1 shard_map.209.refs_1_
  70.4 1.1 %adam.2 = (f32[32,3712]{1,0:T(8,128)}, f32[32,3712]{1,0:T(8,128)}, f32[32,3712]{1,0:T(8,128)}) custom-call(f32[1,1]{1,0:T(1,128)} %bitcast.34.refs_0_, f32[32,3712]{1,0:T(8,128)S(1)} %shard_map.209.refs_1_, bf16[32,2304]{1,0:T(8,128)(2,1)S(1)} %collective-permute-done.22.refs_2_, f32[32,3712]{1,0:T(8,128)S(1)} %bitcast.36, f32[32,3712]{1,0:T(8,128)S(1)} %bitcast.38, ...), custom_call_target="tpu_custom_call" | custom-call | flops 1474560 | bytes 2359296 | tf_op jit(solution)/shard_map/adam/pallas_call | solution.py:518
  71.5 1.7 %collective-permute-done.21.refs_2_.refs_6_ = bf16[32,1664]{1,0:T(8,128)(2,1)S(1)} collective-permute-done((bf16[32,1664]{1,0:T(8,128)(2,1)S(1)}, bf16[32,1664]{1,0:T(8,128)(2,1)S(1)}, u32[]{:S(2)}, u32[]{:S(2)}) %collective-permute-start.21) | collective-permute-done | bytes 106528 | tf_op jit(solution)/shard_map/ppermute | solution.py:565
  73.2 1.0 %adam.3 = (f32[32,3712]{1,0:T(8,128)}, f32[32,3712]{1,0:T(8,128)}, f32[32,3712]{1,0:T(8,128)}, f32[19,1,256]{2,1,0:T(1,128)}, f32[19,1,256]{2,1,0:T(1,128)}, /*index=5*/f32[19,1,256]{2,1,0:T(1,128)}) custom-call(f32[1,1]{1,0:T(1,128)} %bitcast.35.refs_0_, ...), custom_call_target="tpu_custom_call", output_to_operand_aliasing={{0}: (13, {}), {1}: (14, {}), {2}: (15, {})} | custom-call | flops 901120 | bytes 1441792 | tf_op jit(solution)/shard_map/adam/pallas_call | solution.py:518
  (28 shorter events, 0.1 us)
Async XLA Ops:
  1.7 10.3 %collective-permute-start.1 = (bf16[32,3712]{1,0:T(8,128)(2,1)S(1)}, bf16[32,3712]{1,0:T(8,128)(2,1)S(1)}, u32[]{:S(2)}, u32[]{:S(2)}) collective-permute-start(bf16[32,3712]{1,0:T(8,128)(2,1)S(1)} %bitcast_convert_fusion.refs_0_), channel_id=1, source_target_pairs={{0,4},{1,5},{6,2},{7,3},{2,0},{3,1},{4,6},{5,7},{8,12},{9,13},{14,... | collective-permute-start | bytes 712712 | tf_op jit(solution)/shard_map/ppermute | solution.py:565
  5.8 12.1 %collective-permute-start.4 = (bf16[32,3712]{1,0:T(8,128)(2,1)S(1)}, bf16[32,3712]{1,0:T(8,128)(2,1)S(1)}, u32[]{:S(2)}, u32[]{:S(2)}) collective-permute-start(bf16[32,3712]{1,0:T(8,128)(2,1)S(1)} %bitcast_convert_fusion.refs_0_), channel_id=1, source_target_pairs={{0,2},{1,3},{6,4},{7,5},{2,6},{3,7},{4,0},{5,1},{8,10},{9,11},{14,... | collective-permute-start | bytes 712712 | tf_op jit(solution)/shard_map/ppermute | solution.py:565
  5.8 12.1 %collective-permute-start = (bf16[32,3712]{1,0:T(8,128)(2,1)S(1)}, bf16[32,3712]{1,0:T(8,128)(2,1)S(1)}, u32[]{:S(2)}, u32[]{:S(2)}) collective-permute-start(bf16[32,3712]{1,0:T(8,128)(2,1)S(1)} %bitcast_convert_fusion.refs_0_), channel_id=1, source_target_pairs={{2,4},{3,5},{4,2},{5,3},{10,12},{11,13},{12,10},{13,11},{18,20},{1... | collective-permute-start | bytes 712712 | tf_op jit(solution)/shard_map/ppermute | solution.py:565
  12.0 10.8 %collective-permute-start.2 = (bf16[32,3712]{1,0:T(8,128)(2,1)S(1)}, bf16[32,3712]{1,0:T(8,128)(2,1)S(1)}, u32[]{:S(2)}, u32[]{:S(2)}) collective-permute-start(bf16[32,3712]{1,0:T(8,128)(2,1)S(1)} %collective-permute-done.1.refs_1_), channel_id=1, source_target_pairs={{4,6},{5,7},{2,0},{3,1},{12,14},{13,15},{10,8},{11,9},{20,22},{21,... | collective-permute-start | bytes 712712 | tf_op jit(solution)/shard_map/ppermute | solution.py:565
  13.3 11.8 %collective-permute-start.5 = (bf16[32,3712]{1,0:T(8,128)(2,1)S(1)}, bf16[32,3712]{1,0:T(8,128)(2,1)S(1)}, u32[]{:S(2)}, u32[]{:S(2)}) collective-permute-start(bf16[32,3712]{1,0:T(8,128)(2,1)S(1)} %bitcast_convert_fusion.refs_0_), channel_id=1, source_target_pairs={{0,1},{1,0},{2,3},{3,2},{4,5},{5,4},{6,7},{7,6},{8,9},{9,8},{10,11... | collective-permute-start | bytes 712712 | tf_op jit(solution)/shard_map/ppermute | solution.py:570
  13.4 11.8 %collective-permute-start.6 = (bf16[32,3712]{1,0:T(8,128)(2,1)S(1)}, bf16[32,3712]{1,0:T(8,128)(2,1)S(1)}, u32[]{:S(2)}, u32[]{:S(2)}) collective-permute-start(bf16[32,3712]{1,0:T(8,128)(2,1)S(1)} %collective-permute-done.1.refs_1_), channel_id=1, source_target_pairs={{0,1},{1,0},{2,3},{3,2},{4,5},{5,4},{6,7},{7,6},{8,9},{9,8},{10,11... | collective-permute-start | bytes 712712 | tf_op jit(solution)/shard_map/ppermute | solution.py:570
  17.9 7.3 %collective-permute-start.7 = (bf16[32,3712]{1,0:T(8,128)(2,1)S(1)}, bf16[32,3712]{1,0:T(8,128)(2,1)S(1)}, u32[]{:S(2)}, u32[]{:S(2)}) collective-permute-start(bf16[32,3712]{1,0:T(8,128)(2,1)S(1)} %collective-permute-done.4.refs_2_), channel_id=1, source_target_pairs={{0,1},{1,0},{2,3},{3,2},{4,5},{5,4},{6,7},{7,6},{8,9},{9,8},{10,11... | collective-permute-start | bytes 712712 | tf_op jit(solution)/shard_map/ppermute | solution.py:570
  22.9 5.9 %collective-permute-start.3 = (bf16[32,3712]{1,0:T(8,128)(2,1)S(1)}, bf16[32,3712]{1,0:T(8,128)(2,1)S(1)}, u32[]{:S(2)}, u32[]{:S(2)}) collective-permute-start(bf16[32,3712]{1,0:T(8,128)(2,1)S(1)} %shard_map.206.refs_1_), channel_id=1, source_target_pairs={{0,1},{1,0},{2,3},{3,2},{4,5},{5,4},{6,7},{7,6},{8,9},{9,8},{10,11... | collective-permute-start | bytes 712712 | tf_op jit(solution)/shard_map/ppermute | solution.py:570
  33.7 4.8 %copy-start.3 = (bf16[1,32,3456]{2,1,0:T(8,128)(2,1)S(1)}, bf16[1,32,3456]{2,1,0:T(8,128)(2,1)}, u32[]{:S(2)}) copy-start(bf16[1,32,3456]{2,1,0:T(8,128)(2,1)} %param.17) | copy-start | bytes 663556
  33.7 1.7 %collective-permute-start.16 = (bf16[32,3968]{1,0:T(8,128)(2,1)S(1)}, bf16[32,3968]{1,0:T(8,128)(2,1)S(1)}, u32[]{:S(2)}, u32[]{:S(2)}) collective-permute-start(bf16[32,3968]{1,0:T(8,128)(2,1)S(1)} %get-tuple-element.60), channel_id=1, source_target_pairs={{0,1},{1,0},{2,3},{3,2},{4,5},{5,4},{6,7},{7,6},{8,9},{9,8},{10,11... | collective-permute-start | bytes 761864 | tf_op jit(solution)/shard_map/ppermute | solution.py:570
  35.3 34.4 %copy-start.7 = (s32[1,32,1]{1,2,0:T(1,128)S(1)}, s32[1,32,1]{1,2,0:T(1,128)}, u32[]{:S(2)}) copy-start(s32[1,32,1]{1,2,0:T(1,128)} %param.18) | copy-start | bytes 388
  35.3 6.1 %collective-permute-start.15 = (bf16[32,3712]{1,0:T(8,128)(2,1)S(1)}, bf16[32,3712]{1,0:T(8,128)(2,1)S(1)}, u32[]{:S(2)}, u32[]{:S(2)}) collective-permute-start(bf16[32,3712]{1,0:T(8,128)(2,1)S(1)} %get-tuple-element.58), channel_id=1, source_target_pairs={{0,1},{1,0},{2,3},{3,2},{4,5},{5,4},{6,7},{7,6},{8,9},{9,8},{10,11... | collective-permute-start | bytes 712712 | tf_op jit(solution)/shard_map/ppermute | solution.py:570
  35.4 35.0 %copy-start = (f32[1,32,3712]{2,1,0:T(8,128)S(1)}, f32[1,32,3712]{2,1,0:T(8,128)}, u32[]{:S(2)}) copy-start(f32[1,32,3712]{2,1,0:T(8,128)} %param.23) | copy-start | bytes 1425412
  35.4 35.0 %copy-start.1 = (f32[1,32,3712]{2,1,0:T(8,128)S(1)}, f32[1,32,3712]{2,1,0:T(8,128)}, u32[]{:S(2)}) copy-start(f32[1,32,3712]{2,1,0:T(8,128)} %param.24) | copy-start | bytes 1425412
  35.5 35.0 %copy-start.2 = (f32[1,32,3712]{2,1,0:T(8,128)S(1)}, f32[1,32,3712]{2,1,0:T(8,128)}, u32[]{:S(2)}) copy-start(f32[1,32,3712]{2,1,0:T(8,128)} %param.25) | copy-start | bytes 1425412
  35.5 13.5 %collective-permute-start.20 = (bf16[32,3968]{1,0:T(8,128)(2,1)S(1)}, bf16[32,3968]{1,0:T(8,128)(2,1)S(1)}, u32[]{:S(2)}, u32[]{:S(2)}) collective-permute-start(bf16[32,3968]{1,0:T(8,128)(2,1)S(1)} %shard_map.207.refs_2_.refs_3_), channel_id=1, source_target_pairs={{6,4},{7,5},{0,2},{1,3},{14,12},{15,13},{8,10},{9,11},{22,20},{23,... | collective-permute-start | bytes 761864 | tf_op jit(solution)/shard_map/ppermute | solution.py:565
  38.1 10.2 %collective-permute-start.19 = (bf16[32,3712]{1,0:T(8,128)(2,1)S(1)}, bf16[32,3712]{1,0:T(8,128)(2,1)S(1)}, u32[]{:S(2)}, u32[]{:S(2)}) collective-permute-start(bf16[32,3712]{1,0:T(8,128)(2,1)S(1)} %get-tuple-element.62), channel_id=1, source_target_pairs={{0,1},{1,0},{2,3},{3,2},{4,5},{5,4},{6,7},{7,6},{8,9},{9,8},{10,11... | collective-permute-start | bytes 712712 | tf_op jit(solution)/shard_map/ppermute | solution.py:570
  38.4 9.2 %collective-permute-start.10 = (bf16[32,3456]{1,0:T(8,128)(2,1)S(1)}, bf16[32,3456]{1,0:T(8,128)(2,1)S(1)}, u32[]{:S(2)}, u32[]{:S(2)}) collective-permute-start(bf16[32,3456]{1,0:T(8,128)(2,1)S(1)} %bitcast.42), channel_id=1, source_target_pairs={{0,24},{8,16},{16,8},{24,0},{1,25},{9,17},{17,9},{25,1},{2,26},{10... | collective-permute-start | bytes 663560 | tf_op jit(solution)/shard_map/ppermute | solution.py:573
  40.9 10.9 %collective-permute-start.8 = (bf16[32,3456]{1,0:T(8,128)(2,1)S(1)}, bf16[32,3456]{1,0:T(8,128)(2,1)S(1)}, u32[]{:S(2)}, u32[]{:S(2)}) collective-permute-start(bf16[32,3456]{1,0:T(8,128)(2,1)S(1)} %bitcast.43), channel_id=1, source_target_pairs={{0,8},{8,0},{16,24},{24,16},{1,9},{9,1},{17,25},{25,17},{2,10},{10... | collective-permute-start | bytes 663560 | tf_op jit(solution)/shard_map/ppermute | solution.py:573
  41.4 12.1 %collective-permute-start.9 = (bf16[32,3456]{1,0:T(8,128)(2,1)S(1)}, bf16[32,3456]{1,0:T(8,128)(2,1)S(1)}, u32[]{:S(2)}, u32[]{:S(2)}) collective-permute-start(bf16[32,3456]{1,0:T(8,128)(2,1)S(1)} %bitcast.44), channel_id=1, source_target_pairs={{0,16},{8,24},{16,0},{24,8},{1,17},{9,25},{17,1},{25,9},{2,18},{10... | collective-permute-start | bytes 663560 | tf_op jit(solution)/shard_map/ppermute | solution.py:573
  47.7 22.6 %collective-permute-start.17 = (bf16[32,3968]{1,0:T(8,128)(2,1)S(1)}, bf16[32,3968]{1,0:T(8,128)(2,1)S(1)}, u32[]{:S(2)}, u32[]{:S(2)}) collective-permute-start(bf16[32,3968]{1,0:T(8,128)(2,1)S(1)} %shard_map.208), channel_id=1, source_target_pairs={{2,0},{3,1},{4,6},{5,7},{6,2},{7,3},{0,4},{1,5},{10,8},{11,9},{12,... | collective-permute-start | bytes 761864 | tf_op jit(solution)/shard_map/ppermute | solution.py:565
  48.3 21.9 %collective-permute-start.18 = (bf16[32,3968]{1,0:T(8,128)(2,1)S(1)}, bf16[32,3968]{1,0:T(8,128)(2,1)S(1)}, u32[]{:S(2)}, u32[]{:S(2)}) collective-permute-start(bf16[32,3968]{1,0:T(8,128)(2,1)S(1)} %shard_map.207.refs_2_.refs_3_), channel_id=1, source_target_pairs={{2,4},{3,5},{4,2},{5,3},{10,12},{11,13},{12,10},{13,11},{18,20},{1... | collective-permute-start | bytes 761864 | tf_op jit(solution)/shard_map/ppermute | solution.py:565
  49.0 21.2 %collective-permute-start.14 = (bf16[32,3712]{1,0:T(8,128)(2,1)S(1)}, bf16[32,3712]{1,0:T(8,128)(2,1)S(1)}, u32[]{:S(2)}, u32[]{:S(2)}) collective-permute-start(bf16[32,3712]{1,0:T(8,128)(2,1)S(1)} %get-tuple-element.56), channel_id=1, source_target_pairs={{0,1},{1,0},{2,3},{3,2},{4,5},{5,4},{6,7},{7,6},{8,9},{9,8},{10,11... | collective-permute-start | bytes 712712 | tf_op jit(solution)/shard_map/ppermute | solution.py:570
  49.1 24.1 %copy-start.4 = (f32[1,19,256]{2,0,1:T(1,128)S(1)}, f32[1,19,256]{2,0,1:T(1,128)}, u32[]{:S(2)}) copy-start(f32[1,19,256]{2,0,1:T(1,128)} %param.26) | copy-start | bytes 58372
  49.1 24.1 %copy-start.5 = (f32[1,19,256]{2,0,1:T(1,128)S(1)}, f32[1,19,256]{2,0,1:T(1,128)}, u32[]{:S(2)}) copy-start(f32[1,19,256]{2,0,1:T(1,128)} %param.27) | copy-start | bytes 58372
  49.1 24.1 %copy-start.6 = (f32[1,19,256]{2,0,1:T(1,128)S(1)}, f32[1,19,256]{2,0,1:T(1,128)}, u32[]{:S(2)}) copy-start(f32[1,19,256]{2,0,1:T(1,128)} %param.28) | copy-start | bytes 58372
  51.8 18.6 %collective-permute-start.22 = (bf16[32,2304]{1,0:T(8,128)(2,1)S(1)}, bf16[32,2304]{1,0:T(8,128)(2,1)S(1)}, u32[]{:S(2)}, u32[]{:S(2)}) collective-permute-start(bf16[32,2304]{1,0:T(8,128)(2,1)S(1)} %get-tuple-element.64), channel_id=1, source_target_pairs={{4,0},{5,1},{2,6},{3,7},{0,2},{1,3},{6,4},{7,5},{12,8},{13,9},{10,... | collective-permute-start | bytes 442376 | tf_op jit(solution)/shard_map/ppermute | solution.py:565
  55.7 3.7 %collective-permute-start.11 = (bf16[32,32]{1,0:T(8,128)(2,1)S(1)}, bf16[32,32]{1,0:T(8,128)(2,1)S(1)}, u32[]{:S(2)}, u32[]{:S(2)}) collective-permute-start(bf16[32,32]{1,0:T(8,128)(2,1)S(1)} %get-tuple-element.50), channel_id=1, source_target_pairs={{0,8},{8,0},{16,24},{24,16},{1,9},{9,1},{17,25},{25,17},{2,10},{10... | collective-permute-start | bytes 6152 | tf_op jit(solution)/shard_map/ppermute | solution.py:573
  59.4 3.7 %collective-permute-start.12 = (bf16[32,32]{1,0:T(8,128)(2,1)S(1)}, bf16[32,32]{1,0:T(8,128)(2,1)S(1)}, u32[]{:S(2)}, u32[]{:S(2)}) collective-permute-start(bf16[32,32]{1,0:T(8,128)(2,1)S(1)} %get-tuple-element.51), channel_id=1, source_target_pairs={{0,16},{8,24},{16,0},{24,8},{1,17},{9,25},{17,1},{25,9},{2,18},{10... | collective-permute-start | bytes 6152 | tf_op jit(solution)/shard_map/ppermute | solution.py:573
  63.0 4.5 %collective-permute-start.13 = (bf16[32,32]{1,0:T(8,128)(2,1)S(1)}, bf16[32,32]{1,0:T(8,128)(2,1)S(1)}, u32[]{:S(2)}, u32[]{:S(2)}) collective-permute-start(bf16[32,32]{1,0:T(8,128)(2,1)S(1)} %get-tuple-element.52), channel_id=1, source_target_pairs={{0,24},{8,16},{16,8},{24,0},{1,25},{9,17},{17,9},{25,1},{2,26},{10... | collective-permute-start | bytes 6152 | tf_op jit(solution)/shard_map/ppermute | solution.py:573
  67.6 5.6 %collective-permute-start.21 = (bf16[32,1664]{1,0:T(8,128)(2,1)S(1)}, bf16[32,1664]{1,0:T(8,128)(2,1)S(1)}, u32[]{:S(2)}, u32[]{:S(2)}) collective-permute-start(bf16[32,1664]{1,0:T(8,128)(2,1)S(1)} %get-tuple-element.63), channel_id=1, source_target_pairs={{4,0},{5,1},{2,6},{3,7},{0,2},{1,3},{6,4},{7,5},{12,8},{13,9},{10,... | collective-permute-start | bytes 319496 | tf_op jit(solution)/shard_map/ppermute | solution.py:565

commit v5 on v4

--- a/solution.py
+++ b/solution.py
@@ -162,9 +162,9 @@
     return pl.ds(pl.multiple_of((table(source, chip) * CORES + owner) * rows, rows), rows)
 
 
-def each_piece(pieces, w_refs, ws, sems, act):
-    for i, piece in enumerate(pieces):
-        act(pltpu.make_async_copy(w_refs[i], ws.at[piece_rows(piece)], sems.at[i]))
+def place_pieces(pieces, w_refs, ws):
+    for piece, ref in zip(pieces, w_refs):
+        ws[piece_rows(piece), :] = ref[...]
 
 
 def multiply_pieces(pieces, w_refs, xs, width, first, first_bf):
@@ -180,10 +180,9 @@
 
 
 def early_kernel(pieces, width, xs, *refs):
-    w_refs, (ws, first, first_bf, sems) = refs[: len(pieces)], refs[len(pieces) :]
-    each_piece(pieces, w_refs, ws, sems, lambda copy: copy.start())
+    w_refs, (ws, first, first_bf) = refs[: len(pieces)], refs[len(pieces) :]
+    place_pieces(pieces, w_refs, ws)
     multiply_pieces(pieces, w_refs, xs, width, first, first_bf)
-    each_piece(pieces, w_refs, ws, sems, lambda copy: copy.wait())
 
 
 def early(staged, pieces, piece_list, units):
@@ -197,7 +196,6 @@
         ),
         in_specs=[LOCAL] * (1 + len(pieces)),
         out_specs=(LOCAL,) * 3,
-        scratch_shapes=[pltpu.SemaphoreType.DMA((len(pieces),))],
         compiler_params=pltpu.CompilerParams(vmem_limit_bytes=24 << 20),
         cost_estimate=pl.CostEstimate(
             flops=2 * units * total * width, bytes_accessed=4 * units * width, transcendentals=0
@@ -219,8 +217,7 @@
     aux_ref, head_ref, refs = refs[0], refs[1], refs[2:]
     if roles is not None:
         refs = refs[3:]
-    ws, first, first_bf, own_ref, gp, refs = *refs[:5], refs[5:]
-    lead, sw = refs[:-1], refs[-1]
+    ws, first, first_bf, own_ref, gp, lead = *refs[:5], refs[5:]
     learn, width, units, length = cfg["learn"], cfg["width"], cfg["units"], cfg["length"]
     envs = learn // length
 
@@ -229,9 +226,8 @@
         first[...] = jnp.maximum(dot(ws[:, :width], xs[...], NT), 0.0)
         first_bf[...] = first[...].astype(jnp.bfloat16)
     else:
-        each_piece(pieces, w_refs, ws, sw, lambda copy: copy.start())
+        place_pieces(pieces, w_refs, ws)
         multiply_pieces(pieces, w_refs, xs, width, first, first_bf)
-        each_piece(pieces, w_refs, ws, sw, lambda copy: copy.wait())
     out, pre_two, second_bf = forward(first[...], first_bf[...], ws[...], head_ref[...], width)
     own_ref[...] = out[: heads - 1, learn:].reshape(heads - 1, 1, envs)
     spread = lax.broadcasted_iota(jnp.int32, (envs, learn), 1) // length
@@ -314,7 +310,6 @@
         + [LOCAL] * (2 + len(before)),
         out_specs=(LOCAL,) * (5 + len(lead)),
         input_output_aliases=aliases,
-        scratch_shapes=[pltpu.SemaphoreType.DMA((len(piece_list),))],
         compiler_params=pltpu.CompilerParams(vmem_limit_bytes=32 << 20),
         cost_estimate=pl.CostEstimate(
             flops=4 * units * total * width, bytes_accessed=4 * total * width, transcendentals=0
@@ -335,20 +330,11 @@
     return weights, own, first_outs, list(rest_outs)
 
 
-def opponent_kernel(cfg, count, *refs):
-    frames, (weights, head), refs = refs[:count], refs[count : count + 2], refs[count + 2 :]
-    outs, (xs, sems) = refs[:count], refs[count:]
-    envs = frames[0].shape[0]
-    copies = [
-        pltpu.make_async_copy(f, xs.at[pl.ds(i * envs, envs)], sems.at[i])
-        for i, f in enumerate(frames)
-    ]
-    for copy in copies:
-        copy.start()
-    for copy in copies:
-        copy.wait()
-    width = cfg["width"]
-    first = jnp.maximum(dot(weights[:, :width], xs[...], NT), 0.0)
+def opponent_kernel(count, *refs):
+    frames, (weights, head), outs = refs[:count], refs[count : count + 2], refs[count + 2 :]
+    envs, width = frames[0].shape
+    rows = jnp.concatenate([f[...] for f in frames], 0)
+    first = jnp.maximum(dot(weights[:, :width], rows, NT), 0.0)
     first_bf = first.astype(jnp.bfloat16)
     result = forward(first, first_bf, weights[...], head[...], width)[0].astype(jnp.bfloat16)
     for i, out in enumerate(outs):
@@ -358,14 +344,10 @@
 def opponents(frames, weights, head, cfg):
     count, (envs, width) = len(frames), frames[0].shape
     return pl.pallas_call(
-        functools.partial(opponent_kernel, cfg, count),
+        functools.partial(opponent_kernel, count),
         out_shape=(jax.ShapeDtypeStruct((head.shape[0], envs), jnp.bfloat16),) * count,
-        in_specs=[ANYWHERE] * count + [LOCAL] * 2,
+        in_specs=[LOCAL] * (count + 2),
         out_specs=(LOCAL,) * count,
-        scratch_shapes=[
-            pltpu.VMEM((count * envs, width), jnp.bfloat16),
-            pltpu.SemaphoreType.DMA((count,)),
-        ],
         compiler_params=pltpu.CompilerParams(vmem_limit_bytes=24 << 20),
         cost_estimate=pl.CostEstimate(
             flops=2 * cfg["units"] * count * envs * width,
@@ -439,10 +421,10 @@
         for out, start, stop in zip(outs, edges, edges[1:]):
             out[:, : stop - start] = total_of(ins, slice(start, stop)).astype(out.dtype)
         tail = slice(width, wide)
-        outs[-1][:, width - edges[-2] :] = total_of(tops, tail).astype(outs[-1].dtype)
+        outs[0][:, edges[1] :] = total_of(tops, tail).astype(outs[0].dtype)
 
     args = (*arrays, *heads)
-    widths = [wide] if cut is None else [cut, wide - cut]
+    widths = [wide] if cut is None else [cut + units, width - cut]
     shape = [jax.ShapeDtypeStruct((rows, w), jnp.bfloat16) for w in widths]
     result = small_kernel(body, tuple(shape), args)
     return result[0] if cut is None else result
@@ -634,7 +616,7 @@
         known = add(keep[3], came[3], part_near, part_mid, dtype=wide)
         spans = ((0, cut), (cut, width + units))
         parts = [((known, 0), (far, at)) for far, (at, _) in zip(part_far, spans)]
-        head_parts = (last, part_mid, part_near, part_far[1])
+        head_parts = (last, part_mid, part_near, part_far[0])
     else:
         spans = ((0, width + units),)
         total = lax.psum_scatter(rest[0], "dp", scatter_dimension=0, tiled=True)
@@ -642,9 +624,9 @@
     core = (core_master[0], core_mom[0], core_vel[0])
     head = (by_row(head_master), by_row(head_mom), by_row(head_vel))
     new = ()
-    for span, part in zip(spans, parts):
-        final = span is spans[-1]
-        new = adam(rates, part, head_parts if final else (), core, head, span, new)
+    for n, (span, part) in enumerate(zip(spans, parts)):
+        done = adam(rates, part, () if n else head_parts, core, head, span, new[:3])
+        new = (*done[:3], *(new[3:] or done[3:]))
     return (own_logits, opp_logits.T[None], *[x[None] for x in new[:3]], *map(by_row, new[3:]))
 
 

time: 74.5 us -> 70.5 us (0.946)
  Pallas kernels: 17 us -> 13.4 us
    pallas_call x1, Pallas kernels: 3.59 us -> 1.81 us  [early(): pl.pallas_call(functools.partial(early_kernel, pieces, width), out_shape=...]
    pallas_call x1, Pallas kernels: 2.21 us -> 1.05 us  [opponents(): pl.pallas_call(functools.partial(opponent_kernel, count), out_shape=(jax....]
  transfers between devices with their start and end apart: 23 -> 23, of which waited for: 9 -> 9; matrix products, arithmetic and copies ran while one was open for 0% -> 0% of each run, Pallas kernels for 15% -> 12%
where the time goes in v5:
time: 70.5 us; the launch traced here: 70.3 us
  waiting for transfers between devices  30.6 us (43%)
  starting transfers between devices  23.7 us (34%)
  Pallas kernels  13.4 us (19%)
  between operations  1.57 us (2%)
  other arithmetic  1.05 us (1%)
    ppermute x9, waiting for transfers between devices, along(): lax.ppermute(x, 'dp', [(a * CORES + c, b * CORES + c) for a, b in pairs f...  15.8 us
    ppermute x6, waiting for transfers between devices, swap(): lax.ppermute(x, 'agent', [(i, other_agent(i, by, agents)) for i in range(...  14.7 us
    ppermute x9, starting transfers between devices, along(): lax.ppermute(x, 'dp', [(a * CORES + c, b * CORES + c) for a, b in pairs f...  13.1 us
    ppermute x6, starting transfers between devices, swap(): lax.ppermute(x, 'agent', [(i, other_agent(i, by, agents)) for i in range(...  9.02 us
    pallas_call x1, Pallas kernels, learner(): pl.pallas_call(functools.partial(learner_kernel, cfg), out_shape=(block(u...  4.24 us
    pallas_call x1, Pallas kernels, stage(): pl.pallas_call(stage_kernel, out_shape=(jax.ShapeDtypeStruct((total, widt...  2.15 us
    pallas_call x2, Pallas kernels, adam(): pl.pallas_call(functools.partial(adam_kernel, len(parts), offsets, len(he...  2.09 us
    pallas_call x1, Pallas kernels, early(): pl.pallas_call(functools.partial(early_kernel, pieces, width), out_shape=...  1.81 us
  transfers between devices with their start and end apart: 23, of which 9 were waited for; matrix products, arithmetic and copies ran while one was open for 0% of the time, Pallas kernels for 12%

profile of v5, /device:TPU:0, one launch (start us, length us, event | category | flops | bytes accessed | tf_op | source)
XLA Modules:
  0.0 70.3 jit_solution(1909116862469662546)
XLA Ops:
  0.6 1.1 %bitcast_convert_fusion.refs_0_ = bf16[32,3712]{1,0:T(8,128)(2,1)S(1)} fusion(f32[1,32,3712]{2,1,0:T(8,128)} %param.23), kind=kLoop, calls=%fused_computation | loop fusion | flops 118784 | bytes 712704 | tf_op jit(solution)/shard_map/convert_element_type | solution.py:557
  1.7 4.1 %collective-permute-start.1 = (bf16[32,3712]{1,0:T(8,128)(2,1)S(1)}, bf16[32,3712]{1,0:T(8,128)(2,1)S(1)}, u32[]{:S(2)}, u32[]{:S(2)}) collective-permute-start(bf16[32,3712]{1,0:T(8,128)(2,1)S(1)} %bitcast_convert_fusion.refs_0_), channel_id=1, source_target_pairs={{0,4},{1,5},{6,2},{7,3},{2,0},{3,1},{4,6},{5,7},{8,12},{9,13},{14,... | collective-permute-start | bytes 712712 | tf_op jit(solution)/shard_map/ppermute | solution.py:547
  5.8 0.7 collective-permute-start
  6.5 5.5 %collective-permute-done.1.refs_1_ = bf16[32,3712]{1,0:T(8,128)(2,1)S(1)} collective-permute-done((bf16[32,3712]{1,0:T(8,128)(2,1)S(1)}, bf16[32,3712]{1,0:T(8,128)(2,1)S(1)}, u32[]{:S(2)}, u32[]{:S(2)}) %collective-permute-start.1) | collective-permute-done | bytes 237600 | tf_op jit(solution)/shard_map/ppermute | solution.py:547
  12.0 1.3 %collective-permute-start.2 = (bf16[32,3712]{1,0:T(8,128)(2,1)S(1)}, bf16[32,3712]{1,0:T(8,128)(2,1)S(1)}, u32[]{:S(2)}, u32[]{:S(2)}) collective-permute-start(bf16[32,3712]{1,0:T(8,128)(2,1)S(1)} %collective-permute-done.1.refs_1_), channel_id=1, source_target_pairs={{4,6},{5,7},{2,0},{3,1},{12,14},{13,15},{10,8},{11,9},{20,22},{21,... | collective-permute-start | bytes 712712 | tf_op jit(solution)/shard_map/ppermute | solution.py:547
  13.3 0.1 collective-permute-start.5
  13.4 0.5 collective-permute-start.6
  13.9 4.0 %collective-permute-done.4.refs_2_ = bf16[32,3712]{1,0:T(8,128)(2,1)S(1)} collective-permute-done((bf16[32,3712]{1,0:T(8,128)(2,1)S(1)}, bf16[32,3712]{1,0:T(8,128)(2,1)S(1)}, u32[]{:S(2)}, u32[]{:S(2)}) %collective-permute-start.4) | collective-permute-done | bytes 237600 | tf_op jit(solution)/shard_map/ppermute | solution.py:547
  17.9 4.9 %collective-permute-done.2.refs_1_ = bf16[32,3712]{1,0:T(8,128)(2,1)S(1)} collective-permute-done((bf16[32,3712]{1,0:T(8,128)(2,1)S(1)}, bf16[32,3712]{1,0:T(8,128)(2,1)S(1)}, u32[]{:S(2)}, u32[]{:S(2)}) %collective-permute-start.2) | collective-permute-done | bytes 237600 | tf_op jit(solution)/shard_map/ppermute | solution.py:547
  22.8 0.1 shard_map.206.refs_1_
  22.9 0.1 collective-permute-start.3
  23.0 2.1 %stage.1 = (bf16[544,3456]{1,0:T(8,128)(2,1)S(1)}, f32[4,512]{1,0:T(4,128)S(1)}, bf16[32,256]{1,0:T(8,128)(2,1)S(1)}) custom-call(bf16[512,3456]{1,0:T(8,128)(2,1)} %bitcast.51, bf16[32,3456]{1,0:T(8,128)(2,1)} %bitcast.55, s32[16,32]{1,0:T(8,128)} %bitcast.56, s32[16,32]{1,0:T(8,128)} %bitcast.57, f32[16,32]{1,0:T(8,128)} %bitcast.58, f32[16,32]{1,0:T(8,128)} %bitcast.59, ...), custom_call_target="tpu_custom_call" | custom-call | bytes 7520256 | tf_op jit(solution)/shard_map/stage/pallas_call | solution.py:134
  25.2 1.8 %early.1 = (bf16[256,3712]{1,0:T(8,128)(2,1)S(1)}, f32[256,544]{1,0:T(8,128)S(1)}, bf16[256,544]{1,0:T(8,128)(2,1)S(1)}) custom-call(bf16[544,3456]{1,0:T(8,128)(2,1)S(1)} %get-tuple-element.41.xs.refs_0_, bf16[32,3712]{1,0:T(8,128)(2,1)S(1)} %bitcast_convert_fusion.refs_0_, bf16[32,3712]{1,0:T(8,128)(2,1)S(1)} %collective-permute-done.1.refs_1_, ...), custom_call_target="tpu_custom_call" | custom-call | flops 962592768 | bytes 3538944 | tf_op jit(solution)/shard_map/early/pallas_call | solution.py:190
  27.0 4.2 %learner.1 = (bf16[256,3712]{1,0:T(8,128)(2,1)S(1)}, f32[256,544]{1,0:T(8,128)S(1)}, bf16[256,544]{1,0:T(8,128)(2,1)S(1)}, f32[18,1,32]{2,1,0:T(1,128)}, bf16[25...) custom-call(bf16[544,3456]{1,0:T(8,128)(2,1)S(1)} %get-tuple-element, ...), custom_call_target="tpu_custom_call", output_to_operand_aliasing={{0}: (5, {}), {1}: (6, {}), {2}: (7, {})} | custom-call | flops 1925185536 | bytes 7520256 | tf_op jit(solution)/shard_map/learner/pallas_call | solution.py:299
  31.2 0.5 collective-permute-start.16
  31.7 1.0 %rest.1 = (bf16[32,3712]{1,0:T(8,128)(2,1)S(1)}, bf16[32,3712]{1,0:T(8,128)(2,1)S(1)}, bf16[32,3712]{1,0:T(8,128)(2,1)S(1)}, bf16[32,3712]{1,0:T(8,128)(2,1)S(1)...) custom-call(bf16[544,3456]{1,0:T(8,128)(2,1)S(1)} %get-tuple-element.41.xs.refs_0_, ...), custom_call_target="tpu_custom_call" | custom-call | flops 905969664 | bytes 3538944 | tf_op jit(solution)/shard_map/rest/pallas_call | solution.py:319
  32.7 0.0 copy-start.7
  32.7 0.1 collective-permute-start.15
  32.8 0.0 collective-permute-done.16.refs_1_.refs_3_
  32.9 0.1 shard_map.207.refs_2_.refs_3_
  32.9 0.0 copy-start
  33.0 0.0 copy-start.4
  33.0 2.7 %collective-permute-start.20 = (bf16[32,3968]{1,0:T(8,128)(2,1)S(1)}, bf16[32,3968]{1,0:T(8,128)(2,1)S(1)}, u32[]{:S(2)}, u32[]{:S(2)}) collective-permute-start(bf16[32,3968]{1,0:T(8,128)(2,1)S(1)} %shard_map.207.refs_2_.refs_3_), channel_id=1, source_target_pairs={{6,4},{7,5},{0,2},{1,3},{14,12},{15,13},{8,10},{9,11},{22,20},{23,... | collective-permute-start | bytes 761864 | tf_op jit(solution)/shard_map/ppermute | solution.py:547
  35.7 0.3 collective-permute-start.19
  35.9 2.5 %collective-permute-start.10 = (bf16[32,3456]{1,0:T(8,128)(2,1)S(1)}, bf16[32,3456]{1,0:T(8,128)(2,1)S(1)}, u32[]{:S(2)}, u32[]{:S(2)}) collective-permute-start(bf16[32,3456]{1,0:T(8,128)(2,1)S(1)} %bitcast.42), channel_id=1, source_target_pairs={{0,24},{8,16},{16,8},{24,0},{1,25},{9,17},{17,9},{25,1},{2,26},{10... | collective-permute-start | bytes 663560 | tf_op jit(solution)/shard_map/ppermute | solution.py:555
  38.4 0.5 collective-permute-start.8
  38.9 0.5 collective-permute-start.9
  39.4 0.1 shard_map.208
  39.5 5.7 %collective-permute-done.10.refs_3_ = bf16[32,3456]{1,0:T(8,128)(2,1)S(1)} collective-permute-done((bf16[32,3456]{1,0:T(8,128)(2,1)S(1)}, bf16[32,3456]{1,0:T(8,128)(2,1)S(1)}, u32[]{:S(2)}, u32[]{:S(2)}) %collective-permute-start.10) | collective-permute-done | bytes 221216 | tf_op jit(solution)/shard_map/ppermute | solution.py:555
  45.2 0.7 collective-permute-start.17
  45.8 0.7 collective-permute-start.18
  46.5 0.1 collective-permute-start.14
  46.6 0.1 shard_map.210
  46.7 2.6 %collective-permute-done.8.refs_1_ = bf16[32,3456]{1,0:T(8,128)(2,1)S(1)} collective-permute-done((bf16[32,3456]{1,0:T(8,128)(2,1)S(1)}, bf16[32,3456]{1,0:T(8,128)(2,1)S(1)}, u32[]{:S(2)}, u32[]{:S(2)}) %collective-permute-start.8) | collective-permute-done | bytes 221216 | tf_op jit(solution)/shard_map/ppermute | solution.py:555
  49.3 1.6 %collective-permute-start.22 = (bf16[32,2560]{1,0:T(8,128)(2,1)S(1)}, bf16[32,2560]{1,0:T(8,128)(2,1)S(1)}, u32[]{:S(2)}, u32[]{:S(2)}) collective-permute-start(bf16[32,2560]{1,0:T(8,128)(2,1)S(1)} %get-tuple-element.64), channel_id=1, source_target_pairs={{4,0},{5,1},{2,6},{3,7},{0,2},{1,3},{6,4},{7,5},{12,8},{13,9},{10,... | collective-permute-start | bytes 491528 | tf_op jit(solution)/shard_map/ppermute | solution.py:547
  50.9 1.1 %opponents.1 = (bf16[32,32]{1,0:T(8,128)(2,1)S(1)}, bf16[32,32]{1,0:T(8,128)(2,1)S(1)}, bf16[32,32]{1,0:T(8,128)(2,1)S(1)}, bf16[32,32]{1,0:T(8,128)(2,1)S(1)}) custom-call(bf16[32,3456]{1,0:T(8,128)(2,1)S(1)} %bitcast.45, bf16[32,3456]{1,0:T(8,128)(2,1)S(1)} %collective-permute-done.8.refs_1_, bf16[32,3456]{1,0:T(8,128)(2,1)S(1)} %collective-permute-done.9.refs_2_, ...), custom_call_target="tpu_custom_call" | custom-call | flops 226492416 | bytes 884736 | tf_op jit(solution)/shard_map/opponents/pallas_call | solution.py:346
  52.0 1.6 %collective-permute-start.11 = (bf16[32,32]{1,0:T(8,128)(2,1)S(1)}, bf16[32,32]{1,0:T(8,128)(2,1)S(1)}, u32[]{:S(2)}, u32[]{:S(2)}) collective-permute-start(bf16[32,32]{1,0:T(8,128)(2,1)S(1)} %get-tuple-element.50), channel_id=1, source_target_pairs={{0,8},{8,0},{16,24},{24,16},{1,9},{9,1},{17,25},{25,17},{2,10},{10... | collective-permute-start | bytes 6152 | tf_op jit(solution)/shard_map/ppermute | solution.py:555
  53.6 2.2 %collective-permute-done.11.refs_1_ = bf16[32,32]{1,0:T(8,128)(2,1)S(1)} collective-permute-done((bf16[32,32]{1,0:T(8,128)(2,1)S(1)}, bf16[32,32]{1,0:T(8,128)(2,1)S(1)}, u32[]{:S(2)}, u32[]{:S(2)}) %collective-permute-start.11) | collective-permute-done | bytes 2080 | tf_op jit(solution)/shard_map/ppermute | solution.py:555
  55.7 1.5 %collective-permute-start.12 = (bf16[32,32]{1,0:T(8,128)(2,1)S(1)}, bf16[32,32]{1,0:T(8,128)(2,1)S(1)}, u32[]{:S(2)}, u32[]{:S(2)}) collective-permute-start(bf16[32,32]{1,0:T(8,128)(2,1)S(1)} %get-tuple-element.51), channel_id=1, source_target_pairs={{0,16},{8,24},{16,0},{24,8},{1,17},{9,25},{17,1},{25,9},{2,18},{10... | collective-permute-start | bytes 6152 | tf_op jit(solution)/shard_map/ppermute | solution.py:555
  57.2 2.1 %collective-permute-done.12.refs_2_ = bf16[32,32]{1,0:T(8,128)(2,1)S(1)} collective-permute-done((bf16[32,32]{1,0:T(8,128)(2,1)S(1)}, bf16[32,32]{1,0:T(8,128)(2,1)S(1)}, u32[]{:S(2)}, u32[]{:S(2)}) %collective-permute-start.12) | collective-permute-done | bytes 2080 | tf_op jit(solution)/shard_map/ppermute | solution.py:555
  59.4 2.5 %collective-permute-start.13 = (bf16[32,32]{1,0:T(8,128)(2,1)S(1)}, bf16[32,32]{1,0:T(8,128)(2,1)S(1)}, u32[]{:S(2)}, u32[]{:S(2)}) collective-permute-start(bf16[32,32]{1,0:T(8,128)(2,1)S(1)} %get-tuple-element.52), channel_id=1, source_target_pairs={{0,24},{8,16},{16,8},{24,0},{1,25},{9,17},{17,9},{25,1},{2,26},{10... | collective-permute-start | bytes 6152 | tf_op jit(solution)/shard_map/ppermute | solution.py:555
  61.8 2.1 %collective-permute-done.13.refs_3_ = bf16[32,32]{1,0:T(8,128)(2,1)S(1)} collective-permute-done((bf16[32,32]{1,0:T(8,128)(2,1)S(1)}, bf16[32,32]{1,0:T(8,128)(2,1)S(1)}, u32[]{:S(2)}, u32[]{:S(2)}) %collective-permute-start.13) | collective-permute-done | bytes 2080 | tf_op jit(solution)/shard_map/ppermute | solution.py:555
  63.9 1.4 %collective-permute-start.21 = (bf16[32,1408]{1,0:T(8,128)(2,1)S(1)}, bf16[32,1408]{1,0:T(8,128)(2,1)S(1)}, u32[]{:S(2)}, u32[]{:S(2)}) collective-permute-start(bf16[32,1408]{1,0:T(8,128)(2,1)S(1)} %get-tuple-element.63), channel_id=1, source_target_pairs={{4,0},{5,1},{2,6},{3,7},{0,2},{1,3},{6,4},{7,5},{12,8},{13,9},{10,... | collective-permute-start | bytes 270344 | tf_op jit(solution)/shard_map/ppermute | solution.py:547
  66.0 0.6 choose.1
  66.6 0.1 shard_map.209.refs_1_
  66.8 1.2 %adam.2 = (f32[32,3712]{1,0:T(8,128)}, f32[32,3712]{1,0:T(8,128)}, f32[32,3712]{1,0:T(8,128)}, f32[19,1,256]{2,1,0:T(1,128)}, f32[19,1,256]{2,1,0:T(1,128)}, /*index=5*/f32[19,1,256]{2,1,0:T(1,128)}) custom-call(f32[1,1]{1,0:T(1,128)} %bitcast.34.refs_0_, f32[32,3712]{1,0:T(8,128)S(1)} %shard_map.209.refs_1_, ...), custom_call_target="tpu_custom_call" | custom-call | flops 1474560 | bytes 2359296 | tf_op jit(solution)/shard_map/adam/pallas_call | solution.py:500
  68.0 1.4 %collective-permute-done.21.refs_2_ = bf16[32,1408]{1,0:T(8,128)(2,1)S(1)} collective-permute-done((bf16[32,1408]{1,0:T(8,128)(2,1)S(1)}, bf16[32,1408]{1,0:T(8,128)(2,1)S(1)}, u32[]{:S(2)}, u32[]{:S(2)}) %collective-permute-start.21) | collective-permute-done | bytes 90144 | tf_op jit(solution)/shard_map/ppermute | solution.py:547
  69.3 0.9 %adam.3 = (f32[32,3712]{1,0:T(8,128)}, f32[32,3712]{1,0:T(8,128)}, f32[32,3712]{1,0:T(8,128)}) custom-call(f32[1,1]{1,0:T(1,128)} %bitcast.35.refs_0_, f32[32,3712]{1,0:T(8,128)S(1)} %shard_map.209.refs_1_, bf16[32,1408]{1,0:T(8,128)(2,1)S(1)} %collective-permute-done.21.refs_2_, ...), custom_call_target="tpu_custom_call", output_to_operand_aliasing={{0}: (6, {}), {1}: (7, {}), {2}: (8, {})} | custom-call | flops 901120 | bytes 1441792 | tf_op jit(solution)/shard_map/adam/pallas_call | solution.py:500
  (28 shorter events, 0.1 us)
Async XLA Ops:
  1.7 10.3 %collective-permute-start.1 = (bf16[32,3712]{1,0:T(8,128)(2,1)S(1)}, bf16[32,3712]{1,0:T(8,128)(2,1)S(1)}, u32[]{:S(2)}, u32[]{:S(2)}) collective-permute-start(bf16[32,3712]{1,0:T(8,128)(2,1)S(1)} %bitcast_convert_fusion.refs_0_), channel_id=1, source_target_pairs={{0,4},{1,5},{6,2},{7,3},{2,0},{3,1},{4,6},{5,7},{8,12},{9,13},{14,... | collective-permute-start | bytes 712712 | tf_op jit(solution)/shard_map/ppermute | solution.py:547
  5.8 12.1 %collective-permute-start.4 = (bf16[32,3712]{1,0:T(8,128)(2,1)S(1)}, bf16[32,3712]{1,0:T(8,128)(2,1)S(1)}, u32[]{:S(2)}, u32[]{:S(2)}) collective-permute-start(bf16[32,3712]{1,0:T(8,128)(2,1)S(1)} %bitcast_convert_fusion.refs_0_), channel_id=1, source_target_pairs={{0,2},{1,3},{6,4},{7,5},{2,6},{3,7},{4,0},{5,1},{8,10},{9,11},{14,... | collective-permute-start | bytes 712712 | tf_op jit(solution)/shard_map/ppermute | solution.py:547
  5.8 12.1 %collective-permute-start = (bf16[32,3712]{1,0:T(8,128)(2,1)S(1)}, bf16[32,3712]{1,0:T(8,128)(2,1)S(1)}, u32[]{:S(2)}, u32[]{:S(2)}) collective-permute-start(bf16[32,3712]{1,0:T(8,128)(2,1)S(1)} %bitcast_convert_fusion.refs_0_), channel_id=1, source_target_pairs={{2,4},{3,5},{4,2},{5,3},{10,12},{11,13},{12,10},{13,11},{18,20},{1... | collective-permute-start | bytes 712712 | tf_op jit(solution)/shard_map/ppermute | solution.py:547
  12.0 10.8 %collective-permute-start.2 = (bf16[32,3712]{1,0:T(8,128)(2,1)S(1)}, bf16[32,3712]{1,0:T(8,128)(2,1)S(1)}, u32[]{:S(2)}, u32[]{:S(2)}) collective-permute-start(bf16[32,3712]{1,0:T(8,128)(2,1)S(1)} %collective-permute-done.1.refs_1_), channel_id=1, source_target_pairs={{4,6},{5,7},{2,0},{3,1},{12,14},{13,15},{10,8},{11,9},{20,22},{21,... | collective-permute-start | bytes 712712 | tf_op jit(solution)/shard_map/ppermute | solution.py:547
  13.3 11.8 %collective-permute-start.5 = (bf16[32,3712]{1,0:T(8,128)(2,1)S(1)}, bf16[32,3712]{1,0:T(8,128)(2,1)S(1)}, u32[]{:S(2)}, u32[]{:S(2)}) collective-permute-start(bf16[32,3712]{1,0:T(8,128)(2,1)S(1)} %bitcast_convert_fusion.refs_0_), channel_id=1, source_target_pairs={{0,1},{1,0},{2,3},{3,2},{4,5},{5,4},{6,7},{7,6},{8,9},{9,8},{10,11... | collective-permute-start | bytes 712712 | tf_op jit(solution)/shard_map/ppermute | solution.py:552
  13.4 11.8 %collective-permute-start.6 = (bf16[32,3712]{1,0:T(8,128)(2,1)S(1)}, bf16[32,3712]{1,0:T(8,128)(2,1)S(1)}, u32[]{:S(2)}, u32[]{:S(2)}) collective-permute-start(bf16[32,3712]{1,0:T(8,128)(2,1)S(1)} %collective-permute-done.1.refs_1_), channel_id=1, source_target_pairs={{0,1},{1,0},{2,3},{3,2},{4,5},{5,4},{6,7},{7,6},{8,9},{9,8},{10,11... | collective-permute-start | bytes 712712 | tf_op jit(solution)/shard_map/ppermute | solution.py:552
  17.9 7.3 %collective-permute-start.7 = (bf16[32,3712]{1,0:T(8,128)(2,1)S(1)}, bf16[32,3712]{1,0:T(8,128)(2,1)S(1)}, u32[]{:S(2)}, u32[]{:S(2)}) collective-permute-start(bf16[32,3712]{1,0:T(8,128)(2,1)S(1)} %collective-permute-done.4.refs_2_), channel_id=1, source_target_pairs={{0,1},{1,0},{2,3},{3,2},{4,5},{5,4},{6,7},{7,6},{8,9},{9,8},{10,11... | collective-permute-start | bytes 712712 | tf_op jit(solution)/shard_map/ppermute | solution.py:552
  22.9 4.1 %collective-permute-start.3 = (bf16[32,3712]{1,0:T(8,128)(2,1)S(1)}, bf16[32,3712]{1,0:T(8,128)(2,1)S(1)}, u32[]{:S(2)}, u32[]{:S(2)}) collective-permute-start(bf16[32,3712]{1,0:T(8,128)(2,1)S(1)} %shard_map.206.refs_1_), channel_id=1, source_target_pairs={{0,1},{1,0},{2,3},{3,2},{4,5},{5,4},{6,7},{7,6},{8,9},{9,8},{10,11... | collective-permute-start | bytes 712712 | tf_op jit(solution)/shard_map/ppermute | solution.py:552
  31.2 4.7 %copy-start.3 = (bf16[1,32,3456]{2,1,0:T(8,128)(2,1)S(1)}, bf16[1,32,3456]{2,1,0:T(8,128)(2,1)}, u32[]{:S(2)}) copy-start(bf16[1,32,3456]{2,1,0:T(8,128)(2,1)} %param.17) | copy-start | bytes 663556
  31.2 1.6 %collective-permute-start.16 = (bf16[32,3968]{1,0:T(8,128)(2,1)S(1)}, bf16[32,3968]{1,0:T(8,128)(2,1)S(1)}, u32[]{:S(2)}, u32[]{:S(2)}) collective-permute-start(bf16[32,3968]{1,0:T(8,128)(2,1)S(1)} %get-tuple-element.60), channel_id=1, source_target_pairs={{0,1},{1,0},{2,3},{3,2},{4,5},{5,4},{6,7},{7,6},{8,9},{9,8},{10,11... | collective-permute-start | bytes 761864 | tf_op jit(solution)/shard_map/ppermute | solution.py:552
  32.7 33.3 %copy-start.7 = (s32[1,32,1]{1,2,0:T(1,128)S(1)}, s32[1,32,1]{1,2,0:T(1,128)}, u32[]{:S(2)}) copy-start(s32[1,32,1]{1,2,0:T(1,128)} %param.18) | copy-start | bytes 388
  32.7 6.2 %collective-permute-start.15 = (bf16[32,3712]{1,0:T(8,128)(2,1)S(1)}, bf16[32,3712]{1,0:T(8,128)(2,1)S(1)}, u32[]{:S(2)}, u32[]{:S(2)}) collective-permute-start(bf16[32,3712]{1,0:T(8,128)(2,1)S(1)} %get-tuple-element.58), channel_id=1, source_target_pairs={{0,1},{1,0},{2,3},{3,2},{4,5},{5,4},{6,7},{7,6},{8,9},{9,8},{10,11... | collective-permute-start | bytes 712712 | tf_op jit(solution)/shard_map/ppermute | solution.py:552
  32.9 33.8 %copy-start = (f32[1,32,3712]{2,1,0:T(8,128)S(1)}, f32[1,32,3712]{2,1,0:T(8,128)}, u32[]{:S(2)}) copy-start(f32[1,32,3712]{2,1,0:T(8,128)} %param.23) | copy-start | bytes 1425412
  32.9 33.8 %copy-start.1 = (f32[1,32,3712]{2,1,0:T(8,128)S(1)}, f32[1,32,3712]{2,1,0:T(8,128)}, u32[]{:S(2)}) copy-start(f32[1,32,3712]{2,1,0:T(8,128)} %param.24) | copy-start | bytes 1425412
  32.9 33.8 %copy-start.2 = (f32[1,32,3712]{2,1,0:T(8,128)S(1)}, f32[1,32,3712]{2,1,0:T(8,128)}, u32[]{:S(2)}) copy-start(f32[1,32,3712]{2,1,0:T(8,128)} %param.25) | copy-start | bytes 1425412
  33.0 33.8 %copy-start.4 = (f32[1,19,256]{2,0,1:T(1,128)S(1)}, f32[1,19,256]{2,0,1:T(1,128)}, u32[]{:S(2)}) copy-start(f32[1,19,256]{2,0,1:T(1,128)} %param.26) | copy-start | bytes 58372
  33.0 33.8 %copy-start.5 = (f32[1,19,256]{2,0,1:T(1,128)S(1)}, f32[1,19,256]{2,0,1:T(1,128)}, u32[]{:S(2)}) copy-start(f32[1,19,256]{2,0,1:T(1,128)} %param.27) | copy-start | bytes 58372
  33.0 33.8 %copy-start.6 = (f32[1,19,256]{2,0,1:T(1,128)S(1)}, f32[1,19,256]{2,0,1:T(1,128)}, u32[]{:S(2)}) copy-start(f32[1,19,256]{2,0,1:T(1,128)} %param.28) | copy-start | bytes 58372
  33.0 13.5 %collective-permute-start.20 = (bf16[32,3968]{1,0:T(8,128)(2,1)S(1)}, bf16[32,3968]{1,0:T(8,128)(2,1)S(1)}, u32[]{:S(2)}, u32[]{:S(2)}) collective-permute-start(bf16[32,3968]{1,0:T(8,128)(2,1)S(1)} %shard_map.207.refs_2_.refs_3_), channel_id=1, source_target_pairs={{6,4},{7,5},{0,2},{1,3},{14,12},{15,13},{8,10},{9,11},{22,20},{23,... | collective-permute-start | bytes 761864 | tf_op jit(solution)/shard_map/ppermute | solution.py:547
  35.7 10.2 %collective-permute-start.19 = (bf16[32,3712]{1,0:T(8,128)(2,1)S(1)}, bf16[32,3712]{1,0:T(8,128)(2,1)S(1)}, u32[]{:S(2)}, u32[]{:S(2)}) collective-permute-start(bf16[32,3712]{1,0:T(8,128)(2,1)S(1)} %get-tuple-element.62), channel_id=1, source_target_pairs={{0,1},{1,0},{2,3},{3,2},{4,5},{5,4},{6,7},{7,6},{8,9},{9,8},{10,11... | collective-permute-start | bytes 712712 | tf_op jit(solution)/shard_map/ppermute | solution.py:552
  35.9 9.2 %collective-permute-start.10 = (bf16[32,3456]{1,0:T(8,128)(2,1)S(1)}, bf16[32,3456]{1,0:T(8,128)(2,1)S(1)}, u32[]{:S(2)}, u32[]{:S(2)}) collective-permute-start(bf16[32,3456]{1,0:T(8,128)(2,1)S(1)} %bitcast.42), channel_id=1, source_target_pairs={{0,24},{8,16},{16,8},{24,0},{1,25},{9,17},{17,9},{25,1},{2,26},{10... | collective-permute-start | bytes 663560 | tf_op jit(solution)/shard_map/ppermute | solution.py:555
  38.4 10.9 %collective-permute-start.8 = (bf16[32,3456]{1,0:T(8,128)(2,1)S(1)}, bf16[32,3456]{1,0:T(8,128)(2,1)S(1)}, u32[]{:S(2)}, u32[]{:S(2)}) collective-permute-start(bf16[32,3456]{1,0:T(8,128)(2,1)S(1)} %bitcast.43), channel_id=1, source_target_pairs={{0,8},{8,0},{16,24},{24,16},{1,9},{9,1},{17,25},{25,17},{2,10},{10... | collective-permute-start | bytes 663560 | tf_op jit(solution)/shard_map/ppermute | solution.py:555
  38.9 12.0 %collective-permute-start.9 = (bf16[32,3456]{1,0:T(8,128)(2,1)S(1)}, bf16[32,3456]{1,0:T(8,128)(2,1)S(1)}, u32[]{:S(2)}, u32[]{:S(2)}) collective-permute-start(bf16[32,3456]{1,0:T(8,128)(2,1)S(1)} %bitcast.44), channel_id=1, source_target_pairs={{0,16},{8,24},{16,0},{24,8},{1,17},{9,25},{17,1},{25,9},{2,18},{10... | collective-permute-start | bytes 663560 | tf_op jit(solution)/shard_map/ppermute | solution.py:555
  45.2 21.4 %collective-permute-start.17 = (bf16[32,3968]{1,0:T(8,128)(2,1)S(1)}, bf16[32,3968]{1,0:T(8,128)(2,1)S(1)}, u32[]{:S(2)}, u32[]{:S(2)}) collective-permute-start(bf16[32,3968]{1,0:T(8,128)(2,1)S(1)} %shard_map.208), channel_id=1, source_target_pairs={{2,0},{3,1},{4,6},{5,7},{6,2},{7,3},{0,4},{1,5},{10,8},{11,9},{12,... | collective-permute-start | bytes 761864 | tf_op jit(solution)/shard_map/ppermute | solution.py:547
  45.8 20.8 %collective-permute-start.18 = (bf16[32,3968]{1,0:T(8,128)(2,1)S(1)}, bf16[32,3968]{1,0:T(8,128)(2,1)S(1)}, u32[]{:S(2)}, u32[]{:S(2)}) collective-permute-start(bf16[32,3968]{1,0:T(8,128)(2,1)S(1)} %shard_map.207.refs_2_.refs_3_), channel_id=1, source_target_pairs={{2,4},{3,5},{4,2},{5,3},{10,12},{11,13},{12,10},{13,11},{18,20},{1... | collective-permute-start | bytes 761864 | tf_op jit(solution)/shard_map/ppermute | solution.py:547
  46.5 20.1 %collective-permute-start.14 = (bf16[32,3712]{1,0:T(8,128)(2,1)S(1)}, bf16[32,3712]{1,0:T(8,128)(2,1)S(1)}, u32[]{:S(2)}, u32[]{:S(2)}) collective-permute-start(bf16[32,3712]{1,0:T(8,128)(2,1)S(1)} %get-tuple-element.56), channel_id=1, source_target_pairs={{0,1},{1,0},{2,3},{3,2},{4,5},{5,4},{6,7},{7,6},{8,9},{9,8},{10,11... | collective-permute-start | bytes 712712 | tf_op jit(solution)/shard_map/ppermute | solution.py:552
  49.3 17.4 %collective-permute-start.22 = (bf16[32,2560]{1,0:T(8,128)(2,1)S(1)}, bf16[32,2560]{1,0:T(8,128)(2,1)S(1)}, u32[]{:S(2)}, u32[]{:S(2)}) collective-permute-start(bf16[32,2560]{1,0:T(8,128)(2,1)S(1)} %get-tuple-element.64), channel_id=1, source_target_pairs={{4,0},{5,1},{2,6},{3,7},{0,2},{1,3},{6,4},{7,5},{12,8},{13,9},{10,... | collective-permute-start | bytes 491528 | tf_op jit(solution)/shard_map/ppermute | solution.py:547
  52.0 3.7 %collective-permute-start.11 = (bf16[32,32]{1,0:T(8,128)(2,1)S(1)}, bf16[32,32]{1,0:T(8,128)(2,1)S(1)}, u32[]{:S(2)}, u32[]{:S(2)}) collective-permute-start(bf16[32,32]{1,0:T(8,128)(2,1)S(1)} %get-tuple-element.50), channel_id=1, source_target_pairs={{0,8},{8,0},{16,24},{24,16},{1,9},{9,1},{17,25},{25,17},{2,10},{10... | collective-permute-start | bytes 6152 | tf_op jit(solution)/shard_map/ppermute | solution.py:555
  55.7 3.7 %collective-permute-start.12 = (bf16[32,32]{1,0:T(8,128)(2,1)S(1)}, bf16[32,32]{1,0:T(8,128)(2,1)S(1)}, u32[]{:S(2)}, u32[]{:S(2)}) collective-permute-start(bf16[32,32]{1,0:T(8,128)(2,1)S(1)} %get-tuple-element.51), channel_id=1, source_target_pairs={{0,16},{8,24},{16,0},{24,8},{1,17},{9,25},{17,1},{25,9},{2,18},{10... | collective-permute-start | bytes 6152 | tf_op jit(solution)/shard_map/ppermute | solution.py:555
  59.4 4.5 %collective-permute-start.13 = (bf16[32,32]{1,0:T(8,128)(2,1)S(1)}, bf16[32,32]{1,0:T(8,128)(2,1)S(1)}, u32[]{:S(2)}, u32[]{:S(2)}) collective-permute-start(bf16[32,32]{1,0:T(8,128)(2,1)S(1)} %get-tuple-element.52), channel_id=1, source_target_pairs={{0,24},{8,16},{16,8},{24,0},{1,25},{9,17},{17,9},{25,1},{2,26},{10... | collective-permute-start | bytes 6152 | tf_op jit(solution)/shard_map/ppermute | solution.py:555
  63.9 5.4 %collective-permute-start.21 = (bf16[32,1408]{1,0:T(8,128)(2,1)S(1)}, bf16[32,1408]{1,0:T(8,128)(2,1)S(1)}, u32[]{:S(2)}, u32[]{:S(2)}) collective-permute-start(bf16[32,1408]{1,0:T(8,128)(2,1)S(1)} %get-tuple-element.63), channel_id=1, source_target_pairs={{4,0},{5,1},{2,6},{3,7},{0,2},{1,3},{6,4},{7,5},{12,8},{13,9},{10,... | collective-permute-start | bytes 270344 | tf_op jit(solution)/shard_map/ppermute | solution.py:547

commit v6 on v5

--- a/solution.py
+++ b/solution.py
@@ -22,13 +22,13 @@
 GATHER_FAR = ((0, 2), (3, 1), (1, 0), (2, 3))
 GATHER_NEAR = ((0, 1), (3, 2), (1, 3), (2, 0))
 GATHER_MID = ((1, 2), (2, 1))
-GATHER_FORWARD = ((2, 3), (1, 0))
+GATHER_FORWARD = ((2, 3), (1, 0), (0, 1), (3, 2))
 FAR_FROM = (1, 3, 0, 2)
 NEAR_FROM = (2, 0, 3, 1)
 LAST_FROM = (3, 2, 1, 0)
 SELF_FROM = (0, 1, 2, 3)
 ROLES = (LAST_FROM, NEAR_FROM, FAR_FROM, SELF_FROM)
-SCATTER_FORWARD = ((3, 2), (0, 1))
+SCATTER_FORWARD = ((3, 2), (0, 1), (1, 0), (2, 3))
 SCATTER_NEAR = tuple((b, a) for a, b in GATHER_NEAR)
 SCATTER_MID = ((1, 2), (2, 1))
 SCATTER_FAR = tuple((b, a) for a, b in GATHER_FAR)
@@ -383,8 +383,16 @@
     )(*answers, ids)
 
 
-def total_of(refs, columns):
-    return sum(x[:, columns].astype(jnp.float32) for x in refs)
+def total_of(refs, columns, through=0):
+    values = [x[:, columns].astype(jnp.float32) for x in refs]
+    for i in range(len(values) - through, len(values)):
+        values[i] = jnp.where(inner_chip(), values[i], 0.0)
+    return sum(values)
+
+
+def inner_chip():
+    _, chip = where_am_i()
+    return jnp.logical_and(chip > 0, chip < LINE - 1)
 
 
 def small_kernel(body, out_shape, args):
@@ -411,7 +419,15 @@
     return small_kernel(body, shape, arrays)
 
 
-def add_with_heads(arrays, heads, units, cut=None):
+def join(mid, onward):
+    def body(mid_ref, onward_ref, out):
+        out[...] = jnp.where(inner_chip(), mid_ref[...], onward_ref[...])
+
+    return small_kernel(body, jax.ShapeDtypeStruct(mid.shape, mid.dtype), (mid, onward))
+
+
+def add_with_heads(arrays, heads, units, cut=None, through=()):
+    arrays, heads = (*arrays, *through), (*heads, *through)
     rows, wide = heads[0].shape
     width = wide - units
 
@@ -419,9 +435,10 @@
         ins, tops, outs = refs[: len(arrays)], refs[len(arrays) :][: len(heads)], refs[len(args) :]
         edges = [0, width] if cut is None else [0, cut, width]
         for out, start, stop in zip(outs, edges, edges[1:]):
-            out[:, : stop - start] = total_of(ins, slice(start, stop)).astype(out.dtype)
+            value = total_of(ins, slice(start, stop), len(through))
+            out[:, : stop - start] = value.astype(out.dtype)
         tail = slice(width, wide)
-        outs[0][:, edges[1] :] = total_of(tops, tail).astype(outs[0].dtype)
+        outs[0][:, edges[1] :] = total_of(tops, tail, len(through)).astype(outs[0].dtype)
 
     args = (*arrays, *heads)
     widths = [wide] if cut is None else [cut + units, width - cut]
@@ -560,7 +577,7 @@
         near = along(mine, GATHER_NEAR)
         mid = along(mine, GATHER_MID)
         onward = along(far, GATHER_FORWARD)
-        joined = add(mid, onward)
+        joined = join(mid, onward)
         got = [("mine", mine, SELF_FROM), ("far", far, FAR_FROM), ("near", near, NEAR_FROM),
                ("last", joined, LAST_FROM)]
 
@@ -610,8 +627,8 @@
         part_mid = along(last, SCATTER_MID)
         toward = add_with_heads((keep[1], came[1]), (last,), units)
         part_near = along(toward, SCATTER_NEAR)
-        cut = 128 * (5 * (width + units) // (8 * 128))
-        beyond = add_with_heads((keep[2], came[2], through), (last, through), units, cut)
+        cut = 128 * ((width + units) // 256 + 1)
+        beyond = add_with_heads((keep[2], came[2]), (last,), units, cut, (through,))
         part_far = [along(b, SCATTER_FAR) for b in beyond]
         known = add(keep[3], came[3], part_near, part_mid, dtype=wide)
         spans = ((0, cut), (cut, width + units))

time: 70.5 us -> 68.8 us (0.976)
  waiting for transfers between devices: 30.6 us -> 28 us
  starting transfers between devices: 23.7 us -> 24.5 us
    ppermute x6, waiting for transfers between devices: 14.7 us -> 13.2 us  [swap(): lax.ppermute(x, 'agent', [(i, other_agent(i, by, agents)) for i in range(...]
    ppermute x9, waiting for transfers between devices: 15.8 us -> 14.8 us  [along(): lax.ppermute(x, 'dp', [(a * CORES + c, b * CORES + c) for a, b in pairs f...]
    ppermute x9, starting transfers between devices: 13.1 us -> 14.1 us  [along(): lax.ppermute(x, 'dp', [(a * CORES + c, b * CORES + c) for a, b in pairs f...]
where the time goes in v6:
time: 68.8 us; the launch traced here: 68.6 us
  waiting for transfers between devices  28 us (41%)
  starting transfers between devices  24.5 us (36%)
  Pallas kernels  13.4 us (19%)
  between operations  1.55 us (2%)
  other arithmetic  1.05 us (2%)
    ppermute x9, waiting for transfers between devices, along(): lax.ppermute(x, 'dp', [(a * CORES + c, b * CORES + c) for a, b in pairs f...  14.8 us
    ppermute x9, starting transfers between devices, along(): lax.ppermute(x, 'dp', [(a * CORES + c, b * CORES + c) for a, b in pairs f...  14.1 us
    ppermute x6, waiting for transfers between devices, swap(): lax.ppermute(x, 'agent', [(i, other_agent(i, by, agents)) for i in range(...  13.2 us
    ppermute x6, starting transfers between devices, swap(): lax.ppermute(x, 'agent', [(i, other_agent(i, by, agents)) for i in range(...  9.01 us
    pallas_call x1, Pallas kernels, learner(): pl.pallas_call(functools.partial(learner_kernel, cfg), out_shape=(block(u...  4.24 us
    pallas_call x1, Pallas kernels, stage(): pl.pallas_call(stage_kernel, out_shape=(jax.ShapeDtypeStruct((total, widt...  2.15 us
    pallas_call x2, Pallas kernels, adam(): pl.pallas_call(functools.partial(adam_kernel, len(parts), offsets, len(he...  2.1 us
    pallas_call x1, Pallas kernels, early(): pl.pallas_call(functools.partial(early_kernel, pieces, width), out_shape=...  1.8 us
  transfers between devices with their start and end apart: 23, of which 9 were waited for; matrix products, arithmetic and copies ran while one was open for 0% of the time, Pallas kernels for 12%

profile of v6, /device:TPU:0, one launch (start us, length us, event | category | flops | bytes accessed | tf_op | source)
XLA Modules:
  0.0 68.6 jit_solution(4142179186313736116)
XLA Ops:
  0.6 1.1 %bitcast_convert_fusion.refs_0_ = bf16[32,3712]{1,0:T(8,128)(2,1)S(1)} fusion(f32[1,32,3712]{2,1,0:T(8,128)} %param.23), kind=kLoop, calls=%fused_computation | loop fusion | flops 118784 | bytes 712704 | tf_op jit(solution)/shard_map/convert_element_type | solution.py:574
  1.7 4.1 %collective-permute-start.1 = (bf16[32,3712]{1,0:T(8,128)(2,1)S(1)}, bf16[32,3712]{1,0:T(8,128)(2,1)S(1)}, u32[]{:S(2)}, u32[]{:S(2)}) collective-permute-start(bf16[32,3712]{1,0:T(8,128)(2,1)S(1)} %bitcast_convert_fusion.refs_0_), channel_id=1, source_target_pairs={{0,4},{1,5},{6,2},{7,3},{2,0},{3,1},{4,6},{5,7},{8,12},{9,13},{14,... | collective-permute-start | bytes 712712 | tf_op jit(solution)/shard_map/ppermute | solution.py:564
  5.8 0.7 collective-permute-start
  6.5 5.5 %collective-permute-done.1.refs_1_ = bf16[32,3712]{1,0:T(8,128)(2,1)S(1)} collective-permute-done((bf16[32,3712]{1,0:T(8,128)(2,1)S(1)}, bf16[32,3712]{1,0:T(8,128)(2,1)S(1)}, u32[]{:S(2)}, u32[]{:S(2)}) %collective-permute-start.1) | collective-permute-done | bytes 237600 | tf_op jit(solution)/shard_map/ppermute | solution.py:564
  12.0 2.4 %collective-permute-start.2 = (bf16[32,3712]{1,0:T(8,128)(2,1)S(1)}, bf16[32,3712]{1,0:T(8,128)(2,1)S(1)}, u32[]{:S(2)}, u32[]{:S(2)}) collective-permute-start(bf16[32,3712]{1,0:T(8,128)(2,1)S(1)} %collective-permute-done.1.refs_1_), channel_id=1, source_target_pairs={{4,6},{5,7},{2,0},{3,1},{0,2},{1,3},{6,4},{7,5},{12,14},{13,15},{1... | collective-permute-start | bytes 712712 | tf_op jit(solution)/shard_map/ppermute | solution.py:564
  14.4 0.5 collective-permute-start.6
  14.9 3.0 %collective-permute-done.4.refs_2_ = bf16[32,3712]{1,0:T(8,128)(2,1)S(1)} collective-permute-done((bf16[32,3712]{1,0:T(8,128)(2,1)S(1)}, bf16[32,3712]{1,0:T(8,128)(2,1)S(1)}, u32[]{:S(2)}, u32[]{:S(2)}) %collective-permute-start.4) | collective-permute-done | bytes 237600 | tf_op jit(solution)/shard_map/ppermute | solution.py:564
  17.9 4.6 %collective-permute-done.2.onward_ref = bf16[32,3712]{1,0:T(8,128)(2,1)S(1)} collective-permute-done((bf16[32,3712]{1,0:T(8,128)(2,1)S(1)}, bf16[32,3712]{1,0:T(8,128)(2,1)S(1)}, u32[]{:S(2)}, u32[]{:S(2)}) %collective-permute-start.2) | collective-permute-done | bytes 237600 | tf_op jit(solution)/shard_map/ppermute | solution.py:564
  22.5 0.1 collective-permute-start.3
  22.6 2.2 %stage.1 = (bf16[544,3456]{1,0:T(8,128)(2,1)S(1)}, f32[4,512]{1,0:T(4,128)S(1)}, bf16[32,256]{1,0:T(8,128)(2,1)S(1)}) custom-call(bf16[512,3456]{1,0:T(8,128)(2,1)} %bitcast.51, bf16[32,3456]{1,0:T(8,128)(2,1)} %bitcast.55, s32[16,32]{1,0:T(8,128)} %bitcast.56, s32[16,32]{1,0:T(8,128)} %bitcast.57, f32[16,32]{1,0:T(8,128)} %bitcast.58, f32[16,32]{1,0:T(8,128)} %bitcast.59, ...), custom_call_target="tpu_custom_call" | custom-call | bytes 7520256 | tf_op jit(solution)/shard_map/stage/pallas_call | solution.py:134
  24.8 1.8 %early.1 = (bf16[256,3712]{1,0:T(8,128)(2,1)S(1)}, f32[256,544]{1,0:T(8,128)S(1)}, bf16[256,544]{1,0:T(8,128)(2,1)S(1)}) custom-call(bf16[544,3456]{1,0:T(8,128)(2,1)S(1)} %get-tuple-element.41.xs.refs_0_, bf16[32,3712]{1,0:T(8,128)(2,1)S(1)} %bitcast_convert_fusion.refs_0_, bf16[32,3712]{1,0:T(8,128)(2,1)S(1)} %collective-permute-done.1.refs_1_, ...), custom_call_target="tpu_custom_call" | custom-call | flops 962592768 | bytes 3538944 | tf_op jit(solution)/shard_map/early/pallas_call | solution.py:190
  26.6 4.2 %learner.1 = (bf16[256,3712]{1,0:T(8,128)(2,1)S(1)}, f32[256,544]{1,0:T(8,128)S(1)}, bf16[256,544]{1,0:T(8,128)(2,1)S(1)}, f32[18,1,32]{2,1,0:T(1,128)}, bf16[25...) custom-call(bf16[544,3456]{1,0:T(8,128)(2,1)S(1)} %get-tuple-element, ...), custom_call_target="tpu_custom_call", output_to_operand_aliasing={{0}: (5, {}), {1}: (6, {}), {2}: (7, {})} | custom-call | flops 1925185536 | bytes 7520256 | tf_op jit(solution)/shard_map/learner/pallas_call | solution.py:299
  30.8 0.5 collective-permute-start.16
  31.3 1.0 %rest.1 = (bf16[32,3712]{1,0:T(8,128)(2,1)S(1)}, bf16[32,3712]{1,0:T(8,128)(2,1)S(1)}, bf16[32,3712]{1,0:T(8,128)(2,1)S(1)}, bf16[32,3712]{1,0:T(8,128)(2,1)S(1)...) custom-call(bf16[544,3456]{1,0:T(8,128)(2,1)S(1)} %get-tuple-element.41.xs.refs_0_, ...), custom_call_target="tpu_custom_call" | custom-call | flops 905969664 | bytes 3538944 | tf_op jit(solution)/shard_map/rest/pallas_call | solution.py:319
  32.3 0.0 copy-start.7
  32.4 0.1 collective-permute-start.15
  32.4 0.0 collective-permute-done.16.refs_1_.refs_3_
  32.5 0.1 shard_map.207.refs_2_.refs_3_
  32.5 0.0 copy-start
  32.5 0.0 copy-start.1
  32.6 0.0 copy-start.2
  32.6 0.0 copy-start.6
  32.6 1.2 %collective-permute-start.20 = (bf16[32,3968]{1,0:T(8,128)(2,1)S(1)}, bf16[32,3968]{1,0:T(8,128)(2,1)S(1)}, u32[]{:S(2)}, u32[]{:S(2)}) collective-permute-start(bf16[32,3968]{1,0:T(8,128)(2,1)S(1)} %shard_map.207.refs_2_.refs_3_), channel_id=1, source_target_pairs={{6,4},{7,5},{0,2},{1,3},{2,0},{3,1},{4,6},{5,7},{14,12},{15,13},{8... | collective-permute-start | bytes 761864 | tf_op jit(solution)/shard_map/ppermute | solution.py:564
  33.8 0.2 collective-permute-start.19
  34.0 2.4 %collective-permute-start.10 = (bf16[32,3456]{1,0:T(8,128)(2,1)S(1)}, bf16[32,3456]{1,0:T(8,128)(2,1)S(1)}, u32[]{:S(2)}, u32[]{:S(2)}) collective-permute-start(bf16[32,3456]{1,0:T(8,128)(2,1)S(1)} %bitcast.42), channel_id=1, source_target_pairs={{0,24},{8,16},{16,8},{24,0},{1,25},{9,17},{17,9},{25,1},{2,26},{10... | collective-permute-start | bytes 663560 | tf_op jit(solution)/shard_map/ppermute | solution.py:572
  36.4 0.5 collective-permute-start.8
  36.9 0.5 collective-permute-start.9
  37.4 0.1 shard_map.208
  37.5 5.7 %collective-permute-done.10.refs_3_ = bf16[32,3456]{1,0:T(8,128)(2,1)S(1)} collective-permute-done((bf16[32,3456]{1,0:T(8,128)(2,1)S(1)}, bf16[32,3456]{1,0:T(8,128)(2,1)S(1)}, u32[]{:S(2)}, u32[]{:S(2)}) %collective-permute-start.10) | collective-permute-done | bytes 221216 | tf_op jit(solution)/shard_map/ppermute | solution.py:572
  43.2 2.2 %collective-permute-start.17 = (bf16[32,3968]{1,0:T(8,128)(2,1)S(1)}, bf16[32,3968]{1,0:T(8,128)(2,1)S(1)}, u32[]{:S(2)}, u32[]{:S(2)}) collective-permute-start(bf16[32,3968]{1,0:T(8,128)(2,1)S(1)} %shard_map.208), channel_id=1, source_target_pairs={{2,0},{3,1},{4,6},{5,7},{6,2},{7,3},{0,4},{1,5},{10,8},{11,9},{12,... | collective-permute-start | bytes 761864 | tf_op jit(solution)/shard_map/ppermute | solution.py:564
  45.4 0.7 collective-permute-start.18
  46.1 0.1 collective-permute-start.14
  46.1 0.1 shard_map.210
  46.3 1.1 %collective-permute-done.8.refs_1_ = bf16[32,3456]{1,0:T(8,128)(2,1)S(1)} collective-permute-done((bf16[32,3456]{1,0:T(8,128)(2,1)S(1)}, bf16[32,3456]{1,0:T(8,128)(2,1)S(1)}, u32[]{:S(2)}, u32[]{:S(2)}) %collective-permute-start.8) | collective-permute-done | bytes 221216 | tf_op jit(solution)/shard_map/ppermute | solution.py:572
  47.3 1.5 %collective-permute-start.22 = (bf16[32,2176]{1,0:T(8,128)(2,1)S(1)}, bf16[32,2176]{1,0:T(8,128)(2,1)S(1)}, u32[]{:S(2)}, u32[]{:S(2)}) collective-permute-start(bf16[32,2176]{1,0:T(8,128)(2,1)S(1)} %get-tuple-element.64), channel_id=1, source_target_pairs={{4,0},{5,1},{2,6},{3,7},{0,2},{1,3},{6,4},{7,5},{12,8},{13,9},{10,... | collective-permute-start | bytes 417800 | tf_op jit(solution)/shard_map/ppermute | solution.py:564
  48.9 1.1 %opponents.1 = (bf16[32,32]{1,0:T(8,128)(2,1)S(1)}, bf16[32,32]{1,0:T(8,128)(2,1)S(1)}, bf16[32,32]{1,0:T(8,128)(2,1)S(1)}, bf16[32,32]{1,0:T(8,128)(2,1)S(1)}) custom-call(bf16[32,3456]{1,0:T(8,128)(2,1)S(1)} %bitcast.45, bf16[32,3456]{1,0:T(8,128)(2,1)S(1)} %collective-permute-done.8.refs_1_, bf16[32,3456]{1,0:T(8,128)(2,1)S(1)} %collective-permute-done.9.refs_2_, ...), custom_call_target="tpu_custom_call" | custom-call | flops 226492416 | bytes 884736 | tf_op jit(solution)/shard_map/opponents/pallas_call | solution.py:346
  49.9 1.6 %collective-permute-start.11 = (bf16[32,32]{1,0:T(8,128)(2,1)S(1)}, bf16[32,32]{1,0:T(8,128)(2,1)S(1)}, u32[]{:S(2)}, u32[]{:S(2)}) collective-permute-start(bf16[32,32]{1,0:T(8,128)(2,1)S(1)} %get-tuple-element.50), channel_id=1, source_target_pairs={{0,8},{8,0},{16,24},{24,16},{1,9},{9,1},{17,25},{25,17},{2,10},{10... | collective-permute-start | bytes 6152 | tf_op jit(solution)/shard_map/ppermute | solution.py:572
  51.5 2.2 %collective-permute-done.11.refs_1_ = bf16[32,32]{1,0:T(8,128)(2,1)S(1)} collective-permute-done((bf16[32,32]{1,0:T(8,128)(2,1)S(1)}, bf16[32,32]{1,0:T(8,128)(2,1)S(1)}, u32[]{:S(2)}, u32[]{:S(2)}) %collective-permute-start.11) | collective-permute-done | bytes 2080 | tf_op jit(solution)/shard_map/ppermute | solution.py:572
  53.7 1.5 %collective-permute-start.12 = (bf16[32,32]{1,0:T(8,128)(2,1)S(1)}, bf16[32,32]{1,0:T(8,128)(2,1)S(1)}, u32[]{:S(2)}, u32[]{:S(2)}) collective-permute-start(bf16[32,32]{1,0:T(8,128)(2,1)S(1)} %get-tuple-element.51), channel_id=1, source_target_pairs={{0,16},{8,24},{16,0},{24,8},{1,17},{9,25},{17,1},{25,9},{2,18},{10... | collective-permute-start | bytes 6152 | tf_op jit(solution)/shard_map/ppermute | solution.py:572
  55.2 2.1 %collective-permute-done.12.refs_2_ = bf16[32,32]{1,0:T(8,128)(2,1)S(1)} collective-permute-done((bf16[32,32]{1,0:T(8,128)(2,1)S(1)}, bf16[32,32]{1,0:T(8,128)(2,1)S(1)}, u32[]{:S(2)}, u32[]{:S(2)}) %collective-permute-start.12) | collective-permute-done | bytes 2080 | tf_op jit(solution)/shard_map/ppermute | solution.py:572
  57.3 2.4 %collective-permute-start.13 = (bf16[32,32]{1,0:T(8,128)(2,1)S(1)}, bf16[32,32]{1,0:T(8,128)(2,1)S(1)}, u32[]{:S(2)}, u32[]{:S(2)}) collective-permute-start(bf16[32,32]{1,0:T(8,128)(2,1)S(1)} %get-tuple-element.52), channel_id=1, source_target_pairs={{0,24},{8,16},{16,8},{24,0},{1,25},{9,17},{17,9},{25,1},{2,26},{10... | collective-permute-start | bytes 6152 | tf_op jit(solution)/shard_map/ppermute | solution.py:572
  59.7 2.1 %collective-permute-done.13.refs_3_ = bf16[32,32]{1,0:T(8,128)(2,1)S(1)} collective-permute-done((bf16[32,32]{1,0:T(8,128)(2,1)S(1)}, bf16[32,32]{1,0:T(8,128)(2,1)S(1)}, u32[]{:S(2)}, u32[]{:S(2)}) %collective-permute-start.13) | collective-permute-done | bytes 2080 | tf_op jit(solution)/shard_map/ppermute | solution.py:572
  61.9 1.4 %collective-permute-start.21 = (bf16[32,1792]{1,0:T(8,128)(2,1)S(1)}, bf16[32,1792]{1,0:T(8,128)(2,1)S(1)}, u32[]{:S(2)}, u32[]{:S(2)}) collective-permute-start(bf16[32,1792]{1,0:T(8,128)(2,1)S(1)} %get-tuple-element.63), channel_id=1, source_target_pairs={{4,0},{5,1},{2,6},{3,7},{0,2},{1,3},{6,4},{7,5},{12,8},{13,9},{10,... | collective-permute-start | bytes 344072 | tf_op jit(solution)/shard_map/ppermute | solution.py:564
  63.9 0.6 choose.1
  64.5 0.1 shard_map.209.refs_1_
  64.7 1.1 %adam.2 = (f32[32,3712]{1,0:T(8,128)}, f32[32,3712]{1,0:T(8,128)}, f32[32,3712]{1,0:T(8,128)}, f32[19,1,256]{2,1,0:T(1,128)}, f32[19,1,256]{2,1,0:T(1,128)}, /*index=5*/f32[19,1,256]{2,1,0:T(1,128)}) custom-call(f32[1,1]{1,0:T(1,128)} %bitcast.34.refs_0_, f32[32,3712]{1,0:T(8,128)S(1)} %shard_map.209.refs_1_, ...), custom_call_target="tpu_custom_call" | custom-call | flops 1228800 | bytes 1966080 | tf_op jit(solution)/shard_map/adam/pallas_call | solution.py:517
  65.8 1.7 %collective-permute-done.21.refs_2_ = bf16[32,1792]{1,0:T(8,128)(2,1)S(1)} collective-permute-done((bf16[32,1792]{1,0:T(8,128)(2,1)S(1)}, bf16[32,1792]{1,0:T(8,128)(2,1)S(1)}, u32[]{:S(2)}, u32[]{:S(2)}) %collective-permute-start.21) | collective-permute-done | bytes 114720 | tf_op jit(solution)/shard_map/ppermute | solution.py:564
  67.5 1.0 %adam.3 = (f32[32,3712]{1,0:T(8,128)}, f32[32,3712]{1,0:T(8,128)}, f32[32,3712]{1,0:T(8,128)}) custom-call(f32[1,1]{1,0:T(1,128)} %bitcast.35.refs_0_, f32[32,3712]{1,0:T(8,128)S(1)} %shard_map.209.refs_1_, bf16[32,1792]{1,0:T(8,128)(2,1)S(1)} %collective-permute-done.21.refs_2_, ...), custom_call_target="tpu_custom_call", output_to_operand_aliasing={{0}: (6, {}), {1}: (7, {}), {2}: (8, {})} | custom-call | flops 1146880 | bytes 1835008 | tf_op jit(solution)/shard_map/adam/pallas_call | solution.py:517
  (28 shorter events, 0.1 us)
Async XLA Ops:
  1.7 10.3 %collective-permute-start.1 = (bf16[32,3712]{1,0:T(8,128)(2,1)S(1)}, bf16[32,3712]{1,0:T(8,128)(2,1)S(1)}, u32[]{:S(2)}, u32[]{:S(2)}) collective-permute-start(bf16[32,3712]{1,0:T(8,128)(2,1)S(1)} %bitcast_convert_fusion.refs_0_), channel_id=1, source_target_pairs={{0,4},{1,5},{6,2},{7,3},{2,0},{3,1},{4,6},{5,7},{8,12},{9,13},{14,... | collective-permute-start | bytes 712712 | tf_op jit(solution)/shard_map/ppermute | solution.py:564
  5.8 12.1 %collective-permute-start.4 = (bf16[32,3712]{1,0:T(8,128)(2,1)S(1)}, bf16[32,3712]{1,0:T(8,128)(2,1)S(1)}, u32[]{:S(2)}, u32[]{:S(2)}) collective-permute-start(bf16[32,3712]{1,0:T(8,128)(2,1)S(1)} %bitcast_convert_fusion.refs_0_), channel_id=1, source_target_pairs={{0,2},{1,3},{6,4},{7,5},{2,6},{3,7},{4,0},{5,1},{8,10},{9,11},{14,... | collective-permute-start | bytes 712712 | tf_op jit(solution)/shard_map/ppermute | solution.py:564
  5.8 12.1 %collective-permute-start = (bf16[32,3712]{1,0:T(8,128)(2,1)S(1)}, bf16[32,3712]{1,0:T(8,128)(2,1)S(1)}, u32[]{:S(2)}, u32[]{:S(2)}) collective-permute-start(bf16[32,3712]{1,0:T(8,128)(2,1)S(1)} %bitcast_convert_fusion.refs_0_), channel_id=1, source_target_pairs={{2,4},{3,5},{4,2},{5,3},{10,12},{11,13},{12,10},{13,11},{18,20},{1... | collective-permute-start | bytes 712712 | tf_op jit(solution)/shard_map/ppermute | solution.py:564
  12.0 10.4 %collective-permute-start.2 = (bf16[32,3712]{1,0:T(8,128)(2,1)S(1)}, bf16[32,3712]{1,0:T(8,128)(2,1)S(1)}, u32[]{:S(2)}, u32[]{:S(2)}) collective-permute-start(bf16[32,3712]{1,0:T(8,128)(2,1)S(1)} %collective-permute-done.1.refs_1_), channel_id=1, source_target_pairs={{4,6},{5,7},{2,0},{3,1},{0,2},{1,3},{6,4},{7,5},{12,14},{13,15},{1... | collective-permute-start | bytes 712712 | tf_op jit(solution)/shard_map/ppermute | solution.py:564
  14.4 10.4 %collective-permute-start.5 = (bf16[32,3712]{1,0:T(8,128)(2,1)S(1)}, bf16[32,3712]{1,0:T(8,128)(2,1)S(1)}, u32[]{:S(2)}, u32[]{:S(2)}) collective-permute-start(bf16[32,3712]{1,0:T(8,128)(2,1)S(1)} %bitcast_convert_fusion.refs_0_), channel_id=1, source_target_pairs={{0,1},{1,0},{2,3},{3,2},{4,5},{5,4},{6,7},{7,6},{8,9},{9,8},{10,11... | collective-permute-start | bytes 712712 | tf_op jit(solution)/shard_map/ppermute | solution.py:569
  14.4 10.4 %collective-permute-start.6 = (bf16[32,3712]{1,0:T(8,128)(2,1)S(1)}, bf16[32,3712]{1,0:T(8,128)(2,1)S(1)}, u32[]{:S(2)}, u32[]{:S(2)}) collective-permute-start(bf16[32,3712]{1,0:T(8,128)(2,1)S(1)} %collective-permute-done.1.refs_1_), channel_id=1, source_target_pairs={{0,1},{1,0},{2,3},{3,2},{4,5},{5,4},{6,7},{7,6},{8,9},{9,8},{10,11... | collective-permute-start | bytes 712712 | tf_op jit(solution)/shard_map/ppermute | solution.py:569
  17.9 6.9 %collective-permute-start.7 = (bf16[32,3712]{1,0:T(8,128)(2,1)S(1)}, bf16[32,3712]{1,0:T(8,128)(2,1)S(1)}, u32[]{:S(2)}, u32[]{:S(2)}) collective-permute-start(bf16[32,3712]{1,0:T(8,128)(2,1)S(1)} %collective-permute-done.4.refs_2_), channel_id=1, source_target_pairs={{0,1},{1,0},{2,3},{3,2},{4,5},{5,4},{6,7},{7,6},{8,9},{9,8},{10,11... | collective-permute-start | bytes 712712 | tf_op jit(solution)/shard_map/ppermute | solution.py:569
  22.5 4.1 %collective-permute-start.3 = (bf16[32,3712]{1,0:T(8,128)(2,1)S(1)}, bf16[32,3712]{1,0:T(8,128)(2,1)S(1)}, u32[]{:S(2)}, u32[]{:S(2)}) collective-permute-start(bf16[32,3712]{1,0:T(8,128)(2,1)S(1)} %shard_map.206.refs_1_), channel_id=1, source_target_pairs={{0,1},{1,0},{2,3},{3,2},{4,5},{5,4},{6,7},{7,6},{8,9},{9,8},{10,11... | collective-permute-start | bytes 712712 | tf_op jit(solution)/shard_map/ppermute | solution.py:569
  30.8 3.1 %copy-start.3 = (bf16[1,32,3456]{2,1,0:T(8,128)(2,1)S(1)}, bf16[1,32,3456]{2,1,0:T(8,128)(2,1)}, u32[]{:S(2)}) copy-start(bf16[1,32,3456]{2,1,0:T(8,128)(2,1)} %param.17) | copy-start | bytes 663556
  30.8 1.6 %collective-permute-start.16 = (bf16[32,3968]{1,0:T(8,128)(2,1)S(1)}, bf16[32,3968]{1,0:T(8,128)(2,1)S(1)}, u32[]{:S(2)}, u32[]{:S(2)}) collective-permute-start(bf16[32,3968]{1,0:T(8,128)(2,1)S(1)} %get-tuple-element.60), channel_id=1, source_target_pairs={{0,1},{1,0},{2,3},{3,2},{4,5},{5,4},{6,7},{7,6},{8,9},{9,8},{10,11... | collective-permute-start | bytes 761864 | tf_op jit(solution)/shard_map/ppermute | solution.py:569
  32.3 31.6 %copy-start.7 = (s32[1,32,1]{1,2,0:T(1,128)S(1)}, s32[1,32,1]{1,2,0:T(1,128)}, u32[]{:S(2)}) copy-start(s32[1,32,1]{1,2,0:T(1,128)} %param.18) | copy-start | bytes 388
  32.4 4.6 %collective-permute-start.15 = (bf16[32,3712]{1,0:T(8,128)(2,1)S(1)}, bf16[32,3712]{1,0:T(8,128)(2,1)S(1)}, u32[]{:S(2)}, u32[]{:S(2)}) collective-permute-start(bf16[32,3712]{1,0:T(8,128)(2,1)S(1)} %get-tuple-element.58), channel_id=1, source_target_pairs={{0,1},{1,0},{2,3},{3,2},{4,5},{5,4},{6,7},{7,6},{8,9},{9,8},{10,11... | collective-permute-start | bytes 712712 | tf_op jit(solution)/shard_map/ppermute | solution.py:569
  32.5 32.1 %copy-start = (f32[1,32,3712]{2,1,0:T(8,128)S(1)}, f32[1,32,3712]{2,1,0:T(8,128)}, u32[]{:S(2)}) copy-start(f32[1,32,3712]{2,1,0:T(8,128)} %param.23) | copy-start | bytes 1425412
  32.5 32.1 %copy-start.1 = (f32[1,32,3712]{2,1,0:T(8,128)S(1)}, f32[1,32,3712]{2,1,0:T(8,128)}, u32[]{:S(2)}) copy-start(f32[1,32,3712]{2,1,0:T(8,128)} %param.24) | copy-start | bytes 1425412
  32.6 32.1 %copy-start.2 = (f32[1,32,3712]{2,1,0:T(8,128)S(1)}, f32[1,32,3712]{2,1,0:T(8,128)}, u32[]{:S(2)}) copy-start(f32[1,32,3712]{2,1,0:T(8,128)} %param.25) | copy-start | bytes 1425412
  32.6 32.1 %copy-start.4 = (f32[1,19,256]{2,0,1:T(1,128)S(1)}, f32[1,19,256]{2,0,1:T(1,128)}, u32[]{:S(2)}) copy-start(f32[1,19,256]{2,0,1:T(1,128)} %param.26) | copy-start | bytes 58372
  32.6 32.1 %copy-start.5 = (f32[1,19,256]{2,0,1:T(1,128)S(1)}, f32[1,19,256]{2,0,1:T(1,128)}, u32[]{:S(2)}) copy-start(f32[1,19,256]{2,0,1:T(1,128)} %param.27) | copy-start | bytes 58372
  32.6 32.1 %copy-start.6 = (f32[1,19,256]{2,0,1:T(1,128)S(1)}, f32[1,19,256]{2,0,1:T(1,128)}, u32[]{:S(2)}) copy-start(f32[1,19,256]{2,0,1:T(1,128)} %param.28) | copy-start | bytes 58372
  32.6 13.5 %collective-permute-start.20 = (bf16[32,3968]{1,0:T(8,128)(2,1)S(1)}, bf16[32,3968]{1,0:T(8,128)(2,1)S(1)}, u32[]{:S(2)}, u32[]{:S(2)}) collective-permute-start(bf16[32,3968]{1,0:T(8,128)(2,1)S(1)} %shard_map.207.refs_2_.refs_3_), channel_id=1, source_target_pairs={{6,4},{7,5},{0,2},{1,3},{2,0},{3,1},{4,6},{5,7},{14,12},{15,13},{8... | collective-permute-start | bytes 761864 | tf_op jit(solution)/shard_map/ppermute | solution.py:564
  33.8 11.6 %collective-permute-start.19 = (bf16[32,3712]{1,0:T(8,128)(2,1)S(1)}, bf16[32,3712]{1,0:T(8,128)(2,1)S(1)}, u32[]{:S(2)}, u32[]{:S(2)}) collective-permute-start(bf16[32,3712]{1,0:T(8,128)(2,1)S(1)} %get-tuple-element.62), channel_id=1, source_target_pairs={{0,1},{1,0},{2,3},{3,2},{4,5},{5,4},{6,7},{7,6},{8,9},{9,8},{10,11... | collective-permute-start | bytes 712712 | tf_op jit(solution)/shard_map/ppermute | solution.py:569
  34.0 9.2 %collective-permute-start.10 = (bf16[32,3456]{1,0:T(8,128)(2,1)S(1)}, bf16[32,3456]{1,0:T(8,128)(2,1)S(1)}, u32[]{:S(2)}, u32[]{:S(2)}) collective-permute-start(bf16[32,3456]{1,0:T(8,128)(2,1)S(1)} %bitcast.42), channel_id=1, source_target_pairs={{0,24},{8,16},{16,8},{24,0},{1,25},{9,17},{17,9},{25,1},{2,26},{10... | collective-permute-start | bytes 663560 | tf_op jit(solution)/shard_map/ppermute | solution.py:572
  36.4 10.9 %collective-permute-start.8 = (bf16[32,3456]{1,0:T(8,128)(2,1)S(1)}, bf16[32,3456]{1,0:T(8,128)(2,1)S(1)}, u32[]{:S(2)}, u32[]{:S(2)}) collective-permute-start(bf16[32,3456]{1,0:T(8,128)(2,1)S(1)} %bitcast.43), channel_id=1, source_target_pairs={{0,8},{8,0},{16,24},{24,16},{1,9},{9,1},{17,25},{25,17},{2,10},{10... | collective-permute-start | bytes 663560 | tf_op jit(solution)/shard_map/ppermute | solution.py:572
  36.9 11.9 %collective-permute-start.9 = (bf16[32,3456]{1,0:T(8,128)(2,1)S(1)}, bf16[32,3456]{1,0:T(8,128)(2,1)S(1)}, u32[]{:S(2)}, u32[]{:S(2)}) collective-permute-start(bf16[32,3456]{1,0:T(8,128)(2,1)S(1)} %bitcast.44), channel_id=1, source_target_pairs={{0,16},{8,24},{16,0},{24,8},{1,17},{9,25},{17,1},{25,9},{2,18},{10... | collective-permute-start | bytes 663560 | tf_op jit(solution)/shard_map/ppermute | solution.py:572
  43.2 21.3 %collective-permute-start.17 = (bf16[32,3968]{1,0:T(8,128)(2,1)S(1)}, bf16[32,3968]{1,0:T(8,128)(2,1)S(1)}, u32[]{:S(2)}, u32[]{:S(2)}) collective-permute-start(bf16[32,3968]{1,0:T(8,128)(2,1)S(1)} %shard_map.208), channel_id=1, source_target_pairs={{2,0},{3,1},{4,6},{5,7},{6,2},{7,3},{0,4},{1,5},{10,8},{11,9},{12,... | collective-permute-start | bytes 761864 | tf_op jit(solution)/shard_map/ppermute | solution.py:564
  45.4 19.2 %collective-permute-start.18 = (bf16[32,3968]{1,0:T(8,128)(2,1)S(1)}, bf16[32,3968]{1,0:T(8,128)(2,1)S(1)}, u32[]{:S(2)}, u32[]{:S(2)}) collective-permute-start(bf16[32,3968]{1,0:T(8,128)(2,1)S(1)} %shard_map.207.refs_2_.refs_3_), channel_id=1, source_target_pairs={{2,4},{3,5},{4,2},{5,3},{10,12},{11,13},{12,10},{13,11},{18,20},{1... | collective-permute-start | bytes 761864 | tf_op jit(solution)/shard_map/ppermute | solution.py:564
  46.1 18.5 %collective-permute-start.14 = (bf16[32,3712]{1,0:T(8,128)(2,1)S(1)}, bf16[32,3712]{1,0:T(8,128)(2,1)S(1)}, u32[]{:S(2)}, u32[]{:S(2)}) collective-permute-start(bf16[32,3712]{1,0:T(8,128)(2,1)S(1)} %get-tuple-element.56), channel_id=1, source_target_pairs={{0,1},{1,0},{2,3},{3,2},{4,5},{5,4},{6,7},{7,6},{8,9},{9,8},{10,11... | collective-permute-start | bytes 712712 | tf_op jit(solution)/shard_map/ppermute | solution.py:569
  47.3 17.3 %collective-permute-start.22 = (bf16[32,2176]{1,0:T(8,128)(2,1)S(1)}, bf16[32,2176]{1,0:T(8,128)(2,1)S(1)}, u32[]{:S(2)}, u32[]{:S(2)}) collective-permute-start(bf16[32,2176]{1,0:T(8,128)(2,1)S(1)} %get-tuple-element.64), channel_id=1, source_target_pairs={{4,0},{5,1},{2,6},{3,7},{0,2},{1,3},{6,4},{7,5},{12,8},{13,9},{10,... | collective-permute-start | bytes 417800 | tf_op jit(solution)/shard_map/ppermute | solution.py:564
  49.9 3.7 %collective-permute-start.11 = (bf16[32,32]{1,0:T(8,128)(2,1)S(1)}, bf16[32,32]{1,0:T(8,128)(2,1)S(1)}, u32[]{:S(2)}, u32[]{:S(2)}) collective-permute-start(bf16[32,32]{1,0:T(8,128)(2,1)S(1)} %get-tuple-element.50), channel_id=1, source_target_pairs={{0,8},{8,0},{16,24},{24,16},{1,9},{9,1},{17,25},{25,17},{2,10},{10... | collective-permute-start | bytes 6152 | tf_op jit(solution)/shard_map/ppermute | solution.py:572
  53.7 3.7 %collective-permute-start.12 = (bf16[32,32]{1,0:T(8,128)(2,1)S(1)}, bf16[32,32]{1,0:T(8,128)(2,1)S(1)}, u32[]{:S(2)}, u32[]{:S(2)}) collective-permute-start(bf16[32,32]{1,0:T(8,128)(2,1)S(1)} %get-tuple-element.51), channel_id=1, source_target_pairs={{0,16},{8,24},{16,0},{24,8},{1,17},{9,25},{17,1},{25,9},{2,18},{10... | collective-permute-start | bytes 6152 | tf_op jit(solution)/shard_map/ppermute | solution.py:572
  57.3 4.5 %collective-permute-start.13 = (bf16[32,32]{1,0:T(8,128)(2,1)S(1)}, bf16[32,32]{1,0:T(8,128)(2,1)S(1)}, u32[]{:S(2)}, u32[]{:S(2)}) collective-permute-start(bf16[32,32]{1,0:T(8,128)(2,1)S(1)} %get-tuple-element.52), channel_id=1, source_target_pairs={{0,24},{8,16},{16,8},{24,0},{1,25},{9,17},{17,9},{25,1},{2,26},{10... | collective-permute-start | bytes 6152 | tf_op jit(solution)/shard_map/ppermute | solution.py:572
  61.9 5.7 %collective-permute-start.21 = (bf16[32,1792]{1,0:T(8,128)(2,1)S(1)}, bf16[32,1792]{1,0:T(8,128)(2,1)S(1)}, u32[]{:S(2)}, u32[]{:S(2)}) collective-permute-start(bf16[32,1792]{1,0:T(8,128)(2,1)S(1)} %get-tuple-element.63), channel_id=1, source_target_pairs={{4,0},{5,1},{2,6},{3,7},{0,2},{1,3},{6,4},{7,5},{12,8},{13,9},{10,... | collective-permute-start | bytes 344072 | tf_op jit(solution)/shard_map/ppermute | solution.py:564

commit v7 on v6

--- a/solution.py
+++ b/solution.py
@@ -249,7 +249,7 @@
         for out in lead:
             out[:, width + units :] = ghead[: out.shape[0]].astype(jnp.bfloat16)
         order = role_rows(gp, roles[:1], lead[0].shape[0])
-        gradient_rows(order, xs, first_bf, lead, learn, width, cfg["chunk"])
+        gradient_rows(order, xs, first_bf, lead, learn, width)
 
 
 def role_rows(gp, roles, rows):
@@ -257,7 +257,7 @@
     return jnp.concatenate(parts, 0)
 
 
-def gradient_rows(order, xs, first_bf, outs, learn, width, chunk):
+def gradient_rows(order, xs, first_bf, outs, learn, width):
     rows = outs[0].shape[0]
 
     def put(columns, value):
@@ -265,9 +265,7 @@
         for i, out in enumerate(outs):
             out[:, columns] = value[i * rows : (i + 1) * rows]
 
-    for start in range(0, width, chunk):
-        columns = slice(start, start + chunk)
-        put(columns, dot(order[:, :learn], xs[:learn, columns], NN))
+    put(slice(0, width), dot(order[:, :learn], xs[:learn], NN))
     columns = slice(width, width + first_bf.shape[0])
     put(columns, dot(order[:, learn:], first_bf[:, :learn], NT))
 
@@ -275,17 +273,12 @@
 def rest_kernel(cfg, xs, gp, first_bf, *outs):
     roles = cfg["roles"]
     order = gp[...] if roles is None else role_rows(gp, roles[1:], outs[0].shape[0])
-    gradient_rows(order, xs, first_bf, outs, cfg["learn"], cfg["width"], cfg["chunk"])
-
-
-def column_chunk(width):
-    return max(c for c in range(128, 1153, 128) if width % c == 0)
+    gradient_rows(order, xs, first_bf, outs, cfg["learn"], cfg["width"])
 
 
 def learner(staged, piece_list, aux, head, before, cfg):
     total, width, units, learn = staged.shape[0], cfg["width"], cfg["units"], cfg["learn"]
     padded = head.shape[0]
-    cfg = dict(cfg, chunk=column_chunk(width))
     roles = cfg["roles"]
     block = lambda rows: jax.ShapeDtypeStruct((rows, width + units), jnp.bfloat16)
     inputs = 3 + len(piece_list)
@@ -627,7 +620,7 @@
         part_mid = along(last, SCATTER_MID)
         toward = add_with_heads((keep[1], came[1]), (last,), units)
         part_near = along(toward, SCATTER_NEAR)
-        cut = 128 * ((width + units) // 256 + 1)
+        cut = 128 * (5 * (width + units) // (8 * 128))
         beyond = add_with_heads((keep[2], came[2]), (last,), units, cut, (through,))
         part_far = [along(b, SCATTER_FAR) for b in beyond]
         known = add(keep[3], came[3], part_near, part_mid, dtype=wide)

time: 68.8 us -> 67.9 us (0.987)
  Pallas kernels: 13.4 us -> 12.7 us
  transfers between devices with their start and end apart: 23 -> 23, of which waited for: 9 -> 10; matrix products, arithmetic and copies ran while one was open for 0% -> 0% of each run, Pallas kernels for 12% -> 12%
where the time goes in v7:
time: 67.9 us; the launch traced here: 67.7 us
  waiting for transfers between devices  27.8 us (41%)
  starting transfers between devices  24.5 us (36%)
  Pallas kernels  12.7 us (19%)
  between operations  1.57 us (2%)
  other arithmetic  1.05 us (2%)
    ppermute x9, waiting for transfers between devices, along(): lax.ppermute(x, 'dp', [(a * CORES + c, b * CORES + c) for a, b in pairs f...  14.4 us
    ppermute x9, starting transfers between devices, along(): lax.ppermute(x, 'dp', [(a * CORES + c, b * CORES + c) for a, b in pairs f...  14.1 us
    ppermute x6, waiting for transfers between devices, swap(): lax.ppermute(x, 'agent', [(i, other_agent(i, by, agents)) for i in range(...  13.2 us
    ppermute x6, starting transfers between devices, swap(): lax.ppermute(x, 'agent', [(i, other_agent(i, by, agents)) for i in range(...  9.01 us
    pallas_call x1, Pallas kernels, learner(): pl.pallas_call(functools.partial(learner_kernel, cfg), out_shape=(block(u...  3.66 us
    pallas_call x1, Pallas kernels, stage(): pl.pallas_call(stage_kernel, out_shape=(jax.ShapeDtypeStruct((total, widt...  2.15 us
    pallas_call x2, Pallas kernels, adam(): pl.pallas_call(functools.partial(adam_kernel, len(parts), offsets, len(he...  2.09 us
    pallas_call x1, Pallas kernels, early(): pl.pallas_call(functools.partial(early_kernel, pieces, width), out_shape=...  1.8 us
  transfers between devices with their start and end apart: 23, of which 10 were waited for; matrix products, arithmetic and copies ran while one was open for 0% of the time, Pallas kernels for 12%

profile of v7, /device:TPU:0, one launch (start us, length us, event | category | flops | bytes accessed | tf_op | source)
XLA Modules:
  0.0 67.7 jit_solution(2134297668932242894)
XLA Ops:
  0.6 1.1 %bitcast_convert_fusion.refs_0_ = bf16[32,3712]{1,0:T(8,128)(2,1)S(1)} fusion(f32[1,32,3712]{2,1,0:T(8,128)} %param.23), kind=kLoop, calls=%fused_computation | loop fusion | flops 118784 | bytes 712704 | tf_op jit(solution)/shard_map/convert_element_type | solution.py:567
  1.7 4.1 %collective-permute-start.1 = (bf16[32,3712]{1,0:T(8,128)(2,1)S(1)}, bf16[32,3712]{1,0:T(8,128)(2,1)S(1)}, u32[]{:S(2)}, u32[]{:S(2)}) collective-permute-start(bf16[32,3712]{1,0:T(8,128)(2,1)S(1)} %bitcast_convert_fusion.refs_0_), channel_id=1, source_target_pairs={{0,4},{1,5},{6,2},{7,3},{2,0},{3,1},{4,6},{5,7},{8,12},{9,13},{14,... | collective-permute-start | bytes 712712 | tf_op jit(solution)/shard_map/ppermute | solution.py:557
  5.8 0.7 collective-permute-start
  6.5 5.5 %collective-permute-done.1.refs_1_ = bf16[32,3712]{1,0:T(8,128)(2,1)S(1)} collective-permute-done((bf16[32,3712]{1,0:T(8,128)(2,1)S(1)}, bf16[32,3712]{1,0:T(8,128)(2,1)S(1)}, u32[]{:S(2)}, u32[]{:S(2)}) %collective-permute-start.1) | collective-permute-done | bytes 237600 | tf_op jit(solution)/shard_map/ppermute | solution.py:557
  12.0 2.4 %collective-permute-start.2 = (bf16[32,3712]{1,0:T(8,128)(2,1)S(1)}, bf16[32,3712]{1,0:T(8,128)(2,1)S(1)}, u32[]{:S(2)}, u32[]{:S(2)}) collective-permute-start(bf16[32,3712]{1,0:T(8,128)(2,1)S(1)} %collective-permute-done.1.refs_1_), channel_id=1, source_target_pairs={{4,6},{5,7},{2,0},{3,1},{0,2},{1,3},{6,4},{7,5},{12,14},{13,15},{1... | collective-permute-start | bytes 712712 | tf_op jit(solution)/shard_map/ppermute | solution.py:557
  14.4 0.5 collective-permute-start.6
  14.9 3.0 %collective-permute-done.4.refs_2_ = bf16[32,3712]{1,0:T(8,128)(2,1)S(1)} collective-permute-done((bf16[32,3712]{1,0:T(8,128)(2,1)S(1)}, bf16[32,3712]{1,0:T(8,128)(2,1)S(1)}, u32[]{:S(2)}, u32[]{:S(2)}) %collective-permute-start.4) | collective-permute-done | bytes 237600 | tf_op jit(solution)/shard_map/ppermute | solution.py:557
  17.9 4.6 %collective-permute-done.2.onward_ref = bf16[32,3712]{1,0:T(8,128)(2,1)S(1)} collective-permute-done((bf16[32,3712]{1,0:T(8,128)(2,1)S(1)}, bf16[32,3712]{1,0:T(8,128)(2,1)S(1)}, u32[]{:S(2)}, u32[]{:S(2)}) %collective-permute-start.2) | collective-permute-done | bytes 237600 | tf_op jit(solution)/shard_map/ppermute | solution.py:557
  22.5 0.1 collective-permute-start.3
  22.6 2.2 %stage.1 = (bf16[544,3456]{1,0:T(8,128)(2,1)S(1)}, f32[4,512]{1,0:T(4,128)S(1)}, bf16[32,256]{1,0:T(8,128)(2,1)S(1)}) custom-call(bf16[512,3456]{1,0:T(8,128)(2,1)} %bitcast.51, bf16[32,3456]{1,0:T(8,128)(2,1)} %bitcast.55, s32[16,32]{1,0:T(8,128)} %bitcast.56, s32[16,32]{1,0:T(8,128)} %bitcast.57, f32[16,32]{1,0:T(8,128)} %bitcast.58, f32[16,32]{1,0:T(8,128)} %bitcast.59, ...), custom_call_target="tpu_custom_call" | custom-call | bytes 7520256 | tf_op jit(solution)/shard_map/stage/pallas_call | solution.py:134
  24.8 1.8 %early.1 = (bf16[256,3712]{1,0:T(8,128)(2,1)S(1)}, f32[256,544]{1,0:T(8,128)S(1)}, bf16[256,544]{1,0:T(8,128)(2,1)S(1)}) custom-call(bf16[544,3456]{1,0:T(8,128)(2,1)S(1)} %get-tuple-element.41.xs.refs_0_, bf16[32,3712]{1,0:T(8,128)(2,1)S(1)} %bitcast_convert_fusion.refs_0_, bf16[32,3712]{1,0:T(8,128)(2,1)S(1)} %collective-permute-done.1.refs_1_, ...), custom_call_target="tpu_custom_call" | custom-call | flops 962592768 | bytes 3538944 | tf_op jit(solution)/shard_map/early/pallas_call | solution.py:190
  26.6 3.7 %learner.1 = (bf16[256,3712]{1,0:T(8,128)(2,1)S(1)}, f32[256,544]{1,0:T(8,128)S(1)}, bf16[256,544]{1,0:T(8,128)(2,1)S(1)}, f32[18,1,32]{2,1,0:T(1,128)}, bf16[25...) custom-call(bf16[544,3456]{1,0:T(8,128)(2,1)S(1)} %get-tuple-element, ...), custom_call_target="tpu_custom_call", output_to_operand_aliasing={{0}: (5, {}), {1}: (6, {}), {2}: (7, {})} | custom-call | flops 1925185536 | bytes 7520256 | tf_op jit(solution)/shard_map/learner/pallas_call | solution.py:292
  30.3 0.0 copy-start.3
  30.3 0.6 collective-permute-start.16
  30.8 1.0 %rest.1 = (bf16[32,3712]{1,0:T(8,128)(2,1)S(1)}, bf16[32,3712]{1,0:T(8,128)(2,1)S(1)}, bf16[32,3712]{1,0:T(8,128)(2,1)S(1)}, bf16[32,3712]{1,0:T(8,128)(2,1)S(1)...) custom-call(bf16[544,3456]{1,0:T(8,128)(2,1)S(1)} %get-tuple-element.41.xs.refs_0_, ...), custom_call_target="tpu_custom_call" | custom-call | flops 905969664 | bytes 3538944 | tf_op jit(solution)/shard_map/rest/pallas_call | solution.py:312
  31.8 0.0 copy-start.7
  31.8 0.1 collective-permute-start.15
  31.9 0.1 collective-permute-done.16.refs_1_.refs_3_
  32.0 0.1 shard_map.207.refs_2_.refs_3_
  32.0 0.0 copy-start
  32.1 0.0 copy-start.1
  32.1 0.0 copy-start.4
  32.1 1.2 %collective-permute-start.20 = (bf16[32,3968]{1,0:T(8,128)(2,1)S(1)}, bf16[32,3968]{1,0:T(8,128)(2,1)S(1)}, u32[]{:S(2)}, u32[]{:S(2)}) collective-permute-start(bf16[32,3968]{1,0:T(8,128)(2,1)S(1)} %shard_map.207.refs_2_.refs_3_), channel_id=1, source_target_pairs={{6,4},{7,5},{0,2},{1,3},{2,0},{3,1},{4,6},{5,7},{14,12},{15,13},{8... | collective-permute-start | bytes 761864 | tf_op jit(solution)/shard_map/ppermute | solution.py:557
  33.3 0.1 collective-permute-start.19
  33.4 2.4 %collective-permute-start.10 = (bf16[32,3456]{1,0:T(8,128)(2,1)S(1)}, bf16[32,3456]{1,0:T(8,128)(2,1)S(1)}, u32[]{:S(2)}, u32[]{:S(2)}) collective-permute-start(bf16[32,3456]{1,0:T(8,128)(2,1)S(1)} %bitcast.42), channel_id=1, source_target_pairs={{0,24},{8,16},{16,8},{24,0},{1,25},{9,17},{17,9},{25,1},{2,26},{10... | collective-permute-start | bytes 663560 | tf_op jit(solution)/shard_map/ppermute | solution.py:565
  35.9 0.5 collective-permute-start.8
  36.4 0.5 collective-permute-start.9
  36.9 0.1 shard_map.208
  37.0 5.7 %collective-permute-done.10.refs_3_ = bf16[32,3456]{1,0:T(8,128)(2,1)S(1)} collective-permute-done((bf16[32,3456]{1,0:T(8,128)(2,1)S(1)}, bf16[32,3456]{1,0:T(8,128)(2,1)S(1)}, u32[]{:S(2)}, u32[]{:S(2)}) %collective-permute-start.10) | collective-permute-done | bytes 221216 | tf_op jit(solution)/shard_map/ppermute | solution.py:565
  42.7 2.2 %collective-permute-start.17 = (bf16[32,3968]{1,0:T(8,128)(2,1)S(1)}, bf16[32,3968]{1,0:T(8,128)(2,1)S(1)}, u32[]{:S(2)}, u32[]{:S(2)}) collective-permute-start(bf16[32,3968]{1,0:T(8,128)(2,1)S(1)} %shard_map.208), channel_id=1, source_target_pairs={{2,0},{3,1},{4,6},{5,7},{6,2},{7,3},{0,4},{1,5},{10,8},{11,9},{12,... | collective-permute-start | bytes 761864 | tf_op jit(solution)/shard_map/ppermute | solution.py:557
  44.8 0.7 collective-permute-start.18
  45.5 0.1 collective-permute-start.14
  45.6 0.1 shard_map.210
  45.7 1.1 %collective-permute-done.8.refs_1_ = bf16[32,3456]{1,0:T(8,128)(2,1)S(1)} collective-permute-done((bf16[32,3456]{1,0:T(8,128)(2,1)S(1)}, bf16[32,3456]{1,0:T(8,128)(2,1)S(1)}, u32[]{:S(2)}, u32[]{:S(2)}) %collective-permute-start.8) | collective-permute-done | bytes 221216 | tf_op jit(solution)/shard_map/ppermute | solution.py:565
  46.8 1.5 %collective-permute-start.22 = (bf16[32,2560]{1,0:T(8,128)(2,1)S(1)}, bf16[32,2560]{1,0:T(8,128)(2,1)S(1)}, u32[]{:S(2)}, u32[]{:S(2)}) collective-permute-start(bf16[32,2560]{1,0:T(8,128)(2,1)S(1)} %get-tuple-element.64), channel_id=1, source_target_pairs={{4,0},{5,1},{2,6},{3,7},{0,2},{1,3},{6,4},{7,5},{12,8},{13,9},{10,... | collective-permute-start | bytes 491528 | tf_op jit(solution)/shard_map/ppermute | solution.py:557
  48.3 1.1 %opponents.1 = (bf16[32,32]{1,0:T(8,128)(2,1)S(1)}, bf16[32,32]{1,0:T(8,128)(2,1)S(1)}, bf16[32,32]{1,0:T(8,128)(2,1)S(1)}, bf16[32,32]{1,0:T(8,128)(2,1)S(1)}) custom-call(bf16[32,3456]{1,0:T(8,128)(2,1)S(1)} %bitcast.45, bf16[32,3456]{1,0:T(8,128)(2,1)S(1)} %collective-permute-done.8.refs_1_, bf16[32,3456]{1,0:T(8,128)(2,1)S(1)} %collective-permute-done.9.refs_2_, ...), custom_call_target="tpu_custom_call" | custom-call | flops 226492416 | bytes 884736 | tf_op jit(solution)/shard_map/opponents/pallas_call | solution.py:339
  49.4 1.6 %collective-permute-start.11 = (bf16[32,32]{1,0:T(8,128)(2,1)S(1)}, bf16[32,32]{1,0:T(8,128)(2,1)S(1)}, u32[]{:S(2)}, u32[]{:S(2)}) collective-permute-start(bf16[32,32]{1,0:T(8,128)(2,1)S(1)} %get-tuple-element.50), channel_id=1, source_target_pairs={{0,8},{8,0},{16,24},{24,16},{1,9},{9,1},{17,25},{25,17},{2,10},{10... | collective-permute-start | bytes 6152 | tf_op jit(solution)/shard_map/ppermute | solution.py:565
  50.9 2.2 %collective-permute-done.11.refs_1_ = bf16[32,32]{1,0:T(8,128)(2,1)S(1)} collective-permute-done((bf16[32,32]{1,0:T(8,128)(2,1)S(1)}, bf16[32,32]{1,0:T(8,128)(2,1)S(1)}, u32[]{:S(2)}, u32[]{:S(2)}) %collective-permute-start.11) | collective-permute-done | bytes 2080 | tf_op jit(solution)/shard_map/ppermute | solution.py:565
  53.1 1.5 %collective-permute-start.12 = (bf16[32,32]{1,0:T(8,128)(2,1)S(1)}, bf16[32,32]{1,0:T(8,128)(2,1)S(1)}, u32[]{:S(2)}, u32[]{:S(2)}) collective-permute-start(bf16[32,32]{1,0:T(8,128)(2,1)S(1)} %get-tuple-element.51), channel_id=1, source_target_pairs={{0,16},{8,24},{16,0},{24,8},{1,17},{9,25},{17,1},{25,9},{2,18},{10... | collective-permute-start | bytes 6152 | tf_op jit(solution)/shard_map/ppermute | solution.py:565
  54.6 2.1 %collective-permute-done.12.refs_2_ = bf16[32,32]{1,0:T(8,128)(2,1)S(1)} collective-permute-done((bf16[32,32]{1,0:T(8,128)(2,1)S(1)}, bf16[32,32]{1,0:T(8,128)(2,1)S(1)}, u32[]{:S(2)}, u32[]{:S(2)}) %collective-permute-start.12) | collective-permute-done | bytes 2080 | tf_op jit(solution)/shard_map/ppermute | solution.py:565
  56.8 2.4 %collective-permute-start.13 = (bf16[32,32]{1,0:T(8,128)(2,1)S(1)}, bf16[32,32]{1,0:T(8,128)(2,1)S(1)}, u32[]{:S(2)}, u32[]{:S(2)}) collective-permute-start(bf16[32,32]{1,0:T(8,128)(2,1)S(1)} %get-tuple-element.52), channel_id=1, source_target_pairs={{0,24},{8,16},{16,8},{24,0},{1,25},{9,17},{17,9},{25,1},{2,26},{10... | collective-permute-start | bytes 6152 | tf_op jit(solution)/shard_map/ppermute | solution.py:565
  59.2 2.1 %collective-permute-done.13.refs_3_ = bf16[32,32]{1,0:T(8,128)(2,1)S(1)} collective-permute-done((bf16[32,32]{1,0:T(8,128)(2,1)S(1)}, bf16[32,32]{1,0:T(8,128)(2,1)S(1)}, u32[]{:S(2)}, u32[]{:S(2)}) %collective-permute-start.13) | collective-permute-done | bytes 2080 | tf_op jit(solution)/shard_map/ppermute | solution.py:565
  61.3 1.5 %collective-permute-start.21 = (bf16[32,1408]{1,0:T(8,128)(2,1)S(1)}, bf16[32,1408]{1,0:T(8,128)(2,1)S(1)}, u32[]{:S(2)}, u32[]{:S(2)}) collective-permute-start(bf16[32,1408]{1,0:T(8,128)(2,1)S(1)} %get-tuple-element.63), channel_id=1, source_target_pairs={{4,0},{5,1},{2,6},{3,7},{0,2},{1,3},{6,4},{7,5},{12,8},{13,9},{10,... | collective-permute-start | bytes 270344 | tf_op jit(solution)/shard_map/ppermute | solution.py:557
  63.4 0.6 choose.1
  64.0 0.1 shard_map.209.refs_1_
  64.2 1.2 %adam.2 = (f32[32,3712]{1,0:T(8,128)}, f32[32,3712]{1,0:T(8,128)}, f32[32,3712]{1,0:T(8,128)}, f32[19,1,256]{2,1,0:T(1,128)}, f32[19,1,256]{2,1,0:T(1,128)}, /*index=5*/f32[19,1,256]{2,1,0:T(1,128)}) custom-call(f32[1,1]{1,0:T(1,128)} %bitcast.34.refs_0_, f32[32,3712]{1,0:T(8,128)S(1)} %shard_map.209.refs_1_, ...), custom_call_target="tpu_custom_call" | custom-call | flops 1474560 | bytes 2359296 | tf_op jit(solution)/shard_map/adam/pallas_call | solution.py:510
  65.4 1.3 %collective-permute-done.21.refs_2_ = bf16[32,1408]{1,0:T(8,128)(2,1)S(1)} collective-permute-done((bf16[32,1408]{1,0:T(8,128)(2,1)S(1)}, bf16[32,1408]{1,0:T(8,128)(2,1)S(1)}, u32[]{:S(2)}, u32[]{:S(2)}) %collective-permute-start.21) | collective-permute-done | bytes 90144 | tf_op jit(solution)/shard_map/ppermute | solution.py:557
  66.7 0.9 %adam.3 = (f32[32,3712]{1,0:T(8,128)}, f32[32,3712]{1,0:T(8,128)}, f32[32,3712]{1,0:T(8,128)}) custom-call(f32[1,1]{1,0:T(1,128)} %bitcast.35.refs_0_, f32[32,3712]{1,0:T(8,128)S(1)} %shard_map.209.refs_1_, bf16[32,1408]{1,0:T(8,128)(2,1)S(1)} %collective-permute-done.21.refs_2_, ...), custom_call_target="tpu_custom_call", output_to_operand_aliasing={{0}: (6, {}), {1}: (7, {}), {2}: (8, {})} | custom-call | flops 901120 | bytes 1441792 | tf_op jit(solution)/shard_map/adam/pallas_call | solution.py:510
  (28 shorter events, 0.1 us)
Async XLA Ops:
  1.7 10.3 %collective-permute-start.1 = (bf16[32,3712]{1,0:T(8,128)(2,1)S(1)}, bf16[32,3712]{1,0:T(8,128)(2,1)S(1)}, u32[]{:S(2)}, u32[]{:S(2)}) collective-permute-start(bf16[32,3712]{1,0:T(8,128)(2,1)S(1)} %bitcast_convert_fusion.refs_0_), channel_id=1, source_target_pairs={{0,4},{1,5},{6,2},{7,3},{2,0},{3,1},{4,6},{5,7},{8,12},{9,13},{14,... | collective-permute-start | bytes 712712 | tf_op jit(solution)/shard_map/ppermute | solution.py:557
  5.8 12.1 %collective-permute-start.4 = (bf16[32,3712]{1,0:T(8,128)(2,1)S(1)}, bf16[32,3712]{1,0:T(8,128)(2,1)S(1)}, u32[]{:S(2)}, u32[]{:S(2)}) collective-permute-start(bf16[32,3712]{1,0:T(8,128)(2,1)S(1)} %bitcast_convert_fusion.refs_0_), channel_id=1, source_target_pairs={{0,2},{1,3},{6,4},{7,5},{2,6},{3,7},{4,0},{5,1},{8,10},{9,11},{14,... | collective-permute-start | bytes 712712 | tf_op jit(solution)/shard_map/ppermute | solution.py:557
  5.8 12.1 %collective-permute-start = (bf16[32,3712]{1,0:T(8,128)(2,1)S(1)}, bf16[32,3712]{1,0:T(8,128)(2,1)S(1)}, u32[]{:S(2)}, u32[]{:S(2)}) collective-permute-start(bf16[32,3712]{1,0:T(8,128)(2,1)S(1)} %bitcast_convert_fusion.refs_0_), channel_id=1, source_target_pairs={{2,4},{3,5},{4,2},{5,3},{10,12},{11,13},{12,10},{13,11},{18,20},{1... | collective-permute-start | bytes 712712 | tf_op jit(solution)/shard_map/ppermute | solution.py:557
  12.0 10.4 %collective-permute-start.2 = (bf16[32,3712]{1,0:T(8,128)(2,1)S(1)}, bf16[32,3712]{1,0:T(8,128)(2,1)S(1)}, u32[]{:S(2)}, u32[]{:S(2)}) collective-permute-start(bf16[32,3712]{1,0:T(8,128)(2,1)S(1)} %collective-permute-done.1.refs_1_), channel_id=1, source_target_pairs={{4,6},{5,7},{2,0},{3,1},{0,2},{1,3},{6,4},{7,5},{12,14},{13,15},{1... | collective-permute-start | bytes 712712 | tf_op jit(solution)/shard_map/ppermute | solution.py:557
  14.4 10.4 %collective-permute-start.5 = (bf16[32,3712]{1,0:T(8,128)(2,1)S(1)}, bf16[32,3712]{1,0:T(8,128)(2,1)S(1)}, u32[]{:S(2)}, u32[]{:S(2)}) collective-permute-start(bf16[32,3712]{1,0:T(8,128)(2,1)S(1)} %bitcast_convert_fusion.refs_0_), channel_id=1, source_target_pairs={{0,1},{1,0},{2,3},{3,2},{4,5},{5,4},{6,7},{7,6},{8,9},{9,8},{10,11... | collective-permute-start | bytes 712712 | tf_op jit(solution)/shard_map/ppermute | solution.py:562
  14.4 10.4 %collective-permute-start.6 = (bf16[32,3712]{1,0:T(8,128)(2,1)S(1)}, bf16[32,3712]{1,0:T(8,128)(2,1)S(1)}, u32[]{:S(2)}, u32[]{:S(2)}) collective-permute-start(bf16[32,3712]{1,0:T(8,128)(2,1)S(1)} %collective-permute-done.1.refs_1_), channel_id=1, source_target_pairs={{0,1},{1,0},{2,3},{3,2},{4,5},{5,4},{6,7},{7,6},{8,9},{9,8},{10,11... | collective-permute-start | bytes 712712 | tf_op jit(solution)/shard_map/ppermute | solution.py:562
  17.9 6.9 %collective-permute-start.7 = (bf16[32,3712]{1,0:T(8,128)(2,1)S(1)}, bf16[32,3712]{1,0:T(8,128)(2,1)S(1)}, u32[]{:S(2)}, u32[]{:S(2)}) collective-permute-start(bf16[32,3712]{1,0:T(8,128)(2,1)S(1)} %collective-permute-done.4.refs_2_), channel_id=1, source_target_pairs={{0,1},{1,0},{2,3},{3,2},{4,5},{5,4},{6,7},{7,6},{8,9},{9,8},{10,11... | collective-permute-start | bytes 712712 | tf_op jit(solution)/shard_map/ppermute | solution.py:562
  22.5 4.1 %collective-permute-start.3 = (bf16[32,3712]{1,0:T(8,128)(2,1)S(1)}, bf16[32,3712]{1,0:T(8,128)(2,1)S(1)}, u32[]{:S(2)}, u32[]{:S(2)}) collective-permute-start(bf16[32,3712]{1,0:T(8,128)(2,1)S(1)} %shard_map.206.refs_1_), channel_id=1, source_target_pairs={{0,1},{1,0},{2,3},{3,2},{4,5},{5,4},{6,7},{7,6},{8,9},{9,8},{10,11... | collective-permute-start | bytes 712712 | tf_op jit(solution)/shard_map/ppermute | solution.py:562
  30.3 3.2 %copy-start.3 = (bf16[1,32,3456]{2,1,0:T(8,128)(2,1)S(1)}, bf16[1,32,3456]{2,1,0:T(8,128)(2,1)}, u32[]{:S(2)}) copy-start(bf16[1,32,3456]{2,1,0:T(8,128)(2,1)} %param.17) | copy-start | bytes 663556
  30.3 1.7 %collective-permute-start.16 = (bf16[32,3968]{1,0:T(8,128)(2,1)S(1)}, bf16[32,3968]{1,0:T(8,128)(2,1)S(1)}, u32[]{:S(2)}, u32[]{:S(2)}) collective-permute-start(bf16[32,3968]{1,0:T(8,128)(2,1)S(1)} %get-tuple-element.60), channel_id=1, source_target_pairs={{0,1},{1,0},{2,3},{3,2},{4,5},{5,4},{6,7},{7,6},{8,9},{9,8},{10,11... | collective-permute-start | bytes 761864 | tf_op jit(solution)/shard_map/ppermute | solution.py:562
  31.8 31.6 %copy-start.7 = (s32[1,32,1]{1,2,0:T(1,128)S(1)}, s32[1,32,1]{1,2,0:T(1,128)}, u32[]{:S(2)}) copy-start(s32[1,32,1]{1,2,0:T(1,128)} %param.18) | copy-start | bytes 388
  31.8 4.6 %collective-permute-start.15 = (bf16[32,3712]{1,0:T(8,128)(2,1)S(1)}, bf16[32,3712]{1,0:T(8,128)(2,1)S(1)}, u32[]{:S(2)}, u32[]{:S(2)}) collective-permute-start(bf16[32,3712]{1,0:T(8,128)(2,1)S(1)} %get-tuple-element.58), channel_id=1, source_target_pairs={{0,1},{1,0},{2,3},{3,2},{4,5},{5,4},{6,7},{7,6},{8,9},{9,8},{10,11... | collective-permute-start | bytes 712712 | tf_op jit(solution)/shard_map/ppermute | solution.py:562
  32.0 32.1 %copy-start = (f32[1,32,3712]{2,1,0:T(8,128)S(1)}, f32[1,32,3712]{2,1,0:T(8,128)}, u32[]{:S(2)}) copy-start(f32[1,32,3712]{2,1,0:T(8,128)} %param.23) | copy-start | bytes 1425412
  32.1 32.1 %copy-start.1 = (f32[1,32,3712]{2,1,0:T(8,128)S(1)}, f32[1,32,3712]{2,1,0:T(8,128)}, u32[]{:S(2)}) copy-start(f32[1,32,3712]{2,1,0:T(8,128)} %param.24) | copy-start | bytes 1425412
  32.1 32.1 %copy-start.2 = (f32[1,32,3712]{2,1,0:T(8,128)S(1)}, f32[1,32,3712]{2,1,0:T(8,128)}, u32[]{:S(2)}) copy-start(f32[1,32,3712]{2,1,0:T(8,128)} %param.25) | copy-start | bytes 1425412
  32.1 32.1 %copy-start.4 = (f32[1,19,256]{2,0,1:T(1,128)S(1)}, f32[1,19,256]{2,0,1:T(1,128)}, u32[]{:S(2)}) copy-start(f32[1,19,256]{2,0,1:T(1,128)} %param.26) | copy-start | bytes 58372
  32.1 32.1 %copy-start.5 = (f32[1,19,256]{2,0,1:T(1,128)S(1)}, f32[1,19,256]{2,0,1:T(1,128)}, u32[]{:S(2)}) copy-start(f32[1,19,256]{2,0,1:T(1,128)} %param.27) | copy-start | bytes 58372
  32.1 32.1 %copy-start.6 = (f32[1,19,256]{2,0,1:T(1,128)S(1)}, f32[1,19,256]{2,0,1:T(1,128)}, u32[]{:S(2)}) copy-start(f32[1,19,256]{2,0,1:T(1,128)} %param.28) | copy-start | bytes 58372
  32.1 13.4 %collective-permute-start.20 = (bf16[32,3968]{1,0:T(8,128)(2,1)S(1)}, bf16[32,3968]{1,0:T(8,128)(2,1)S(1)}, u32[]{:S(2)}, u32[]{:S(2)}) collective-permute-start(bf16[32,3968]{1,0:T(8,128)(2,1)S(1)} %shard_map.207.refs_2_.refs_3_), channel_id=1, source_target_pairs={{6,4},{7,5},{0,2},{1,3},{2,0},{3,1},{4,6},{5,7},{14,12},{15,13},{8... | collective-permute-start | bytes 761864 | tf_op jit(solution)/shard_map/ppermute | solution.py:557
  33.3 11.6 %collective-permute-start.19 = (bf16[32,3712]{1,0:T(8,128)(2,1)S(1)}, bf16[32,3712]{1,0:T(8,128)(2,1)S(1)}, u32[]{:S(2)}, u32[]{:S(2)}) collective-permute-start(bf16[32,3712]{1,0:T(8,128)(2,1)S(1)} %get-tuple-element.62), channel_id=1, source_target_pairs={{0,1},{1,0},{2,3},{3,2},{4,5},{5,4},{6,7},{7,6},{8,9},{9,8},{10,11... | collective-permute-start | bytes 712712 | tf_op jit(solution)/shard_map/ppermute | solution.py:562
  33.4 9.2 %collective-permute-start.10 = (bf16[32,3456]{1,0:T(8,128)(2,1)S(1)}, bf16[32,3456]{1,0:T(8,128)(2,1)S(1)}, u32[]{:S(2)}, u32[]{:S(2)}) collective-permute-start(bf16[32,3456]{1,0:T(8,128)(2,1)S(1)} %bitcast.42), channel_id=1, source_target_pairs={{0,24},{8,16},{16,8},{24,0},{1,25},{9,17},{17,9},{25,1},{2,26},{10... | collective-permute-start | bytes 663560 | tf_op jit(solution)/shard_map/ppermute | solution.py:565
  35.9 11.0 %collective-permute-start.8 = (bf16[32,3456]{1,0:T(8,128)(2,1)S(1)}, bf16[32,3456]{1,0:T(8,128)(2,1)S(1)}, u32[]{:S(2)}, u32[]{:S(2)}) collective-permute-start(bf16[32,3456]{1,0:T(8,128)(2,1)S(1)} %bitcast.43), channel_id=1, source_target_pairs={{0,8},{8,0},{16,24},{24,16},{1,9},{9,1},{17,25},{25,17},{2,10},{10... | collective-permute-start | bytes 663560 | tf_op jit(solution)/shard_map/ppermute | solution.py:565
  36.4 11.9 %collective-permute-start.9 = (bf16[32,3456]{1,0:T(8,128)(2,1)S(1)}, bf16[32,3456]{1,0:T(8,128)(2,1)S(1)}, u32[]{:S(2)}, u32[]{:S(2)}) collective-permute-start(bf16[32,3456]{1,0:T(8,128)(2,1)S(1)} %bitcast.44), channel_id=1, source_target_pairs={{0,16},{8,24},{16,0},{24,8},{1,17},{9,25},{17,1},{25,9},{2,18},{10... | collective-permute-start | bytes 663560 | tf_op jit(solution)/shard_map/ppermute | solution.py:565
  42.7 21.4 %collective-permute-start.17 = (bf16[32,3968]{1,0:T(8,128)(2,1)S(1)}, bf16[32,3968]{1,0:T(8,128)(2,1)S(1)}, u32[]{:S(2)}, u32[]{:S(2)}) collective-permute-start(bf16[32,3968]{1,0:T(8,128)(2,1)S(1)} %shard_map.208), channel_id=1, source_target_pairs={{2,0},{3,1},{4,6},{5,7},{6,2},{7,3},{0,4},{1,5},{10,8},{11,9},{12,... | collective-permute-start | bytes 761864 | tf_op jit(solution)/shard_map/ppermute | solution.py:557
  44.8 19.2 %collective-permute-start.18 = (bf16[32,3968]{1,0:T(8,128)(2,1)S(1)}, bf16[32,3968]{1,0:T(8,128)(2,1)S(1)}, u32[]{:S(2)}, u32[]{:S(2)}) collective-permute-start(bf16[32,3968]{1,0:T(8,128)(2,1)S(1)} %shard_map.207.refs_2_.refs_3_), channel_id=1, source_target_pairs={{2,4},{3,5},{4,2},{5,3},{10,12},{11,13},{12,10},{13,11},{18,20},{1... | collective-permute-start | bytes 761864 | tf_op jit(solution)/shard_map/ppermute | solution.py:557
  45.5 18.5 %collective-permute-start.14 = (bf16[32,3712]{1,0:T(8,128)(2,1)S(1)}, bf16[32,3712]{1,0:T(8,128)(2,1)S(1)}, u32[]{:S(2)}, u32[]{:S(2)}) collective-permute-start(bf16[32,3712]{1,0:T(8,128)(2,1)S(1)} %get-tuple-element.56), channel_id=1, source_target_pairs={{0,1},{1,0},{2,3},{3,2},{4,5},{5,4},{6,7},{7,6},{8,9},{9,8},{10,11... | collective-permute-start | bytes 712712 | tf_op jit(solution)/shard_map/ppermute | solution.py:562
  46.8 17.3 %collective-permute-start.22 = (bf16[32,2560]{1,0:T(8,128)(2,1)S(1)}, bf16[32,2560]{1,0:T(8,128)(2,1)S(1)}, u32[]{:S(2)}, u32[]{:S(2)}) collective-permute-start(bf16[32,2560]{1,0:T(8,128)(2,1)S(1)} %get-tuple-element.64), channel_id=1, source_target_pairs={{4,0},{5,1},{2,6},{3,7},{0,2},{1,3},{6,4},{7,5},{12,8},{13,9},{10,... | collective-permute-start | bytes 491528 | tf_op jit(solution)/shard_map/ppermute | solution.py:557
  49.4 3.7 %collective-permute-start.11 = (bf16[32,32]{1,0:T(8,128)(2,1)S(1)}, bf16[32,32]{1,0:T(8,128)(2,1)S(1)}, u32[]{:S(2)}, u32[]{:S(2)}) collective-permute-start(bf16[32,32]{1,0:T(8,128)(2,1)S(1)} %get-tuple-element.50), channel_id=1, source_target_pairs={{0,8},{8,0},{16,24},{24,16},{1,9},{9,1},{17,25},{25,17},{2,10},{10... | collective-permute-start | bytes 6152 | tf_op jit(solution)/shard_map/ppermute | solution.py:565
  53.1 3.7 %collective-permute-start.12 = (bf16[32,32]{1,0:T(8,128)(2,1)S(1)}, bf16[32,32]{1,0:T(8,128)(2,1)S(1)}, u32[]{:S(2)}, u32[]{:S(2)}) collective-permute-start(bf16[32,32]{1,0:T(8,128)(2,1)S(1)} %get-tuple-element.51), channel_id=1, source_target_pairs={{0,16},{8,24},{16,0},{24,8},{1,17},{9,25},{17,1},{25,9},{2,18},{10... | collective-permute-start | bytes 6152 | tf_op jit(solution)/shard_map/ppermute | solution.py:565
  56.8 4.5 %collective-permute-start.13 = (bf16[32,32]{1,0:T(8,128)(2,1)S(1)}, bf16[32,32]{1,0:T(8,128)(2,1)S(1)}, u32[]{:S(2)}, u32[]{:S(2)}) collective-permute-start(bf16[32,32]{1,0:T(8,128)(2,1)S(1)} %get-tuple-element.52), channel_id=1, source_target_pairs={{0,24},{8,16},{16,8},{24,0},{1,25},{9,17},{17,9},{25,1},{2,26},{10... | collective-permute-start | bytes 6152 | tf_op jit(solution)/shard_map/ppermute | solution.py:565
  61.3 5.4 %collective-permute-start.21 = (bf16[32,1408]{1,0:T(8,128)(2,1)S(1)}, bf16[32,1408]{1,0:T(8,128)(2,1)S(1)}, u32[]{:S(2)}, u32[]{:S(2)}) collective-permute-start(bf16[32,1408]{1,0:T(8,128)(2,1)S(1)} %get-tuple-element.63), channel_id=1, source_target_pairs={{4,0},{5,1},{2,6},{3,7},{0,2},{1,3},{6,4},{7,5},{12,8},{13,9},{10,... | collective-permute-start | bytes 270344 | tf_op jit(solution)/shard_map/ppermute | solution.py:557
